TPU v7x, 32 devices: a whole 2x2x4 slice. The times are simulated.
32 devices in a mesh: grp: 2 (over y), pan: 4 (over z), en: 4 (over x, core).
Axes of the slice: x: 2, y: 2, z: 4, core: 2. Of those that a mesh axis runs over, the one named last changes fastest.
Arguments:
- retarded: float32 [2, 8, 2048, 2048], P(None, ('grp', 'en'), 'pan'), parts along dimension 1, may hold values from -0.75 to 0.75
- contact: float32 [2, 8, 2048, 128], P(None, ('grp', 'en'), 'pan'), parts along dimension 1, may hold values from -6 to 6
- atom_kind: int32 [256], replicated, may hold values from 0 to 3
- coupling: float32 [4, 3], replicated, may hold values from 0.2 to 1
- shifts: int32 [3], replicated, may hold values from 1 to 3, as said below
Outputs:
- lesser_diag: float32 [2, 8, 2048, 128], P(None, ('grp', 'en'), 'pan'), parts along dimension 1
- lesser_upper: float32 [2, 8, 2048, 128], P(None, ('grp', 'en'), 'pan'), parts along dimension 1
- sigma_next: float32 [2, 8, 2048, 128], P(None, ('grp', 'en'), 'pan'), parts along dimension 1
There are 2 independent parts, one for each index of `grp`. A program takes and returns all parts, laid end to end along the dimension named above; an argument that names none is the same for every part. Nothing has to cross between parts.
Inputs may be any that keep to these rules, and one draw needn't show every extreme that they name: `shifts`: the three entries are distinct: one is 1, one is 3, and one lies strictly between them.
All inputs are finite; a program needn't handle non-finite values.
Results may differ from a plain program's by a relative error of at most 0.0001.
Values sent between devices are 32-bit elements; how exact they have to be, the bound alone decides.
No kernel may reach another device: no remote copies, remote signals or barrier semaphores. Data moves between devices by JAX's collectives and lax.ppermute only.
A program may use at most 128 MiB of HBM per device.

v0:
```python
import functools
import math

import jax
import jax.numpy as jnp
from jax import lax
from jax.experimental import pallas as pl
from jax.experimental.pallas import tpu as pltpu
from jax.sharding import PartitionSpec as P

B = 128
ORB = 8
ITERS = 2

F32 = jnp.float32
BF16 = jnp.bfloat16


def shifted(x, axis, by):
    devices = lax.axis_size(axis)
    pairs = [(i, i + by) for i in range(devices) if 0 <= i + by < devices]
    return lax.ppermute(x, axis, pairs)


def swapped(x, axis, bit):
    return lax.ppermute(x, axis, [(i, i ^ bit) for i in range(lax.axis_size(axis))])


def spread(x, axis):
    pieces = [(0, x)]
    bit = lax.axis_size(axis) // 2
    while bit:
        pieces += [(far ^ bit, swapped(piece, axis, bit)) for far, piece in pieces]
        bit //= 2
    return pieces


def split(x):
    high = x.astype(BF16)
    return high, (x - high.astype(F32)).astype(BF16)


def dot(a, b):
    return jnp.dot(a, b, preferred_element_type=F32)


def dot_t(a, b):
    return lax.dot_general(a, b, (((1,), (1,)), ((), ())), preferred_element_type=F32)


def times(a, b):
    return dot(a[0], b[0]) + (dot(a[1], b[0]) + dot(a[0], b[1]))


def times_t(a, b):
    return dot_t(a[0], b[0]) + (dot_t(a[1], b[0]) + dot_t(a[0], b[1]))


def pair_rows(x):
    return tuple(
        jnp.concatenate([v, jnp.concatenate([v[:, B:], -v[:, :B]], axis=1)], axis=0) for v in x
    )


def rows_of(x, start, size):
    return tuple(v[start : start + size] for v in x)


def panel_kernel(local, steps, half, first, final, last, scale, *refs):
    refs = list(refs)
    k_ref = refs.pop(0)
    g_ref = refs.pop(0)
    s_ref = refs.pop(0)
    x_ref, y_ref = (refs.pop(0), refs.pop(0)) if final else (None, None)
    in_ref = None if first else refs.pop(0)
    if last:
        acc_ref = refs.pop()
        out_refs = refs
    else:
        (acc_ref,) = refs
    step = pl.program_id(0)
    k = k_ref[step]

    @pl.when(step == 0)
    def _():
        acc_ref[...] = jnp.zeros_like(acc_ref) if first else in_ref[...]

    green = split(jnp.concatenate([g_ref[0, 0], g_ref[1, 0]], axis=1))
    sr, si = s_ref[0, 0], s_ref[1, 0]
    sigma = split(
        jnp.concatenate(
            [jnp.concatenate([sr, si], axis=1), jnp.concatenate([-si, sr], axis=1)], axis=0
        )
    )
    product = split(times(green, sigma))
    for i in range(local):
        right = pair_rows(rows_of(product, i * B, B))
        if final and i < local - 1:
            both = times_t(rows_of(green, i * B, 2 * B), right)
            acc_ref[i] += both[:B]
            acc_ref[local + i] += both[B:]
        else:
            acc_ref[i] += times_t(rows_of(green, i * B, B), right)
    if final:

        @pl.when(k < half)
        def _():
            over = split(jnp.concatenate([x_ref[0, 0], x_ref[1, 0]], axis=1))
            right = pair_rows(rows_of(product, (local - 1) * B, B))
            acc_ref[2 * local - 1] += times_t(over, right)

        @pl.when(k >= half)
        def _():
            under = split(jnp.concatenate([y_ref[0, 0], y_ref[1, 0]], axis=1))
            right = pair_rows(split(times(under, sigma)))
            acc_ref[2 * local] += times_t(rows_of(green, 0, B), right)

    if last:

        @pl.when(step == steps - 1)
        def _():
            def put(ref, row, where):
                ref[0, 0, row * B : (row + 1) * B] = acc_ref[where, :, :B].T * scale
                ref[1, 0, row * B : (row + 1) * B] = acc_ref[where, :, B:].T * scale

            for i in range(local):
                put(out_refs[0], i, i)
                if final:
                    put(out_refs[1], i, local + i)
            if final:
                put(out_refs[2], 0, 2 * local)


def panel(green, source, piece, carry, edges, final, last, name):
    rows, columns = green.shape[2:]
    local = rows // B
    half = columns // B // 2
    ks = source * local + jnp.arange(local, dtype=jnp.int32)
    specs = [
        pl.BlockSpec((2, 1, rows, B), lambda j, k: (0, 0, 0, k[j])),
        pl.BlockSpec((2, 1, B, B), lambda j, k: (0, 0, j, 0)),
    ]
    operands = [green, piece]
    if final:
        specs += [
            pl.BlockSpec((2, 1, B, B), lambda j, k: (0, 0, 0, jnp.minimum(k[j], half - 1))),
            pl.BlockSpec((2, 1, B, B), lambda j, k: (0, 0, 0, jnp.maximum(k[j] - half, 0))),
        ]
        operands += edges
    count = 2 * local + 1 if final else local
    whole = pl.BlockSpec((count, B, 2 * B), lambda j, k: (0, 0, 0))
    if carry is not None:
        specs.append(whole)
        operands.append(carry)
    if last:
        tall = jax.ShapeDtypeStruct((2, 1, rows, B), F32)
        shapes = [tall] + ([tall, jax.ShapeDtypeStruct((2, 1, B, B), F32)] if final else [])
        out_specs = [pl.BlockSpec(s.shape, lambda j, k: (0, 0, 0, 0)) for s in shapes]
        scratch = [pltpu.VMEM((count, B, 2 * B), F32)]
    else:
        shapes = [jax.ShapeDtypeStruct((count, B, 2 * B), F32)]
        out_specs = [whole]
        scratch = []
    work = 3 * 2 * (2 * B) * (2 * B) * (rows + (2 * rows if final else rows)) * local
    out = pl.pallas_call(
        functools.partial(
            panel_kernel, local, local, half, carry is None, final, last, 1.0 / math.sqrt(B)
        ),
        grid_spec=pltpu.PrefetchScalarGridSpec(
            num_scalar_prefetch=1,
            grid=(local,),
            in_specs=specs,
            out_specs=out_specs,
            scratch_shapes=scratch,
        ),
        out_shape=shapes,
        cost_estimate=pl.CostEstimate(
            flops=work, bytes_accessed=8 * rows * B * local, transcendentals=0
        ),
        name=name,
    )(ks, *operands)
    return out if last else out[0]


def phonon_kernel(fars, modes, shift_ref, en_ref, contact_ref, col_ref, row_ref, *refs):
    out_ref = refs[-1]
    energy = en_ref[0]
    outer = [col_ref[:, m : m + 1] * row_ref[m : m + 1, :] for m in range(modes)]
    re, im = contact_ref[0, 0], contact_ref[1, 0]
    for far, ref in zip(fars, refs[:-1]):
        apart = jnp.abs((energy ^ far) - energy)
        weight = sum(
            jnp.where(apart == shift_ref[m], 1.0, 0.0).astype(F32) * outer[m] for m in range(modes)
        )
        re += weight * ref[0, 0]
        im += weight * ref[1, 0]
    out_ref[0, 0] = re
    out_ref[1, 0] = im


def phonon(shifts, energy, contact, columns, lines, pieces):
    rows = contact.shape[2]
    modes = shifts.shape[0]
    block = pl.BlockSpec((2, 1, B, B), lambda i, *_: (0, 0, i, 0))
    return pl.pallas_call(
        functools.partial(phonon_kernel, [far for far, _ in pieces], modes),
        grid_spec=pltpu.PrefetchScalarGridSpec(
            num_scalar_prefetch=2,
            grid=(rows // B,),
            in_specs=[
                block,
                pl.BlockSpec((B, modes), lambda i, *_: (i, 0)),
                pl.BlockSpec((modes, B), lambda i, *_: (0, i)),
            ]
            + [block] * len(pieces),
            out_specs=block,
        ),
        out_shape=jax.ShapeDtypeStruct(contact.shape, F32),
        cost_estimate=pl.CostEstimate(
            flops=rows * B * 20, bytes_accessed=8 * rows * B * 5, transcendentals=0
        ),
        name="phonon",
    )(shifts, energy, contact, columns, lines, *[piece for _, piece in pieces])


def body(retarded, contact, atom_kind, coupling, shifts):
    rows, columns = retarded.shape[2:]
    pan = lax.axis_index("pan")
    energy = lax.axis_index("en").astype(jnp.int32).reshape(1)
    atoms = rows // ORB
    kinds = lax.dynamic_slice_in_dim(atom_kind, pan * atoms, atoms, 0)
    per_atom = sum(
        jnp.where(kinds[:, None] == kind, coupling[kind][None, :], 0.0)
        for kind in range(coupling.shape[0])
    )
    per_row = jnp.repeat(per_atom, ORB, axis=0)
    per_line = jnp.repeat(per_atom.T, ORB, axis=1)
    edges = None
    sigma = contact
    for rounds in range(ITERS):
        final = rounds == ITERS - 1
        pieces = spread(sigma, "pan")
        if final:
            edges = [
                shifted(retarded[:, :, :B, : columns // 2], "pan", -1),
                shifted(retarded[:, :, -B:, columns // 2 :], "pan", 1),
            ]
        carry = None
        for number, (far, piece) in enumerate(pieces):
            last = number == len(pieces) - 1
            carry = panel(
                retarded, pan ^ far, piece, carry, edges, final, last, f"panel{rounds}{number}"
            )
        lesser_diag = carry[0]
        if final:
            upper, above = carry[1:]
            lesser_upper = upper.at[:, :, -B:].add(shifted(above, "pan", -1))
        found = spread(lesser_diag, "en")[1:]
        sigma = phonon(shifts, energy, contact, per_row, per_line, found)
    return (lesser_diag, lesser_upper, sigma)


def solution(mesh):
    spread_spec = P(None, ("grp", "en"), "pan", None)
    return jax.shard_map(
        body,
        mesh=mesh,
        in_specs=(spread_spec, spread_spec, P(), P(), P()),
        out_specs=(spread_spec, spread_spec, spread_spec),
        check_vma=False,
    )
```

profile of v0, /device:TPU:0, one launch (start us, length us, event | category | flops | bytes accessed | tf_op | source)
XLA Modules:
  0.0 187.6 jit_solution(8925997603551950143)
XLA Ops:
  0.6 4.1 %collective-permute-start = (f32[2,1,512,128]{3,2,1,0:T(8,128)}, f32[2,1,512,128]{3,2,1,0:T(8,128)}, u32[]{:S(2)}, u32[]{:S(2)}) collective-permute-start(f32[2,1,512,128]{3,2,1,0:T(8,128)} %contact_ref.3), channel_id=1, source_target_pairs={{0,8},{4,12},{8,0},{12,4},{1,9},{5,13},{9,1},{13,5},{2,10},{6,14},... | collective-permute-start | bytes 1572872 | tf_op jit(solution)/shard_map/ppermute | solution.py:26
  4.8 1.6 collective-permute-start.2
  6.3 2.8 %fusion = (f32[2,1,128,1024]{3,2,1,0:T(8,128)S(1)}, f32[2,1,128,1024]{3,2,1,0:T(8,128)}) fusion(f32[2,1,512,2048]{3,2,1,0:T(8,128)} %refs_1_.15), kind=kLoop, calls=%fused_computation.16 | loop fusion | bytes 4194304 | tf_op jit(solution)/shard_map/slice | solution.py:246
  10.4 4.6 %collective-permute-start.9 = (f32[2,1,128,1024]{3,2,1,0:T(8,128)S(1)}, f32[2,1,128,1024]{3,2,1,0:T(8,128)S(1)}, u32[]{:S(2)}, u32[]{:S(2)}) collective-permute-start(f32[2,1,128,1024]{3,2,1,0:T(8,128)S(1)} %get-tuple-element.23), channel_id=1, source_target_pairs={{0,4},{4,8},{8,12},{1,5},{5,9},{9,13},{2,6},{6,10},{10,14},{3,7},{... | collective-permute-start | bytes 3145736 | tf_op jit(solution)/shard_map/ppermute | solution.py:22
  16.6 12.5 %collective-permute-done.refs_2_ = f32[2,1,512,128]{3,2,1,0:T(8,128)} collective-permute-done((f32[2,1,512,128]{3,2,1,0:T(8,128)}, f32[2,1,512,128]{3,2,1,0:T(8,128)}, u32[]{:S(2)}, u32[]{:S(2)}) %collective-permute-start) | collective-permute-done | bytes 524320 | tf_op jit(solution)/shard_map/ppermute | solution.py:26
  29.7 7.6 %panel00.1.refs_3_ = f32[4,128,256]{2,1,0:T(8,128)} custom-call(s32[4]{0:T(128)} %iota_add_fusion.refs_0_, f32[2,1,512,2048]{3,2,1,0:T(8,128)} %refs_1_.15, f32[2,1,512,128]{3,2,1,0:T(8,128)} %contact_ref.3), custom_call_target="tpu_custom_call" | custom-call | flops 1610612736 | bytes 2097152 | tf_op jit(solution)/shard_map/panel00/pallas_call | solution.py:165
  37.4 7.8 %panel01.1.refs_3_ = f32[4,128,256]{2,1,0:T(8,128)} custom-call(s32[4]{0:T(128)} %iota_add_fusion.1.refs_0_, f32[2,1,512,2048]{3,2,1,0:T(8,128)} %refs_1_.15, f32[2,1,512,128]{3,2,1,0:T(8,128)} %collective-permute-done.refs_2_, f32[4,128,256]{2,1,0:T(8,128)} %panel00.1.refs_3_), custom_call_target="tpu_custom_call" | custom-call | flops 1610612736 | bytes 2097152 | tf_op jit(solution)/shard_map/panel01/pallas_call | solution.py:165
  45.2 7.8 %panel02.1.refs_3_ = f32[4,128,256]{2,1,0:T(8,128)} custom-call(s32[4]{0:T(128)} %iota_add_fusion.2.refs_0_, f32[2,1,512,2048]{3,2,1,0:T(8,128)} %refs_1_.15, f32[2,1,512,128]{3,2,1,0:T(8,128)} %collective-permute-done.2.refs_2_, f32[4,128,256]{2,1,0:T(8,128)} %panel01.1.refs_3_), custom_call_target="tpu_custom_call" | custom-call | flops 1610612736 | bytes 2097152 | tf_op jit(solution)/shard_map/panel02/pallas_call | solution.py:165
  53.0 9.2 %collective-permute-done.1.refs_2_ = f32[2,1,512,128]{3,2,1,0:T(8,128)} collective-permute-done((f32[2,1,512,128]{3,2,1,0:T(8,128)}, f32[2,1,512,128]{3,2,1,0:T(8,128)}, u32[]{:S(2)}, u32[]{:S(2)}) %collective-permute-start.1) | collective-permute-done | bytes 524320 | tf_op jit(solution)/shard_map/ppermute | solution.py:26
  62.2 8.0 %panel03.1 = f32[2,1,512,128]{3,2,1,0:T(8,128)} custom-call(s32[4]{0:T(128)} %iota_add_fusion.3.refs_0_, f32[2,1,512,2048]{3,2,1,0:T(8,128)} %refs_1_.15, f32[2,1,512,128]{3,2,1,0:T(8,128)} %collective-permute-done.1.refs_2_, f32[4,128,256]{2,1,0:T(8,128)} %panel02.1.refs_3_), custom_call_target="tpu_custom_call" | custom-call | flops 1610612736 | bytes 2097152 | tf_op jit(solution)/shard_map/panel03/pallas_call | solution.py:165
  70.3 1.5 collective-permute-start.3
  72.0 11.1 %collective-permute-done.3.refs_0_ = f32[2,1,512,128]{3,2,1,0:T(8,128)} collective-permute-done((f32[2,1,512,128]{3,2,1,0:T(8,128)}, f32[2,1,512,128]{3,2,1,0:T(8,128)}, u32[]{:S(2)}, u32[]{:S(2)}) %collective-permute-start.3) | collective-permute-done | bytes 524320 | tf_op jit(solution)/shard_map/ppermute | solution.py:26
  85.4 4.5 %phonon.2.refs_2_ = f32[2,1,512,128]{3,2,1,0:T(8,128)} custom-call(s32[3]{0:T(128)} %shift_ref.3, s32[1]{0:T(128)} %bitcast.en_ref, f32[2,1,512,128]{3,2,1,0:T(8,128)} %contact_ref.3, f32[512,3]{1,0:T(8,128)} %broadcast_bitcast_fusion.col_ref, f32[3,512]{1,0:T(4,128)} %reshape.61.row_ref, f32[2,1,512,128]{3,2,1,0:T(8,128)} %collective-permute-done.3.refs_0_, ...), custom_call_target="tpu_custom_call" | custom-call | flops 1310720 | bytes 2621440 | tf_op jit(solution)/shard_map/phonon/pallas_call | solution.py:205
  89.9 1.7 collective-permute-start.6
  93.1 23.2 %collective-permute-done.6.refs_2_ = f32[2,1,512,128]{3,2,1,0:T(8,128)} collective-permute-done((f32[2,1,512,128]{3,2,1,0:T(8,128)}, f32[2,1,512,128]{3,2,1,0:T(8,128)}, u32[]{:S(2)}, u32[]{:S(2)}) %collective-permute-start.6) | collective-permute-done | bytes 524320 | tf_op jit(solution)/shard_map/ppermute | solution.py:26
  118.3 9.1 %panel10.1.refs_5_ = f32[9,128,256]{2,1,0:T(8,128)} custom-call(s32[4]{0:T(128)} %iota_add_fusion.refs_0_, f32[2,1,512,2048]{3,2,1,0:T(8,128)} %refs_1_.15, f32[2,1,512,128]{3,2,1,0:T(8,128)} %phonon.2.refs_2_, f32[2,1,128,1024]{3,2,1,0:T(8,128)} %copy-done, f32[2,1,128,1024]{3,2,1,0:T(8,128)} %copy-done.1), custom_call_target="tpu_custom_call" | custom-call | flops 2415919104 | bytes 2097152 | tf_op jit(solution)/shard_map/panel10/pallas_call | solution.py:165
  127.4 10.5 %panel11.1.refs_5_ = f32[9,128,256]{2,1,0:T(8,128)} custom-call(s32[4]{0:T(128)} %iota_add_fusion.1.refs_0_, f32[2,1,512,2048]{3,2,1,0:T(8,128)} %refs_1_.15, f32[2,1,512,128]{3,2,1,0:T(8,128)} %collective-permute-done.6.refs_2_, f32[2,1,128,1024]{3,2,1,0:T(8,128)} %copy-done, f32[2,1,128,1024]{3,2,1,0:T(8,128)} %copy-done.1, f32[9,128,256]{2,1,0:T(8,128)} %panel10.1.refs_5_), custom_call_target="tpu_custom_call" | custom-call | flops 2415919104 | bytes 2097152 | tf_op jit(solution)/shard_map/panel11/pallas_call | solution.py:165
  137.9 9.5 %panel12.1.refs_5_ = f32[9,128,256]{2,1,0:T(8,128)} custom-call(s32[4]{0:T(128)} %iota_add_fusion.2.refs_0_, f32[2,1,512,2048]{3,2,1,0:T(8,128)} %refs_1_.15, f32[2,1,512,128]{3,2,1,0:T(8,128)} %collective-permute-done.10.refs_2_, f32[2,1,128,1024]{3,2,1,0:T(8,128)} %copy-done, f32[2,1,128,1024]{3,2,1,0:T(8,128)} %copy-done.1, f32[9,128,256]{2,1,0:T(8,128)} %panel11.1.refs_5_), custom_call_target="tpu_custom_call" | custom-call | flops 2415919104 | bytes 2097152 | tf_op jit(solution)/shard_map/panel12/pallas_call | solution.py:165
  147.4 10.8 %panel13.1 = (f32[2,1,512,128]{3,2,1,0:T(8,128)}, f32[2,1,512,128]{3,2,1,0:T(8,128)}, f32[2,1,128,128]{3,2,1,0:T(8,128)}) custom-call(s32[4]{0:T(128)} %iota_add_fusion.3.refs_0_, f32[2,1,512,2048]{3,2,1,0:T(8,128)} %refs_1_.15, f32[2,1,512,128]{3,2,1,0:T(8,128)} %collective-permute-done.7.refs_2_, f32[2,1,128,1024]{3,2,1,0:T(8,128)} %copy-done, ...), custom_call_target="tpu_custom_call" | custom-call | flops 2415919104 | bytes 2097152 | tf_op jit(solution)/shard_map/panel13/pallas_call | solution.py:165
  158.2 1.5 collective-permute-start.12
  159.8 12.1 %collective-permute-done.12.refs_0_ = f32[2,1,512,128]{3,2,1,0:T(8,128)S(1)} collective-permute-done((f32[2,1,512,128]{3,2,1,0:T(8,128)}, f32[2,1,512,128]{3,2,1,0:T(8,128)S(1)}, u32[]{:S(2)}, u32[]{:S(2)}) %collective-permute-start.12) | collective-permute-done | bytes 524320 | tf_op jit(solution)/shard_map/ppermute | solution.py:26
  173.1 6.7 %collective-permute-done.11 = f32[2,1,128,128]{3,2,1,0:T(8,128)S(1)} collective-permute-done((f32[2,1,128,128]{3,2,1,0:T(8,128)}, f32[2,1,128,128]{3,2,1,0:T(8,128)S(1)}, u32[]{:S(2)}, u32[]{:S(2)}) %collective-permute-start.11) | collective-permute-done | bytes 131104 | tf_op jit(solution)/shard_map/ppermute | solution.py:22
  179.8 1.6 add_dynamic-update-slice_fusion
  183.1 4.5 %phonon.3 = f32[2,1,512,128]{3,2,1,0:T(8,128)} custom-call(s32[3]{0:T(128)} %shift_ref.3, s32[1]{0:T(128)} %bitcast.en_ref, f32[2,1,512,128]{3,2,1,0:T(8,128)} %contact_ref.3, f32[512,3]{1,0:T(8,128)} %broadcast_bitcast_fusion.col_ref, f32[3,512]{1,0:T(4,128)} %reshape.61.row_ref, f32[2,1,512,128]{3,2,1,0:T(8,128)} %copy-done.2, ...), custom_call_target="tpu_custom_call" | custom-call | flops 1310720 | bytes 2621440 | tf_op jit(solution)/shard_map/phonon/pallas_call | solution.py:205
  (44 shorter events, 12.2 us)
Async XLA Ops:
  0.6 28.5 %collective-permute-start = (f32[2,1,512,128]{3,2,1,0:T(8,128)}, f32[2,1,512,128]{3,2,1,0:T(8,128)}, u32[]{:S(2)}, u32[]{:S(2)}) collective-permute-start(f32[2,1,512,128]{3,2,1,0:T(8,128)} %contact_ref.3), channel_id=1, source_target_pairs={{0,8},{4,12},{8,0},{12,4},{1,9},{5,13},{9,1},{13,5},{2,10},{6,14},... | collective-permute-start | bytes 1572872 | tf_op jit(solution)/shard_map/ppermute | solution.py:26
  4.8 40.4 %collective-permute-start.2 = (f32[2,1,512,128]{3,2,1,0:T(8,128)}, f32[2,1,512,128]{3,2,1,0:T(8,128)}, u32[]{:S(2)}, u32[]{:S(2)}) collective-permute-start(f32[2,1,512,128]{3,2,1,0:T(8,128)} %contact_ref.3), channel_id=1, source_target_pairs={{0,4},{4,0},{8,12},{12,8},{1,5},{5,1},{9,13},{13,9},{2,6},{6,2},{1... | collective-permute-start | bytes 1572872 | tf_op jit(solution)/shard_map/ppermute | solution.py:26
  9.1 107.2 %collective-permute-start.8 = (f32[2,1,128,1024]{3,2,1,0:T(8,128)}, f32[2,1,128,1024]{3,2,1,0:T(8,128)S(1)}, u32[]{:S(2)}, u32[]{:S(2)}) collective-permute-start(f32[2,1,128,1024]{3,2,1,0:T(8,128)} %get-tuple-element.24), channel_id=1, source_target_pairs={{4,0},{8,4},{12,8},{5,1},{9,5},{13,9},{6,2},{10,6},{14,10},{7,3},{... | collective-permute-start | bytes 3145736 | tf_op jit(solution)/shard_map/ppermute | solution.py:22
  10.4 105.9 %collective-permute-start.9 = (f32[2,1,128,1024]{3,2,1,0:T(8,128)S(1)}, f32[2,1,128,1024]{3,2,1,0:T(8,128)S(1)}, u32[]{:S(2)}, u32[]{:S(2)}) collective-permute-start(f32[2,1,128,1024]{3,2,1,0:T(8,128)S(1)} %get-tuple-element.23), channel_id=1, source_target_pairs={{0,4},{4,8},{8,12},{1,5},{5,9},{9,13},{2,6},{6,10},{10,14},{3,7},{... | collective-permute-start | bytes 3145736 | tf_op jit(solution)/shard_map/ppermute | solution.py:22
  29.1 33.1 %collective-permute-start.1 = (f32[2,1,512,128]{3,2,1,0:T(8,128)}, f32[2,1,512,128]{3,2,1,0:T(8,128)}, u32[]{:S(2)}, u32[]{:S(2)}) collective-permute-start(f32[2,1,512,128]{3,2,1,0:T(8,128)} %collective-permute-done.refs_2_), channel_id=1, source_target_pairs={{0,4},{4,0},{8,12},{12,8},{1,5},{5,1},{9,13},{13,9},{2,6},{6,2},{1... | collective-permute-start | bytes 1572872 | tf_op jit(solution)/shard_map/ppermute | solution.py:26
  53.0 18.8 %copy-start.6 = (s32[256]{0:T(256)S(1)}, s32[256]{0:T(256)}, u32[]{:S(2)}) copy-start(s32[256]{0:T(256)} %param.9) | copy-start | bytes 3076
  53.0 18.9 %copy-start.5 = (f32[4,3]{1,0:T(4,128)S(1)}, f32[4,3]{1,0:T(4,128)}, u32[]{:S(2)}) copy-start(f32[4,3]{1,0:T(4,128)} %param.10) | copy-start | bytes 148
  70.3 12.8 %collective-permute-start.3 = (f32[2,1,512,128]{3,2,1,0:T(8,128)}, f32[2,1,512,128]{3,2,1,0:T(8,128)}, u32[]{:S(2)}, u32[]{:S(2)}) collective-permute-start(f32[2,1,512,128]{3,2,1,0:T(8,128)} %panel03.1), channel_id=1, source_target_pairs={{0,2},{1,3},{2,0},{3,1},{4,6},{5,7},{6,4},{7,5},{8,10},{9,11},{10,... | collective-permute-start | bytes 1572872 | tf_op jit(solution)/shard_map/ppermute | solution.py:26
  71.9 12.9 %collective-permute-start.4 = (f32[2,1,512,128]{3,2,1,0:T(8,128)}, f32[2,1,512,128]{3,2,1,0:T(8,128)}, u32[]{:S(2)}, u32[]{:S(2)}) collective-permute-start(f32[2,1,512,128]{3,2,1,0:T(8,128)} %panel03.1), channel_id=1, source_target_pairs={{0,1},{1,0},{2,3},{3,2},{4,5},{5,4},{6,7},{7,6},{8,9},{9,8},{10,11... | collective-permute-start | bytes 1572872 | tf_op jit(solution)/shard_map/ppermute | solution.py:26
  83.1 2.3 %collective-permute-start.5 = (f32[2,1,512,128]{3,2,1,0:T(8,128)}, f32[2,1,512,128]{3,2,1,0:T(8,128)}, u32[]{:S(2)}, u32[]{:S(2)}) collective-permute-start(f32[2,1,512,128]{3,2,1,0:T(8,128)} %collective-permute-done.3.refs_0_), channel_id=1, source_target_pairs={{0,1},{1,0},{2,3},{3,2},{4,5},{5,4},{6,7},{7,6},{8,9},{9,8},{10,11... | collective-permute-start | bytes 1572872 | tf_op jit(solution)/shard_map/ppermute | solution.py:26
  89.9 26.4 %collective-permute-start.6 = (f32[2,1,512,128]{3,2,1,0:T(8,128)}, f32[2,1,512,128]{3,2,1,0:T(8,128)}, u32[]{:S(2)}, u32[]{:S(2)}) collective-permute-start(f32[2,1,512,128]{3,2,1,0:T(8,128)} %phonon.2.refs_2_), channel_id=1, source_target_pairs={{0,8},{4,12},{8,0},{12,4},{1,9},{5,13},{9,1},{13,5},{2,10},{6,14},... | collective-permute-start | bytes 1572872 | tf_op jit(solution)/shard_map/ppermute | solution.py:26
  91.6 46.3 %collective-permute-start.10 = (f32[2,1,512,128]{3,2,1,0:T(8,128)}, f32[2,1,512,128]{3,2,1,0:T(8,128)}, u32[]{:S(2)}, u32[]{:S(2)}) collective-permute-start(f32[2,1,512,128]{3,2,1,0:T(8,128)} %phonon.2.refs_2_), channel_id=1, source_target_pairs={{0,4},{4,0},{8,12},{12,8},{1,5},{5,1},{9,13},{13,9},{2,6},{6,2},{1... | collective-permute-start | bytes 1572872 | tf_op jit(solution)/shard_map/ppermute | solution.py:26
  116.3 31.1 %collective-permute-start.7 = (f32[2,1,512,128]{3,2,1,0:T(8,128)}, f32[2,1,512,128]{3,2,1,0:T(8,128)}, u32[]{:S(2)}, u32[]{:S(2)}) collective-permute-start(f32[2,1,512,128]{3,2,1,0:T(8,128)} %collective-permute-done.6.refs_2_), channel_id=1, source_target_pairs={{0,4},{4,0},{8,12},{12,8},{1,5},{5,1},{9,13},{13,9},{2,6},{6,2},{1... | collective-permute-start | bytes 1572872 | tf_op jit(solution)/shard_map/ppermute | solution.py:26
  116.3 1.0 copy-start
  117.3 1.0 copy-start.1
  158.2 13.6 %collective-permute-start.12 = (f32[2,1,512,128]{3,2,1,0:T(8,128)}, f32[2,1,512,128]{3,2,1,0:T(8,128)S(1)}, u32[]{:S(2)}, u32[]{:S(2)}) collective-permute-start(f32[2,1,512,128]{3,2,1,0:T(8,128)} %get-tuple-element.15), channel_id=1, source_target_pairs={{0,2},{1,3},{2,0},{3,1},{4,6},{5,7},{6,4},{7,5},{8,10},{9,11},{10,... | collective-permute-start | bytes 1572872 | tf_op jit(solution)/shard_map/ppermute | solution.py:26
  159.8 21.7 %collective-permute-start.13 = (f32[2,1,512,128]{3,2,1,0:T(8,128)}, f32[2,1,512,128]{3,2,1,0:T(8,128)S(1)}, u32[]{:S(2)}, u32[]{:S(2)}) collective-permute-start(f32[2,1,512,128]{3,2,1,0:T(8,128)} %get-tuple-element.15), channel_id=1, source_target_pairs={{0,1},{1,0},{2,3},{3,2},{4,5},{5,4},{6,7},{7,6},{8,9},{9,8},{10,11... | collective-permute-start | bytes 1572872 | tf_op jit(solution)/shard_map/ppermute | solution.py:26
  171.8 9.6 %copy-start.2 = (f32[2,1,512,128]{3,2,1,0:T(8,128)}, f32[2,1,512,128]{3,2,1,0:T(8,128)S(1)}, u32[]{:S(2)}) copy-start(f32[2,1,512,128]{3,2,1,0:T(8,128)S(1)} %collective-permute-done.12.refs_0_) | copy-start | bytes 1572868
  171.8 9.6 %collective-permute-start.14 = (f32[2,1,512,128]{3,2,1,0:T(8,128)S(1)}, f32[2,1,512,128]{3,2,1,0:T(8,128)S(1)}, u32[]{:S(2)}, u32[]{:S(2)}) collective-permute-start(f32[2,1,512,128]{3,2,1,0:T(8,128)S(1)} %collective-permute-done.12.refs_0_), channel_id=1, source_target_pairs={{0,1},{1,0},{2,3},{3,2},{4,5},{5,4},{6,7},{7,6},{8,9},{9,8},{10,11... | collective-permute-start | bytes 1572872 | tf_op jit(solution)/shard_map/ppermute | solution.py:26
  171.8 8.0 %collective-permute-start.11 = (f32[2,1,128,128]{3,2,1,0:T(8,128)}, f32[2,1,128,128]{3,2,1,0:T(8,128)S(1)}, u32[]{:S(2)}, u32[]{:S(2)}) collective-permute-start(f32[2,1,128,128]{3,2,1,0:T(8,128)} %get-tuple-element.20), channel_id=1, source_target_pairs={{4,0},{8,4},{12,8},{5,1},{9,5},{13,9},{6,2},{10,6},{14,10},{7,3},{... | collective-permute-start | bytes 393224 | tf_op jit(solution)/shard_map/ppermute | solution.py:22
  181.4 0.8 copy-start.3
  182.2 0.8 copy-start.4
where the time goes:
time: 188 us
  Pallas kernels  80.3 us (43%)
  waiting for transfers between devices  75.4 us (40%)
  starting transfers between devices  19.2 us (10%)
  local copies, waits for them, and re-layouts  7.89 us (4%)
  other arithmetic  4 us (2%)
    pallas_call x8, Pallas kernels, panel(): pl.pallas_call(functools.partial(panel_kernel, local, local, half, carry...  71.2 us
    ppermute x12, waiting for transfers between devices, swapped(): lax.ppermute(x, axis, [(i, i ^ bit) for i in range(lax.axis_size(axis))])  68.7 us
    ppermute x12, starting transfers between devices, swapped(): lax.ppermute(x, axis, [(i, i ^ bit) for i in range(lax.axis_size(axis))])  12 us
    pallas_call x2, Pallas kernels, phonon(): pl.pallas_call(functools.partial(phonon_kernel, [far for far, _ in pieces...  9.06 us
    ppermute x3, starting transfers between devices, shifted(): return lax.ppermute(x, axis, pairs)  7.17 us
    ppermute x3, waiting for transfers between devices, shifted(): return lax.ppermute(x, axis, pairs)  6.72 us
  transfers between devices with their start and end apart: 15, of which 7 were waited for; matrix products, arithmetic and copies ran while one was open for 4% of the time, Pallas kernels for 35%

commit v1 on v0

v1 whole, which is shorter than its diff:
```python
import functools
import math

import jax
import jax.numpy as jnp
from jax import lax
from jax.experimental import pallas as pl
from jax.experimental.pallas import tpu as pltpu
from jax.sharding import PartitionSpec as P


B = 128
ORB = 8
ITERS = 2
VMEM_BYTES = 28 * 2**20

F32 = jnp.float32
BF16 = jnp.bfloat16


def swapped(x, axis, bit):
    return lax.ppermute(x, axis, [(i, i ^ bit) for i in range(lax.axis_size(axis))])


def spread(x, axis):
    pieces = [(0, x)]
    bit = lax.axis_size(axis) // 2
    while bit:
        found = []
        for far, piece in pieces:
            found.append((far ^ bit, swapped(piece, axis, bit)))
        pieces += found
        bit //= 2
    return pieces


def split(x):
    high = x.astype(BF16)
    return high, (x - high.astype(F32)).astype(BF16)


def dot(a, b):
    return jnp.dot(a, b, preferred_element_type=F32)


def dot_t(a, b):
    return lax.dot_general(a, b, (((1,), (1,)), ((), ())), preferred_element_type=F32)


def times(a, b):
    return dot(a[0], b[0]) + (dot(a[1], b[0]) + dot(a[0], b[1]))


def times_t(a, b):
    return dot_t(a[0], b[0]) + (dot_t(a[1], b[0]) + dot_t(a[0], b[1]))


def total(terms):
    return functools.reduce(lambda a, b: a + b, terms)


def pair_rows(x):
    return tuple(
        jnp.concatenate([v, jnp.concatenate([v[:, B:], -v[:, :B]], axis=1)], axis=0) for v in x
    )


def rows_of(x, start, size):
    return tuple(v[start : start + size] for v in x)


def panel_kernel(local, many, far, half, diag, upper, first, last, scale, *refs):
    refs = list(refs)
    at_ref, g_ref, s_ref = refs[:3]
    refs = refs[3:]
    if upper:
        even_ref, odd_ref = refs[:2]
        refs = refs[2:]
    kinds = ([local] if diag else []) + ([local + 1] if upper else [])
    ins = []
    if not first:
        ins, refs = refs[: len(kinds)], refs[len(kinds) :]
    if last:
        outs, accs = refs[: len(refs) - len(kinds)], refs[len(refs) - len(kinds) :]
    else:
        accs = refs
    step = pl.program_id(0)

    @pl.when(step == 0)
    def _():
        for i, acc in enumerate(accs):
            acc[...] = jnp.zeros_like(acc) if first else ins[i][...]

    greens, sigmas, products = [], [], []
    for u in range(many):
        cut = slice(u * B, (u + 1) * B)
        green = split(jnp.concatenate([g_ref[0, 0, :, cut], g_ref[1, 0, :, cut]], axis=1))
        sr, si = s_ref[0, 0, cut], s_ref[1, 0, cut]
        sigma = split(
            jnp.concatenate(
                [jnp.concatenate([sr, si], axis=1), jnp.concatenate([-si, sr], axis=1)], axis=0
            )
        )
        greens.append(green)
        sigmas.append(sigma)
        products.append(split(times(green, sigma)))
    acc_diag = accs[0] if diag else None
    acc_upper = accs[-1] if upper else None
    for i in range(local):
        start = 0 if diag else 1
        size = (1 if diag else 0) + (1 if upper and i < local - 1 else 0)
        if not size:
            continue
        terms = total(
            times_t(rows_of(green, (i + start) * B, size * B), pair_rows(rows_of(product, i * B, B)))
            for green, product in zip(greens, products)
        )
        if diag:
            acc_diag[i] += terms[:B]
        if upper and i < local - 1:
            acc_upper[i] += terms[-B:]
    if upper:
        pan = at_ref[0]
        below = ((pan ^ far) * (local // many) + step) * many < half
        own = (pan % 2 == 0) == below

        def extra(u):
            cut = slice(u * B, (u + 1) * B)
            return split(
                jnp.concatenate(
                    [
                        jnp.where(own, even_ref[j, 0, :, cut], odd_ref[j, 0, :, cut])
                        for j in range(2)
                    ],
                    axis=1,
                )
            )

        @pl.when(below)
        def _():
            acc_upper[local - 1] += total(
                times_t(extra(u), pair_rows(rows_of(products[u], (local - 1) * B, B)))
                for u in range(many)
            )

        @pl.when(jnp.logical_not(below))
        def _():
            acc_upper[local] += total(
                times_t(rows_of(greens[u], 0, B), pair_rows(split(times(extra(u), sigmas[u]))))
                for u in range(many)
            )

    if last:

        @pl.when(step == local // many - 1)
        def _():
            def put(ref, row, acc, where):
                ref[0, 0, row * B : (row + 1) * B] = acc[where, :, :B].T * scale
                ref[1, 0, row * B : (row + 1) * B] = acc[where, :, B:].T * scale

            free = list(outs)
            if diag:
                ref = free.pop(0)
                for i in range(local):
                    put(ref, i, acc_diag, i)
            if upper:
                for i in range(local):
                    put(free[0], i, acc_upper, i)
                put(free[1], 0, acc_upper, local)


def panel(at, green, far, piece, carry, edges, diag, upper, last):
    rows, columns = green.shape[2:]
    local = rows // B
    many = 2 if local % 2 == 0 else 1
    steps = local // many
    half = columns // B // 2
    specs = [
        pl.BlockSpec((2, 1, rows, many * B), lambda j, at: (0, 0, 0, (at[0] ^ far) * steps + j)),
        pl.BlockSpec((2, 1, many * B, B), lambda j, at: (0, 0, j, 0)),
    ]
    operands = [green, piece]
    if upper:
        parts = half // many
        edge = pl.BlockSpec(
            (2, 1, B, many * B), lambda j, at: (0, 0, 0, ((at[0] ^ far) * steps + j) % parts)
        )
        specs += [edge, edge]
        operands += edges
    counts = ([local] if diag else []) + ([local + 1] if upper else [])
    sums = [jax.ShapeDtypeStruct((count, B, 2 * B), F32) for count in counts]
    sum_specs = [pl.BlockSpec(s.shape, lambda j, at: (0, 0, 0)) for s in sums]
    if carry is not None:
        specs += sum_specs
        operands += carry
    if last:
        tall = jax.ShapeDtypeStruct((2, 1, rows, B), F32)
        small = jax.ShapeDtypeStruct((2, 1, B, B), F32)
        shapes = ([tall] if diag else []) + ([tall, small] if upper else [])
        out_specs = [pl.BlockSpec(s.shape, lambda j, at: (0, 0, 0, 0)) for s in shapes]
        scratch = [pltpu.VMEM(s.shape, F32) for s in sums]
    else:
        shapes, out_specs, scratch = sums, sum_specs, []
    work = 3 * 2 * (2 * B) * (2 * B) * rows * local * (1 + len(counts))
    return pl.pallas_call(
        functools.partial(
            panel_kernel,
            local,
            many,
            far,
            half,
            diag,
            upper,
            carry is None,
            last,
            1.0 / math.sqrt(B),
        ),
        grid_spec=pltpu.PrefetchScalarGridSpec(
            num_scalar_prefetch=1,
            grid=(steps,),
            in_specs=specs,
            out_specs=out_specs,
            scratch_shapes=scratch,
        ),
        out_shape=shapes,
        compiler_params=pltpu.CompilerParams(vmem_limit_bytes=VMEM_BYTES),
        cost_estimate=pl.CostEstimate(
            flops=work, bytes_accessed=8 * rows * B * local, transcendentals=0
        ),
    )(at, *operands)


def phonon_kernel(fars, modes, shift_ref, at_ref, contact_ref, col_ref, row_ref, *refs):
    out_ref = refs[-1]
    energy = at_ref[1]
    chosen = []
    for far in fars:
        apart = jnp.abs((energy ^ far) - energy)
        chosen.append([jnp.where(apart == shift_ref[m], 1.0, 0.0).astype(F32) for m in range(modes)])
    for start in range(0, contact_ref.shape[2], B):
        rows = slice(start, start + B)
        outer = [col_ref[rows, m : m + 1] * row_ref[m : m + 1, rows] for m in range(modes)]
        re, im = contact_ref[0, 0, rows], contact_ref[1, 0, rows]
        for weights, ref in zip(chosen, refs[:-1]):
            weight = total(w * o for w, o in zip(weights, outer))
            re += weight * ref[0, 0, rows]
            im += weight * ref[1, 0, rows]
        out_ref[0, 0, rows] = re
        out_ref[1, 0, rows] = im


def phonon(shifts, at, contact, columns, lines, pieces):
    rows = contact.shape[2]
    modes = shifts.shape[0]
    whole = pl.BlockSpec(contact.shape, lambda i, *_: (0, 0, 0, 0))
    return pl.pallas_call(
        functools.partial(phonon_kernel, [far for far, _ in pieces], modes),
        grid_spec=pltpu.PrefetchScalarGridSpec(
            num_scalar_prefetch=2,
            grid=(1,),
            in_specs=[
                whole,
                pl.BlockSpec((rows, modes), lambda i, *_: (0, 0)),
                pl.BlockSpec((modes, rows), lambda i, *_: (0, 0)),
            ]
            + [whole] * len(pieces),
            out_specs=whole,
        ),
        out_shape=jax.ShapeDtypeStruct(contact.shape, F32),
        compiler_params=pltpu.CompilerParams(vmem_limit_bytes=VMEM_BYTES),
        cost_estimate=pl.CostEstimate(
            flops=rows * B * 20, bytes_accessed=8 * rows * B * 5, transcendentals=0
        ),
    )(shifts, at, contact, columns, lines, *[piece for _, piece in pieces])


def add_kernel(upper_ref, above_ref, out_ref):
    out_ref[...] = upper_ref[...] + above_ref[...]


def with_above(upper, above):
    rows = upper.shape[2]
    tail = pl.BlockSpec((2, 1, B, B), lambda i: (0, 0, rows // B - 1, 0))
    return pl.pallas_call(
        add_kernel,
        grid=(1,),
        in_specs=[tail, pl.BlockSpec((2, 1, B, B), lambda i: (0, 0, 0, 0))],
        out_specs=tail,
        out_shape=jax.ShapeDtypeStruct(upper.shape, F32),
        input_output_aliases={0: 0},
        compiler_params=pltpu.CompilerParams(vmem_limit_bytes=VMEM_BYTES),
        cost_estimate=pl.CostEstimate(flops=2 * B * B, bytes_accessed=24 * B * B, transcendentals=0),
        name="above",
    )(upper, above)


def edge_rows(retarded, pan):
    rows, columns = retarded.shape[2:]
    devices = lax.axis_size("pan")
    found, cuts = [], []
    for odd in (0, 1):
        up = (pan % 2 == odd).astype(jnp.int32)
        part = lax.dynamic_slice(
            retarded,
            (0, 0, up * (rows - B), up * (columns // 2)),
            (2, 1, B, columns // 2),
        )
        pairs = []
        for i in range(odd, devices - 1, 2):
            pairs += [(i, i + 1), (i + 1, i)]
        cuts.append(part)
        found.append(lax.ppermute(part, "pan", pairs))
    return found, cuts


def body(retarded, contact, atom_kind, coupling, shifts):
    rows = retarded.shape[2]
    pan = lax.axis_index("pan").astype(jnp.int32)
    energy = lax.axis_index("en").astype(jnp.int32)
    at = jnp.where(jnp.arange(2, dtype=jnp.int32) == 0, pan, energy)
    atoms = rows // ORB
    kinds = lax.dynamic_slice_in_dim(atom_kind, pan * atoms, atoms, 0)
    per_atom = sum(
        jnp.where(kinds[:, None] == kind, coupling[kind][None, :], 0.0)
        for kind in range(coupling.shape[0])
    )
    per_row = jnp.repeat(per_atom, ORB, axis=0)
    per_line = jnp.repeat(per_atom.T, ORB, axis=1)
    edges, cuts = edge_rows(retarded, pan)
    sigma = contact
    for rounds in range(ITERS):
        final = rounds == ITERS - 1
        pieces = spread(sigma, "pan")
        if rounds == 0:
            ready = lax.optimization_barrier((contact, per_row, per_line, *cuts))
            pieces[0] = (0, ready[0])
            per_row, per_line = ready[1:3]
        carry = None
        for far, piece in pieces[:-1]:
            carry = panel(at, retarded, far, piece, carry, edges, True, final, False)
        far, piece = pieces[-1]
        (lesser_diag,) = panel(at, retarded, far, piece, carry[:1], edges, True, False, True)
        found = spread(lesser_diag, "en")[1:]
        if final:
            upper, above = panel(at, retarded, far, piece, carry[1:], edges, False, True, True)
            devices = lax.axis_size("pan")
            above = lax.ppermute(above, "pan", [(i + 1, i) for i in range(devices - 1)])
            lesser_upper = with_above(upper, above)
        sigma = phonon(shifts, at, contact, per_row, per_line, found)
    return (lesser_diag, lesser_upper, sigma)


def solution(mesh):
    spread_spec = P(None, ("grp", "en"), "pan", None)
    return jax.shard_map(
        body,
        mesh=mesh,
        in_specs=(spread_spec, spread_spec, P(), P(), P()),
        out_specs=(spread_spec, spread_spec, spread_spec),
        check_vma=False,
    )
```

time: 188 us -> 166 us (0.88)
  Pallas kernels: 80.3 us -> 46.4 us
  waiting for transfers between devices: 75.4 us -> 92.2 us
  other arithmetic: 4 us -> 0.94 us
    pallas_call x8 -> x10, Pallas kernels: 71.2 us -> 43.6 us  [the longest x9 42 us: panel(): pl.pallas_call(functools.partial(panel_kernel, local, many, far, half, di...]
    ppermute x12, waiting for transfers between devices: 68.7 us -> 85.7 us  [swapped(): lax.ppermute(x, axis, [(i, i ^ bit) for i in range(lax.axis_size(axis))])]
    pallas_call x2, Pallas kernels: 9.06 us -> 2.74 us  [phonon(): pl.pallas_call(functools.partial(phonon_kernel, [far for far, _ in pieces...]
    slice x1 -> x0, local copies, waits for them, and re-layouts: 2.76 us -> none  [body(): retarded[:, :, -B:, columns // 2:]]
    add x4 -> x0, other arithmetic: 2.16 us -> none  [panel(): ks = source * local + jnp.arange(local, dtype=jnp.int32)]
    unnamed x14 -> x12, local copies, waits for them, and re-layouts: 3.6 us -> 4.45 us
  transfers between devices with their start and end apart: 15 -> 15, of which waited for: 7 -> 5; matrix products, arithmetic and copies ran while one was open for 4% -> 2% of each run, Pallas kernels for 35% -> 22%
where the time goes in v1:
time: 166 us
  waiting for transfers between devices  92.2 us (56%)
  Pallas kernels  46.4 us (28%)
  starting transfers between devices  18.3 us (11%)
  local copies, waits for them, and re-layouts  7.2 us (4%)
    ppermute x12, waiting for transfers between devices, swapped(): lax.ppermute(x, axis, [(i, i ^ bit) for i in range(lax.axis_size(axis))])  85.7 us
    pallas_call x9, Pallas kernels, panel(): pl.pallas_call(functools.partial(panel_kernel, local, many, far, half, di...  42 us
    ppermute x12, starting transfers between devices, swapped(): lax.ppermute(x, axis, [(i, i ^ bit) for i in range(lax.axis_size(axis))])  11 us
    ppermute x1, waiting for transfers between devices, body(): above = lax.ppermute(above, 'pan', [(i + 1, i) for i in range(devices - 1)])  6.5 us
    ppermute x2, starting transfers between devices, edge_rows(): found.append(lax.ppermute(part, 'pan', pairs))  5.98 us
    unnamed x12, local copies, waits for them, and re-layouts  4.45 us
  transfers between devices with their start and end apart: 15, of which 5 were waited for; matrix products, arithmetic and copies ran while one was open for 2% of the time, Pallas kernels for 22%

profile of v1, /device:TPU:0, one launch (start us, length us, event | category | flops | bytes accessed | tf_op | source)
XLA Modules:
  0.0 165.9 jit_solution(3889793479665241765)
XLA Ops:
  0.6 4.1 %collective-permute-start = (f32[2,1,512,128]{3,2,1,0:T(8,128)}, f32[2,1,512,128]{3,2,1,0:T(8,128)S(1)}, u32[]{:S(2)}, u32[]{:S(2)}) collective-permute-start(f32[2,1,512,128]{3,2,1,0:T(8,128)} %contact_ref.3), channel_id=1, source_target_pairs={{0,8},{4,12},{8,0},{12,4},{1,9},{5,13},{9,1},{13,5},{2,10},{6,14},... | collective-permute-start | bytes 1572872 | tf_op jit(solution)/shard_map/ppermute | solution.py:22
  4.8 1.6 collective-permute-start.2
  8.4 1.7 %constant_dynamic-slice_fusion = (f32[2,1,128,1024]{3,2,1,0:T(8,128)S(1)}, f32[2,1,128,1024]{3,2,1,0:T(8,128)S(1)}) fusion(f32[2,1,512,2048]{3,2,1,0:T(8,128)} %refs_1_.17, s32[]{:T(128)S(6)} %mul.18, s32[]{:T(128)S(6)} %mul.19, s32[]{:T(128)S(6)} %mul.16, s32[]{:T(128)S(6)} %mul.17), kind=kLoop, calls=%fused_computation.8 | loop fusion | bytes 4194320 | tf_op jit(solution)/shard_map/dynamic_slice | solution.py:303
  10.1 18.2 %collective-permute-done.refs_2_ = f32[2,1,512,128]{3,2,1,0:T(8,128)S(1)} collective-permute-done((f32[2,1,512,128]{3,2,1,0:T(8,128)}, f32[2,1,512,128]{3,2,1,0:T(8,128)S(1)}, u32[]{:S(2)}, u32[]{:S(2)}) %collective-permute-start) | collective-permute-done | bytes 524320 | tf_op jit(solution)/shard_map/ppermute | solution.py:22
  29.0 3.4 %copy-done = f32[2,1,512,2048]{3,2,1,0:T(8,128)S(1)} copy-done((f32[2,1,512,2048]{3,2,1,0:T(8,128)S(1)}, f32[2,1,512,2048]{3,2,1,0:T(8,128)}, u32[]{:S(2)}) %copy-start) | copy-done | bytes 8388632
  33.4 3.8 %shard_map.76.refs_3_ = f32[4,128,256]{2,1,0:T(8,128)S(1)} custom-call(s32[2]{0:T(128)S(1)} %compare_select_fusion.refs_0_.at_ref, f32[2,1,512,2048]{3,2,1,0:T(8,128)S(1)} %copy-done, f32[2,1,512,128]{3,2,1,0:T(8,128)S(1)} %copy-done.1), custom_call_target="tpu_custom_call" | custom-call | flops 1610612736 | bytes 2097152 | tf_op jit(solution)/shard_map/pallas_call | solution.py:205
  37.1 3.8 %shard_map.77.refs_3_ = f32[4,128,256]{2,1,0:T(8,128)S(1)} custom-call(s32[2]{0:T(128)S(1)} %compare_select_fusion.refs_0_.at_ref, f32[2,1,512,2048]{3,2,1,0:T(8,128)S(1)} %copy-done, f32[2,1,512,128]{3,2,1,0:T(8,128)S(1)} %collective-permute-done.refs_2_, f32[4,128,256]{2,1,0:T(8,128)S(1)} %shard_map.76.refs_3_), custom_call_target="tpu_custom_call" | custom-call | flops 1610612736 | bytes 2097152 | tf_op jit(solution)/shard_map/pallas_call | solution.py:205
  41.0 3.8 %shard_map.78.refs_3_ = f32[4,128,256]{2,1,0:T(8,128)S(1)} custom-call(s32[2]{0:T(128)S(1)} %compare_select_fusion.refs_0_.at_ref, f32[2,1,512,2048]{3,2,1,0:T(8,128)S(1)} %copy-done, f32[2,1,512,128]{3,2,1,0:T(8,128)S(1)} %collective-permute-done.2.refs_2_, f32[4,128,256]{2,1,0:T(8,128)S(1)} %shard_map.77.refs_3_), custom_call_target="tpu_custom_call" | custom-call | flops 1610612736 | bytes 2097152 | tf_op jit(solution)/shard_map/pallas_call | solution.py:205
  44.8 3.9 %shard_map.79 = f32[2,1,512,128]{3,2,1,0:T(8,128)S(1)} custom-call(s32[2]{0:T(128)S(1)} %compare_select_fusion.refs_0_.at_ref, f32[2,1,512,2048]{3,2,1,0:T(8,128)S(1)} %copy-done, f32[2,1,512,128]{3,2,1,0:T(8,128)S(1)} %collective-permute-done.1.refs_2_, f32[4,128,256]{2,1,0:T(8,128)S(1)} %shard_map.78.refs_3_), custom_call_target="tpu_custom_call" | custom-call | flops 1610612736 | bytes 2097152 | tf_op jit(solution)/shard_map/pallas_call | solution.py:205
  48.7 1.6 collective-permute-start.3
  50.3 12.1 %collective-permute-done.3.refs_0_ = f32[2,1,512,128]{3,2,1,0:T(8,128)S(1)} collective-permute-done((f32[2,1,512,128]{3,2,1,0:T(8,128)S(1)}, f32[2,1,512,128]{3,2,1,0:T(8,128)S(1)}, u32[]{:S(2)}, u32[]{:S(2)}) %collective-permute-start.3) | collective-permute-done | bytes 524320 | tf_op jit(solution)/shard_map/ppermute | solution.py:22
  63.2 5.1 %collective-permute-start.9 = (f32[2,1,128,1024]{3,2,1,0:T(8,128)S(1)}, f32[2,1,128,1024]{3,2,1,0:T(8,128)S(1)}, u32[]{:S(2)}, u32[]{:S(2)}) collective-permute-start(f32[2,1,128,1024]{3,2,1,0:T(8,128)S(1)} %get-tuple-element.28), channel_id=1, source_target_pairs={{0,4},{4,0},{8,12},{12,8},{1,5},{5,1},{9,13},{13,9},{2,6},{6,2},{1... | collective-permute-start | bytes 3145736 | tf_op jit(solution)/shard_map/ppermute | solution.py:312
  69.4 1.5 collective-permute-start.8
  70.9 43.0 %collective-permute-done.6.refs_2_ = f32[2,1,512,128]{3,2,1,0:T(8,128)S(1)} collective-permute-done((f32[2,1,512,128]{3,2,1,0:T(8,128)S(1)}, f32[2,1,512,128]{3,2,1,0:T(8,128)S(1)}, u32[]{:S(2)}, u32[]{:S(2)}) %collective-permute-start.6) | collective-permute-done | bytes 524320 | tf_op jit(solution)/shard_map/ppermute | solution.py:22
  114.0 4.8 %shard_map.81 = (f32[4,128,256]{2,1,0:T(8,128)S(1)}, f32[5,128,256]{2,1,0:T(8,128)S(1)}) custom-call(s32[2]{0:T(128)S(1)} %compare_select_fusion.refs_0_.at_ref, f32[2,1,512,2048]{3,2,1,0:T(8,128)S(1)} %bitcast.11, f32[2,1,512,128]{3,2,1,0:T(8,128)S(1)} %shard_map.80.refs_2_, f32[2,1,128,1024]{3,2,1,0:T(8,128)S(1)} %collective-permute-done.9.refs_3_, ...), custom_call_target="tpu_custom_call" | custom-call | flops 2415919104 | bytes 2097152 | tf_op jit(solution)/shard_map/pallas_call | solution.py:205
  118.8 5.8 %shard_map.82 = (f32[4,128,256]{2,1,0:T(8,128)S(1)}, f32[5,128,256]{2,1,0:T(8,128)S(1)}) custom-call(s32[2]{0:T(128)S(1)} %compare_select_fusion.refs_0_.at_ref, f32[2,1,512,2048]{3,2,1,0:T(8,128)S(1)} %bitcast.11, f32[2,1,512,128]{3,2,1,0:T(8,128)S(1)} %collective-permute-done.6.refs_2_, f32[2,1,128,1024]{3,2,1,0:T(8,128)S(1)} %collective-permute-done.9.refs_3_, ...), custom_call_target="tpu_custom_call" | custom-call | flops 2415919104 | bytes 2097152 | tf_op jit(solution)/shard_map/pallas_call | solution.py:205
  124.6 4.8 %shard_map.83 = (f32[4,128,256]{2,1,0:T(8,128)S(1)}, f32[5,128,256]{2,1,0:T(8,128)S(1)}) custom-call(s32[2]{0:T(128)S(1)} %compare_select_fusion.refs_0_.at_ref, f32[2,1,512,2048]{3,2,1,0:T(8,128)S(1)} %bitcast.11, f32[2,1,512,128]{3,2,1,0:T(8,128)S(1)} %collective-permute-done.8.refs_2_, f32[2,1,128,1024]{3,2,1,0:T(8,128)S(1)} %collective-permute-done.9.refs_3_, ...), custom_call_target="tpu_custom_call" | custom-call | flops 2415919104 | bytes 2097152 | tf_op jit(solution)/shard_map/pallas_call | solution.py:205
  129.4 4.7 %shard_map.84 = f32[2,1,512,128]{3,2,1,0:T(8,128)} custom-call(s32[2]{0:T(128)S(1)} %compare_select_fusion.refs_0_.at_ref, f32[2,1,512,2048]{3,2,1,0:T(8,128)S(1)} %bitcast.11, f32[2,1,512,128]{3,2,1,0:T(8,128)S(1)} %collective-permute-done.7.refs_2_, f32[4,128,256]{2,1,0:T(8,128)S(1)} %get-tuple-element.21.refs_3_), custom_call_target="tpu_custom_call" | custom-call | flops 1610612736 | bytes 2097152 | tf_op jit(solution)/shard_map/pallas_call | solution.py:205
  134.1 1.5 collective-permute-start.12
  135.6 12.4 %collective-permute-done.12.refs_0_ = f32[2,1,512,128]{3,2,1,0:T(8,128)S(1)} collective-permute-done((f32[2,1,512,128]{3,2,1,0:T(8,128)}, f32[2,1,512,128]{3,2,1,0:T(8,128)S(1)}, u32[]{:S(2)}, u32[]{:S(2)}) %collective-permute-start.12) | collective-permute-done | bytes 524320 | tf_op jit(solution)/shard_map/ppermute | solution.py:22
  148.0 6.7 %shard_map.85 = (f32[2,1,512,128]{3,2,1,0:T(8,128)}, f32[2,1,128,128]{3,2,1,0:T(8,128)S(1)}) custom-call(s32[2]{0:T(128)S(1)} %compare_select_fusion.refs_0_.at_ref, f32[2,1,512,2048]{3,2,1,0:T(8,128)S(1)} %bitcast.11, f32[2,1,512,128]{3,2,1,0:T(8,128)S(1)} %collective-permute-done.7.refs_2_, f32[2,1,128,1024]{3,2,1,0:T(8,128)S(1)} %collective-permute-done.9.refs_3_, ...), custom_call_target="tpu_custom_call" | custom-call | flops 1610612736 | bytes 2097152 | tf_op jit(solution)/shard_map/pallas_call | solution.py:205
  156.0 6.5 %collective-permute-done.11.above_ref = f32[2,1,128,128]{3,2,1,0:T(8,128)S(1)} collective-permute-done((f32[2,1,128,128]{3,2,1,0:T(8,128)S(1)}, f32[2,1,128,128]{3,2,1,0:T(8,128)S(1)}, u32[]{:S(2)}, u32[]{:S(2)}) %collective-permute-start.11) | collective-permute-done | bytes 131104 | tf_op jit(solution)/shard_map/ppermute | solution.py:347
  162.5 1.6 above.1
  164.1 1.8 %shard_map.86 = f32[2,1,512,128]{3,2,1,0:T(8,128)} custom-call(s32[3]{0:T(128)S(1)} %copy-done.3, s32[2]{0:T(128)S(1)} %compare_select_fusion.refs_0_.at_ref, f32[2,1,512,128]{3,2,1,0:T(8,128)S(1)} %copy-done.2, f32[512,3]{1,0:T(8,128)S(1)} %broadcast_bitcast_fusion.col_ref, f32[3,512]{1,0:T(4,128)S(1)} %reshape.21.row_ref, ...), custom_call_target="tpu_custom_call" | custom-call | flops 1310720 | bytes 2621440 | tf_op jit(solution)/shard_map/pallas_call | solution.py:256
  (41 shorter events, 7.0 us)
Async XLA Ops:
  0.6 27.6 %collective-permute-start = (f32[2,1,512,128]{3,2,1,0:T(8,128)}, f32[2,1,512,128]{3,2,1,0:T(8,128)S(1)}, u32[]{:S(2)}, u32[]{:S(2)}) collective-permute-start(f32[2,1,512,128]{3,2,1,0:T(8,128)} %contact_ref.3), channel_id=1, source_target_pairs={{0,8},{4,12},{8,0},{12,4},{1,9},{5,13},{9,1},{13,5},{2,10},{6,14},... | collective-permute-start | bytes 1572872 | tf_op jit(solution)/shard_map/ppermute | solution.py:22
  4.8 36.2 %collective-permute-start.2 = (f32[2,1,512,128]{3,2,1,0:T(8,128)}, f32[2,1,512,128]{3,2,1,0:T(8,128)S(1)}, u32[]{:S(2)}, u32[]{:S(2)}) collective-permute-start(f32[2,1,512,128]{3,2,1,0:T(8,128)} %contact_ref.3), channel_id=1, source_target_pairs={{0,4},{4,0},{8,12},{12,8},{1,5},{5,1},{9,13},{13,9},{2,6},{6,2},{1... | collective-permute-start | bytes 1572872 | tf_op jit(solution)/shard_map/ppermute | solution.py:22
  28.2 16.5 %collective-permute-start.1 = (f32[2,1,512,128]{3,2,1,0:T(8,128)S(1)}, f32[2,1,512,128]{3,2,1,0:T(8,128)S(1)}, u32[]{:S(2)}, u32[]{:S(2)}) collective-permute-start(f32[2,1,512,128]{3,2,1,0:T(8,128)S(1)} %collective-permute-done.refs_2_), channel_id=1, source_target_pairs={{0,4},{4,0},{8,12},{12,8},{1,5},{5,1},{9,13},{13,9},{2,6},{6,2},{1... | collective-permute-start | bytes 1572872 | tf_op jit(solution)/shard_map/ppermute | solution.py:22
  29.0 3.4 %copy-start = (f32[2,1,512,2048]{3,2,1,0:T(8,128)S(1)}, f32[2,1,512,2048]{3,2,1,0:T(8,128)}, u32[]{:S(2)}) copy-start(f32[2,1,512,2048]{3,2,1,0:T(8,128)} %refs_1_.17) | copy-start | bytes 25165828
  32.3 1.0 copy-start.1
  40.9 27.4 %copy-start.2 = (f32[2,1,512,128]{3,2,1,0:T(8,128)S(1)}, f32[2,1,512,128]{3,2,1,0:T(8,128)}, u32[]{:S(2)}) copy-start(f32[2,1,512,128]{3,2,1,0:T(8,128)} %contact_ref.3) | copy-start | bytes 1572868
  40.9 27.4 %copy-start.3 = (s32[3]{0:T(128)S(1)}, s32[3]{0:T(128)}, u32[]{:S(2)}) copy-start(s32[3]{0:T(128)} %shift_ref.3) | copy-start | bytes 40
  41.0 73.0 %slice-start = ((s8[8388608]{0:T(1024)(128)(4,1)}), s8[4194304]{0:T(1024)(128)(4,1)S(1)}, s32[]{:S(2)}) async-start(s8[8388608]{0:T(1024)(128)(4,1)} %bitcast.10), calls=%async_computation | async-start | bytes 8388608
  44.7 69.2 %slice-start.1 = ((s8[8388608]{0:T(1024)(128)(4,1)}), s8[4194304]{0:T(1024)(128)(4,1)S(1)}, s32[]{:S(2)}) async-start(s8[8388608]{0:T(1024)(128)(4,1)} %bitcast.10), calls=%async_computation.1 | async-start | bytes 8388608
  48.7 13.6 %collective-permute-start.3 = (f32[2,1,512,128]{3,2,1,0:T(8,128)S(1)}, f32[2,1,512,128]{3,2,1,0:T(8,128)S(1)}, u32[]{:S(2)}, u32[]{:S(2)}) collective-permute-start(f32[2,1,512,128]{3,2,1,0:T(8,128)S(1)} %shard_map.79), channel_id=1, source_target_pairs={{0,2},{1,3},{2,0},{3,1},{4,6},{5,7},{6,4},{7,5},{8,10},{9,11},{10,... | collective-permute-start | bytes 1572872 | tf_op jit(solution)/shard_map/ppermute | solution.py:22
  50.3 18.1 %collective-permute-start.4 = (f32[2,1,512,128]{3,2,1,0:T(8,128)S(1)}, f32[2,1,512,128]{3,2,1,0:T(8,128)S(1)}, u32[]{:S(2)}, u32[]{:S(2)}) collective-permute-start(f32[2,1,512,128]{3,2,1,0:T(8,128)S(1)} %shard_map.79), channel_id=1, source_target_pairs={{0,1},{1,0},{2,3},{3,2},{4,5},{5,4},{6,7},{7,6},{8,9},{9,8},{10,11... | collective-permute-start | bytes 1572872 | tf_op jit(solution)/shard_map/ppermute | solution.py:22
  62.3 6.0 %collective-permute-start.5 = (f32[2,1,512,128]{3,2,1,0:T(8,128)S(1)}, f32[2,1,512,128]{3,2,1,0:T(8,128)S(1)}, u32[]{:S(2)}, u32[]{:S(2)}) collective-permute-start(f32[2,1,512,128]{3,2,1,0:T(8,128)S(1)} %collective-permute-done.3.refs_0_), channel_id=1, source_target_pairs={{0,1},{1,0},{2,3},{3,2},{4,5},{5,4},{6,7},{7,6},{8,9},{9,8},{10,11... | collective-permute-start | bytes 1572872 | tf_op jit(solution)/shard_map/ppermute | solution.py:22
  62.3 51.6 %collective-permute-start.10 = (f32[2,1,128,1024]{3,2,1,0:T(8,128)S(1)}, f32[2,1,128,1024]{3,2,1,0:T(8,128)S(1)}, u32[]{:S(2)}, u32[]{:S(2)}) collective-permute-start(f32[2,1,128,1024]{3,2,1,0:T(8,128)S(1)} %get-tuple-element.27), channel_id=1, source_target_pairs={{4,8},{8,4},{5,9},{9,5},{6,10},{10,6},{7,11},{11,7},{20,24},{24,20... | collective-permute-start | bytes 3145736 | tf_op jit(solution)/shard_map/ppermute | solution.py:312
  63.2 50.7 %collective-permute-start.9 = (f32[2,1,128,1024]{3,2,1,0:T(8,128)S(1)}, f32[2,1,128,1024]{3,2,1,0:T(8,128)S(1)}, u32[]{:S(2)}, u32[]{:S(2)}) collective-permute-start(f32[2,1,128,1024]{3,2,1,0:T(8,128)S(1)} %get-tuple-element.28), channel_id=1, source_target_pairs={{0,4},{4,0},{8,12},{12,8},{1,5},{5,1},{9,13},{13,9},{2,6},{6,2},{1... | collective-permute-start | bytes 3145736 | tf_op jit(solution)/shard_map/ppermute | solution.py:312
  69.3 44.6 %collective-permute-start.6 = (f32[2,1,512,128]{3,2,1,0:T(8,128)S(1)}, f32[2,1,512,128]{3,2,1,0:T(8,128)S(1)}, u32[]{:S(2)}, u32[]{:S(2)}) collective-permute-start(f32[2,1,512,128]{3,2,1,0:T(8,128)S(1)} %shard_map.80.refs_2_), channel_id=1, source_target_pairs={{0,8},{4,12},{8,0},{12,4},{1,9},{5,13},{9,1},{13,5},{2,10},{6,14},... | collective-permute-start | bytes 1572872 | tf_op jit(solution)/shard_map/ppermute | solution.py:22
  69.4 55.1 %collective-permute-start.8 = (f32[2,1,512,128]{3,2,1,0:T(8,128)S(1)}, f32[2,1,512,128]{3,2,1,0:T(8,128)S(1)}, u32[]{:S(2)}, u32[]{:S(2)}) collective-permute-start(f32[2,1,512,128]{3,2,1,0:T(8,128)S(1)} %shard_map.80.refs_2_), channel_id=1, source_target_pairs={{0,4},{4,0},{8,12},{12,8},{1,5},{5,1},{9,13},{13,9},{2,6},{6,2},{1... | collective-permute-start | bytes 1572872 | tf_op jit(solution)/shard_map/ppermute | solution.py:22
  113.9 15.5 %collective-permute-start.7 = (f32[2,1,512,128]{3,2,1,0:T(8,128)S(1)}, f32[2,1,512,128]{3,2,1,0:T(8,128)S(1)}, u32[]{:S(2)}, u32[]{:S(2)}) collective-permute-start(f32[2,1,512,128]{3,2,1,0:T(8,128)S(1)} %collective-permute-done.6.refs_2_), channel_id=1, source_target_pairs={{0,4},{4,0},{8,12},{12,8},{1,5},{5,1},{9,13},{13,9},{2,6},{6,2},{1... | collective-permute-start | bytes 1572872 | tf_op jit(solution)/shard_map/ppermute | solution.py:22
  134.1 13.9 %collective-permute-start.12 = (f32[2,1,512,128]{3,2,1,0:T(8,128)}, f32[2,1,512,128]{3,2,1,0:T(8,128)S(1)}, u32[]{:S(2)}, u32[]{:S(2)}) collective-permute-start(f32[2,1,512,128]{3,2,1,0:T(8,128)} %shard_map.84), channel_id=1, source_target_pairs={{0,2},{1,3},{2,0},{3,1},{4,6},{5,7},{6,4},{7,5},{8,10},{9,11},{10,... | collective-permute-start | bytes 1572872 | tf_op jit(solution)/shard_map/ppermute | solution.py:22
  135.6 28.5 %collective-permute-start.13 = (f32[2,1,512,128]{3,2,1,0:T(8,128)}, f32[2,1,512,128]{3,2,1,0:T(8,128)S(1)}, u32[]{:S(2)}, u32[]{:S(2)}) collective-permute-start(f32[2,1,512,128]{3,2,1,0:T(8,128)} %shard_map.84), channel_id=1, source_target_pairs={{0,1},{1,0},{2,3},{3,2},{4,5},{5,4},{6,7},{7,6},{8,9},{9,8},{10,11... | collective-permute-start | bytes 1572872 | tf_op jit(solution)/shard_map/ppermute | solution.py:22
  148.0 16.1 %collective-permute-start.14 = (f32[2,1,512,128]{3,2,1,0:T(8,128)S(1)}, f32[2,1,512,128]{3,2,1,0:T(8,128)S(1)}, u32[]{:S(2)}, u32[]{:S(2)}) collective-permute-start(f32[2,1,512,128]{3,2,1,0:T(8,128)S(1)} %collective-permute-done.12.refs_0_), channel_id=1, source_target_pairs={{0,1},{1,0},{2,3},{3,2},{4,5},{5,4},{6,7},{7,6},{8,9},{9,8},{10,11... | collective-permute-start | bytes 1572872 | tf_op jit(solution)/shard_map/ppermute | solution.py:22
  154.7 7.8 %collective-permute-start.11 = (f32[2,1,128,128]{3,2,1,0:T(8,128)S(1)}, f32[2,1,128,128]{3,2,1,0:T(8,128)S(1)}, u32[]{:S(2)}, u32[]{:S(2)}) collective-permute-start(f32[2,1,128,128]{3,2,1,0:T(8,128)S(1)} %get-tuple-element.24), channel_id=1, source_target_pairs={{4,0},{8,4},{12,8},{5,1},{9,5},{13,9},{6,2},{10,6},{14,10},{7,3},{... | collective-permute-start | bytes 393224 | tf_op jit(solution)/shard_map/ppermute | solution.py:347

commit v2 on v1

v2 whole, which is shorter than its diff:
```python
import functools
import math

import jax
import jax.numpy as jnp
from jax import lax
from jax.experimental import pallas as pl
from jax.experimental.pallas import tpu as pltpu
from jax.sharding import PartitionSpec as P


B = 128
ORB = 8
ITERS = 2
VMEM_BYTES = 28 * 2**20

F32 = jnp.float32
BF16 = jnp.bfloat16


def swapped(x, axis, bit):
    return lax.ppermute(x, axis, [(i, i ^ bit) for i in range(lax.axis_size(axis))])


def spread(x, axis):
    pieces = [(0, x)]
    bit = lax.axis_size(axis) // 2
    while bit:
        found = []
        for far, piece in pieces:
            found.append((far ^ bit, swapped(piece, axis, bit)))
        pieces += found
        bit //= 2
    return pieces


def split(x):
    high = x.astype(BF16)
    return high, (x - high.astype(F32)).astype(BF16)


def dot(a, b):
    return jnp.dot(a, b, preferred_element_type=F32)


def dot_t(a, b):
    return lax.dot_general(a, b, (((1,), (1,)), ((), ())), preferred_element_type=F32)


def times(a, b):
    return dot(a[0], b[0]) + (dot(a[1], b[0]) + dot(a[0], b[1]))


def times_t(a, b):
    return dot_t(a[0], b[0]) + (dot_t(a[1], b[0]) + dot_t(a[0], b[1]))


def total(terms):
    return functools.reduce(lambda a, b: a + b, terms)


def pair_rows(x):
    return tuple(
        jnp.concatenate([v, jnp.concatenate([v[:, B:], -v[:, :B]], axis=1)], axis=0) for v in x
    )


def rows_of(x, start, size):
    return tuple(v[start : start + size] for v in x)


def panel_kernel(local, far, starts, diag, upper, back, first, last, devices, scale, *refs):
    refs = list(refs)
    at_ref, g_ref = refs[:2]
    piece_refs, refs = refs[2 : 2 + len(starts)], refs[2 + len(starts) :]
    if upper:
        even_ref, odd_ref = refs[:2]
        refs = refs[2:]
    count = int(diag) + int(upper) + int(back)
    ins = []
    if not first:
        ins, refs = refs[:count], refs[count:]
    if last and upper:
        above_ref, refs = refs[0], refs[1:]
    outs = refs
    pan = at_ref[0]
    source = pan ^ far
    middle = devices // 2
    half = devices * local // 2

    greens, sigmas, products, columns = [], [], [], []
    for start, s_ref in zip(starts, piece_refs):
        for u in range(s_ref.shape[2] // B):
            k = source * local + start + u
            columns.append(pl.ds(pl.multiple_of((k % half) * B, B), B))
            cut = pl.ds(pl.multiple_of(k * B, B), B)
            green = split(jnp.concatenate([g_ref[0, 0, :, cut], g_ref[1, 0, :, cut]], axis=1))
            rows = slice(u * B, (u + 1) * B)
            sr, si = s_ref[0, 0, rows], s_ref[1, 0, rows]
            sigma = split(
                jnp.concatenate(
                    [jnp.concatenate([sr, si], axis=1), jnp.concatenate([-si, sr], axis=1)], axis=0
                )
            )
            greens.append(green)
            sigmas.append(sigma)
            products.append(split(times(green, sigma)))

    def old(which, i):
        return 0.0 if first else ins[which][i]

    def put(ref, row, value):
        ref[0, 0, row * B : (row + 1) * B] = value[:, :B].T * scale
        ref[1, 0, row * B : (row + 1) * B] = value[:, B:].T * scale

    at_upper = int(diag)
    for i in range(local):
        start = 0 if diag else 1
        size = int(diag) + int(upper and i < local - 1)
        if not size:
            continue
        terms = total(
            times_t(rows_of(green, (i + start) * B, size * B), pair_rows(rows_of(product, i * B, B)))
            for green, product in zip(greens, products)
        )
        if diag:
            value = old(0, i) + terms[:B]
            if last:
                put(outs[0], i, value)
            else:
                outs[0][i] = value
        if upper and i < local - 1:
            value = old(at_upper, i) + terms[-B:]
            if last:
                put(outs[at_upper], i, value)
            else:
                outs[at_upper][i] = value
    if upper:
        source_high = source >= middle
        ours = (source_high == (pan >= middle)) if back else None
        theirs = source_high != (pan + 1 >= middle)
        even = pan % 2 == 0

        def edge(near, column):
            return split(
                jnp.concatenate(
                    [
                        jnp.where(near, even_ref[j, 0, :, column], odd_ref[j, 0, :, column])
                        for j in range(2)
                    ],
                    axis=1,
                )
            )

        if first:
            outs[at_upper][local - 1] = jnp.zeros((B, 2 * B), F32)
            outs[at_upper + 1][0] = jnp.zeros((B, 2 * B), F32)
        if last:
            edge_sum = ins[at_upper]
        else:
            edge_sum = outs[at_upper]

        @pl.when(theirs)
        def _():
            terms = total(
                times_t(edge(even, column), pair_rows(rows_of(product, (local - 1) * B, B)))
                for product, column in zip(products, columns)
            )
            if last:
                put(outs[at_upper], local - 1, edge_sum[local - 1] + terms + above_ref[0])
            else:
                edge_sum[local - 1] += terms

        if last:

            @pl.when(jnp.logical_not(theirs))
            def _():
                put(outs[at_upper], local - 1, edge_sum[local - 1] + above_ref[0])

        if back:

            @pl.when(ours)
            def _():
                outs[at_upper + 1][0] += total(
                    times_t(
                        rows_of(green, 0, B),
                        pair_rows(split(times(edge(jnp.logical_not(even), column), sigma))),
                    )
                    for green, sigma, column in zip(greens, sigmas, columns)
                )


def panel(at, green, far, pieces, carry, edges, kinds, last, above=None):
    rows = green.shape[2]
    local = rows // B
    devices = lax.axis_size("pan")
    counts = {"diag": local, "upper": local, "back": 1}
    vmem = pl.BlockSpec(memory_space=pltpu.VMEM)
    starts, many = [], 0
    for start, piece in pieces:
        starts.append(start)
        many += piece.shape[2] // B
    operands = [at, green] + [piece for _, piece in pieces]
    if "upper" in kinds:
        operands += edges
    shapes = {kind: jax.ShapeDtypeStruct((counts[kind], B, 2 * B), F32) for kind in kinds}
    aliases = {}
    if carry is not None:
        for number, kind in enumerate(kinds):
            if not last:
                aliases[len(operands)] = number
            operands.append(carry[kind])
    if last:
        shapes = {kind: jax.ShapeDtypeStruct((2, 1, rows, B), F32) for kind in kinds}
        if above is not None:
            operands.append(above)
    work = 3 * 2 * (2 * B) * (2 * B) * rows * many * (1 + len(kinds))
    out = pl.pallas_call(
        functools.partial(
            panel_kernel,
            local,
            far,
            starts,
            "diag" in kinds,
            "upper" in kinds,
            "back" in kinds,
            carry is None,
            last,
            devices,
            1.0 / math.sqrt(B),
        ),
        in_specs=[pl.BlockSpec(memory_space=pltpu.SMEM)] + [vmem] * (len(operands) - 1),
        out_specs=[vmem] * len(shapes),
        out_shape=list(shapes.values()),
        input_output_aliases=aliases,
        compiler_params=pltpu.CompilerParams(vmem_limit_bytes=VMEM_BYTES),
        cost_estimate=pl.CostEstimate(
            flops=work, bytes_accessed=8 * rows * B * many, transcendentals=0
        ),
    )(*operands)
    return dict(zip(kinds, out))


def phonon_kernel(fars, modes, shift_ref, at_ref, contact_ref, col_ref, row_ref, *refs):
    out_refs = refs[len(fars) :]
    energy = at_ref[1]
    chosen = []
    for far in fars:
        apart = jnp.abs((energy ^ far) - energy)
        chosen.append([jnp.where(apart == shift_ref[m], 1.0, 0.0).astype(F32) for m in range(modes)])
    for start in range(0, contact_ref.shape[2], B):
        rows = slice(start, start + B)
        outer = [col_ref[rows, m : m + 1] * row_ref[m : m + 1, rows] for m in range(modes)]
        values = [contact_ref[0, 0, rows], contact_ref[1, 0, rows]]
        for weights, ref in zip(chosen, refs):
            weight = total(w * o for w, o in zip(weights, outer))
            values = [value + weight * ref[j, 0, rows] for j, value in enumerate(values)]
        first = 0
        for number, ref in enumerate(out_refs):
            at = start if number == 0 else start - first
            if 0 <= at < ref.shape[2]:
                for j in range(2):
                    ref[j, 0, at : at + B] = values[j]
            if number > 0:
                first += ref.shape[2]


def phonon(shifts, at, contact, columns, lines, pieces, chunks):
    parts, energies, rows = contact.shape[:3]
    modes = shifts.shape[0]
    vmem = pl.BlockSpec(memory_space=pltpu.VMEM)
    smem = pl.BlockSpec(memory_space=pltpu.SMEM)
    shapes = [jax.ShapeDtypeStruct(contact.shape, F32)]
    if chunks > 1:
        shapes += [jax.ShapeDtypeStruct((parts, energies, rows // chunks, B), F32)] * chunks
    return pl.pallas_call(
        functools.partial(phonon_kernel, [far for far, _ in pieces], modes),
        in_specs=[smem, smem] + [vmem] * (3 + len(pieces)),
        out_specs=[vmem] * len(shapes),
        out_shape=shapes,
        compiler_params=pltpu.CompilerParams(vmem_limit_bytes=VMEM_BYTES),
        cost_estimate=pl.CostEstimate(
            flops=rows * B * 20, bytes_accessed=8 * rows * B * 5, transcendentals=0
        ),
    )(shifts, at, contact, columns, lines, *[piece for _, piece in pieces])


def edge_rows(retarded, pan):
    rows, columns = retarded.shape[2:]
    devices = lax.axis_size("pan")
    middle = devices // 2
    up_start = (pan + 1 >= middle).astype(jnp.int32)
    down_start = (pan < middle).astype(jnp.int32)
    found, cuts = [], []
    for odd in (0, 1):
        up = pan % 2 == odd
        row = jnp.where(up, rows - B, 0)
        column = jnp.where(up, up_start, down_start) * (columns // 2)
        part = lax.dynamic_slice(retarded, (0, 0, row, column), (2, 1, B, columns // 2))
        pairs = []
        for i in range(odd, devices - 1, 2):
            pairs += [(i, i + 1), (i + 1, i)]
        cuts.append(part)
        found.append(lax.ppermute(part, "pan", pairs))
    return found, cuts


def gathered(whole, chunks):
    size = whole.shape[2] // B // len(chunks)
    parts = [(i * size, chunk) for i, chunk in enumerate(chunks)]
    first = lax.axis_size("pan") // 2
    pieces = [(0, [(0, whole)])]
    bit = first
    while bit:
        found = []
        for far, piece in pieces:
            if bit == first:
                piece = parts
            sent = []
            for start, block in piece:
                sent.append((start, swapped(block, "pan", bit)))
            found.append((far ^ bit, sent))
        pieces += found
        bit //= 2
    return pieces


def body(retarded, contact, atom_kind, coupling, shifts):
    rows = retarded.shape[2]
    local = rows // B
    chunks = 2 if local % 2 == 0 else 1
    pan = lax.axis_index("pan").astype(jnp.int32)
    energy = lax.axis_index("en").astype(jnp.int32)
    at = jnp.where(jnp.arange(2, dtype=jnp.int32) == 0, pan, energy)
    atoms = rows // ORB
    kinds = lax.dynamic_slice_in_dim(atom_kind, pan * atoms, atoms, 0)
    per_atom = sum(
        jnp.where(kinds[:, None] == kind, coupling[kind][None, :], 0.0)
        for kind in range(coupling.shape[0])
    )
    per_row = jnp.repeat(per_atom, ORB, axis=0)
    per_line = jnp.repeat(per_atom.T, ORB, axis=1)
    edges, cuts = edge_rows(retarded, pan)
    sigma = contact
    parts = [contact]
    if chunks > 1:
        size = rows // chunks
        parts = [contact[:, :, i * size : (i + 1) * size] for i in range(chunks)]
    for rounds in range(ITERS):
        final = rounds == ITERS - 1
        pieces = gathered(sigma, parts)
        if rounds == 0:
            ready = lax.optimization_barrier((contact, per_row, per_line, *cuts))
            pieces[0] = (0, [(0, ready[0])])
            per_row, per_line = ready[1:3]
        work = ("diag", "upper", "back") if final else ("diag",)
        sums = None
        order = sorted(pieces[:-1], key=lambda piece: (piece[0] != 0, piece[0] >= lax.axis_size("pan") // 2))
        for far, blocks in order:
            kinds_here = work
            if final and far >= lax.axis_size("pan") // 2:
                kinds_here = work[:2]
            new = panel(at, retarded, far, blocks, sums, edges, kinds_here, False)
            sums = dict(sums or {}, **new)
        far, blocks = pieces[-1]
        for number, block in enumerate(blocks):
            last = number == len(blocks) - 1
            new = panel(at, retarded, far, [block], sums, edges, ("diag",), last)
            sums = dict(sums, **new)
        lesser_diag = sums["diag"]
        found = spread(lesser_diag, "en")[1:]
        if final:
            devices = lax.axis_size("pan")
            above = lax.ppermute(sums["back"], "pan", [(i + 1, i) for i in range(devices - 1)])
            lesser_upper = panel(
                at, retarded, far, blocks, sums, edges, ("upper",), True, above
            )["upper"]
        out = phonon(shifts, at, contact, per_row, per_line, found, 1 if final else chunks)
        sigma, parts = out[0], (out[1:] if len(out) > 1 else out)
    return (lesser_diag, lesser_upper, sigma)


def solution(mesh):
    def step(retarded, *args):
        spread_spec = P(None, ("grp", "en"), "pan", None)
        inner = jax.shard_map(
            body,
            mesh=mesh,
            in_specs=(spread_spec, spread_spec, P(), P(), P()),
            out_specs=(spread_spec, spread_spec, spread_spec),
            check_vma=False,
        )
        return inner(retarded, *args)

    return step
```

time: 166 us -> 135 us (0.81)
  waiting for transfers between devices: 92.2 us -> 61 us
  Pallas kernels: 46.4 us -> 41 us
  starting transfers between devices: 18.3 us -> 22.4 us
  local copies, waits for them, and re-layouts: 7.2 us -> 9.02 us
    ppermute x12 -> x16, waiting for transfers between devices: 85.7 us -> 38.8 us  [swapped(): lax.ppermute(x, axis, [(i, i ^ bit) for i in range(lax.axis_size(axis))])]
    ppermute x2, waiting for transfers between devices: 0.01 us -> 15.7 us  [edge_rows(): found.append(lax.ppermute(part, 'pan', pairs))]
    ppermute x12 -> x16, starting transfers between devices: 11 us -> 19.9 us  [swapped(): lax.ppermute(x, axis, [(i, i ^ bit) for i in range(lax.axis_size(axis))])]
    pallas_call x10 -> x11, Pallas kernels: 43.6 us -> 38.3 us  [panel(): pl.pallas_call(functools.partial(panel_kernel, local, far, starts, 'diag'...]
    ppermute x2, starting transfers between devices: 5.98 us -> 1.18 us  [edge_rows(): found.append(lax.ppermute(part, 'pan', pairs))]
    slice x0 -> x1, local copies, waits for them, and re-layouts: none -> 1.85 us  [body(): parts = [contact[:, :, i * size:(i + 1) * size] for i in range(chunks)]]
    unnamed x12 -> x10, local copies, waits for them, and re-layouts: 4.45 us -> 4.44 us
  transfers between devices with their start and end apart: 15 -> 19, of which waited for: 5 -> 9; matrix products, arithmetic and copies ran while one was open for 2% -> 4% of each run, Pallas kernels for 22% -> 25%
where the time goes in v2:
time: 135 us
  waiting for transfers between devices  61 us (45%)
  Pallas kernels  41 us (30%)
  starting transfers between devices  22.4 us (17%)
  local copies, waits for them, and re-layouts  9.02 us (7%)
    ppermute x16, waiting for transfers between devices, swapped(): lax.ppermute(x, axis, [(i, i ^ bit) for i in range(lax.axis_size(axis))])  38.8 us
    pallas_call x11, Pallas kernels, panel(): pl.pallas_call(functools.partial(panel_kernel, local, far, starts, 'diag'...  38.3 us
    ppermute x16, starting transfers between devices, swapped(): lax.ppermute(x, axis, [(i, i ^ bit) for i in range(lax.axis_size(axis))])  19.9 us
    ppermute x2, waiting for transfers between devices, edge_rows(): found.append(lax.ppermute(part, 'pan', pairs))  15.7 us
    ppermute x1, waiting for transfers between devices, body(): lax.ppermute(sums['back'], 'pan', [(i + 1, i) for i in range(devices - 1)])  6.5 us
    unnamed x10, local copies, waits for them, and re-layouts  4.44 us
    pallas_call x2, Pallas kernels, phonon(): pl.pallas_call(functools.partial(phonon_kernel, [far for far, _ in pieces...  2.72 us
  transfers between devices with their start and end apart: 19, of which 9 were waited for; matrix products, arithmetic and copies ran while one was open for 4% of the time, Pallas kernels for 25%

profile of v2, /device:TPU:0, one launch (start us, length us, event | category | flops | bytes accessed | tf_op | source)
XLA Modules:
  0.0 135.1 jit_solution(11720739259148630477)
XLA Ops:
  0.6 3.1 %collective-permute-start.4 = (f32[2,1,512,128]{3,2,1,0:T(8,128)}, f32[2,1,512,128]{3,2,1,0:T(8,128)S(1)}, u32[]{:S(2)}, u32[]{:S(2)}) collective-permute-start(f32[2,1,512,128]{3,2,1,0:T(8,128)} %contact_ref.3), channel_id=1, source_target_pairs={{0,4},{4,0},{8,12},{12,8},{1,5},{5,1},{9,13},{13,9},{2,6},{6,2},{1... | collective-permute-start | bytes 1572872 | tf_op jit(solution)/shard_map/ppermute | solution.py:22
  5.6 2.6 %collective-permute-start = (f32[2,1,256,128]{3,2,1,0:T(8,128)}, f32[2,1,256,128]{3,2,1,0:T(8,128)S(1)}, u32[]{:S(2)}, u32[]{:S(2)}) collective-permute-start(f32[2,1,256,128]{3,2,1,0:T(8,128)} %get-tuple-element.36), channel_id=1, source_target_pairs={{0,8},{4,12},{8,0},{12,4},{1,9},{5,13},{9,1},{13,5},{2,10},{6,14},... | collective-permute-start | bytes 786440 | tf_op jit(solution)/shard_map/ppermute | solution.py:22
  12.3 3.4 %copy-done = f32[2,1,512,2048]{3,2,1,0:T(8,128)S(1)} copy-done((f32[2,1,512,2048]{3,2,1,0:T(8,128)S(1)}, f32[2,1,512,2048]{3,2,1,0:T(8,128)}, u32[]{:S(2)}) %copy-start) | copy-done | bytes 8388632
  16.7 3.5 %shard_map.76.refs_3_ = f32[4,128,256]{2,1,0:T(8,128)S(1)} custom-call(s32[2]{0:T(128)S(1)} %compare_select_fusion.refs_0_.at_ref, f32[2,1,512,2048]{3,2,1,0:T(8,128)S(1)} %copy-done, f32[2,1,512,128]{3,2,1,0:T(8,128)S(1)} %copy-done.1), custom_call_target="tpu_custom_call" | custom-call | flops 1610612736 | bytes 2097152 | tf_op jit(solution)/shard_map/pallas_call | solution.py:218
  20.2 11.2 %collective-permute-done.2.refs_2_ = f32[2,1,256,128]{3,2,1,0:T(8,128)S(1)} collective-permute-done((f32[2,1,256,128]{3,2,1,0:T(8,128)}, f32[2,1,256,128]{3,2,1,0:T(8,128)S(1)}, u32[]{:S(2)}, u32[]{:S(2)}) %collective-permute-start.2) | collective-permute-done | bytes 262176 | tf_op jit(solution)/shard_map/ppermute | solution.py:22
  33.4 3.6 %shard_map.77.refs_4_ = f32[4,128,256]{2,1,0:T(8,128)S(1)} custom-call(s32[2]{0:T(128)S(1)} %compare_select_fusion.refs_0_.at_ref, f32[2,1,512,2048]{3,2,1,0:T(8,128)S(1)} %copy-done, f32[2,1,512,128]{3,2,1,0:T(8,128)S(1)} %collective-permute-done.4.refs_2_, f32[4,128,256]{2,1,0:T(8,128)S(1)} %shard_map.76.refs_3_), custom_call_target="tpu_custom_call", output_to_operand_aliasing={{}: (3, {})} | custom-call | flops 1610612736 | bytes 2097152 | tf_op jit(solution)/shard_map/pallas_call | solution.py:218
  37.0 3.6 %shard_map.78.refs_3_ = f32[4,128,256]{2,1,0:T(8,128)S(1)} custom-call(s32[2]{0:T(128)S(1)} %compare_select_fusion.refs_0_.at_ref, f32[2,1,512,2048]{3,2,1,0:T(8,128)S(1)} %copy-done, f32[2,1,256,128]{3,2,1,0:T(8,128)S(1)} %collective-permute-done.2.refs_2_, f32[2,1,256,128]{3,2,1,0:T(8,128)S(1)} %collective-permute-done.refs_3_, ...), custom_call_target="tpu_custom_call", output_to_operand_aliasing={{}: (4, {})} | custom-call | flops 1610612736 | bytes 2097152 | tf_op jit(solution)/shard_map/pallas_call | solution.py:218
  40.6 2.1 %shard_map.79.refs_3_ = f32[4,128,256]{2,1,0:T(8,128)S(1)} custom-call(s32[2]{0:T(128)S(1)} %compare_select_fusion.refs_0_.at_ref, f32[2,1,512,2048]{3,2,1,0:T(8,128)S(1)} %copy-done, f32[2,1,256,128]{3,2,1,0:T(8,128)S(1)} %collective-permute-done.3.refs_2_, f32[4,128,256]{2,1,0:T(8,128)S(1)} %shard_map.78.refs_3_), custom_call_target="tpu_custom_call", output_to_operand_aliasing={{}: (3, {})} | custom-call | flops 805306368 | bytes 1048576 | tf_op jit(solution)/shard_map/pallas_call | solution.py:218
  43.9 2.1 %shard_map.80 = f32[2,1,512,128]{3,2,1,0:T(8,128)S(1)} custom-call(s32[2]{0:T(128)S(1)} %compare_select_fusion.refs_0_.at_ref, f32[2,1,512,2048]{3,2,1,0:T(8,128)S(1)} %copy-done, f32[2,1,256,128]{3,2,1,0:T(8,128)S(1)} %collective-permute-done.1.refs_2_, f32[4,128,256]{2,1,0:T(8,128)S(1)} %shard_map.79.refs_3_), custom_call_target="tpu_custom_call" | custom-call | flops 805306368 | bytes 1048576 | tf_op jit(solution)/shard_map/pallas_call | solution.py:218
  48.9 9.0 %collective-permute-done.5.refs_0_ = f32[2,1,512,128]{3,2,1,0:T(8,128)S(1)} collective-permute-done((f32[2,1,512,128]{3,2,1,0:T(8,128)S(1)}, f32[2,1,512,128]{3,2,1,0:T(8,128)S(1)}, u32[]{:S(2)}, u32[]{:S(2)}) %collective-permute-start.5) | collective-permute-done | bytes 524320 | tf_op jit(solution)/shard_map/ppermute | solution.py:22
  61.3 2.5 %collective-permute-start.10 = (f32[2,1,256,128]{3,2,1,0:T(8,128)S(1)}, f32[2,1,256,128]{3,2,1,0:T(8,128)S(1)}, u32[]{:S(2)}, u32[]{:S(2)}) collective-permute-start(f32[2,1,256,128]{3,2,1,0:T(8,128)S(1)} %get-tuple-element.21), channel_id=1, source_target_pairs={{0,8},{4,12},{8,0},{12,4},{1,9},{5,13},{9,1},{13,5},{2,10},{6,14},... | collective-permute-start | bytes 786440 | tf_op jit(solution)/shard_map/ppermute | solution.py:22
  64.3 15.7 %collective-permute-done.12.refs_3_.refs_4_ = f32[2,1,128,1024]{3,2,1,0:T(8,128)S(1)} collective-permute-done((f32[2,1,128,1024]{3,2,1,0:T(8,128)S(1)}, f32[2,1,128,1024]{3,2,1,0:T(8,128)S(1)}, u32[]{:S(2)}, u32[]{:S(2)}) %collective-permute-start.12) | collective-permute-done | bytes 1048608 | tf_op jit(solution)/shard_map/ppermute | solution.py:304
  80.0 4.8 %shard_map.82 = (f32[4,128,256]{2,1,0:T(8,128)S(1)}, f32[4,128,256]{2,1,0:T(8,128)S(1)}, f32[1,128,256]{2,1,0:T(8,128)S(1)}) custom-call(s32[2]{0:T(128)S(1)} %compare_select_fusion.refs_0_.at_ref, f32[2,1,512,2048]{3,2,1,0:T(8,128)S(1)} %bitcast.11, f32[2,1,512,128]{3,2,1,0:T(8,128)S(1)} %get-tuple-element.22.refs_2_, ...), custom_call_target="tpu_custom_call" | custom-call | flops 3221225472 | bytes 2097152 | tf_op jit(solution)/shard_map/pallas_call | solution.py:218
  84.7 3.6 %collective-permute-done.10.refs_2_ = f32[2,1,256,128]{3,2,1,0:T(8,128)S(1)} collective-permute-done((f32[2,1,256,128]{3,2,1,0:T(8,128)S(1)}, f32[2,1,256,128]{3,2,1,0:T(8,128)S(1)}, u32[]{:S(2)}, u32[]{:S(2)}) %collective-permute-start.10) | collective-permute-done | bytes 262176 | tf_op jit(solution)/shard_map/ppermute | solution.py:22
  88.3 3.5 %collective-permute-start.11 = (f32[2,1,256,128]{3,2,1,0:T(8,128)S(1)}, f32[2,1,256,128]{3,2,1,0:T(8,128)S(1)}, u32[]{:S(2)}, u32[]{:S(2)}) collective-permute-start(f32[2,1,256,128]{3,2,1,0:T(8,128)S(1)} %collective-permute-done.10.refs_2_), channel_id=1, source_target_pairs={{0,4},{4,0},{8,12},{12,8},{1,5},{5,1},{9,13},{13,9},{2,6},{6,2},{1... | collective-permute-start | bytes 786440 | tf_op jit(solution)/shard_map/ppermute | solution.py:22
  91.8 3.0 %collective-permute-done.8.refs_3_ = f32[2,1,256,128]{3,2,1,0:T(8,128)S(1)} collective-permute-done((f32[2,1,256,128]{3,2,1,0:T(8,128)S(1)}, f32[2,1,256,128]{3,2,1,0:T(8,128)S(1)}, u32[]{:S(2)}, u32[]{:S(2)}) %collective-permute-start.8) | collective-permute-done | bytes 262176 | tf_op jit(solution)/shard_map/ppermute | solution.py:22
  94.8 2.6 %collective-permute-start.9 = (f32[2,1,256,128]{3,2,1,0:T(8,128)S(1)}, f32[2,1,256,128]{3,2,1,0:T(8,128)S(1)}, u32[]{:S(2)}, u32[]{:S(2)}) collective-permute-start(f32[2,1,256,128]{3,2,1,0:T(8,128)S(1)} %collective-permute-done.8.refs_3_), channel_id=1, source_target_pairs={{0,4},{4,0},{8,12},{12,8},{1,5},{5,1},{9,13},{13,9},{2,6},{6,2},{1... | collective-permute-start | bytes 786440 | tf_op jit(solution)/shard_map/ppermute | solution.py:22
  97.5 4.8 %shard_map.83 = (f32[4,128,256]{2,1,0:T(8,128)S(1)}, f32[4,128,256]{2,1,0:T(8,128)S(1)}, f32[1,128,256]{2,1,0:T(8,128)S(1)}) custom-call(s32[2]{0:T(128)S(1)} %compare_select_fusion.refs_0_.at_ref, f32[2,1,512,2048]{3,2,1,0:T(8,128)S(1)} %bitcast.11, ...), custom_call_target="tpu_custom_call", output_to_operand_aliasing={{0}: (5, {}), {1}: (6, {}), {2}: (7, {})} | custom-call | flops 3221225472 | bytes 2097152 | tf_op jit(solution)/shard_map/pallas_call | solution.py:218
  102.3 4.2 %shard_map.84 = (f32[4,128,256]{2,1,0:T(8,128)S(1)}, f32[4,128,256]{2,1,0:T(8,128)S(1)}) custom-call(s32[2]{0:T(128)S(1)} %compare_select_fusion.refs_0_.at_ref, f32[2,1,512,2048]{3,2,1,0:T(8,128)S(1)} %bitcast.11, f32[2,1,256,128]{3,2,1,0:T(8,128)S(1)} %collective-permute-done.10.refs_2_, ...), custom_call_target="tpu_custom_call", output_to_operand_aliasing={{0}: (6, {}), {1}: (7, {})} | custom-call | flops 2415919104 | bytes 2097152 | tf_op jit(solution)/shard_map/pallas_call | solution.py:218
  106.5 2.1 %shard_map.85.refs_3_ = f32[4,128,256]{2,1,0:T(8,128)S(1)} custom-call(s32[2]{0:T(128)S(1)} %compare_select_fusion.refs_0_.at_ref, f32[2,1,512,2048]{3,2,1,0:T(8,128)S(1)} %bitcast.11, f32[2,1,256,128]{3,2,1,0:T(8,128)S(1)} %collective-permute-done.11.refs_2_, f32[4,128,256]{2,1,0:T(8,128)S(1)} %get-tuple-element.28.refs_3_), custom_call_target="tpu_custom_call", output_to_operand_aliasing={{}: (3, {})} | custom-call | flops 805306368 | bytes 1048576 | tf_op jit(solution)/shard_map/pallas_call | solution.py:218
  108.6 2.9 %shard_map.86 = f32[2,1,512,128]{3,2,1,0:T(8,128)} custom-call(s32[2]{0:T(128)S(1)} %compare_select_fusion.refs_0_.at_ref, f32[2,1,512,2048]{3,2,1,0:T(8,128)S(1)} %bitcast.11, f32[2,1,256,128]{3,2,1,0:T(8,128)S(1)} %collective-permute-done.9.refs_2_.refs_3_, f32[4,128,256]{2,1,0:T(8,128)S(1)} %shard_map.85.refs_3_), custom_call_target="tpu_custom_call" | custom-call | flops 805306368 | bytes 1048576 | tf_op jit(solution)/shard_map/pallas_call | solution.py:218
  112.0 8.9 %collective-permute-done.16.refs_0_ = f32[2,1,512,128]{3,2,1,0:T(8,128)S(1)} collective-permute-done((f32[2,1,512,128]{3,2,1,0:T(8,128)}, f32[2,1,512,128]{3,2,1,0:T(8,128)S(1)}, u32[]{:S(2)}, u32[]{:S(2)}) %collective-permute-start.16) | collective-permute-done | bytes 524320 | tf_op jit(solution)/shard_map/ppermute | solution.py:22
  122.2 6.5 %collective-permute-done.15.refs_7_ = f32[1,128,256]{2,1,0:T(8,128)S(1)} collective-permute-done((f32[1,128,256]{2,1,0:T(8,128)S(1)}, f32[1,128,256]{2,1,0:T(8,128)S(1)}, u32[]{:S(2)}, u32[]{:S(2)}) %collective-permute-start.15) | collective-permute-done | bytes 131104 | tf_op jit(solution)/shard_map/ppermute | solution.py:374
  128.7 4.7 %shard_map.87 = f32[2,1,512,128]{3,2,1,0:T(8,128)} custom-call(s32[2]{0:T(128)S(1)} %compare_select_fusion.refs_0_.at_ref, f32[2,1,512,2048]{3,2,1,0:T(8,128)S(1)} %bitcast.11, f32[2,1,256,128]{3,2,1,0:T(8,128)S(1)} %collective-permute-done.11.refs_2_, f32[2,1,256,128]{3,2,1,0:T(8,128)S(1)} %collective-permute-done.9.refs_2_.refs_3_, ...), custom_call_target="tpu_custom_call" | custom-call | flops 1610612736 | bytes 2097152 | tf_op jit(solution)/shard_map/pallas_call | solution.py:218
  (49 shorter events, 20.6 us)
Async XLA Ops:
  0.6 32.8 %collective-permute-start.4 = (f32[2,1,512,128]{3,2,1,0:T(8,128)}, f32[2,1,512,128]{3,2,1,0:T(8,128)S(1)}, u32[]{:S(2)}, u32[]{:S(2)}) collective-permute-start(f32[2,1,512,128]{3,2,1,0:T(8,128)} %contact_ref.3), channel_id=1, source_target_pairs={{0,4},{4,0},{8,12},{12,8},{1,5},{5,1},{9,13},{13,9},{2,6},{6,2},{1... | collective-permute-start | bytes 1572872 | tf_op jit(solution)/shard_map/ppermute | solution.py:22
  5.6 25.8 %collective-permute-start = (f32[2,1,256,128]{3,2,1,0:T(8,128)}, f32[2,1,256,128]{3,2,1,0:T(8,128)S(1)}, u32[]{:S(2)}, u32[]{:S(2)}) collective-permute-start(f32[2,1,256,128]{3,2,1,0:T(8,128)} %get-tuple-element.36), channel_id=1, source_target_pairs={{0,8},{4,12},{8,0},{12,4},{1,9},{5,13},{9,1},{13,5},{2,10},{6,14},... | collective-permute-start | bytes 786440 | tf_op jit(solution)/shard_map/ppermute | solution.py:22
  8.2 23.2 %collective-permute-start.2 = (f32[2,1,256,128]{3,2,1,0:T(8,128)}, f32[2,1,256,128]{3,2,1,0:T(8,128)S(1)}, u32[]{:S(2)}, u32[]{:S(2)}) collective-permute-start(f32[2,1,256,128]{3,2,1,0:T(8,128)} %get-tuple-element.35), channel_id=1, source_target_pairs={{0,8},{4,12},{8,0},{12,4},{1,9},{5,13},{9,1},{13,5},{2,10},{6,14},... | collective-permute-start | bytes 786440 | tf_op jit(solution)/shard_map/ppermute | solution.py:22
  12.2 3.4 %copy-start = (f32[2,1,512,2048]{3,2,1,0:T(8,128)S(1)}, f32[2,1,512,2048]{3,2,1,0:T(8,128)}, u32[]{:S(2)}) copy-start(f32[2,1,512,2048]{3,2,1,0:T(8,128)} %refs_1_.21) | copy-start | bytes 25165828
  15.6 1.0 copy-start.1
  31.4 9.2 %collective-permute-start.3 = (f32[2,1,256,128]{3,2,1,0:T(8,128)S(1)}, f32[2,1,256,128]{3,2,1,0:T(8,128)S(1)}, u32[]{:S(2)}, u32[]{:S(2)}) collective-permute-start(f32[2,1,256,128]{3,2,1,0:T(8,128)S(1)} %collective-permute-done.2.refs_2_), channel_id=1, source_target_pairs={{0,4},{4,0},{8,12},{12,8},{1,5},{5,1},{9,13},{13,9},{2,6},{6,2},{1... | collective-permute-start | bytes 786440 | tf_op jit(solution)/shard_map/ppermute | solution.py:22
  31.4 12.6 %collective-permute-start.1 = (f32[2,1,256,128]{3,2,1,0:T(8,128)S(1)}, f32[2,1,256,128]{3,2,1,0:T(8,128)S(1)}, u32[]{:S(2)}, u32[]{:S(2)}) collective-permute-start(f32[2,1,256,128]{3,2,1,0:T(8,128)S(1)} %collective-permute-done.refs_3_), channel_id=1, source_target_pairs={{0,4},{4,0},{8,12},{12,8},{1,5},{5,1},{9,13},{13,9},{2,6},{6,2},{1... | collective-permute-start | bytes 786440 | tf_op jit(solution)/shard_map/ppermute | solution.py:22
  40.5 19.2 %copy-start.2 = (s32[3]{0:T(128)S(1)}, s32[3]{0:T(128)}, u32[]{:S(2)}) copy-start(s32[3]{0:T(128)} %shift_ref.3) | copy-start | bytes 40
  40.6 39.4 %slice-start = ((s8[8388608]{0:T(1024)(128)(4,1)}), s8[4194304]{0:T(1024)(128)(4,1)S(1)}, s32[]{:S(2)}) async-start(s8[8388608]{0:T(1024)(128)(4,1)} %bitcast.10), calls=%async_computation | async-start | bytes 8388608
  42.6 37.3 %slice-start.1 = ((s8[8388608]{0:T(1024)(128)(4,1)}), s8[4194304]{0:T(1024)(128)(4,1)S(1)}, s32[]{:S(2)}) async-start(s8[8388608]{0:T(1024)(128)(4,1)} %bitcast.10), calls=%async_computation.1 | async-start | bytes 8388608
  46.1 11.8 %collective-permute-start.5 = (f32[2,1,512,128]{3,2,1,0:T(8,128)S(1)}, f32[2,1,512,128]{3,2,1,0:T(8,128)S(1)}, u32[]{:S(2)}, u32[]{:S(2)}) collective-permute-start(f32[2,1,512,128]{3,2,1,0:T(8,128)S(1)} %shard_map.80), channel_id=1, source_target_pairs={{0,2},{1,3},{2,0},{3,1},{4,6},{5,7},{6,4},{7,5},{8,10},{9,11},{10,... | collective-permute-start | bytes 1572872 | tf_op jit(solution)/shard_map/ppermute | solution.py:22
  47.6 32.3 %collective-permute-start.12 = (f32[2,1,128,1024]{3,2,1,0:T(8,128)S(1)}, f32[2,1,128,1024]{3,2,1,0:T(8,128)S(1)}, u32[]{:S(2)}, u32[]{:S(2)}) collective-permute-start(f32[2,1,128,1024]{3,2,1,0:T(8,128)S(1)} %get-tuple-element.34), channel_id=1, source_target_pairs={{0,4},{4,0},{8,12},{12,8},{1,5},{5,1},{9,13},{13,9},{2,6},{6,2},{1... | collective-permute-start | bytes 3145736 | tf_op jit(solution)/shard_map/ppermute | solution.py:304
  47.9 32.0 %collective-permute-start.13 = (f32[2,1,128,1024]{3,2,1,0:T(8,128)S(1)}, f32[2,1,128,1024]{3,2,1,0:T(8,128)S(1)}, u32[]{:S(2)}, u32[]{:S(2)}) collective-permute-start(f32[2,1,128,1024]{3,2,1,0:T(8,128)S(1)} %get-tuple-element.33), channel_id=1, source_target_pairs={{4,8},{8,4},{5,9},{9,5},{6,10},{10,6},{7,11},{11,7},{20,24},{24,20... | collective-permute-start | bytes 3145736 | tf_op jit(solution)/shard_map/ppermute | solution.py:304
  48.8 9.0 %collective-permute-start.6 = (f32[2,1,512,128]{3,2,1,0:T(8,128)S(1)}, f32[2,1,512,128]{3,2,1,0:T(8,128)S(1)}, u32[]{:S(2)}, u32[]{:S(2)}) collective-permute-start(f32[2,1,512,128]{3,2,1,0:T(8,128)S(1)} %shard_map.80), channel_id=1, source_target_pairs={{0,1},{1,0},{2,3},{3,2},{4,5},{5,4},{6,7},{7,6},{8,9},{9,8},{10,11... | collective-permute-start | bytes 1572872 | tf_op jit(solution)/shard_map/ppermute | solution.py:22
  57.8 1.9 %collective-permute-start.7 = (f32[2,1,512,128]{3,2,1,0:T(8,128)S(1)}, f32[2,1,512,128]{3,2,1,0:T(8,128)S(1)}, u32[]{:S(2)}, u32[]{:S(2)}) collective-permute-start(f32[2,1,512,128]{3,2,1,0:T(8,128)S(1)} %collective-permute-done.5.refs_0_), channel_id=1, source_target_pairs={{0,1},{1,0},{2,3},{3,2},{4,5},{5,4},{6,7},{7,6},{8,9},{9,8},{10,11... | collective-permute-start | bytes 1572872 | tf_op jit(solution)/shard_map/ppermute | solution.py:22
  60.7 36.7 %collective-permute-start.14 = (f32[2,1,512,128]{3,2,1,0:T(8,128)S(1)}, f32[2,1,512,128]{3,2,1,0:T(8,128)S(1)}, u32[]{:S(2)}, u32[]{:S(2)}) collective-permute-start(f32[2,1,512,128]{3,2,1,0:T(8,128)S(1)} %get-tuple-element.22.refs_2_), channel_id=1, source_target_pairs={{0,4},{4,0},{8,12},{12,8},{1,5},{5,1},{9,13},{13,9},{2,6},{6,2},{1... | collective-permute-start | bytes 1572872 | tf_op jit(solution)/shard_map/ppermute | solution.py:22
  61.3 27.0 %collective-permute-start.10 = (f32[2,1,256,128]{3,2,1,0:T(8,128)S(1)}, f32[2,1,256,128]{3,2,1,0:T(8,128)S(1)}, u32[]{:S(2)}, u32[]{:S(2)}) collective-permute-start(f32[2,1,256,128]{3,2,1,0:T(8,128)S(1)} %get-tuple-element.21), channel_id=1, source_target_pairs={{0,8},{4,12},{8,0},{12,4},{1,9},{5,13},{9,1},{13,5},{2,10},{6,14},... | collective-permute-start | bytes 786440 | tf_op jit(solution)/shard_map/ppermute | solution.py:22
  63.8 31.0 %collective-permute-start.8 = (f32[2,1,256,128]{3,2,1,0:T(8,128)S(1)}, f32[2,1,256,128]{3,2,1,0:T(8,128)S(1)}, u32[]{:S(2)}, u32[]{:S(2)}) collective-permute-start(f32[2,1,256,128]{3,2,1,0:T(8,128)S(1)} %get-tuple-element.20), channel_id=1, source_target_pairs={{0,8},{4,12},{8,0},{12,4},{1,9},{5,13},{9,1},{13,5},{2,10},{6,14},... | collective-permute-start | bytes 786440 | tf_op jit(solution)/shard_map/ppermute | solution.py:22
  88.3 18.2 %collective-permute-start.11 = (f32[2,1,256,128]{3,2,1,0:T(8,128)S(1)}, f32[2,1,256,128]{3,2,1,0:T(8,128)S(1)}, u32[]{:S(2)}, u32[]{:S(2)}) collective-permute-start(f32[2,1,256,128]{3,2,1,0:T(8,128)S(1)} %collective-permute-done.10.refs_2_), channel_id=1, source_target_pairs={{0,4},{4,0},{8,12},{12,8},{1,5},{5,1},{9,13},{13,9},{2,6},{6,2},{1... | collective-permute-start | bytes 786440 | tf_op jit(solution)/shard_map/ppermute | solution.py:22
  94.8 13.7 %collective-permute-start.9 = (f32[2,1,256,128]{3,2,1,0:T(8,128)S(1)}, f32[2,1,256,128]{3,2,1,0:T(8,128)S(1)}, u32[]{:S(2)}, u32[]{:S(2)}) collective-permute-start(f32[2,1,256,128]{3,2,1,0:T(8,128)S(1)} %collective-permute-done.8.refs_3_), channel_id=1, source_target_pairs={{0,4},{4,0},{8,12},{12,8},{1,5},{5,1},{9,13},{13,9},{2,6},{6,2},{1... | collective-permute-start | bytes 786440 | tf_op jit(solution)/shard_map/ppermute | solution.py:22
  111.5 9.4 %collective-permute-start.16 = (f32[2,1,512,128]{3,2,1,0:T(8,128)}, f32[2,1,512,128]{3,2,1,0:T(8,128)S(1)}, u32[]{:S(2)}, u32[]{:S(2)}) collective-permute-start(f32[2,1,512,128]{3,2,1,0:T(8,128)} %shard_map.86), channel_id=1, source_target_pairs={{0,2},{1,3},{2,0},{3,1},{4,6},{5,7},{6,4},{7,5},{8,10},{9,11},{10,... | collective-permute-start | bytes 1572872 | tf_op jit(solution)/shard_map/ppermute | solution.py:22
  112.0 21.4 %collective-permute-start.17 = (f32[2,1,512,128]{3,2,1,0:T(8,128)}, f32[2,1,512,128]{3,2,1,0:T(8,128)S(1)}, u32[]{:S(2)}, u32[]{:S(2)}) collective-permute-start(f32[2,1,512,128]{3,2,1,0:T(8,128)} %shard_map.86), channel_id=1, source_target_pairs={{0,1},{1,0},{2,3},{3,2},{4,5},{5,4},{6,7},{7,6},{8,9},{9,8},{10,11... | collective-permute-start | bytes 1572872 | tf_op jit(solution)/shard_map/ppermute | solution.py:22
  120.9 12.5 %collective-permute-start.18 = (f32[2,1,512,128]{3,2,1,0:T(8,128)S(1)}, f32[2,1,512,128]{3,2,1,0:T(8,128)S(1)}, u32[]{:S(2)}, u32[]{:S(2)}) collective-permute-start(f32[2,1,512,128]{3,2,1,0:T(8,128)S(1)} %collective-permute-done.16.refs_0_), channel_id=1, source_target_pairs={{0,1},{1,0},{2,3},{3,2},{4,5},{5,4},{6,7},{7,6},{8,9},{9,8},{10,11... | collective-permute-start | bytes 1572872 | tf_op jit(solution)/shard_map/ppermute | solution.py:22
  120.9 7.8 %collective-permute-start.15 = (f32[1,128,256]{2,1,0:T(8,128)S(1)}, f32[1,128,256]{2,1,0:T(8,128)S(1)}, u32[]{:S(2)}, u32[]{:S(2)}) collective-permute-start(f32[1,128,256]{2,1,0:T(8,128)S(1)} %get-tuple-element.30), channel_id=1, source_target_pairs={{4,0},{8,4},{12,8},{5,1},{9,5},{13,9},{6,2},{10,6},{14,10},{7,3},{... | collective-permute-start | bytes 393224 | tf_op jit(solution)/shard_map/ppermute | solution.py:374

commit v3 on v2

--- a/solution.py
+++ b/solution.py
@@ -22,14 +22,15 @@
     return lax.ppermute(x, axis, [(i, i ^ bit) for i in range(lax.axis_size(axis))])
 
 
-def spread(x, axis):
-    pieces = [(0, x)]
+def spread(chunks, axis):
+    pieces = [[(0, chunk)] for chunk in chunks]
     bit = lax.axis_size(axis) // 2
     while bit:
-        found = []
-        for far, piece in pieces:
-            found.append((far ^ bit, swapped(piece, axis, bit)))
-        pieces += found
+        for own in pieces:
+            found = []
+            for far, piece in own:
+                found.append((far ^ bit, swapped(piece, axis, bit)))
+            own += found
         bit //= 2
     return pieces
 
@@ -69,7 +70,7 @@
     return tuple(v[start : start + size] for v in x)
 
 
-def panel_kernel(local, far, starts, diag, upper, back, first, last, devices, scale, *refs):
+def panel_kernel(local, far, starts, diag, upper, back, first, last, chunks, devices, scale, *refs):
     refs = list(refs)
     at_ref, g_ref = refs[:2]
     piece_refs, refs = refs[2 : 2 + len(starts)], refs[2 + len(starts) :]
@@ -80,8 +81,6 @@
     ins = []
     if not first:
         ins, refs = refs[:count], refs[count:]
-    if last and upper:
-        above_ref, refs = refs[0], refs[1:]
     outs = refs
     pan = at_ref[0]
     source = pan ^ far
@@ -126,7 +125,9 @@
         if diag:
             value = old(0, i) + terms[:B]
             if last:
-                put(outs[0], i, value)
+                for ref in outs[chunks:]:
+                    put(ref, i, value)
+                put(outs[i * chunks // local], i % (local // chunks), value)
             else:
                 outs[0][i] = value
         if upper and i < local - 1:
@@ -167,7 +168,7 @@
                 for product, column in zip(products, columns)
             )
             if last:
-                put(outs[at_upper], local - 1, edge_sum[local - 1] + terms + above_ref[0])
+                put(outs[at_upper], local - 1, edge_sum[local - 1] + terms)
             else:
                 edge_sum[local - 1] += terms
 
@@ -175,7 +176,7 @@
 
             @pl.when(jnp.logical_not(theirs))
             def _():
-                put(outs[at_upper], local - 1, edge_sum[local - 1] + above_ref[0])
+                put(outs[at_upper], local - 1, edge_sum[local - 1])
 
         if back:
 
@@ -190,7 +191,7 @@
                 )
 
 
-def panel(at, green, far, pieces, carry, edges, kinds, last, above=None):
+def panel(at, green, far, pieces, carry, edges, kinds, last, chunks=1, whole=False):
     rows = green.shape[2]
     local = rows // B
     devices = lax.axis_size("pan")
@@ -212,8 +213,11 @@
             operands.append(carry[kind])
     if last:
         shapes = {kind: jax.ShapeDtypeStruct((2, 1, rows, B), F32) for kind in kinds}
-        if above is not None:
-            operands.append(above)
+        if "diag" in kinds:
+            part = jax.ShapeDtypeStruct((2, 1, rows // chunks, B), F32)
+            shapes = {number: part for number in range(chunks)}
+            if whole:
+                shapes["whole"] = jax.ShapeDtypeStruct((2, 1, rows, B), F32)
     work = 3 * 2 * (2 * B) * (2 * B) * rows * many * (1 + len(kinds))
     out = pl.pallas_call(
         functools.partial(
@@ -226,6 +230,7 @@
             "back" in kinds,
             carry is None,
             last,
+            chunks,
             devices,
             1.0 / math.sqrt(B),
         ),
@@ -238,51 +243,145 @@
             flops=work, bytes_accessed=8 * rows * B * many, transcendentals=0
         ),
     )(*operands)
+    if last and "diag" in kinds:
+        return {"diag": out}
     return dict(zip(kinds, out))
 
 
-def phonon_kernel(fars, modes, shift_ref, at_ref, contact_ref, col_ref, row_ref, *refs):
-    out_refs = refs[len(fars) :]
+def phonon_kernel(fars, modes, row, size, final, scale, shift_ref, at_ref, contact_ref, *refs):
+    col_ref, row_ref = refs[:2]
+    piece_refs, refs = refs[2 : 2 + len(fars)], refs[2 + len(fars) :]
     energy = at_ref[1]
     chosen = []
     for far in fars:
         apart = jnp.abs((energy ^ far) - energy)
         chosen.append([jnp.where(apart == shift_ref[m], 1.0, 0.0).astype(F32) for m in range(modes)])
-    for start in range(0, contact_ref.shape[2], B):
-        rows = slice(start, start + B)
+    out_ref = refs[-2] if final and len(refs) > 2 else refs[-1]
+    for start in range(0, size, B):
+        rows = slice(row + start, row + start + B)
+        here = slice(start, start + B)
         outer = [col_ref[rows, m : m + 1] * row_ref[m : m + 1, rows] for m in range(modes)]
         values = [contact_ref[0, 0, rows], contact_ref[1, 0, rows]]
-        for weights, ref in zip(chosen, refs):
+        for weights, ref in zip(chosen, piece_refs):
             weight = total(w * o for w, o in zip(weights, outer))
-            values = [value + weight * ref[j, 0, rows] for j, value in enumerate(values)]
-        first = 0
-        for number, ref in enumerate(out_refs):
-            at = start if number == 0 else start - first
-            if 0 <= at < ref.shape[2]:
-                for j in range(2):
-                    ref[j, 0, at : at + B] = values[j]
-            if number > 0:
-                first += ref.shape[2]
-
-
-def phonon(shifts, at, contact, columns, lines, pieces, chunks):
+            values = [value + weight * ref[j, 0, here] for j, value in enumerate(values)]
+        for j in range(2):
+            out_ref[j, 0, here] = values[j]
+    if final and len(refs) > 2:
+        upper_ref, above_ref = refs[:2]
+        for j in range(2):
+            more = above_ref[0, :, j * B : (j + 1) * B].T * scale
+            refs[-1][j, 0] = upper_ref[j, 0] + more
+
+
+def phonon(shifts, at, contact, columns, lines, pieces, number, chunks):
     parts, energies, rows = contact.shape[:3]
-    modes = shifts.shape[0]
+    size = rows // chunks
     vmem = pl.BlockSpec(memory_space=pltpu.VMEM)
     smem = pl.BlockSpec(memory_space=pltpu.SMEM)
-    shapes = [jax.ShapeDtypeStruct(contact.shape, F32)]
-    if chunks > 1:
-        shapes += [jax.ShapeDtypeStruct((parts, energies, rows // chunks, B), F32)] * chunks
     return pl.pallas_call(
-        functools.partial(phonon_kernel, [far for far, _ in pieces], modes),
+        functools.partial(
+            phonon_kernel,
+            [far for far, _ in pieces],
+            shifts.shape[0],
+            number * size,
+            size,
+            False,
+            1.0,
+        ),
         in_specs=[smem, smem] + [vmem] * (3 + len(pieces)),
-        out_specs=[vmem] * len(shapes),
-        out_shape=shapes,
+        out_specs=vmem,
+        out_shape=jax.ShapeDtypeStruct((parts, energies, size, B), F32),
         compiler_params=pltpu.CompilerParams(vmem_limit_bytes=VMEM_BYTES),
         cost_estimate=pl.CostEstimate(
-            flops=rows * B * 20, bytes_accessed=8 * rows * B * 5, transcendentals=0
+            flops=size * B * 20, bytes_accessed=8 * size * B * 5, transcendentals=0
         ),
     )(shifts, at, contact, columns, lines, *[piece for _, piece in pieces])
+
+
+def skip_kernel(count, kernel, *refs):
+    kernel(*refs[:count], *refs[count + 1 :])
+
+
+def phonon_final(shifts, at, contact, columns, lines, pieces, number, chunks, so_far, ends):
+    rows = contact.shape[2]
+    size = rows // chunks
+    vmem = pl.BlockSpec(memory_space=pltpu.VMEM)
+    smem = pl.BlockSpec(memory_space=pltpu.SMEM)
+    kernel = functools.partial(
+        phonon_kernel,
+        [far for far, _ in pieces],
+        shifts.shape[0],
+        number * size,
+        size,
+        True,
+        1.0 / math.sqrt(B),
+    )
+    operands = [shifts, at, contact, columns, lines, *[piece for _, piece in pieces]]
+    specs = [smem, smem] + [vmem] * (3 + len(pieces))
+    shapes = [jax.ShapeDtypeStruct(contact.shape, F32)]
+    out_specs = [pl.BlockSpec((2, 1, size, B), lambda i: (0, 0, number, 0))]
+    aliases = {}
+    if so_far is not None:
+        kernel = functools.partial(skip_kernel, len(operands), kernel)
+        aliases[len(operands)] = 0
+        operands.append(so_far)
+        specs.append(pl.BlockSpec(memory_space=pl.ANY))
+    if ends is not None:
+        upper, above = ends
+        tail = pl.BlockSpec((2, 1, B, B), lambda i: (0, 0, rows // B - 1, 0))
+        aliases[len(operands)] = 1
+        operands += [upper, above]
+        specs += [tail, vmem]
+        shapes.append(jax.ShapeDtypeStruct(upper.shape, F32))
+        out_specs.append(tail)
+    return pl.pallas_call(
+        kernel,
+        grid=(1,),
+        in_specs=specs,
+        out_specs=out_specs,
+        out_shape=shapes,
+        input_output_aliases=aliases,
+        compiler_params=pltpu.CompilerParams(vmem_limit_bytes=VMEM_BYTES),
+        cost_estimate=pl.CostEstimate(
+            flops=size * B * 20, bytes_accessed=8 * size * B * 5, transcendentals=0
+        ),
+    )(*operands)
+
+
+def cut_kernel(contact_ref, *refs):
+    outs, sems = refs[:-1], refs[-1]
+    copies = []
+    start = 0
+    for number, ref in enumerate(outs):
+        size = ref.shape[2]
+        at = 0 if number == len(outs) - 1 else start
+        start += size
+        copies.append(
+            pltpu.make_async_copy(contact_ref.at[:, :, pl.ds(at, size)], ref, sems.at[number])
+        )
+    for copy in copies:
+        copy.start()
+    for copy in copies:
+        copy.wait()
+
+
+def cut(contact, chunks):
+    parts, energies, rows = contact.shape[:3]
+    part = jax.ShapeDtypeStruct((parts, energies, rows // chunks, B), F32)
+    vmem = pl.BlockSpec(memory_space=pltpu.VMEM)
+    return pl.pallas_call(
+        cut_kernel,
+        in_specs=[pl.BlockSpec(memory_space=pltpu.HBM)],
+        out_specs=[vmem] * (chunks + 1),
+        out_shape=[part] * chunks + [jax.ShapeDtypeStruct(contact.shape, F32)],
+        scratch_shapes=[pltpu.SemaphoreType.DMA((chunks + 1,))],
+        compiler_params=pltpu.CompilerParams(vmem_limit_bytes=VMEM_BYTES),
+        cost_estimate=pl.CostEstimate(
+            flops=0, bytes_accessed=32 * rows * B, transcendentals=0
+        ),
+        name="cut",
+    )(contact)
 
 
 def edge_rows(retarded, pan):
@@ -305,11 +404,11 @@
     return found, cuts
 
 
-def gathered(whole, chunks):
-    size = whole.shape[2] // B // len(chunks)
+def gathered(near, chunks):
+    size = chunks[0].shape[2] // B
     parts = [(i * size, chunk) for i, chunk in enumerate(chunks)]
     first = lax.axis_size("pan") // 2
-    pieces = [(0, [(0, whole)])]
+    pieces = [(0, near)]
     bit = first
     while bit:
         found = []
@@ -329,6 +428,7 @@
     rows = retarded.shape[2]
     local = rows // B
     chunks = 2 if local % 2 == 0 else 1
+    high = lax.axis_size("pan") // 2
     pan = lax.axis_index("pan").astype(jnp.int32)
     energy = lax.axis_index("en").astype(jnp.int32)
     at = jnp.where(jnp.arange(2, dtype=jnp.int32) == 0, pan, energy)
@@ -341,43 +441,47 @@
     per_row = jnp.repeat(per_atom, ORB, axis=0)
     per_line = jnp.repeat(per_atom.T, ORB, axis=1)
     edges, cuts = edge_rows(retarded, pan)
-    sigma = contact
-    parts = [contact]
-    if chunks > 1:
-        size = rows // chunks
-        parts = [contact[:, :, i * size : (i + 1) * size] for i in range(chunks)]
+    *parts, copied = cut(contact, chunks)
+    near = [(0, contact)]
     for rounds in range(ITERS):
         final = rounds == ITERS - 1
-        pieces = gathered(sigma, parts)
+        pieces = gathered(near, parts)
         if rounds == 0:
-            ready = lax.optimization_barrier((contact, per_row, per_line, *cuts))
+            ready = lax.optimization_barrier((copied, per_row, per_line, *cuts))
             pieces[0] = (0, [(0, ready[0])])
-            per_row, per_line = ready[1:3]
+            copied, per_row, per_line = ready[:3]
         work = ("diag", "upper", "back") if final else ("diag",)
         sums = None
-        order = sorted(pieces[:-1], key=lambda piece: (piece[0] != 0, piece[0] >= lax.axis_size("pan") // 2))
-        for far, blocks in order:
-            kinds_here = work
-            if final and far >= lax.axis_size("pan") // 2:
-                kinds_here = work[:2]
+        groups = [(far, 0, blocks) for far, blocks in pieces[:-1]]
+        groups.sort(key=lambda group: (group[0] != 0, group[0] >= high))
+        if final and chunks > 1 and 1 < high:
+            far, _, blocks = groups.pop([far for far, _, _ in groups].index(high))
+            groups.insert(1, (far, 0, blocks[:1]))
+            groups.append((far, 1, blocks[1:]))
+        for far, number, blocks in groups:
+            kinds_here = work[:2] if final and far >= high else work
             new = panel(at, retarded, far, blocks, sums, edges, kinds_here, False)
             sums = dict(sums or {}, **new)
         far, blocks = pieces[-1]
         for number, block in enumerate(blocks):
             last = number == len(blocks) - 1
-            new = panel(at, retarded, far, [block], sums, edges, ("diag",), last)
+            new = panel(
+                at, retarded, far, [block], sums, edges, ("diag",), last, chunks, final and last
+            )
             sums = dict(sums, **new)
-        lesser_diag = sums["diag"]
-        found = spread(lesser_diag, "en")[1:]
-        if final:
-            devices = lax.axis_size("pan")
-            above = lax.ppermute(sums["back"], "pan", [(i + 1, i) for i in range(devices - 1)])
-            lesser_upper = panel(
-                at, retarded, far, blocks, sums, edges, ("upper",), True, above
-            )["upper"]
-        out = phonon(shifts, at, contact, per_row, per_line, found, 1 if final else chunks)
-        sigma, parts = out[0], (out[1:] if len(out) > 1 else out)
-    return (lesser_diag, lesser_upper, sigma)
+        found = spread(sums["diag"][:chunks], "en")
+        settings = (shifts, at, copied, per_row, per_line)
+        if not final:
+            parts = [phonon(*settings, own[1:], number, chunks) for number, own in enumerate(found)]
+            near = [(i * (local // chunks), part) for i, part in enumerate(parts)]
+    devices = lax.axis_size("pan")
+    above = lax.ppermute(sums["back"], "pan", [(i + 1, i) for i in range(devices - 1)])
+    upper = panel(at, retarded, far, blocks, sums, edges, ("upper",), True)["upper"]
+    sigma = None
+    for number, own in enumerate(found):
+        ends = (upper, above) if number == chunks - 1 else None
+        sigma, *rest = phonon_final(*settings, own[1:], number, chunks, sigma, ends)
+    return (sums["diag"][chunks], rest[0], sigma)
 
 
 def solution(mesh):

time: 135 us -> 143 us (1.059)
  Pallas kernels: 41 us -> 45.5 us
  waiting for transfers between devices: 61 us -> 63.7 us
    ppermute x16 -> x23, waiting for transfers between devices: 38.8 us -> 63.3 us  [swapped(): lax.ppermute(x, axis, [(i, i ^ bit) for i in range(lax.axis_size(axis))])]
    ppermute x2, waiting for transfers between devices: 15.7 us -> 0.01 us  [edge_rows(): found.append(lax.ppermute(part, 'pan', pairs))]
    ppermute x1, waiting for transfers between devices: 6.5 us -> 0.32 us  [body(): lax.ppermute(sums['back'], 'pan', [(i + 1, i) for i in range(devices - 1)])]
    pallas_call x0 -> x3, Pallas kernels: none -> 4.27 us  [the longest x2 3.38 us: phonon_final(): pl.pallas_call(kernel, grid=(1,), in_specs=specs, out_specs=out_specs, ou...]
    slice x1 -> x0, local copies, waits for them, and re-layouts: 1.85 us -> none  [body(): parts = [contact[:, :, i * size:(i + 1) * size] for i in range(chunks)]]
    dynamic_slice x1, local copies, waits for them, and re-layouts: 1.68 us -> 3.15 us  [edge_rows(): lax.dynamic_slice(retarded, (0, 0, row, column), (2, 1, B, columns // 2))]
    pallas_call x11 -> x12, Pallas kernels: 38.3 us -> 39.7 us  [panel(): pl.pallas_call(functools.partial(panel_kernel, local, far, starts, 'diag'...]
    ppermute x16 -> x23, starting transfers between devices: 19.9 us -> 20.8 us  [swapped(): lax.ppermute(x, axis, [(i, i ^ bit) for i in range(lax.axis_size(axis))])]
  transfers between devices with their start and end apart: 19 -> 26, of which waited for: 9 -> 10; matrix products, arithmetic and copies ran while one was open for 4% -> 4% of each run, Pallas kernels for 25% -> 29%
where the time goes in v3:
time: 143 us
  waiting for transfers between devices  63.7 us (45%)
  Pallas kernels  45.5 us (32%)
  starting transfers between devices  23 us (16%)
  local copies, waits for them, and re-layouts  8.67 us (6%)
    ppermute x23, waiting for transfers between devices, swapped(): lax.ppermute(x, axis, [(i, i ^ bit) for i in range(lax.axis_size(axis))])  63.3 us
    pallas_call x12, Pallas kernels, panel(): pl.pallas_call(functools.partial(panel_kernel, local, far, starts, 'diag'...  39.7 us
    ppermute x23, starting transfers between devices, swapped(): lax.ppermute(x, axis, [(i, i ^ bit) for i in range(lax.axis_size(axis))])  20.8 us
    unnamed x10, local copies, waits for them, and re-layouts  4.47 us
    pallas_call x2, Pallas kernels, phonon_final(): pl.pallas_call(kernel, grid=(1,), in_specs=specs, out_specs=out_specs, ou...  3.38 us
    dynamic_slice x1, local copies, waits for them, and re-layouts, edge_rows(): lax.dynamic_slice(retarded, (0, 0, row, column), (2, 1, B, columns // 2))  3.15 us
  transfers between devices with their start and end apart: 26, of which 10 were waited for; matrix products, arithmetic and copies ran while one was open for 4% of the time, Pallas kernels for 29%

profile of v3, /device:TPU:0, one launch (start us, length us, event | category | flops | bytes accessed | tf_op | source)
XLA Modules:
  0.0 142.7 jit_solution(11323642793517796934)
XLA Ops:
  0.6 3.1 %collective-permute-start.4 = (f32[2,1,512,128]{3,2,1,0:T(8,128)}, f32[2,1,512,128]{3,2,1,0:T(8,128)S(1)}, u32[]{:S(2)}, u32[]{:S(2)}) collective-permute-start(f32[2,1,512,128]{3,2,1,0:T(8,128)} %contact_ref.1), channel_id=1, source_target_pairs={{0,4},{4,0},{8,12},{12,8},{1,5},{5,1},{9,13},{13,9},{2,6},{6,2},{1... | collective-permute-start | bytes 1572872 | tf_op jit(solution)/shard_map/ppermute | solution.py:22
  5.7 2.7 %collective-permute-start = (f32[2,1,256,128]{3,2,1,0:T(8,128)}, f32[2,1,256,128]{3,2,1,0:T(8,128)}, u32[]{:S(2)}, u32[]{:S(2)}) collective-permute-start(f32[2,1,256,128]{3,2,1,0:T(8,128)} %get-tuple-element.30), channel_id=1, source_target_pairs={{0,8},{4,12},{8,0},{12,4},{1,9},{5,13},{9,1},{13,5},{2,10},{6,14},... | collective-permute-start | bytes 786440 | tf_op jit(solution)/shard_map/ppermute | solution.py:22
  8.7 3.2 %constant_dynamic-slice_fusion = (f32[2,1,128,1024]{3,2,1,0:T(8,128)}, f32[2,1,128,1024]{3,2,1,0:T(8,128)}) fusion(f32[2,1,512,2048]{3,2,1,0:T(8,128)} %refs_1_.23, s32[]{:T(128)S(6)} %select_n.76, s32[]{:T(128)S(6)} %select_n.78, s32[]{:T(128)S(6)} %select_n.73, s32[]{:T(128)S(6)} %select_n.75), kind=kLoop, calls=%fused_computation.8 | loop fusion | bytes 4194320 | tf_op jit(solution)/shard_map/dynamic_slice | solution.py:398
  14.8 3.4 %copy-done = f32[2,1,512,2048]{3,2,1,0:T(8,128)S(1)} copy-done((f32[2,1,512,2048]{3,2,1,0:T(8,128)S(1)}, f32[2,1,512,2048]{3,2,1,0:T(8,128)}, u32[]{:S(2)}) %copy-start) | copy-done | bytes 8388632
  18.2 3.5 %shard_map.76.refs_3_ = f32[4,128,256]{2,1,0:T(8,128)S(1)} custom-call(s32[2]{0:T(128)S(1)} %compare_select_fusion.refs_0_.at_ref.refs_1_, f32[2,1,512,2048]{3,2,1,0:T(8,128)S(1)} %copy-done, f32[2,1,512,128]{3,2,1,0:T(8,128)S(1)} %get-tuple-element.27.refs_2_.contact_ref), custom_call_target="tpu_custom_call" | custom-call | flops 1610612736 | bytes 2097152 | tf_op jit(solution)/shard_map/pallas_call | solution.py:222
  21.7 11.3 %collective-permute-done.2.refs_2_ = f32[2,1,256,128]{3,2,1,0:T(8,128)} collective-permute-done((f32[2,1,256,128]{3,2,1,0:T(8,128)}, f32[2,1,256,128]{3,2,1,0:T(8,128)}, u32[]{:S(2)}, u32[]{:S(2)}) %collective-permute-start.2) | collective-permute-done | bytes 262176 | tf_op jit(solution)/shard_map/ppermute | solution.py:22
  35.1 3.5 %shard_map.77.refs_4_ = f32[4,128,256]{2,1,0:T(8,128)S(1)} custom-call(s32[2]{0:T(128)S(1)} %compare_select_fusion.refs_0_.at_ref.refs_1_, f32[2,1,512,2048]{3,2,1,0:T(8,128)S(1)} %copy-done, f32[2,1,512,128]{3,2,1,0:T(8,128)S(1)} %collective-permute-done.4.refs_2_, f32[4,128,256]{2,1,0:T(8,128)S(1)} %shard_map.76.refs_3_), custom_call_target="tpu_custom_call", output_to_operand_aliasing={{}: (3, {})} | custom-call | flops 1610612736 | bytes 2097152 | tf_op jit(solution)/shard_map/pallas_call | solution.py:222
  38.6 4.1 %shard_map.78.refs_3_ = f32[4,128,256]{2,1,0:T(8,128)S(1)} custom-call(s32[2]{0:T(128)S(1)} %compare_select_fusion.refs_0_.at_ref.refs_1_, f32[2,1,512,2048]{3,2,1,0:T(8,128)S(1)} %copy-done, f32[2,1,256,128]{3,2,1,0:T(8,128)} %collective-permute-done.2.refs_2_, f32[2,1,256,128]{3,2,1,0:T(8,128)} %collective-permute-done.refs_3_, ...), custom_call_target="tpu_custom_call", output_to_operand_aliasing={{}: (4, {})} | custom-call | flops 1610612736 | bytes 2097152 | tf_op jit(solution)/shard_map/pallas_call | solution.py:222
  42.7 13.4 %collective-permute-done.3.refs_2_ = f32[2,1,256,128]{3,2,1,0:T(8,128)S(1)} collective-permute-done((f32[2,1,256,128]{3,2,1,0:T(8,128)}, f32[2,1,256,128]{3,2,1,0:T(8,128)S(1)}, u32[]{:S(2)}, u32[]{:S(2)}) %collective-permute-start.3) | collective-permute-done | bytes 262176 | tf_op jit(solution)/shard_map/ppermute | solution.py:22
  58.1 2.7 %collective-permute-done.1.refs_2_ = f32[2,1,256,128]{3,2,1,0:T(8,128)S(1)} collective-permute-done((f32[2,1,256,128]{3,2,1,0:T(8,128)}, f32[2,1,256,128]{3,2,1,0:T(8,128)S(1)}, u32[]{:S(2)}, u32[]{:S(2)}) %collective-permute-start.1) | collective-permute-done | bytes 262176 | tf_op jit(solution)/shard_map/ppermute | solution.py:22
  65.0 7.1 %collective-permute-done.10.refs_2_ = f32[2,1,256,128]{3,2,1,0:T(8,128)S(1)} collective-permute-done((f32[2,1,256,128]{3,2,1,0:T(8,128)S(1)}, f32[2,1,256,128]{3,2,1,0:T(8,128)S(1)}, u32[]{:S(2)}, u32[]{:S(2)}) %collective-permute-start.10) | collective-permute-done | bytes 262176 | tf_op jit(solution)/shard_map/ppermute | solution.py:22
  72.7 3.4 %collective-permute-done.5.refs_2_ = f32[2,1,256,128]{3,2,1,0:T(8,128)S(1)} collective-permute-done((f32[2,1,256,128]{3,2,1,0:T(8,128)S(1)}, f32[2,1,256,128]{3,2,1,0:T(8,128)S(1)}, u32[]{:S(2)}, u32[]{:S(2)}) %collective-permute-start.5) | collective-permute-done | bytes 262176 | tf_op jit(solution)/shard_map/ppermute | solution.py:22
  76.9 2.6 %collective-permute-start.13 = (f32[2,1,256,128]{3,2,1,0:T(8,128)S(1)}, f32[2,1,256,128]{3,2,1,0:T(8,128)S(1)}, u32[]{:S(2)}, u32[]{:S(2)}) collective-permute-start(f32[2,1,256,128]{3,2,1,0:T(8,128)S(1)} %shard_map.82.refs_2_), channel_id=1, source_target_pairs={{0,8},{4,12},{8,0},{12,4},{1,9},{5,13},{9,1},{13,5},{2,10},{6,14},... | collective-permute-start | bytes 786440 | tf_op jit(solution)/shard_map/ppermute | solution.py:22
  82.7 4.9 %shard_map.83 = (f32[4,128,256]{2,1,0:T(8,128)S(1)}, f32[4,128,256]{2,1,0:T(8,128)S(1)}, f32[1,128,256]{2,1,0:T(8,128)S(1)}) custom-call(s32[2]{0:T(128)S(1)} %compare_select_fusion.refs_0_.at_ref.refs_1_, f32[2,1,512,2048]{3,2,1,0:T(8,128)S(1)} %bitcast.11, f32[2,1,256,128]{3,2,1,0:T(8,128)S(1)} %shard_map.82.refs_2_, ...), custom_call_target="tpu_custom_call" | custom-call | flops 3221225472 | bytes 2097152 | tf_op jit(solution)/shard_map/pallas_call | solution.py:222
  87.7 5.0 %collective-permute-done.13.refs_2_ = f32[2,1,256,128]{3,2,1,0:T(8,128)S(1)} collective-permute-done((f32[2,1,256,128]{3,2,1,0:T(8,128)S(1)}, f32[2,1,256,128]{3,2,1,0:T(8,128)S(1)}, u32[]{:S(2)}, u32[]{:S(2)}) %collective-permute-start.13) | collective-permute-done | bytes 262176 | tf_op jit(solution)/shard_map/ppermute | solution.py:22
  92.9 10.2 %collective-permute-done.8.refs_2_ = f32[2,1,256,128]{3,2,1,0:T(8,128)S(1)} collective-permute-done((f32[2,1,256,128]{3,2,1,0:T(8,128)S(1)}, f32[2,1,256,128]{3,2,1,0:T(8,128)S(1)}, u32[]{:S(2)}, u32[]{:S(2)}) %collective-permute-start.8) | collective-permute-done | bytes 262176 | tf_op jit(solution)/shard_map/ppermute | solution.py:22
  103.1 2.4 %collective-permute-start.9 = (f32[2,1,256,128]{3,2,1,0:T(8,128)S(1)}, f32[2,1,256,128]{3,2,1,0:T(8,128)S(1)}, u32[]{:S(2)}, u32[]{:S(2)}) collective-permute-start(f32[2,1,256,128]{3,2,1,0:T(8,128)S(1)} %collective-permute-done.8.refs_2_), channel_id=1, source_target_pairs={{0,4},{4,0},{8,12},{12,8},{1,5},{5,1},{9,13},{13,9},{2,6},{6,2},{1... | collective-permute-start | bytes 786440 | tf_op jit(solution)/shard_map/ppermute | solution.py:22
  105.4 2.5 %shard_map.84 = (f32[4,128,256]{2,1,0:T(8,128)S(1)}, f32[4,128,256]{2,1,0:T(8,128)S(1)}) custom-call(s32[2]{0:T(128)S(1)} %compare_select_fusion.refs_0_.at_ref.refs_1_, f32[2,1,512,2048]{3,2,1,0:T(8,128)S(1)} %bitcast.11, f32[2,1,256,128]{3,2,1,0:T(8,128)S(1)} %collective-permute-done.13.refs_2_, ...), custom_call_target="tpu_custom_call", output_to_operand_aliasing={{0}: (5, {}), {1}: (6, {})} | custom-call | flops 1207959552 | bytes 1048576 | tf_op jit(solution)/shard_map/pallas_call | solution.py:222
  108.0 4.8 %shard_map.85 = (f32[4,128,256]{2,1,0:T(8,128)S(1)}, f32[4,128,256]{2,1,0:T(8,128)S(1)}, f32[1,128,256]{2,1,0:T(8,128)S(1)}) custom-call(s32[2]{0:T(128)S(1)} %compare_select_fusion.refs_0_.at_ref.refs_1_, f32[2,1,512,2048]{3,2,1,0:T(8,128)S(1)} %bitcast.11, ...), custom_call_target="tpu_custom_call", output_to_operand_aliasing={{0}: (6, {}), {1}: (7, {}), {2}: (8, {})} | custom-call | flops 3221225472 | bytes 2097152 | tf_op jit(solution)/shard_map/pallas_call | solution.py:222
  112.8 2.5 %shard_map.86 = (f32[4,128,256]{2,1,0:T(8,128)S(1)}, f32[4,128,256]{2,1,0:T(8,128)S(1)}) custom-call(s32[2]{0:T(128)S(1)} %compare_select_fusion.refs_0_.at_ref.refs_1_, f32[2,1,512,2048]{3,2,1,0:T(8,128)S(1)} %bitcast.11, f32[2,1,256,128]{3,2,1,0:T(8,128)S(1)} %collective-permute-done.8.refs_2_, ...), custom_call_target="tpu_custom_call", output_to_operand_aliasing={{0}: (5, {}), {1}: (6, {})} | custom-call | flops 1207959552 | bytes 1048576 | tf_op jit(solution)/shard_map/pallas_call | solution.py:222
  117.4 2.9 %shard_map.88 = (f32[2,1,256,128]{3,2,1,0:T(8,128)S(1)}, f32[2,1,256,128]{3,2,1,0:T(8,128)S(1)}, f32[2,1,512,128]{3,2,1,0:T(8,128)}) custom-call(s32[2]{0:T(128)S(1)} %compare_select_fusion.refs_0_.at_ref.refs_1_, f32[2,1,512,2048]{3,2,1,0:T(8,128)S(1)} %bitcast.11, f32[2,1,256,128]{3,2,1,0:T(8,128)S(1)} %collective-permute-done.9.refs_2_.refs_3_, ...), custom_call_target="tpu_custom_call" | custom-call | flops 805306368 | bytes 1048576 | tf_op jit(solution)/shard_map/pallas_call | solution.py:222
  122.3 7.1 %collective-permute-done.22.refs_2_ = f32[2,1,256,128]{3,2,1,0:T(8,128)S(1)} collective-permute-done((f32[2,1,256,128]{3,2,1,0:T(8,128)S(1)}, f32[2,1,256,128]{3,2,1,0:T(8,128)S(1)}, u32[]{:S(2)}, u32[]{:S(2)}) %collective-permute-start.22) | collective-permute-done | bytes 262176 | tf_op jit(solution)/shard_map/ppermute | solution.py:22
  129.9 3.0 %collective-permute-done.19.refs_5_ = f32[2,1,256,128]{3,2,1,0:T(8,128)S(1)} collective-permute-done((f32[2,1,256,128]{3,2,1,0:T(8,128)S(1)}, f32[2,1,256,128]{3,2,1,0:T(8,128)S(1)}, u32[]{:S(2)}, u32[]{:S(2)}) %collective-permute-start.19) | collective-permute-done | bytes 262176 | tf_op jit(solution)/shard_map/ppermute | solution.py:22
  134.3 4.7 %shard_map.90.refs_9_ = f32[2,1,512,128]{3,2,1,0:T(8,128)} custom-call(s32[2]{0:T(128)S(1)} %compare_select_fusion.refs_0_.at_ref.refs_1_, f32[2,1,512,2048]{3,2,1,0:T(8,128)S(1)} %bitcast.11, f32[2,1,256,128]{3,2,1,0:T(8,128)S(1)} %collective-permute-done.14.refs_2_, f32[2,1,256,128]{3,2,1,0:T(8,128)S(1)} %collective-permute-done.9.refs_2_.refs_3_, ...), custom_call_target="tpu_custom_call" | custom-call | flops 1610612736 | bytes 2097152 | tf_op jit(solution)/shard_map/pallas_call | solution.py:222
  (66 shorter events, 27.8 us)
Async XLA Ops:
  0.6 34.4 %collective-permute-start.4 = (f32[2,1,512,128]{3,2,1,0:T(8,128)}, f32[2,1,512,128]{3,2,1,0:T(8,128)S(1)}, u32[]{:S(2)}, u32[]{:S(2)}) collective-permute-start(f32[2,1,512,128]{3,2,1,0:T(8,128)} %contact_ref.1), channel_id=1, source_target_pairs={{0,4},{4,0},{8,12},{12,8},{1,5},{5,1},{9,13},{13,9},{2,6},{6,2},{1... | collective-permute-start | bytes 1572872 | tf_op jit(solution)/shard_map/ppermute | solution.py:22
  5.7 27.3 %collective-permute-start = (f32[2,1,256,128]{3,2,1,0:T(8,128)}, f32[2,1,256,128]{3,2,1,0:T(8,128)}, u32[]{:S(2)}, u32[]{:S(2)}) collective-permute-start(f32[2,1,256,128]{3,2,1,0:T(8,128)} %get-tuple-element.30), channel_id=1, source_target_pairs={{0,8},{4,12},{8,0},{12,4},{1,9},{5,13},{9,1},{13,5},{2,10},{6,14},... | collective-permute-start | bytes 786440 | tf_op jit(solution)/shard_map/ppermute | solution.py:22
  8.4 24.7 %collective-permute-start.2 = (f32[2,1,256,128]{3,2,1,0:T(8,128)}, f32[2,1,256,128]{3,2,1,0:T(8,128)}, u32[]{:S(2)}, u32[]{:S(2)}) collective-permute-start(f32[2,1,256,128]{3,2,1,0:T(8,128)} %get-tuple-element.31), channel_id=1, source_target_pairs={{0,8},{4,12},{8,0},{12,4},{1,9},{5,13},{9,1},{13,5},{2,10},{6,14},... | collective-permute-start | bytes 786440 | tf_op jit(solution)/shard_map/ppermute | solution.py:22
  11.9 70.5 %collective-permute-start.15 = (f32[2,1,128,1024]{3,2,1,0:T(8,128)}, f32[2,1,128,1024]{3,2,1,0:T(8,128)S(1)}, u32[]{:S(2)}, u32[]{:S(2)}) collective-permute-start(f32[2,1,128,1024]{3,2,1,0:T(8,128)} %get-tuple-element.52), channel_id=1, source_target_pairs={{0,4},{4,0},{8,12},{12,8},{1,5},{5,1},{9,13},{13,9},{2,6},{6,2},{1... | collective-permute-start | bytes 3145736 | tf_op jit(solution)/shard_map/ppermute | solution.py:403
  12.1 70.7 %collective-permute-start.16 = (f32[2,1,128,1024]{3,2,1,0:T(8,128)}, f32[2,1,128,1024]{3,2,1,0:T(8,128)S(1)}, u32[]{:S(2)}, u32[]{:S(2)}) collective-permute-start(f32[2,1,128,1024]{3,2,1,0:T(8,128)} %get-tuple-element.51), channel_id=1, source_target_pairs={{4,8},{8,4},{5,9},{9,5},{6,10},{10,6},{7,11},{11,7},{20,24},{24,20... | collective-permute-start | bytes 3145736 | tf_op jit(solution)/shard_map/ppermute | solution.py:403
  33.0 23.0 %collective-permute-start.3 = (f32[2,1,256,128]{3,2,1,0:T(8,128)}, f32[2,1,256,128]{3,2,1,0:T(8,128)S(1)}, u32[]{:S(2)}, u32[]{:S(2)}) collective-permute-start(f32[2,1,256,128]{3,2,1,0:T(8,128)} %collective-permute-done.2.refs_2_), channel_id=1, source_target_pairs={{0,4},{4,0},{8,12},{12,8},{1,5},{5,1},{9,13},{13,9},{2,6},{6,2},{1... | collective-permute-start | bytes 786440 | tf_op jit(solution)/shard_map/ppermute | solution.py:22
  33.0 27.8 %collective-permute-start.1 = (f32[2,1,256,128]{3,2,1,0:T(8,128)}, f32[2,1,256,128]{3,2,1,0:T(8,128)S(1)}, u32[]{:S(2)}, u32[]{:S(2)}) collective-permute-start(f32[2,1,256,128]{3,2,1,0:T(8,128)} %collective-permute-done.refs_3_), channel_id=1, source_target_pairs={{0,4},{4,0},{8,12},{12,8},{1,5},{5,1},{9,13},{13,9},{2,6},{6,2},{1... | collective-permute-start | bytes 786440 | tf_op jit(solution)/shard_map/ppermute | solution.py:22
  62.9 9.2 %collective-permute-start.10 = (f32[2,1,256,128]{3,2,1,0:T(8,128)S(1)}, f32[2,1,256,128]{3,2,1,0:T(8,128)S(1)}, u32[]{:S(2)}, u32[]{:S(2)}) collective-permute-start(f32[2,1,256,128]{3,2,1,0:T(8,128)S(1)} %get-tuple-element.33), channel_id=1, source_target_pairs={{0,2},{1,3},{2,0},{3,1},{4,6},{5,7},{6,4},{7,5},{8,10},{9,11},{10,... | collective-permute-start | bytes 786440 | tf_op jit(solution)/shard_map/ppermute | solution.py:22
  64.7 7.5 %collective-permute-start.11 = (f32[2,1,256,128]{3,2,1,0:T(8,128)S(1)}, f32[2,1,256,128]{3,2,1,0:T(8,128)S(1)}, u32[]{:S(2)}, u32[]{:S(2)}) collective-permute-start(f32[2,1,256,128]{3,2,1,0:T(8,128)S(1)} %get-tuple-element.33), channel_id=1, source_target_pairs={{0,1},{1,0},{2,3},{3,2},{4,5},{5,4},{6,7},{7,6},{8,9},{9,8},{10,11... | collective-permute-start | bytes 786440 | tf_op jit(solution)/shard_map/ppermute | solution.py:22
  64.7 11.4 %collective-permute-start.5 = (f32[2,1,256,128]{3,2,1,0:T(8,128)S(1)}, f32[2,1,256,128]{3,2,1,0:T(8,128)S(1)}, u32[]{:S(2)}, u32[]{:S(2)}) collective-permute-start(f32[2,1,256,128]{3,2,1,0:T(8,128)S(1)} %get-tuple-element.32), channel_id=1, source_target_pairs={{0,2},{1,3},{2,0},{3,1},{4,6},{5,7},{6,4},{7,5},{8,10},{9,11},{10,... | collective-permute-start | bytes 786440 | tf_op jit(solution)/shard_map/ppermute | solution.py:22
  72.2 7.3 %collective-permute-start.6 = (f32[2,1,256,128]{3,2,1,0:T(8,128)S(1)}, f32[2,1,256,128]{3,2,1,0:T(8,128)S(1)}, u32[]{:S(2)}, u32[]{:S(2)}) collective-permute-start(f32[2,1,256,128]{3,2,1,0:T(8,128)S(1)} %get-tuple-element.32), channel_id=1, source_target_pairs={{0,1},{1,0},{2,3},{3,2},{4,5},{5,4},{6,7},{7,6},{8,9},{9,8},{10,11... | collective-permute-start | bytes 786440 | tf_op jit(solution)/shard_map/ppermute | solution.py:22
  76.9 15.9 %collective-permute-start.13 = (f32[2,1,256,128]{3,2,1,0:T(8,128)S(1)}, f32[2,1,256,128]{3,2,1,0:T(8,128)S(1)}, u32[]{:S(2)}, u32[]{:S(2)}) collective-permute-start(f32[2,1,256,128]{3,2,1,0:T(8,128)S(1)} %shard_map.82.refs_2_), channel_id=1, source_target_pairs={{0,8},{4,12},{8,0},{12,4},{1,9},{5,13},{9,1},{13,5},{2,10},{6,14},... | collective-permute-start | bytes 786440 | tf_op jit(solution)/shard_map/ppermute | solution.py:22
  79.5 28.5 %collective-permute-start.17 = (f32[2,1,256,128]{3,2,1,0:T(8,128)S(1)}, f32[2,1,256,128]{3,2,1,0:T(8,128)S(1)}, u32[]{:S(2)}, u32[]{:S(2)}) collective-permute-start(f32[2,1,256,128]{3,2,1,0:T(8,128)S(1)} %shard_map.82.refs_2_), channel_id=1, source_target_pairs={{0,4},{4,0},{8,12},{12,8},{1,5},{5,1},{9,13},{13,9},{2,6},{6,2},{1... | collective-permute-start | bytes 786440 | tf_op jit(solution)/shard_map/ppermute | solution.py:22
  81.8 26.2 %collective-permute-start.18 = (f32[2,1,256,128]{3,2,1,0:T(8,128)S(1)}, f32[2,1,256,128]{3,2,1,0:T(8,128)S(1)}, u32[]{:S(2)}, u32[]{:S(2)}) collective-permute-start(f32[2,1,256,128]{3,2,1,0:T(8,128)S(1)} %shard_map.81.refs_3_), channel_id=1, source_target_pairs={{0,4},{4,0},{8,12},{12,8},{1,5},{5,1},{9,13},{13,9},{2,6},{6,2},{1... | collective-permute-start | bytes 786440 | tf_op jit(solution)/shard_map/ppermute | solution.py:22
  82.3 20.7 %collective-permute-start.8 = (f32[2,1,256,128]{3,2,1,0:T(8,128)S(1)}, f32[2,1,256,128]{3,2,1,0:T(8,128)S(1)}, u32[]{:S(2)}, u32[]{:S(2)}) collective-permute-start(f32[2,1,256,128]{3,2,1,0:T(8,128)S(1)} %shard_map.81.refs_3_), channel_id=1, source_target_pairs={{0,8},{4,12},{8,0},{12,4},{1,9},{5,13},{9,1},{13,5},{2,10},{6,14},... | collective-permute-start | bytes 786440 | tf_op jit(solution)/shard_map/ppermute | solution.py:22
  92.7 22.5 %collective-permute-start.14 = (f32[2,1,256,128]{3,2,1,0:T(8,128)S(1)}, f32[2,1,256,128]{3,2,1,0:T(8,128)S(1)}, u32[]{:S(2)}, u32[]{:S(2)}) collective-permute-start(f32[2,1,256,128]{3,2,1,0:T(8,128)S(1)} %collective-permute-done.13.refs_2_), channel_id=1, source_target_pairs={{0,4},{4,0},{8,12},{12,8},{1,5},{5,1},{9,13},{13,9},{2,6},{6,2},{1... | collective-permute-start | bytes 786440 | tf_op jit(solution)/shard_map/ppermute | solution.py:22
  103.1 14.3 %collective-permute-start.9 = (f32[2,1,256,128]{3,2,1,0:T(8,128)S(1)}, f32[2,1,256,128]{3,2,1,0:T(8,128)S(1)}, u32[]{:S(2)}, u32[]{:S(2)}) collective-permute-start(f32[2,1,256,128]{3,2,1,0:T(8,128)S(1)} %collective-permute-done.8.refs_2_), channel_id=1, source_target_pairs={{0,4},{4,0},{8,12},{12,8},{1,5},{5,1},{9,13},{13,9},{2,6},{6,2},{1... | collective-permute-start | bytes 786440 | tf_op jit(solution)/shard_map/ppermute | solution.py:22
  120.3 9.2 %collective-permute-start.22 = (f32[2,1,256,128]{3,2,1,0:T(8,128)S(1)}, f32[2,1,256,128]{3,2,1,0:T(8,128)S(1)}, u32[]{:S(2)}, u32[]{:S(2)}) collective-permute-start(f32[2,1,256,128]{3,2,1,0:T(8,128)S(1)} %get-tuple-element.44), channel_id=1, source_target_pairs={{0,2},{1,3},{2,0},{3,1},{4,6},{5,7},{6,4},{7,5},{8,10},{9,11},{10,... | collective-permute-start | bytes 786440 | tf_op jit(solution)/shard_map/ppermute | solution.py:22
  121.8 11.2 %collective-permute-start.19 = (f32[2,1,256,128]{3,2,1,0:T(8,128)S(1)}, f32[2,1,256,128]{3,2,1,0:T(8,128)S(1)}, u32[]{:S(2)}, u32[]{:S(2)}) collective-permute-start(f32[2,1,256,128]{3,2,1,0:T(8,128)S(1)} %get-tuple-element.43), channel_id=1, source_target_pairs={{0,2},{1,3},{2,0},{3,1},{4,6},{5,7},{6,4},{7,5},{8,10},{9,11},{10,... | collective-permute-start | bytes 786440 | tf_op jit(solution)/shard_map/ppermute | solution.py:22
  122.3 16.7 %collective-permute-start.23 = (f32[2,1,256,128]{3,2,1,0:T(8,128)S(1)}, f32[2,1,256,128]{3,2,1,0:T(8,128)S(1)}, u32[]{:S(2)}, u32[]{:S(2)}) collective-permute-start(f32[2,1,256,128]{3,2,1,0:T(8,128)S(1)} %get-tuple-element.44), channel_id=1, source_target_pairs={{0,1},{1,0},{2,3},{3,2},{4,5},{5,4},{6,7},{7,6},{8,9},{9,8},{10,11... | collective-permute-start | bytes 786440 | tf_op jit(solution)/shard_map/ppermute | solution.py:22
  129.4 9.5 %collective-permute-start.24 = (f32[2,1,256,128]{3,2,1,0:T(8,128)S(1)}, f32[2,1,256,128]{3,2,1,0:T(8,128)S(1)}, u32[]{:S(2)}, u32[]{:S(2)}) collective-permute-start(f32[2,1,256,128]{3,2,1,0:T(8,128)S(1)} %collective-permute-done.22.refs_2_), channel_id=1, source_target_pairs={{0,1},{1,0},{2,3},{3,2},{4,5},{5,4},{6,7},{7,6},{8,9},{9,8},{10,11... | collective-permute-start | bytes 786440 | tf_op jit(solution)/shard_map/ppermute | solution.py:22
  129.4 11.3 %collective-permute-start.20 = (f32[2,1,256,128]{3,2,1,0:T(8,128)S(1)}, f32[2,1,256,128]{3,2,1,0:T(8,128)S(1)}, u32[]{:S(2)}, u32[]{:S(2)}) collective-permute-start(f32[2,1,256,128]{3,2,1,0:T(8,128)S(1)} %get-tuple-element.43), channel_id=1, source_target_pairs={{0,1},{1,0},{2,3},{3,2},{4,5},{5,4},{6,7},{7,6},{8,9},{9,8},{10,11... | collective-permute-start | bytes 786440 | tf_op jit(solution)/shard_map/ppermute | solution.py:22
  133.0 7.8 %collective-permute-start.21 = (f32[2,1,256,128]{3,2,1,0:T(8,128)S(1)}, f32[2,1,256,128]{3,2,1,0:T(8,128)S(1)}, u32[]{:S(2)}, u32[]{:S(2)}) collective-permute-start(f32[2,1,256,128]{3,2,1,0:T(8,128)S(1)} %collective-permute-done.19.refs_5_), channel_id=1, source_target_pairs={{0,1},{1,0},{2,3},{3,2},{4,5},{5,4},{6,7},{7,6},{8,9},{9,8},{10,11... | collective-permute-start | bytes 786440 | tf_op jit(solution)/shard_map/ppermute | solution.py:22
  133.0 7.8 %collective-permute-start.25 = (f32[1,128,256]{2,1,0:T(8,128)S(1)}, f32[1,128,256]{2,1,0:T(8,128)S(1)}, u32[]{:S(2)}, u32[]{:S(2)}) collective-permute-start(f32[1,128,256]{2,1,0:T(8,128)S(1)} %get-tuple-element.46), channel_id=1, source_target_pairs={{4,0},{8,4},{12,8},{5,1},{9,5},{13,9},{6,2},{10,6},{14,10},{7,3},{... | collective-permute-start | bytes 393224 | tf_op jit(solution)/shard_map/ppermute | solution.py:478
  (7 other events, 98.0 us)

commit v4 on v3

--- a/solution.py
+++ b/solution.py
@@ -70,22 +70,25 @@
     return tuple(v[start : start + size] for v in x)
 
 
-def panel_kernel(local, far, starts, diag, upper, back, first, last, chunks, devices, scale, *refs):
+def panel_kernel(local, far, starts, kinds, first, last, chunks, devices, scale, *refs):
     refs = list(refs)
     at_ref, g_ref = refs[:2]
     piece_refs, refs = refs[2 : 2 + len(starts)], refs[2 + len(starts) :]
-    if upper:
+    edges = "over" in kinds or "back" in kinds
+    if edges:
         even_ref, odd_ref = refs[:2]
         refs = refs[2:]
-    count = int(diag) + int(upper) + int(back)
-    ins = []
-    if not first:
-        ins, refs = refs[:count], refs[count:]
-    outs = refs
+    ins = {}
+    for kind in kinds:
+        if kind not in first:
+            ins[kind] = refs.pop(0)
+    outs = refs if last else dict(zip(kinds, refs))
     pan = at_ref[0]
     source = pan ^ far
     middle = devices // 2
     half = devices * local // 2
+    whole = "diag" in kinds or "upper" in kinds
+    low = 0 if whole else (local - 1) * B
 
     greens, sigmas, products, columns = [], [], [], []
     for start, s_ref in zip(starts, piece_refs):
@@ -93,53 +96,59 @@
             k = source * local + start + u
             columns.append(pl.ds(pl.multiple_of((k % half) * B, B), B))
             cut = pl.ds(pl.multiple_of(k * B, B), B)
-            green = split(jnp.concatenate([g_ref[0, 0, :, cut], g_ref[1, 0, :, cut]], axis=1))
             rows = slice(u * B, (u + 1) * B)
             sr, si = s_ref[0, 0, rows], s_ref[1, 0, rows]
-            sigma = split(
-                jnp.concatenate(
-                    [jnp.concatenate([sr, si], axis=1), jnp.concatenate([-si, sr], axis=1)], axis=0
+            sigmas.append(
+                split(
+                    jnp.concatenate(
+                        [jnp.concatenate([sr, si], axis=1), jnp.concatenate([-si, sr], axis=1)],
+                        axis=0,
+                    )
                 )
             )
-            greens.append(green)
-            sigmas.append(sigma)
-            products.append(split(times(green, sigma)))
-
-    def old(which, i):
-        return 0.0 if first else ins[which][i]
+            greens.append(lambda low, high, cut=cut: split(
+                jnp.concatenate([g_ref[0, 0, low:high, cut], g_ref[1, 0, low:high, cut]], axis=1)
+            ))
+            if whole:
+                greens[-1] = functools.partial(
+                    lambda whole, low, high: rows_of(whole, low, high - low),
+                    greens[-1](0, local * B),
+                )
+                products.append(split(times(greens[-1](0, local * B), sigmas[-1])))
+
+    def old(kind, i):
+        return ins[kind][i] if kind in ins else 0.0
 
     def put(ref, row, value):
         ref[0, 0, row * B : (row + 1) * B] = value[:, :B].T * scale
         ref[1, 0, row * B : (row + 1) * B] = value[:, B:].T * scale
 
-    at_upper = int(diag)
+    diag, upper = "diag" in kinds, "upper" in kinds
     for i in range(local):
         start = 0 if diag else 1
         size = int(diag) + int(upper and i < local - 1)
         if not size:
             continue
         terms = total(
-            times_t(rows_of(green, (i + start) * B, size * B), pair_rows(rows_of(product, i * B, B)))
+            times_t(green((i + start) * B, (i + start + size) * B), pair_rows(rows_of(product, i * B, B)))
             for green, product in zip(greens, products)
         )
         if diag:
-            value = old(0, i) + terms[:B]
+            value = old("diag", i) + terms[:B]
             if last:
                 for ref in outs[chunks:]:
                     put(ref, i, value)
                 put(outs[i * chunks // local], i % (local // chunks), value)
             else:
-                outs[0][i] = value
+                outs["diag"][i] = value
         if upper and i < local - 1:
-            value = old(at_upper, i) + terms[-B:]
+            value = old("upper", i) + terms[-B:]
             if last:
-                put(outs[at_upper], i, value)
+                put(outs[0], i, value)
             else:
-                outs[at_upper][i] = value
-    if upper:
+                outs["upper"][i] = value
+    if edges:
         source_high = source >= middle
-        ours = (source_high == (pan >= middle)) if back else None
-        theirs = source_high != (pan + 1 >= middle)
         even = pan % 2 == 0
 
         def edge(near, column):
@@ -153,82 +162,94 @@
                 )
             )
 
-        if first:
-            outs[at_upper][local - 1] = jnp.zeros((B, 2 * B), F32)
-            outs[at_upper + 1][0] = jnp.zeros((B, 2 * B), F32)
-        if last:
-            edge_sum = ins[at_upper]
-        else:
-            edge_sum = outs[at_upper]
-
-        @pl.when(theirs)
-        def _():
-            terms = total(
-                times_t(edge(even, column), pair_rows(rows_of(product, (local - 1) * B, B)))
-                for product, column in zip(products, columns)
+        def over_terms():
+            terms = []
+            for number, column in enumerate(columns):
+                if whole:
+                    product = rows_of(products[number], (local - 1) * B, B)
+                else:
+                    product = split(times(greens[number](low, local * B), sigmas[number]))
+                terms.append(times_t(edge(even, column), pair_rows(product)))
+            return total(terms)
+
+        def back_terms():
+            return total(
+                times_t(green(0, B), pair_rows(split(times(edge(jnp.logical_not(even), column), sigma))))
+                for green, sigma, column in zip(greens, sigmas, columns)
             )
+
+        if "over" in kinds:
+            theirs = source_high != (pan + 1 >= middle)
             if last:
-                put(outs[at_upper], local - 1, edge_sum[local - 1] + terms)
+                end = outs[0]
+
+                @pl.when(theirs)
+                def _():
+                    put(end, local - 1, old("over", 0) + over_terms())
+
+                @pl.when(jnp.logical_not(theirs))
+                def _():
+                    put(end, local - 1, jnp.zeros((B, 2 * B), F32) + old("over", 0))
+
             else:
-                edge_sum[local - 1] += terms
-
-        if last:
-
-            @pl.when(jnp.logical_not(theirs))
+                if "over" not in ins:
+                    outs["over"][0] = jnp.zeros((B, 2 * B), F32)
+
+                @pl.when(theirs)
+                def _():
+                    outs["over"][0] += over_terms()
+
+        if "back" in kinds:
+            if "back" not in ins:
+                outs["back"][0] = jnp.zeros((B, 2 * B), F32)
+
+            @pl.when(source_high == (pan >= middle))
             def _():
-                put(outs[at_upper], local - 1, edge_sum[local - 1])
-
-        if back:
-
-            @pl.when(ours)
-            def _():
-                outs[at_upper + 1][0] += total(
-                    times_t(
-                        rows_of(green, 0, B),
-                        pair_rows(split(times(edge(jnp.logical_not(even), column), sigma))),
-                    )
-                    for green, sigma, column in zip(greens, sigmas, columns)
-                )
+                outs["back"][0] += back_terms()
 
 
 def panel(at, green, far, pieces, carry, edges, kinds, last, chunks=1, whole=False):
     rows = green.shape[2]
     local = rows // B
     devices = lax.axis_size("pan")
-    counts = {"diag": local, "upper": local, "back": 1}
+    counts = {"diag": local, "upper": local - 1, "over": 1, "back": 1}
+    kinds = tuple(kind for kind in kinds if counts[kind])
     vmem = pl.BlockSpec(memory_space=pltpu.VMEM)
     starts, many = [], 0
     for start, piece in pieces:
         starts.append(start)
         many += piece.shape[2] // B
     operands = [at, green] + [piece for _, piece in pieces]
-    if "upper" in kinds:
+    if "over" in kinds or "back" in kinds:
         operands += edges
     shapes = {kind: jax.ShapeDtypeStruct((counts[kind], B, 2 * B), F32) for kind in kinds}
     aliases = {}
-    if carry is not None:
-        for number, kind in enumerate(kinds):
-            if not last:
-                aliases[len(operands)] = number
-            operands.append(carry[kind])
+    first = []
+    for number, kind in enumerate(kinds):
+        if kind not in carry:
+            first.append(kind)
+            continue
+        if not last:
+            aliases[len(operands)] = number
+        operands.append(carry[kind])
     if last:
-        shapes = {kind: jax.ShapeDtypeStruct((2, 1, rows, B), F32) for kind in kinds}
+        tall = jax.ShapeDtypeStruct((2, 1, rows, B), F32)
+        shapes = {"upper": tall}
         if "diag" in kinds:
             part = jax.ShapeDtypeStruct((2, 1, rows // chunks, B), F32)
             shapes = {number: part for number in range(chunks)}
             if whole:
-                shapes["whole"] = jax.ShapeDtypeStruct((2, 1, rows, B), F32)
-    work = 3 * 2 * (2 * B) * (2 * B) * rows * many * (1 + len(kinds))
+                shapes["whole"] = tall
+    full = "diag" in kinds or "upper" in kinds
+    work = 3 * 2 * (2 * B) * (2 * B) * many * (rows if full else B) * (1 + len(kinds))
     out = pl.pallas_call(
         functools.partial(
             panel_kernel,
             local,
             far,
             starts,
-            "diag" in kinds,
-            "upper" in kinds,
-            "back" in kinds,
-            carry is None,
+            kinds,
+            first,
             last,
             chunks,
             devices,
@@ -243,9 +264,9 @@
             flops=work, bytes_accessed=8 * rows * B * many, transcendentals=0
         ),
     )(*operands)
-    if last and "diag" in kinds:
-        return {"diag": out}
-    return dict(zip(kinds, out))
+    if last:
+        return {"diag": out} if "diag" in kinds else {"upper": out[0]}
+    return dict(carry, **dict(zip(kinds, out)))
 
 
 def phonon_kernel(fars, modes, row, size, final, scale, shift_ref, at_ref, contact_ref, *refs):
@@ -450,18 +471,22 @@
             ready = lax.optimization_barrier((copied, per_row, per_line, *cuts))
             pieces[0] = (0, [(0, ready[0])])
             copied, per_row, per_line = ready[:3]
-        work = ("diag", "upper", "back") if final else ("diag",)
-        sums = None
         groups = [(far, 0, blocks) for far, blocks in pieces[:-1]]
         groups.sort(key=lambda group: (group[0] != 0, group[0] >= high))
-        if final and chunks > 1 and 1 < high:
+        if chunks > 1 and high > 1:
             far, _, blocks = groups.pop([far for far, _, _ in groups].index(high))
             groups.insert(1, (far, 0, blocks[:1]))
             groups.append((far, 1, blocks[1:]))
+        sums = {}
         for far, number, blocks in groups:
-            kinds_here = work[:2] if final and far >= high else work
-            new = panel(at, retarded, far, blocks, sums, edges, kinds_here, False)
-            sums = dict(sums or {}, **new)
+            work = ("diag", "upper") if final else ("diag",)
+            if final and 0 < far < high:
+                work += ("over", "back")
+            sums = panel(at, retarded, far, blocks, sums, edges, work, False)
+            if final and far == 0:
+                held = blocks
+        if final:
+            sums = panel(at, retarded, 0, held, sums, edges, ("over", "back"), False)
         far, blocks = pieces[-1]
         for number, block in enumerate(blocks):
             last = number == len(blocks) - 1
@@ -476,12 +501,18 @@
             near = [(i * (local // chunks), part) for i, part in enumerate(parts)]
     devices = lax.axis_size("pan")
     above = lax.ppermute(sums["back"], "pan", [(i + 1, i) for i in range(devices - 1)])
-    upper = panel(at, retarded, far, blocks, sums, edges, ("upper",), True)["upper"]
+    for far, blocks in pieces[1:-1]:
+        if far >= high:
+            sums = panel(at, retarded, far, blocks, sums, edges, ("over",), False)
+    far, blocks = pieces[-1]
+    upper = panel(at, retarded, far, blocks, sums, edges, ("upper", "over"), True)["upper"]
     sigma = None
     for number, own in enumerate(found):
-        ends = (upper, above) if number == chunks - 1 else None
-        sigma, *rest = phonon_final(*settings, own[1:], number, chunks, sigma, ends)
-    return (sums["diag"][chunks], rest[0], sigma)
+        ends = (upper, above) if number == 0 else None
+        sigma, *more = phonon_final(*settings, own[1:], number, chunks, sigma, ends)
+        if more:
+            (lesser_upper,) = more
+    return (sums["diag"][chunks], lesser_upper, sigma)
 
 
 def solution(mesh):

time: 143 us -> 129 us (0.902)
  waiting for transfers between devices: 63.7 us -> 43.2 us
  starting transfers between devices: 23 us -> 28.1 us
    ppermute x23, waiting for transfers between devices: 63.3 us -> 43.2 us  [swapped(): lax.ppermute(x, axis, [(i, i ^ bit) for i in range(lax.axis_size(axis))])]
    ppermute x23, starting transfers between devices: 20.8 us -> 24.3 us  [swapped(): lax.ppermute(x, axis, [(i, i ^ bit) for i in range(lax.axis_size(axis))])]
    pallas_call x12 -> x15, Pallas kernels: 39.7 us -> 41.6 us  [panel(): pl.pallas_call(functools.partial(panel_kernel, local, far, starts, kinds,...]
    ppermute x2, starting transfers between devices: 0.91 us -> 2.54 us  [edge_rows(): found.append(lax.ppermute(part, 'pan', pairs))]
    unnamed x10 -> x12, local copies, waits for them, and re-layouts: 4.47 us -> 4.48 us
  transfers between devices with their start and end apart: 26 -> 26, of which waited for: 10 -> 8; matrix products, arithmetic and copies ran while one was open for 4% -> 4% of each run, Pallas kernels for 29% -> 31%
where the time goes in v4:
time: 129 us; the launch traced here: 128 us
  Pallas kernels  46.7 us (36%)
  waiting for transfers between devices  43.2 us (33%)
  starting transfers between devices  28.1 us (22%)
  local copies, waits for them, and re-layouts  8.33 us (6%)
    ppermute x23, waiting for transfers between devices, swapped(): lax.ppermute(x, axis, [(i, i ^ bit) for i in range(lax.axis_size(axis))])  43.2 us
    pallas_call x15, Pallas kernels, panel(): pl.pallas_call(functools.partial(panel_kernel, local, far, starts, kinds,...  41.6 us
    ppermute x23, starting transfers between devices, swapped(): lax.ppermute(x, axis, [(i, i ^ bit) for i in range(lax.axis_size(axis))])  24.3 us
    unnamed x12, local copies, waits for them, and re-layouts  4.48 us
    pallas_call x2, Pallas kernels, phonon_final(): pl.pallas_call(kernel, grid=(1,), in_specs=specs, out_specs=out_specs, ou...  3.41 us
    dynamic_slice x1, local copies, waits for them, and re-layouts, edge_rows(): lax.dynamic_slice(retarded, (0, 0, row, column), (2, 1, B, columns // 2))  2.81 us
  transfers between devices with their start and end apart: 26, of which 8 were waited for; matrix products, arithmetic and copies ran while one was open for 4% of the time, Pallas kernels for 31%

profile of v4, /device:TPU:0, one launch (start us, length us, event | category | flops | bytes accessed | tf_op | source)
XLA Modules:
  0.0 128.2 jit_solution(16190569516367238033)
XLA Ops:
  0.6 3.1 %collective-permute-start.4 = (f32[2,1,512,128]{3,2,1,0:T(8,128)}, f32[2,1,512,128]{3,2,1,0:T(8,128)S(1)}, u32[]{:S(2)}, u32[]{:S(2)}) collective-permute-start(f32[2,1,512,128]{3,2,1,0:T(8,128)} %contact_ref.1), channel_id=1, source_target_pairs={{0,4},{4,0},{8,12},{12,8},{1,5},{5,1},{9,13},{13,9},{2,6},{6,2},{1... | collective-permute-start | bytes 1572872 | tf_op jit(solution)/shard_map/ppermute | solution.py:22
  4.9 2.7 %collective-permute-start.2 = (f32[2,1,256,128]{3,2,1,0:T(8,128)S(1)}, f32[2,1,256,128]{3,2,1,0:T(8,128)S(1)}, u32[]{:S(2)}, u32[]{:S(2)}) collective-permute-start(f32[2,1,256,128]{3,2,1,0:T(8,128)S(1)} %get-tuple-element.33), channel_id=1, source_target_pairs={{0,8},{4,12},{8,0},{12,4},{1,9},{5,13},{9,1},{13,5},{2,10},{6,14},... | collective-permute-start | bytes 786440 | tf_op jit(solution)/shard_map/ppermute | solution.py:22
  9.7 2.8 %constant_dynamic-slice_fusion = (f32[2,1,128,1024]{3,2,1,0:T(8,128)S(1)}, f32[2,1,128,1024]{3,2,1,0:T(8,128)}) fusion(f32[2,1,512,2048]{3,2,1,0:T(8,128)} %refs_1_.29, s32[]{:T(128)S(6)} %select_n.76, s32[]{:T(128)S(6)} %select_n.78, s32[]{:T(128)S(6)} %select_n.73, s32[]{:T(128)S(6)} %select_n.75), kind=kLoop, calls=%fused_computation.8 | loop fusion | bytes 4194320 | tf_op jit(solution)/shard_map/dynamic_slice | solution.py:419
  12.8 3.4 %copy-done = f32[2,1,512,2048]{3,2,1,0:T(8,128)S(1)} copy-done((f32[2,1,512,2048]{3,2,1,0:T(8,128)S(1)}, f32[2,1,512,2048]{3,2,1,0:T(8,128)}, u32[]{:S(2)}) %copy-start) | copy-done | bytes 8388632
  16.1 3.5 %shard_map.76.refs_3_ = f32[4,128,256]{2,1,0:T(8,128)S(1)} custom-call(s32[2]{0:T(128)S(1)} %compare_select_fusion.refs_0_.at_ref.refs_1_, f32[2,1,512,2048]{3,2,1,0:T(8,128)S(1)} %copy-done, f32[2,1,512,128]{3,2,1,0:T(8,128)S(1)} %get-tuple-element.29.refs_2_.contact_ref), custom_call_target="tpu_custom_call" | custom-call | flops 1610612736 | bytes 2097152 | tf_op jit(solution)/shard_map/pallas_call | solution.py:245
  19.7 2.3 %collective-permute-done.2.refs_2_ = f32[2,1,256,128]{3,2,1,0:T(8,128)S(1)} collective-permute-done((f32[2,1,256,128]{3,2,1,0:T(8,128)S(1)}, f32[2,1,256,128]{3,2,1,0:T(8,128)S(1)}, u32[]{:S(2)}, u32[]{:S(2)}) %collective-permute-start.2) | collective-permute-done | bytes 262176 | tf_op jit(solution)/shard_map/ppermute | solution.py:22
  21.9 3.6 %collective-permute-start.3 = (f32[2,1,256,128]{3,2,1,0:T(8,128)S(1)}, f32[2,1,256,128]{3,2,1,0:T(8,128)S(1)}, u32[]{:S(2)}, u32[]{:S(2)}) collective-permute-start(f32[2,1,256,128]{3,2,1,0:T(8,128)S(1)} %collective-permute-done.2.refs_2_), channel_id=1, source_target_pairs={{0,4},{4,0},{8,12},{12,8},{1,5},{5,1},{9,13},{13,9},{2,6},{6,2},{1... | collective-permute-start | bytes 786440 | tf_op jit(solution)/shard_map/ppermute | solution.py:22
  27.5 3.1 %collective-permute-done.refs_2_ = f32[2,1,256,128]{3,2,1,0:T(8,128)S(1)} collective-permute-done((f32[2,1,256,128]{3,2,1,0:T(8,128)S(1)}, f32[2,1,256,128]{3,2,1,0:T(8,128)S(1)}, u32[]{:S(2)}, u32[]{:S(2)}) %collective-permute-start) | collective-permute-done | bytes 262176 | tf_op jit(solution)/shard_map/ppermute | solution.py:22
  31.1 3.6 %shard_map.78.refs_3_ = f32[4,128,256]{2,1,0:T(8,128)S(1)} custom-call(s32[2]{0:T(128)S(1)} %compare_select_fusion.refs_0_.at_ref.refs_1_, f32[2,1,512,2048]{3,2,1,0:T(8,128)S(1)} %copy-done, f32[2,1,512,128]{3,2,1,0:T(8,128)S(1)} %collective-permute-done.4.refs_2_, f32[4,128,256]{2,1,0:T(8,128)S(1)} %shard_map.77.refs_3_), custom_call_target="tpu_custom_call", output_to_operand_aliasing={{}: (3, {})} | custom-call | flops 1610612736 | bytes 2097152 | tf_op jit(solution)/shard_map/pallas_call | solution.py:245
  38.8 2.1 %shard_map.81 = (f32[2,1,256,128]{3,2,1,0:T(8,128)S(1)}, f32[2,1,256,128]{3,2,1,0:T(8,128)S(1)}) custom-call(s32[2]{0:T(128)S(1)} %compare_select_fusion.refs_0_.at_ref.refs_1_, f32[2,1,512,2048]{3,2,1,0:T(8,128)S(1)} %copy-done, f32[2,1,256,128]{3,2,1,0:T(8,128)S(1)} %collective-permute-done.1.refs_2_, f32[4,128,256]{2,1,0:T(8,128)S(1)} %shard_map.80.refs_3_), custom_call_target="tpu_custom_call" | custom-call | flops 805306368 | bytes 1048576 | tf_op jit(solution)/shard_map/pallas_call | solution.py:245
  48.0 5.9 %collective-permute-done.5.refs_2_ = f32[2,1,256,128]{3,2,1,0:T(8,128)S(1)} collective-permute-done((f32[2,1,256,128]{3,2,1,0:T(8,128)S(1)}, f32[2,1,256,128]{3,2,1,0:T(8,128)S(1)}, u32[]{:S(2)}, u32[]{:S(2)}) %collective-permute-start.5) | collective-permute-done | bytes 262176 | tf_op jit(solution)/shard_map/ppermute | solution.py:22
  54.6 3.5 %collective-permute-start.13 = (f32[2,1,256,128]{3,2,1,0:T(8,128)S(1)}, f32[2,1,256,128]{3,2,1,0:T(8,128)S(1)}, u32[]{:S(2)}, u32[]{:S(2)}) collective-permute-start(f32[2,1,256,128]{3,2,1,0:T(8,128)S(1)} %shard_map.83.refs_2_), channel_id=1, source_target_pairs={{0,8},{4,12},{8,0},{12,4},{1,9},{5,13},{9,1},{13,5},{2,10},{6,14},... | collective-permute-start | bytes 786440 | tf_op jit(solution)/shard_map/ppermute | solution.py:22
  60.9 20.4 %collective-permute-done.13.refs_2_ = f32[2,1,256,128]{3,2,1,0:T(8,128)S(1)} collective-permute-done((f32[2,1,256,128]{3,2,1,0:T(8,128)S(1)}, f32[2,1,256,128]{3,2,1,0:T(8,128)S(1)}, u32[]{:S(2)}, u32[]{:S(2)}) %collective-permute-start.13) | collective-permute-done | bytes 262176 | tf_op jit(solution)/shard_map/ppermute | solution.py:22
  81.3 3.3 %shard_map.84 = (f32[4,128,256]{2,1,0:T(8,128)S(1)}, f32[3,128,256]{2,1,0:T(8,128)S(1)}) custom-call(s32[2]{0:T(128)S(1)} %compare_select_fusion.refs_0_.at_ref.refs_1_, f32[2,1,512,2048]{3,2,1,0:T(8,128)S(1)} %bitcast.11, f32[2,1,256,128]{3,2,1,0:T(8,128)S(1)} %shard_map.83.refs_2_, f32[2,1,256,128]{3,2,1,0:T(8,128)S(1)} %shard_map.82.refs_3_), custom_call_target="tpu_custom_call" | custom-call | flops 2415919104 | bytes 2097152 | tf_op jit(solution)/shard_map/pallas_call | solution.py:245
  86.7 3.3 %collective-permute-start.14 = (f32[2,1,256,128]{3,2,1,0:T(8,128)S(1)}, f32[2,1,256,128]{3,2,1,0:T(8,128)S(1)}, u32[]{:S(2)}, u32[]{:S(2)}) collective-permute-start(f32[2,1,256,128]{3,2,1,0:T(8,128)S(1)} %collective-permute-done.13.refs_2_), channel_id=1, source_target_pairs={{0,4},{4,0},{8,12},{12,8},{1,5},{5,1},{9,13},{13,9},{2,6},{6,2},{1... | collective-permute-start | bytes 786440 | tf_op jit(solution)/shard_map/ppermute | solution.py:22
  90.0 3.7 %collective-permute-done.8.refs_2_.refs_3_ = f32[2,1,256,128]{3,2,1,0:T(8,128)S(1)} collective-permute-done((f32[2,1,256,128]{3,2,1,0:T(8,128)S(1)}, f32[2,1,256,128]{3,2,1,0:T(8,128)S(1)}, u32[]{:S(2)}, u32[]{:S(2)}) %collective-permute-start.8) | collective-permute-done | bytes 262176 | tf_op jit(solution)/shard_map/ppermute | solution.py:22
  93.8 4.8 %shard_map.86 = (f32[4,128,256]{2,1,0:T(8,128)S(1)}, f32[3,128,256]{2,1,0:T(8,128)S(1)}, f32[1,128,256]{2,1,0:T(8,128)S(1)}, f32[1,128,256]{2,1,0:T(8,128)S(1)}) custom-call(s32[2]{0:T(128)S(1)} %compare_select_fusion.refs_0_.at_ref.refs_1_, f32[2,1,512,2048]{3,2,1,0:T(8,128)S(1)} %bitcast.11, ...), custom_call_target="tpu_custom_call", output_to_operand_aliasing={{0}: (6, {}), {1}: (7, {})} | custom-call | flops 4026531840 | bytes 2097152 | tf_op jit(solution)/shard_map/pallas_call | solution.py:245
  98.6 2.1 %shard_map.87 = (f32[4,128,256]{2,1,0:T(8,128)S(1)}, f32[3,128,256]{2,1,0:T(8,128)S(1)}) custom-call(s32[2]{0:T(128)S(1)} %compare_select_fusion.refs_0_.at_ref.refs_1_, f32[2,1,512,2048]{3,2,1,0:T(8,128)S(1)} %bitcast.11, f32[2,1,256,128]{3,2,1,0:T(8,128)S(1)} %collective-permute-done.8.refs_2_.refs_3_, ...), custom_call_target="tpu_custom_call", output_to_operand_aliasing={{0}: (3, {}), {1}: (4, {})} | custom-call | flops 1207959552 | bytes 1048576 | tf_op jit(solution)/shard_map/pallas_call | solution.py:245
  102.8 2.9 %shard_map.89 = (f32[2,1,256,128]{3,2,1,0:T(8,128)S(1)}, f32[2,1,256,128]{3,2,1,0:T(8,128)S(1)}, f32[2,1,512,128]{3,2,1,0:T(8,128)}) custom-call(s32[2]{0:T(128)S(1)} %compare_select_fusion.refs_0_.at_ref.refs_1_, f32[2,1,512,2048]{3,2,1,0:T(8,128)S(1)} %bitcast.11, f32[2,1,256,128]{3,2,1,0:T(8,128)S(1)} %collective-permute-done.9.refs_2_.refs_3_, ...), custom_call_target="tpu_custom_call" | custom-call | flops 805306368 | bytes 1048576 | tf_op jit(solution)/shard_map/pallas_call | solution.py:245
  107.7 2.3 %shard_map.90 = (f32[1,128,256]{2,1,0:T(8,128)S(1)}, f32[1,128,256]{2,1,0:T(8,128)S(1)}) custom-call(s32[2]{0:T(128)S(1)} %compare_select_fusion.refs_0_.at_ref.refs_1_, f32[2,1,512,2048]{3,2,1,0:T(8,128)S(1)} %bitcast.11, f32[2,1,256,128]{3,2,1,0:T(8,128)S(1)} %shard_map.83.refs_2_, ...), custom_call_target="tpu_custom_call", output_to_operand_aliasing={{0}: (6, {}), {1}: (7, {})} | custom-call | flops 603979776 | bytes 2097152 | tf_op jit(solution)/shard_map/pallas_call | solution.py:245
  111.9 2.9 %collective-permute-done.19.refs_2_ = f32[2,1,256,128]{3,2,1,0:T(8,128)S(1)} collective-permute-done((f32[2,1,256,128]{3,2,1,0:T(8,128)S(1)}, f32[2,1,256,128]{3,2,1,0:T(8,128)S(1)}, u32[]{:S(2)}, u32[]{:S(2)}) %collective-permute-start.19) | collective-permute-done | bytes 262176 | tf_op jit(solution)/shard_map/ppermute | solution.py:22
  114.9 3.1 %collective-permute-done.23.refs_5_ = f32[2,1,256,128]{3,2,1,0:T(8,128)S(1)} collective-permute-done((f32[2,1,256,128]{3,2,1,0:T(8,128)S(1)}, f32[2,1,256,128]{3,2,1,0:T(8,128)S(1)}, u32[]{:S(2)}, u32[]{:S(2)}) %collective-permute-start.23) | collective-permute-done | bytes 262176 | tf_op jit(solution)/shard_map/ppermute | solution.py:22
  118.0 2.1 %shard_map.91.refs_7_ = f32[1,128,256]{2,1,0:T(8,128)S(1)} custom-call(s32[2]{0:T(128)S(1)} %compare_select_fusion.refs_0_.at_ref.refs_1_, f32[2,1,512,2048]{3,2,1,0:T(8,128)S(1)} %bitcast.11, f32[2,1,256,128]{3,2,1,0:T(8,128)S(1)} %collective-permute-done.13.refs_2_, ...), custom_call_target="tpu_custom_call", output_to_operand_aliasing={{}: (6, {})} | custom-call | flops 402653184 | bytes 2097152 | tf_op jit(solution)/shard_map/pallas_call | solution.py:245
  120.1 4.7 %shard_map.92.refs_5_ = f32[2,1,512,128]{3,2,1,0:T(8,128)} custom-call(s32[2]{0:T(128)S(1)} %compare_select_fusion.refs_0_.at_ref.refs_1_, f32[2,1,512,2048]{3,2,1,0:T(8,128)S(1)} %bitcast.11, f32[2,1,256,128]{3,2,1,0:T(8,128)S(1)} %collective-permute-done.14.refs_2_, f32[2,1,256,128]{3,2,1,0:T(8,128)S(1)} %collective-permute-done.9.refs_2_.refs_3_, ...), custom_call_target="tpu_custom_call" | custom-call | flops 2415919104 | bytes 2097152 | tf_op jit(solution)/shard_map/pallas_call | solution.py:245
  (71 shorter events, 32.2 us)
Async XLA Ops:
  0.6 30.4 %collective-permute-start.4 = (f32[2,1,512,128]{3,2,1,0:T(8,128)}, f32[2,1,512,128]{3,2,1,0:T(8,128)S(1)}, u32[]{:S(2)}, u32[]{:S(2)}) collective-permute-start(f32[2,1,512,128]{3,2,1,0:T(8,128)} %contact_ref.1), channel_id=1, source_target_pairs={{0,4},{4,0},{8,12},{12,8},{1,5},{5,1},{9,13},{13,9},{2,6},{6,2},{1... | collective-permute-start | bytes 1572872 | tf_op jit(solution)/shard_map/ppermute | solution.py:22
  4.9 17.0 %collective-permute-start.2 = (f32[2,1,256,128]{3,2,1,0:T(8,128)S(1)}, f32[2,1,256,128]{3,2,1,0:T(8,128)S(1)}, u32[]{:S(2)}, u32[]{:S(2)}) collective-permute-start(f32[2,1,256,128]{3,2,1,0:T(8,128)S(1)} %get-tuple-element.33), channel_id=1, source_target_pairs={{0,8},{4,12},{8,0},{12,4},{1,9},{5,13},{9,1},{13,5},{2,10},{6,14},... | collective-permute-start | bytes 786440 | tf_op jit(solution)/shard_map/ppermute | solution.py:22
  7.6 23.1 %collective-permute-start = (f32[2,1,256,128]{3,2,1,0:T(8,128)S(1)}, f32[2,1,256,128]{3,2,1,0:T(8,128)S(1)}, u32[]{:S(2)}, u32[]{:S(2)}) collective-permute-start(f32[2,1,256,128]{3,2,1,0:T(8,128)S(1)} %get-tuple-element.32), channel_id=1, source_target_pairs={{0,8},{4,12},{8,0},{12,4},{1,9},{5,13},{9,1},{13,5},{2,10},{6,14},... | collective-permute-start | bytes 786440 | tf_op jit(solution)/shard_map/ppermute | solution.py:22
  21.9 14.8 %collective-permute-start.3 = (f32[2,1,256,128]{3,2,1,0:T(8,128)S(1)}, f32[2,1,256,128]{3,2,1,0:T(8,128)S(1)}, u32[]{:S(2)}, u32[]{:S(2)}) collective-permute-start(f32[2,1,256,128]{3,2,1,0:T(8,128)S(1)} %collective-permute-done.2.refs_2_), channel_id=1, source_target_pairs={{0,4},{4,0},{8,12},{12,8},{1,5},{5,1},{9,13},{13,9},{2,6},{6,2},{1... | collective-permute-start | bytes 786440 | tf_op jit(solution)/shard_map/ppermute | solution.py:22
  30.7 8.1 %collective-permute-start.1 = (f32[2,1,256,128]{3,2,1,0:T(8,128)S(1)}, f32[2,1,256,128]{3,2,1,0:T(8,128)S(1)}, u32[]{:S(2)}, u32[]{:S(2)}) collective-permute-start(f32[2,1,256,128]{3,2,1,0:T(8,128)S(1)} %collective-permute-done.refs_2_), channel_id=1, source_target_pairs={{0,4},{4,0},{8,12},{12,8},{1,5},{5,1},{9,13},{13,9},{2,6},{6,2},{1... | collective-permute-start | bytes 786440 | tf_op jit(solution)/shard_map/ppermute | solution.py:22
  40.9 6.5 %collective-permute-start.10 = (f32[2,1,256,128]{3,2,1,0:T(8,128)S(1)}, f32[2,1,256,128]{3,2,1,0:T(8,128)S(1)}, u32[]{:S(2)}, u32[]{:S(2)}) collective-permute-start(f32[2,1,256,128]{3,2,1,0:T(8,128)S(1)} %get-tuple-element.35), channel_id=1, source_target_pairs={{0,2},{1,3},{2,0},{3,1},{4,6},{5,7},{6,4},{7,5},{8,10},{9,11},{10,... | collective-permute-start | bytes 786440 | tf_op jit(solution)/shard_map/ppermute | solution.py:22
  42.5 44.2 %collective-permute-start.17 = (f32[2,1,128,1024]{3,2,1,0:T(8,128)S(1)}, f32[2,1,128,1024]{3,2,1,0:T(8,128)S(1)}, u32[]{:S(2)}, u32[]{:S(2)}) collective-permute-start(f32[2,1,128,1024]{3,2,1,0:T(8,128)S(1)} %copy-done.3), channel_id=1, source_target_pairs={{0,4},{4,0},{8,12},{12,8},{1,5},{5,1},{9,13},{13,9},{2,6},{6,2},{1... | collective-permute-start | bytes 3145736 | tf_op jit(solution)/shard_map/ppermute | solution.py:424
  44.1 49.7 %collective-permute-start.18 = (f32[2,1,128,1024]{3,2,1,0:T(8,128)S(1)}, f32[2,1,128,1024]{3,2,1,0:T(8,128)S(1)}, u32[]{:S(2)}, u32[]{:S(2)}) collective-permute-start(f32[2,1,128,1024]{3,2,1,0:T(8,128)S(1)} %get-tuple-element.55), channel_id=1, source_target_pairs={{4,8},{8,4},{5,9},{9,5},{6,10},{10,6},{7,11},{11,7},{20,24},{24,20... | collective-permute-start | bytes 3145736 | tf_op jit(solution)/shard_map/ppermute | solution.py:424
  45.1 8.7 %collective-permute-start.5 = (f32[2,1,256,128]{3,2,1,0:T(8,128)S(1)}, f32[2,1,256,128]{3,2,1,0:T(8,128)S(1)}, u32[]{:S(2)}, u32[]{:S(2)}) collective-permute-start(f32[2,1,256,128]{3,2,1,0:T(8,128)S(1)} %get-tuple-element.34), channel_id=1, source_target_pairs={{0,2},{1,3},{2,0},{3,1},{4,6},{5,7},{6,4},{7,5},{8,10},{9,11},{10,... | collective-permute-start | bytes 786440 | tf_op jit(solution)/shard_map/ppermute | solution.py:22
  47.4 6.4 %collective-permute-start.12 = (f32[2,1,256,128]{3,2,1,0:T(8,128)S(1)}, f32[2,1,256,128]{3,2,1,0:T(8,128)S(1)}, u32[]{:S(2)}, u32[]{:S(2)}) collective-permute-start(f32[2,1,256,128]{3,2,1,0:T(8,128)S(1)} %collective-permute-done.10.refs_2_), channel_id=1, source_target_pairs={{0,1},{1,0},{2,3},{3,2},{4,5},{5,4},{6,7},{7,6},{8,9},{9,8},{10,11... | collective-permute-start | bytes 786440 | tf_op jit(solution)/shard_map/ppermute | solution.py:22
  47.4 10.6 %collective-permute-start.6 = (f32[2,1,256,128]{3,2,1,0:T(8,128)S(1)}, f32[2,1,256,128]{3,2,1,0:T(8,128)S(1)}, u32[]{:S(2)}, u32[]{:S(2)}) collective-permute-start(f32[2,1,256,128]{3,2,1,0:T(8,128)S(1)} %get-tuple-element.34), channel_id=1, source_target_pairs={{0,1},{1,0},{2,3},{3,2},{4,5},{5,4},{6,7},{7,6},{8,9},{9,8},{10,11... | collective-permute-start | bytes 786440 | tf_op jit(solution)/shard_map/ppermute | solution.py:22
  54.6 26.7 %collective-permute-start.13 = (f32[2,1,256,128]{3,2,1,0:T(8,128)S(1)}, f32[2,1,256,128]{3,2,1,0:T(8,128)S(1)}, u32[]{:S(2)}, u32[]{:S(2)}) collective-permute-start(f32[2,1,256,128]{3,2,1,0:T(8,128)S(1)} %shard_map.83.refs_2_), channel_id=1, source_target_pairs={{0,8},{4,12},{8,0},{12,4},{1,9},{5,13},{9,1},{13,5},{2,10},{6,14},... | collective-permute-start | bytes 786440 | tf_op jit(solution)/shard_map/ppermute | solution.py:22
  58.1 35.7 %collective-permute-start.15 = (f32[2,1,256,128]{3,2,1,0:T(8,128)S(1)}, f32[2,1,256,128]{3,2,1,0:T(8,128)S(1)}, u32[]{:S(2)}, u32[]{:S(2)}) collective-permute-start(f32[2,1,256,128]{3,2,1,0:T(8,128)S(1)} %shard_map.83.refs_2_), channel_id=1, source_target_pairs={{0,4},{4,0},{8,12},{12,8},{1,5},{5,1},{9,13},{13,9},{2,6},{6,2},{1... | collective-permute-start | bytes 786440 | tf_op jit(solution)/shard_map/ppermute | solution.py:22
  59.5 34.3 %collective-permute-start.16 = (f32[2,1,256,128]{3,2,1,0:T(8,128)S(1)}, f32[2,1,256,128]{3,2,1,0:T(8,128)S(1)}, u32[]{:S(2)}, u32[]{:S(2)}) collective-permute-start(f32[2,1,256,128]{3,2,1,0:T(8,128)S(1)} %shard_map.82.refs_3_), channel_id=1, source_target_pairs={{0,4},{4,0},{8,12},{12,8},{1,5},{5,1},{9,13},{13,9},{2,6},{6,2},{1... | collective-permute-start | bytes 786440 | tf_op jit(solution)/shard_map/ppermute | solution.py:22
  81.3 12.5 %collective-permute-start.8 = (f32[2,1,256,128]{3,2,1,0:T(8,128)S(1)}, f32[2,1,256,128]{3,2,1,0:T(8,128)S(1)}, u32[]{:S(2)}, u32[]{:S(2)}) collective-permute-start(f32[2,1,256,128]{3,2,1,0:T(8,128)S(1)} %shard_map.82.refs_3_), channel_id=1, source_target_pairs={{0,8},{4,12},{8,0},{12,4},{1,9},{5,13},{9,1},{13,5},{2,10},{6,14},... | collective-permute-start | bytes 786440 | tf_op jit(solution)/shard_map/ppermute | solution.py:22
  86.7 14.0 %collective-permute-start.14 = (f32[2,1,256,128]{3,2,1,0:T(8,128)S(1)}, f32[2,1,256,128]{3,2,1,0:T(8,128)S(1)}, u32[]{:S(2)}, u32[]{:S(2)}) collective-permute-start(f32[2,1,256,128]{3,2,1,0:T(8,128)S(1)} %collective-permute-done.13.refs_2_), channel_id=1, source_target_pairs={{0,4},{4,0},{8,12},{12,8},{1,5},{5,1},{9,13},{13,9},{2,6},{6,2},{1... | collective-permute-start | bytes 786440 | tf_op jit(solution)/shard_map/ppermute | solution.py:22
  93.8 9.0 %collective-permute-start.9 = (f32[2,1,256,128]{3,2,1,0:T(8,128)S(1)}, f32[2,1,256,128]{3,2,1,0:T(8,128)S(1)}, u32[]{:S(2)}, u32[]{:S(2)}) collective-permute-start(f32[2,1,256,128]{3,2,1,0:T(8,128)S(1)} %collective-permute-done.8.refs_2_.refs_3_), channel_id=1, source_target_pairs={{0,4},{4,0},{8,12},{12,8},{1,5},{5,1},{9,13},{13,9},{2,6},{6,2},{1... | collective-permute-start | bytes 786440 | tf_op jit(solution)/shard_map/ppermute | solution.py:22
  105.7 9.2 %collective-permute-start.19 = (f32[2,1,256,128]{3,2,1,0:T(8,128)S(1)}, f32[2,1,256,128]{3,2,1,0:T(8,128)S(1)}, u32[]{:S(2)}, u32[]{:S(2)}) collective-permute-start(f32[2,1,256,128]{3,2,1,0:T(8,128)S(1)} %get-tuple-element.44), channel_id=1, source_target_pairs={{0,2},{1,3},{2,0},{3,1},{4,6},{5,7},{6,4},{7,5},{8,10},{9,11},{10,... | collective-permute-start | bytes 786440 | tf_op jit(solution)/shard_map/ppermute | solution.py:22
  106.2 11.7 %collective-permute-start.23 = (f32[2,1,256,128]{3,2,1,0:T(8,128)S(1)}, f32[2,1,256,128]{3,2,1,0:T(8,128)S(1)}, u32[]{:S(2)}, u32[]{:S(2)}) collective-permute-start(f32[2,1,256,128]{3,2,1,0:T(8,128)S(1)} %get-tuple-element.51), channel_id=1, source_target_pairs={{0,2},{1,3},{2,0},{3,1},{4,6},{5,7},{6,4},{7,5},{8,10},{9,11},{10,... | collective-permute-start | bytes 786440 | tf_op jit(solution)/shard_map/ppermute | solution.py:22
  110.1 14.7 %collective-permute-start.22 = (f32[1,128,256]{2,1,0:T(8,128)S(1)}, f32[1,128,256]{2,1,0:T(8,128)S(1)}, u32[]{:S(2)}, u32[]{:S(2)}) collective-permute-start(f32[1,128,256]{2,1,0:T(8,128)S(1)} %get-tuple-element.49), channel_id=1, source_target_pairs={{4,0},{8,4},{12,8},{5,1},{9,5},{13,9},{6,2},{10,6},{14,10},{7,3},{... | collective-permute-start | bytes 393224 | tf_op jit(solution)/shard_map/ppermute | solution.py:503
  111.4 13.4 %collective-permute-start.20 = (f32[2,1,256,128]{3,2,1,0:T(8,128)S(1)}, f32[2,1,256,128]{3,2,1,0:T(8,128)S(1)}, u32[]{:S(2)}, u32[]{:S(2)}) collective-permute-start(f32[2,1,256,128]{3,2,1,0:T(8,128)S(1)} %get-tuple-element.44), channel_id=1, source_target_pairs={{0,1},{1,0},{2,3},{3,2},{4,5},{5,4},{6,7},{7,6},{8,9},{9,8},{10,11... | collective-permute-start | bytes 786440 | tf_op jit(solution)/shard_map/ppermute | solution.py:22
  111.4 15.2 %collective-permute-start.24 = (f32[2,1,256,128]{3,2,1,0:T(8,128)S(1)}, f32[2,1,256,128]{3,2,1,0:T(8,128)S(1)}, u32[]{:S(2)}, u32[]{:S(2)}) collective-permute-start(f32[2,1,256,128]{3,2,1,0:T(8,128)S(1)} %get-tuple-element.51), channel_id=1, source_target_pairs={{0,1},{1,0},{2,3},{3,2},{4,5},{5,4},{6,7},{7,6},{8,9},{9,8},{10,11... | collective-permute-start | bytes 786440 | tf_op jit(solution)/shard_map/ppermute | solution.py:22
  114.9 9.9 %collective-permute-start.21 = (f32[2,1,256,128]{3,2,1,0:T(8,128)S(1)}, f32[2,1,256,128]{3,2,1,0:T(8,128)S(1)}, u32[]{:S(2)}, u32[]{:S(2)}) collective-permute-start(f32[2,1,256,128]{3,2,1,0:T(8,128)S(1)} %collective-permute-done.19.refs_2_), channel_id=1, source_target_pairs={{0,1},{1,0},{2,3},{3,2},{4,5},{5,4},{6,7},{7,6},{8,9},{9,8},{10,11... | collective-permute-start | bytes 786440 | tf_op jit(solution)/shard_map/ppermute | solution.py:22
  118.0 8.7 %collective-permute-start.25 = (f32[2,1,256,128]{3,2,1,0:T(8,128)S(1)}, f32[2,1,256,128]{3,2,1,0:T(8,128)S(1)}, u32[]{:S(2)}, u32[]{:S(2)}) collective-permute-start(f32[2,1,256,128]{3,2,1,0:T(8,128)S(1)} %collective-permute-done.23.refs_5_), channel_id=1, source_target_pairs={{0,1},{1,0},{2,3},{3,2},{4,5},{5,4},{6,7},{7,6},{8,9},{9,8},{10,11... | collective-permute-start | bytes 786440 | tf_op jit(solution)/shard_map/ppermute | solution.py:22
  (8 other events, 121.9 us)

commit v5 on v4

--- a/solution.py
+++ b/solution.py
@@ -52,22 +52,37 @@
     return dot(a[0], b[0]) + (dot(a[1], b[0]) + dot(a[0], b[1]))
 
 
-def times_t(a, b):
-    return dot_t(a[0], b[0]) + (dot_t(a[1], b[0]) + dot_t(a[0], b[1]))
-
-
 def total(terms):
     return functools.reduce(lambda a, b: a + b, terms)
 
 
-def pair_rows(x):
-    return tuple(
-        jnp.concatenate([v, jnp.concatenate([v[:, B:], -v[:, :B]], axis=1)], axis=0) for v in x
-    )
-
-
 def rows_of(x, start, size):
     return tuple(v[start : start + size] for v in x)
+
+
+def halves(x):
+    return tuple(v[:, :B] for v in x), tuple(v[:, B:] for v in x)
+
+
+def stacked(blocks):
+    blocks = [halves(block) for block in blocks]
+    return tuple(
+        jnp.concatenate(
+            [jnp.concatenate([block[j][part] for block in blocks], axis=1) for j in range(2)], axis=0
+        )
+        for part in range(2)
+    )
+
+
+def against(lefts, rights):
+    terms = []
+    for i in range(0, len(lefts), 2):
+        left, right = stacked(lefts[i : i + 2]), stacked(rights[i : i + 2])
+        terms += [dot_t(left[0], right[0]), dot_t(left[1], right[0]), dot_t(left[0], right[1])]
+    both = total(terms)
+    rows = both.shape[0] // 2
+    re, im = both[:rows], both[rows:]
+    return jnp.concatenate([re[:, :B] + im[:, B:], re[:, B:] - im[:, :B]], axis=1)
 
 
 def panel_kernel(local, far, starts, kinds, first, last, chunks, devices, scale, *refs):
@@ -129,9 +144,9 @@
         size = int(diag) + int(upper and i < local - 1)
         if not size:
             continue
-        terms = total(
-            times_t(green((i + start) * B, (i + start + size) * B), pair_rows(rows_of(product, i * B, B)))
-            for green, product in zip(greens, products)
+        terms = against(
+            [green((i + start) * B, (i + start + size) * B) for green in greens],
+            [rows_of(product, i * B, B) for product in products],
         )
         if diag:
             value = old("diag", i) + terms[:B]
@@ -163,19 +178,21 @@
             )
 
         def over_terms():
-            terms = []
-            for number, column in enumerate(columns):
+            rights = []
+            for number in range(len(columns)):
                 if whole:
-                    product = rows_of(products[number], (local - 1) * B, B)
+                    rights.append(rows_of(products[number], (local - 1) * B, B))
                 else:
-                    product = split(times(greens[number](low, local * B), sigmas[number]))
-                terms.append(times_t(edge(even, column), pair_rows(product)))
-            return total(terms)
+                    rights.append(split(times(greens[number](low, local * B), sigmas[number])))
+            return against([edge(even, column) for column in columns], rights)
 
         def back_terms():
-            return total(
-                times_t(green(0, B), pair_rows(split(times(edge(jnp.logical_not(even), column), sigma))))
-                for green, sigma, column in zip(greens, sigmas, columns)
+            return against(
+                [green(0, B) for green in greens],
+                [
+                    split(times(edge(jnp.logical_not(even), column), sigma))
+                    for sigma, column in zip(sigmas, columns)
+                ],
             )
 
         if "over" in kinds:

time: 129 us -> 126 us (0.977)
  Pallas kernels: 46.7 us -> 39.6 us
  waiting for transfers between devices: 43.2 us -> 47.1 us
    pallas_call x15, Pallas kernels: 41.6 us -> 34.6 us  [panel(): pl.pallas_call(functools.partial(panel_kernel, local, far, starts, kinds,...]
    ppermute x23, waiting for transfers between devices: 43.2 us -> 47.1 us  [swapped(): lax.ppermute(x, axis, [(i, i ^ bit) for i in range(lax.axis_size(axis))])]
  transfers between devices with their start and end apart: 26 -> 26, of which waited for: 8 -> 10; matrix products, arithmetic and copies ran while one was open for 4% -> 4% of each run, Pallas kernels for 31% -> 27%
where the time goes in v5:
time: 126 us; the launch traced here: 125 us
  waiting for transfers between devices  47.1 us (37%)
  Pallas kernels  39.6 us (31%)
  starting transfers between devices  28.5 us (23%)
  local copies, waits for them, and re-layouts  8.33 us (7%)
    ppermute x23, waiting for transfers between devices, swapped(): lax.ppermute(x, axis, [(i, i ^ bit) for i in range(lax.axis_size(axis))])  47.1 us
    pallas_call x15, Pallas kernels, panel(): pl.pallas_call(functools.partial(panel_kernel, local, far, starts, kinds,...  34.6 us
    ppermute x23, starting transfers between devices, swapped(): lax.ppermute(x, axis, [(i, i ^ bit) for i in range(lax.axis_size(axis))])  24.7 us
    unnamed x12, local copies, waits for them, and re-layouts  4.48 us
    pallas_call x2, Pallas kernels, phonon_final(): pl.pallas_call(kernel, grid=(1,), in_specs=specs, out_specs=out_specs, ou...  3.41 us
    dynamic_slice x1, local copies, waits for them, and re-layouts, edge_rows(): lax.dynamic_slice(retarded, (0, 0, row, column), (2, 1, B, columns // 2))  2.81 us
  transfers between devices with their start and end apart: 26, of which 10 were waited for; matrix products, arithmetic and copies ran while one was open for 4% of the time, Pallas kernels for 27%

profile of v5, /device:TPU:0, one launch (start us, length us, event | category | flops | bytes accessed | tf_op | source)
XLA Modules:
  0.0 125.5 jit_solution(11832550427882402645)
XLA Ops:
  0.6 3.1 %collective-permute-start.4 = (f32[2,1,512,128]{3,2,1,0:T(8,128)}, f32[2,1,512,128]{3,2,1,0:T(8,128)S(1)}, u32[]{:S(2)}, u32[]{:S(2)}) collective-permute-start(f32[2,1,512,128]{3,2,1,0:T(8,128)} %contact_ref.1), channel_id=1, source_target_pairs={{0,4},{4,0},{8,12},{12,8},{1,5},{5,1},{9,13},{13,9},{2,6},{6,2},{1... | collective-permute-start | bytes 1572872 | tf_op jit(solution)/shard_map/ppermute | solution.py:22
  4.9 2.7 %collective-permute-start.2 = (f32[2,1,256,128]{3,2,1,0:T(8,128)S(1)}, f32[2,1,256,128]{3,2,1,0:T(8,128)S(1)}, u32[]{:S(2)}, u32[]{:S(2)}) collective-permute-start(f32[2,1,256,128]{3,2,1,0:T(8,128)S(1)} %get-tuple-element.33), channel_id=1, source_target_pairs={{0,8},{4,12},{8,0},{12,4},{1,9},{5,13},{9,1},{13,5},{2,10},{6,14},... | collective-permute-start | bytes 786440 | tf_op jit(solution)/shard_map/ppermute | solution.py:22
  9.7 2.8 %constant_dynamic-slice_fusion = (f32[2,1,128,1024]{3,2,1,0:T(8,128)S(1)}, f32[2,1,128,1024]{3,2,1,0:T(8,128)}) fusion(f32[2,1,512,2048]{3,2,1,0:T(8,128)} %refs_1_.29, s32[]{:T(128)S(6)} %select_n.76, s32[]{:T(128)S(6)} %select_n.78, s32[]{:T(128)S(6)} %select_n.73, s32[]{:T(128)S(6)} %select_n.75), kind=kLoop, calls=%fused_computation.8 | loop fusion | bytes 4194320 | tf_op jit(solution)/shard_map/dynamic_slice | solution.py:436
  12.8 3.4 %copy-done = f32[2,1,512,2048]{3,2,1,0:T(8,128)S(1)} copy-done((f32[2,1,512,2048]{3,2,1,0:T(8,128)S(1)}, f32[2,1,512,2048]{3,2,1,0:T(8,128)}, u32[]{:S(2)}) %copy-start) | copy-done | bytes 8388632
  16.1 2.4 %shard_map.76.refs_3_ = f32[4,128,256]{2,1,0:T(8,128)S(1)} custom-call(s32[2]{0:T(128)S(1)} %compare_select_fusion.refs_0_.at_ref.refs_1_, f32[2,1,512,2048]{3,2,1,0:T(8,128)S(1)} %copy-done, f32[2,1,512,128]{3,2,1,0:T(8,128)S(1)} %get-tuple-element.29.refs_2_.contact_ref), custom_call_target="tpu_custom_call" | custom-call | flops 1610612736 | bytes 2097152 | tf_op jit(solution)/shard_map/pallas_call | solution.py:262
  18.6 3.4 %collective-permute-done.2.refs_2_ = f32[2,1,256,128]{3,2,1,0:T(8,128)S(1)} collective-permute-done((f32[2,1,256,128]{3,2,1,0:T(8,128)S(1)}, f32[2,1,256,128]{3,2,1,0:T(8,128)S(1)}, u32[]{:S(2)}, u32[]{:S(2)}) %collective-permute-start.2) | collective-permute-done | bytes 262176 | tf_op jit(solution)/shard_map/ppermute | solution.py:22
  21.9 3.6 %collective-permute-start.3 = (f32[2,1,256,128]{3,2,1,0:T(8,128)S(1)}, f32[2,1,256,128]{3,2,1,0:T(8,128)S(1)}, u32[]{:S(2)}, u32[]{:S(2)}) collective-permute-start(f32[2,1,256,128]{3,2,1,0:T(8,128)S(1)} %collective-permute-done.2.refs_2_), channel_id=1, source_target_pairs={{0,4},{4,0},{8,12},{12,8},{1,5},{5,1},{9,13},{13,9},{2,6},{6,2},{1... | collective-permute-start | bytes 786440 | tf_op jit(solution)/shard_map/ppermute | solution.py:22
  27.2 3.5 %collective-permute-done.refs_2_ = f32[2,1,256,128]{3,2,1,0:T(8,128)S(1)} collective-permute-done((f32[2,1,256,128]{3,2,1,0:T(8,128)S(1)}, f32[2,1,256,128]{3,2,1,0:T(8,128)S(1)}, u32[]{:S(2)}, u32[]{:S(2)}) %collective-permute-start) | collective-permute-done | bytes 262176 | tf_op jit(solution)/shard_map/ppermute | solution.py:22
  31.1 2.5 %shard_map.78.refs_3_ = f32[4,128,256]{2,1,0:T(8,128)S(1)} custom-call(s32[2]{0:T(128)S(1)} %compare_select_fusion.refs_0_.at_ref.refs_1_, f32[2,1,512,2048]{3,2,1,0:T(8,128)S(1)} %copy-done, f32[2,1,512,128]{3,2,1,0:T(8,128)S(1)} %collective-permute-done.4.refs_2_, f32[4,128,256]{2,1,0:T(8,128)S(1)} %shard_map.77.refs_3_), custom_call_target="tpu_custom_call", output_to_operand_aliasing={{}: (3, {})} | custom-call | flops 1610612736 | bytes 2097152 | tf_op jit(solution)/shard_map/pallas_call | solution.py:262
  45.0 2.1 %collective-permute-done.10.refs_2_ = f32[2,1,256,128]{3,2,1,0:T(8,128)S(1)} collective-permute-done((f32[2,1,256,128]{3,2,1,0:T(8,128)S(1)}, f32[2,1,256,128]{3,2,1,0:T(8,128)S(1)}, u32[]{:S(2)}, u32[]{:S(2)}) %collective-permute-start.10) | collective-permute-done | bytes 262176 | tf_op jit(solution)/shard_map/ppermute | solution.py:22
  47.6 5.5 %collective-permute-done.5.refs_2_ = f32[2,1,256,128]{3,2,1,0:T(8,128)S(1)} collective-permute-done((f32[2,1,256,128]{3,2,1,0:T(8,128)S(1)}, f32[2,1,256,128]{3,2,1,0:T(8,128)S(1)}, u32[]{:S(2)}, u32[]{:S(2)}) %collective-permute-start.5) | collective-permute-done | bytes 262176 | tf_op jit(solution)/shard_map/ppermute | solution.py:22
  53.9 3.8 %collective-permute-start.13 = (f32[2,1,256,128]{3,2,1,0:T(8,128)S(1)}, f32[2,1,256,128]{3,2,1,0:T(8,128)S(1)}, u32[]{:S(2)}, u32[]{:S(2)}) collective-permute-start(f32[2,1,256,128]{3,2,1,0:T(8,128)S(1)} %shard_map.83.refs_2_), channel_id=1, source_target_pairs={{0,8},{4,12},{8,0},{12,4},{1,9},{5,13},{9,1},{13,5},{2,10},{6,14},... | collective-permute-start | bytes 786440 | tf_op jit(solution)/shard_map/ppermute | solution.py:22
  60.6 20.4 %collective-permute-done.13.refs_2_ = f32[2,1,256,128]{3,2,1,0:T(8,128)S(1)} collective-permute-done((f32[2,1,256,128]{3,2,1,0:T(8,128)S(1)}, f32[2,1,256,128]{3,2,1,0:T(8,128)S(1)}, u32[]{:S(2)}, u32[]{:S(2)}) %collective-permute-start.13) | collective-permute-done | bytes 262176 | tf_op jit(solution)/shard_map/ppermute | solution.py:22
  81.0 3.2 %shard_map.84 = (f32[4,128,256]{2,1,0:T(8,128)S(1)}, f32[3,128,256]{2,1,0:T(8,128)S(1)}) custom-call(s32[2]{0:T(128)S(1)} %compare_select_fusion.refs_0_.at_ref.refs_1_, f32[2,1,512,2048]{3,2,1,0:T(8,128)S(1)} %bitcast.11, f32[2,1,256,128]{3,2,1,0:T(8,128)S(1)} %shard_map.83.refs_2_, f32[2,1,256,128]{3,2,1,0:T(8,128)S(1)} %shard_map.82.refs_3_), custom_call_target="tpu_custom_call" | custom-call | flops 2415919104 | bytes 2097152 | tf_op jit(solution)/shard_map/pallas_call | solution.py:262
  84.2 2.2 %shard_map.85 = (f32[4,128,256]{2,1,0:T(8,128)S(1)}, f32[3,128,256]{2,1,0:T(8,128)S(1)}) custom-call(s32[2]{0:T(128)S(1)} %compare_select_fusion.refs_0_.at_ref.refs_1_, f32[2,1,512,2048]{3,2,1,0:T(8,128)S(1)} %bitcast.11, f32[2,1,256,128]{3,2,1,0:T(8,128)S(1)} %collective-permute-done.13.refs_2_, ...), custom_call_target="tpu_custom_call", output_to_operand_aliasing={{0}: (3, {}), {1}: (4, {})} | custom-call | flops 1207959552 | bytes 1048576 | tf_op jit(solution)/shard_map/pallas_call | solution.py:262
  86.4 3.3 %collective-permute-start.14 = (f32[2,1,256,128]{3,2,1,0:T(8,128)S(1)}, f32[2,1,256,128]{3,2,1,0:T(8,128)S(1)}, u32[]{:S(2)}, u32[]{:S(2)}) collective-permute-start(f32[2,1,256,128]{3,2,1,0:T(8,128)S(1)} %collective-permute-done.13.refs_2_), channel_id=1, source_target_pairs={{0,4},{4,0},{8,12},{12,8},{1,5},{5,1},{9,13},{13,9},{2,6},{6,2},{1... | collective-permute-start | bytes 786440 | tf_op jit(solution)/shard_map/ppermute | solution.py:22
  89.6 4.0 %collective-permute-done.8.refs_2_.refs_3_ = f32[2,1,256,128]{3,2,1,0:T(8,128)S(1)} collective-permute-done((f32[2,1,256,128]{3,2,1,0:T(8,128)S(1)}, f32[2,1,256,128]{3,2,1,0:T(8,128)S(1)}, u32[]{:S(2)}, u32[]{:S(2)}) %collective-permute-start.8) | collective-permute-done | bytes 262176 | tf_op jit(solution)/shard_map/ppermute | solution.py:22
  93.6 4.0 %shard_map.86 = (f32[4,128,256]{2,1,0:T(8,128)S(1)}, f32[3,128,256]{2,1,0:T(8,128)S(1)}, f32[1,128,256]{2,1,0:T(8,128)S(1)}, f32[1,128,256]{2,1,0:T(8,128)S(1)}) custom-call(s32[2]{0:T(128)S(1)} %compare_select_fusion.refs_0_.at_ref.refs_1_, f32[2,1,512,2048]{3,2,1,0:T(8,128)S(1)} %bitcast.11, ...), custom_call_target="tpu_custom_call", output_to_operand_aliasing={{0}: (6, {}), {1}: (7, {})} | custom-call | flops 4026531840 | bytes 2097152 | tf_op jit(solution)/shard_map/pallas_call | solution.py:262
  97.7 2.1 %shard_map.87 = (f32[4,128,256]{2,1,0:T(8,128)S(1)}, f32[3,128,256]{2,1,0:T(8,128)S(1)}) custom-call(s32[2]{0:T(128)S(1)} %compare_select_fusion.refs_0_.at_ref.refs_1_, f32[2,1,512,2048]{3,2,1,0:T(8,128)S(1)} %bitcast.11, f32[2,1,256,128]{3,2,1,0:T(8,128)S(1)} %collective-permute-done.8.refs_2_.refs_3_, ...), custom_call_target="tpu_custom_call", output_to_operand_aliasing={{0}: (3, {}), {1}: (4, {})} | custom-call | flops 1207959552 | bytes 1048576 | tf_op jit(solution)/shard_map/pallas_call | solution.py:262
  102.1 2.5 %shard_map.89 = (f32[2,1,256,128]{3,2,1,0:T(8,128)S(1)}, f32[2,1,256,128]{3,2,1,0:T(8,128)S(1)}, f32[2,1,512,128]{3,2,1,0:T(8,128)}) custom-call(s32[2]{0:T(128)S(1)} %compare_select_fusion.refs_0_.at_ref.refs_1_, f32[2,1,512,2048]{3,2,1,0:T(8,128)S(1)} %bitcast.11, f32[2,1,256,128]{3,2,1,0:T(8,128)S(1)} %collective-permute-done.9.refs_2_.refs_3_, ...), custom_call_target="tpu_custom_call" | custom-call | flops 805306368 | bytes 1048576 | tf_op jit(solution)/shard_map/pallas_call | solution.py:262
  110.2 3.6 %collective-permute-done.19.refs_2_ = f32[2,1,256,128]{3,2,1,0:T(8,128)S(1)} collective-permute-done((f32[2,1,256,128]{3,2,1,0:T(8,128)S(1)}, f32[2,1,256,128]{3,2,1,0:T(8,128)S(1)}, u32[]{:S(2)}, u32[]{:S(2)}) %collective-permute-start.19) | collective-permute-done | bytes 262176 | tf_op jit(solution)/shard_map/ppermute | solution.py:22
  113.8 2.9 %collective-permute-done.23.refs_5_ = f32[2,1,256,128]{3,2,1,0:T(8,128)S(1)} collective-permute-done((f32[2,1,256,128]{3,2,1,0:T(8,128)S(1)}, f32[2,1,256,128]{3,2,1,0:T(8,128)S(1)}, u32[]{:S(2)}, u32[]{:S(2)}) %collective-permute-start.23) | collective-permute-done | bytes 262176 | tf_op jit(solution)/shard_map/ppermute | solution.py:22
  118.1 3.9 %shard_map.92.refs_5_ = f32[2,1,512,128]{3,2,1,0:T(8,128)} custom-call(s32[2]{0:T(128)S(1)} %compare_select_fusion.refs_0_.at_ref.refs_1_, f32[2,1,512,2048]{3,2,1,0:T(8,128)S(1)} %bitcast.11, f32[2,1,256,128]{3,2,1,0:T(8,128)S(1)} %collective-permute-done.14.refs_2_, f32[2,1,256,128]{3,2,1,0:T(8,128)S(1)} %collective-permute-done.9.refs_2_.refs_3_, ...), custom_call_target="tpu_custom_call" | custom-call | flops 2415919104 | bytes 2097152 | tf_op jit(solution)/shard_map/pallas_call | solution.py:262
  122.0 1.9 %shard_map.93 = (f32[2,1,512,128]{3,2,1,0:T(8,128)}, f32[2,1,512,128]{3,2,1,0:T(8,128)}) custom-call(s32[3]{0:T(128)S(1)} %copy-done.2, s32[2]{0:T(128)S(1)} %compare_select_fusion.refs_0_.at_ref.refs_1_, f32[2,1,512,128]{3,2,1,0:T(8,128)S(1)} %get-tuple-element.29.refs_2_.contact_ref, ...), custom_call_target="tpu_custom_call", output_to_operand_aliasing={{1}: (8, {})} | custom-call | flops 655360 | bytes 1310720 | tf_op jit(solution)/shard_map/pallas_call | solution.py:376
  (71 shorter events, 31.9 us)
Async XLA Ops:
  0.6 30.4 %collective-permute-start.4 = (f32[2,1,512,128]{3,2,1,0:T(8,128)}, f32[2,1,512,128]{3,2,1,0:T(8,128)S(1)}, u32[]{:S(2)}, u32[]{:S(2)}) collective-permute-start(f32[2,1,512,128]{3,2,1,0:T(8,128)} %contact_ref.1), channel_id=1, source_target_pairs={{0,4},{4,0},{8,12},{12,8},{1,5},{5,1},{9,13},{13,9},{2,6},{6,2},{1... | collective-permute-start | bytes 1572872 | tf_op jit(solution)/shard_map/ppermute | solution.py:22
  4.9 17.0 %collective-permute-start.2 = (f32[2,1,256,128]{3,2,1,0:T(8,128)S(1)}, f32[2,1,256,128]{3,2,1,0:T(8,128)S(1)}, u32[]{:S(2)}, u32[]{:S(2)}) collective-permute-start(f32[2,1,256,128]{3,2,1,0:T(8,128)S(1)} %get-tuple-element.33), channel_id=1, source_target_pairs={{0,8},{4,12},{8,0},{12,4},{1,9},{5,13},{9,1},{13,5},{2,10},{6,14},... | collective-permute-start | bytes 786440 | tf_op jit(solution)/shard_map/ppermute | solution.py:22
  7.6 23.1 %collective-permute-start = (f32[2,1,256,128]{3,2,1,0:T(8,128)S(1)}, f32[2,1,256,128]{3,2,1,0:T(8,128)S(1)}, u32[]{:S(2)}, u32[]{:S(2)}) collective-permute-start(f32[2,1,256,128]{3,2,1,0:T(8,128)S(1)} %get-tuple-element.32), channel_id=1, source_target_pairs={{0,8},{4,12},{8,0},{12,4},{1,9},{5,13},{9,1},{13,5},{2,10},{6,14},... | collective-permute-start | bytes 786440 | tf_op jit(solution)/shard_map/ppermute | solution.py:22
  21.9 13.3 %collective-permute-start.3 = (f32[2,1,256,128]{3,2,1,0:T(8,128)S(1)}, f32[2,1,256,128]{3,2,1,0:T(8,128)S(1)}, u32[]{:S(2)}, u32[]{:S(2)}) collective-permute-start(f32[2,1,256,128]{3,2,1,0:T(8,128)S(1)} %collective-permute-done.2.refs_2_), channel_id=1, source_target_pairs={{0,4},{4,0},{8,12},{12,8},{1,5},{5,1},{9,13},{13,9},{2,6},{6,2},{1... | collective-permute-start | bytes 786440 | tf_op jit(solution)/shard_map/ppermute | solution.py:22
  30.7 7.7 %collective-permute-start.1 = (f32[2,1,256,128]{3,2,1,0:T(8,128)S(1)}, f32[2,1,256,128]{3,2,1,0:T(8,128)S(1)}, u32[]{:S(2)}, u32[]{:S(2)}) collective-permute-start(f32[2,1,256,128]{3,2,1,0:T(8,128)S(1)} %collective-permute-done.refs_2_), channel_id=1, source_target_pairs={{0,4},{4,0},{8,12},{12,8},{1,5},{5,1},{9,13},{13,9},{2,6},{6,2},{1... | collective-permute-start | bytes 786440 | tf_op jit(solution)/shard_map/ppermute | solution.py:22
  40.1 7.0 %collective-permute-start.10 = (f32[2,1,256,128]{3,2,1,0:T(8,128)S(1)}, f32[2,1,256,128]{3,2,1,0:T(8,128)S(1)}, u32[]{:S(2)}, u32[]{:S(2)}) collective-permute-start(f32[2,1,256,128]{3,2,1,0:T(8,128)S(1)} %get-tuple-element.35), channel_id=1, source_target_pairs={{0,2},{1,3},{2,0},{3,1},{4,6},{5,7},{6,4},{7,5},{8,10},{9,11},{10,... | collective-permute-start | bytes 786440 | tf_op jit(solution)/shard_map/ppermute | solution.py:22
  41.8 44.5 %collective-permute-start.17 = (f32[2,1,128,1024]{3,2,1,0:T(8,128)S(1)}, f32[2,1,128,1024]{3,2,1,0:T(8,128)S(1)}, u32[]{:S(2)}, u32[]{:S(2)}) collective-permute-start(f32[2,1,128,1024]{3,2,1,0:T(8,128)S(1)} %copy-done.3), channel_id=1, source_target_pairs={{0,4},{4,0},{8,12},{12,8},{1,5},{5,1},{9,13},{13,9},{2,6},{6,2},{1... | collective-permute-start | bytes 3145736 | tf_op jit(solution)/shard_map/ppermute | solution.py:441
  43.4 50.1 %collective-permute-start.18 = (f32[2,1,128,1024]{3,2,1,0:T(8,128)S(1)}, f32[2,1,128,1024]{3,2,1,0:T(8,128)S(1)}, u32[]{:S(2)}, u32[]{:S(2)}) collective-permute-start(f32[2,1,128,1024]{3,2,1,0:T(8,128)S(1)} %get-tuple-element.55), channel_id=1, source_target_pairs={{4,8},{8,4},{5,9},{9,5},{6,10},{10,6},{7,11},{11,7},{20,24},{24,20... | collective-permute-start | bytes 3145736 | tf_op jit(solution)/shard_map/ppermute | solution.py:441
  44.4 8.7 %collective-permute-start.5 = (f32[2,1,256,128]{3,2,1,0:T(8,128)S(1)}, f32[2,1,256,128]{3,2,1,0:T(8,128)S(1)}, u32[]{:S(2)}, u32[]{:S(2)}) collective-permute-start(f32[2,1,256,128]{3,2,1,0:T(8,128)S(1)} %get-tuple-element.34), channel_id=1, source_target_pairs={{0,2},{1,3},{2,0},{3,1},{4,6},{5,7},{6,4},{7,5},{8,10},{9,11},{10,... | collective-permute-start | bytes 786440 | tf_op jit(solution)/shard_map/ppermute | solution.py:22
  47.1 6.0 %collective-permute-start.12 = (f32[2,1,256,128]{3,2,1,0:T(8,128)S(1)}, f32[2,1,256,128]{3,2,1,0:T(8,128)S(1)}, u32[]{:S(2)}, u32[]{:S(2)}) collective-permute-start(f32[2,1,256,128]{3,2,1,0:T(8,128)S(1)} %collective-permute-done.10.refs_2_), channel_id=1, source_target_pairs={{0,1},{1,0},{2,3},{3,2},{4,5},{5,4},{6,7},{7,6},{8,9},{9,8},{10,11... | collective-permute-start | bytes 786440 | tf_op jit(solution)/shard_map/ppermute | solution.py:22
  47.1 10.6 %collective-permute-start.6 = (f32[2,1,256,128]{3,2,1,0:T(8,128)S(1)}, f32[2,1,256,128]{3,2,1,0:T(8,128)S(1)}, u32[]{:S(2)}, u32[]{:S(2)}) collective-permute-start(f32[2,1,256,128]{3,2,1,0:T(8,128)S(1)} %get-tuple-element.34), channel_id=1, source_target_pairs={{0,1},{1,0},{2,3},{3,2},{4,5},{5,4},{6,7},{7,6},{8,9},{9,8},{10,11... | collective-permute-start | bytes 786440 | tf_op jit(solution)/shard_map/ppermute | solution.py:22
  53.9 27.1 %collective-permute-start.13 = (f32[2,1,256,128]{3,2,1,0:T(8,128)S(1)}, f32[2,1,256,128]{3,2,1,0:T(8,128)S(1)}, u32[]{:S(2)}, u32[]{:S(2)}) collective-permute-start(f32[2,1,256,128]{3,2,1,0:T(8,128)S(1)} %shard_map.83.refs_2_), channel_id=1, source_target_pairs={{0,8},{4,12},{8,0},{12,4},{1,9},{5,13},{9,1},{13,5},{2,10},{6,14},... | collective-permute-start | bytes 786440 | tf_op jit(solution)/shard_map/ppermute | solution.py:22
  57.7 35.9 %collective-permute-start.15 = (f32[2,1,256,128]{3,2,1,0:T(8,128)S(1)}, f32[2,1,256,128]{3,2,1,0:T(8,128)S(1)}, u32[]{:S(2)}, u32[]{:S(2)}) collective-permute-start(f32[2,1,256,128]{3,2,1,0:T(8,128)S(1)} %shard_map.83.refs_2_), channel_id=1, source_target_pairs={{0,4},{4,0},{8,12},{12,8},{1,5},{5,1},{9,13},{13,9},{2,6},{6,2},{1... | collective-permute-start | bytes 786440 | tf_op jit(solution)/shard_map/ppermute | solution.py:22
  59.1 34.5 %collective-permute-start.16 = (f32[2,1,256,128]{3,2,1,0:T(8,128)S(1)}, f32[2,1,256,128]{3,2,1,0:T(8,128)S(1)}, u32[]{:S(2)}, u32[]{:S(2)}) collective-permute-start(f32[2,1,256,128]{3,2,1,0:T(8,128)S(1)} %shard_map.82.refs_3_), channel_id=1, source_target_pairs={{0,4},{4,0},{8,12},{12,8},{1,5},{5,1},{9,13},{13,9},{2,6},{6,2},{1... | collective-permute-start | bytes 786440 | tf_op jit(solution)/shard_map/ppermute | solution.py:22
  81.0 12.6 %collective-permute-start.8 = (f32[2,1,256,128]{3,2,1,0:T(8,128)S(1)}, f32[2,1,256,128]{3,2,1,0:T(8,128)S(1)}, u32[]{:S(2)}, u32[]{:S(2)}) collective-permute-start(f32[2,1,256,128]{3,2,1,0:T(8,128)S(1)} %shard_map.82.refs_3_), channel_id=1, source_target_pairs={{0,8},{4,12},{8,0},{12,4},{1,9},{5,13},{9,1},{13,5},{2,10},{6,14},... | collective-permute-start | bytes 786440 | tf_op jit(solution)/shard_map/ppermute | solution.py:22
  86.4 13.4 %collective-permute-start.14 = (f32[2,1,256,128]{3,2,1,0:T(8,128)S(1)}, f32[2,1,256,128]{3,2,1,0:T(8,128)S(1)}, u32[]{:S(2)}, u32[]{:S(2)}) collective-permute-start(f32[2,1,256,128]{3,2,1,0:T(8,128)S(1)} %collective-permute-done.13.refs_2_), channel_id=1, source_target_pairs={{0,4},{4,0},{8,12},{12,8},{1,5},{5,1},{9,13},{13,9},{2,6},{6,2},{1... | collective-permute-start | bytes 786440 | tf_op jit(solution)/shard_map/ppermute | solution.py:22
  93.6 8.5 %collective-permute-start.9 = (f32[2,1,256,128]{3,2,1,0:T(8,128)S(1)}, f32[2,1,256,128]{3,2,1,0:T(8,128)S(1)}, u32[]{:S(2)}, u32[]{:S(2)}) collective-permute-start(f32[2,1,256,128]{3,2,1,0:T(8,128)S(1)} %collective-permute-done.8.refs_2_.refs_3_), channel_id=1, source_target_pairs={{0,4},{4,0},{8,12},{12,8},{1,5},{5,1},{9,13},{13,9},{2,6},{6,2},{1... | collective-permute-start | bytes 786440 | tf_op jit(solution)/shard_map/ppermute | solution.py:22
  104.6 9.2 %collective-permute-start.19 = (f32[2,1,256,128]{3,2,1,0:T(8,128)S(1)}, f32[2,1,256,128]{3,2,1,0:T(8,128)S(1)}, u32[]{:S(2)}, u32[]{:S(2)}) collective-permute-start(f32[2,1,256,128]{3,2,1,0:T(8,128)S(1)} %get-tuple-element.44), channel_id=1, source_target_pairs={{0,2},{1,3},{2,0},{3,1},{4,6},{5,7},{6,4},{7,5},{8,10},{9,11},{10,... | collective-permute-start | bytes 786440 | tf_op jit(solution)/shard_map/ppermute | solution.py:22
  105.2 11.5 %collective-permute-start.23 = (f32[2,1,256,128]{3,2,1,0:T(8,128)S(1)}, f32[2,1,256,128]{3,2,1,0:T(8,128)S(1)}, u32[]{:S(2)}, u32[]{:S(2)}) collective-permute-start(f32[2,1,256,128]{3,2,1,0:T(8,128)S(1)} %get-tuple-element.51), channel_id=1, source_target_pairs={{0,2},{1,3},{2,0},{3,1},{4,6},{5,7},{6,4},{7,5},{8,10},{9,11},{10,... | collective-permute-start | bytes 786440 | tf_op jit(solution)/shard_map/ppermute | solution.py:22
  108.4 13.7 %collective-permute-start.22 = (f32[1,128,256]{2,1,0:T(8,128)S(1)}, f32[1,128,256]{2,1,0:T(8,128)S(1)}, u32[]{:S(2)}, u32[]{:S(2)}) collective-permute-start(f32[1,128,256]{2,1,0:T(8,128)S(1)} %get-tuple-element.49), channel_id=1, source_target_pairs={{4,0},{8,4},{12,8},{5,1},{9,5},{13,9},{6,2},{10,6},{14,10},{7,3},{... | collective-permute-start | bytes 393224 | tf_op jit(solution)/shard_map/ppermute | solution.py:520
  109.7 12.4 %collective-permute-start.20 = (f32[2,1,256,128]{3,2,1,0:T(8,128)S(1)}, f32[2,1,256,128]{3,2,1,0:T(8,128)S(1)}, u32[]{:S(2)}, u32[]{:S(2)}) collective-permute-start(f32[2,1,256,128]{3,2,1,0:T(8,128)S(1)} %get-tuple-element.44), channel_id=1, source_target_pairs={{0,1},{1,0},{2,3},{3,2},{4,5},{5,4},{6,7},{7,6},{8,9},{9,8},{10,11... | collective-permute-start | bytes 786440 | tf_op jit(solution)/shard_map/ppermute | solution.py:22
  109.7 14.2 %collective-permute-start.24 = (f32[2,1,256,128]{3,2,1,0:T(8,128)S(1)}, f32[2,1,256,128]{3,2,1,0:T(8,128)S(1)}, u32[]{:S(2)}, u32[]{:S(2)}) collective-permute-start(f32[2,1,256,128]{3,2,1,0:T(8,128)S(1)} %get-tuple-element.51), channel_id=1, source_target_pairs={{0,1},{1,0},{2,3},{3,2},{4,5},{5,4},{6,7},{7,6},{8,9},{9,8},{10,11... | collective-permute-start | bytes 786440 | tf_op jit(solution)/shard_map/ppermute | solution.py:22
  113.8 8.2 %collective-permute-start.21 = (f32[2,1,256,128]{3,2,1,0:T(8,128)S(1)}, f32[2,1,256,128]{3,2,1,0:T(8,128)S(1)}, u32[]{:S(2)}, u32[]{:S(2)}) collective-permute-start(f32[2,1,256,128]{3,2,1,0:T(8,128)S(1)} %collective-permute-done.19.refs_2_), channel_id=1, source_target_pairs={{0,1},{1,0},{2,3},{3,2},{4,5},{5,4},{6,7},{7,6},{8,9},{9,8},{10,11... | collective-permute-start | bytes 786440 | tf_op jit(solution)/shard_map/ppermute | solution.py:22
  116.7 7.3 %collective-permute-start.25 = (f32[2,1,256,128]{3,2,1,0:T(8,128)S(1)}, f32[2,1,256,128]{3,2,1,0:T(8,128)S(1)}, u32[]{:S(2)}, u32[]{:S(2)}) collective-permute-start(f32[2,1,256,128]{3,2,1,0:T(8,128)S(1)} %collective-permute-done.23.refs_5_), channel_id=1, source_target_pairs={{0,1},{1,0},{2,3},{3,2},{4,5},{5,4},{6,7},{7,6},{8,9},{9,8},{10,11... | collective-permute-start | bytes 786440 | tf_op jit(solution)/shard_map/ppermute | solution.py:22
  (8 other events, 126.7 us)

commit v6 on v5

--- a/solution.py
+++ b/solution.py
@@ -198,15 +198,15 @@
         if "over" in kinds:
             theirs = source_high != (pan + 1 >= middle)
             if last:
-                end = outs[0]
+                end = outs[1]
 
                 @pl.when(theirs)
                 def _():
-                    put(end, local - 1, old("over", 0) + over_terms())
+                    put(end, 0, old("over", 0) + over_terms())
 
                 @pl.when(jnp.logical_not(theirs))
                 def _():
-                    put(end, local - 1, jnp.zeros((B, 2 * B), F32) + old("over", 0))
+                    put(end, 0, jnp.zeros((B, 2 * B), F32) + old("over", 0))
 
             else:
                 if "over" not in ins:
@@ -251,7 +251,7 @@
         operands.append(carry[kind])
     if last:
         tall = jax.ShapeDtypeStruct((2, 1, rows, B), F32)
-        shapes = {"upper": tall}
+        shapes = {"upper": tall, "over": jax.ShapeDtypeStruct((2, 1, B, B), F32)}
         if "diag" in kinds:
             part = jax.ShapeDtypeStruct((2, 1, rows // chunks, B), F32)
             shapes = {number: part for number in range(chunks)}
@@ -260,18 +260,7 @@
     full = "diag" in kinds or "upper" in kinds
     work = 3 * 2 * (2 * B) * (2 * B) * many * (rows if full else B) * (1 + len(kinds))
     out = pl.pallas_call(
-        functools.partial(
-            panel_kernel,
-            local,
-            far,
-            starts,
-            kinds,
-            first,
-            last,
-            chunks,
-            devices,
-            1.0 / math.sqrt(B),
-        ),
+        functools.partial(panel_kernel, local, far, starts, kinds, first, last, chunks, devices, 1.0 / math.sqrt(B)),
         in_specs=[pl.BlockSpec(memory_space=pltpu.SMEM)] + [vmem] * (len(operands) - 1),
         out_specs=[vmem] * len(shapes),
         out_shape=list(shapes.values()),
@@ -282,34 +271,31 @@
         ),
     )(*operands)
     if last:
-        return {"diag": out} if "diag" in kinds else {"upper": out[0]}
+        return {"diag": out} if "diag" in kinds else {"upper": out[0], "over": out[1]}
     return dict(carry, **dict(zip(kinds, out)))
 
 
-def phonon_kernel(fars, modes, row, size, final, scale, shift_ref, at_ref, contact_ref, *refs):
-    col_ref, row_ref = refs[:2]
-    piece_refs, refs = refs[2 : 2 + len(fars)], refs[2 + len(fars) :]
+def scattered(fars, modes, row, size, shift_ref, at_ref, contact_ref, col_ref, row_ref, piece_refs):
     energy = at_ref[1]
     chosen = []
     for far in fars:
         apart = jnp.abs((energy ^ far) - energy)
         chosen.append([jnp.where(apart == shift_ref[m], 1.0, 0.0).astype(F32) for m in range(modes)])
-    out_ref = refs[-2] if final and len(refs) > 2 else refs[-1]
     for start in range(0, size, B):
         rows = slice(row + start, row + start + B)
-        here = slice(start, start + B)
         outer = [col_ref[rows, m : m + 1] * row_ref[m : m + 1, rows] for m in range(modes)]
         values = [contact_ref[0, 0, rows], contact_ref[1, 0, rows]]
         for weights, ref in zip(chosen, piece_refs):
             weight = total(w * o for w, o in zip(weights, outer))
-            values = [value + weight * ref[j, 0, here] for j, value in enumerate(values)]
+            values = [value + weight * ref[j, 0, start : start + B] for j, value in enumerate(values)]
+        yield start, values
+
+
+def phonon_kernel(fars, modes, row, size, *refs):
+    out_ref = refs[-1]
+    for start, values in scattered(fars, modes, row, size, *refs[:5], refs[5:-1]):
         for j in range(2):
-            out_ref[j, 0, here] = values[j]
-    if final and len(refs) > 2:
-        upper_ref, above_ref = refs[:2]
-        for j in range(2):
-            more = above_ref[0, :, j * B : (j + 1) * B].T * scale
-            refs[-1][j, 0] = upper_ref[j, 0] + more
+            out_ref[j, 0, start : start + B] = values[j]
 
 
 def phonon(shifts, at, contact, columns, lines, pieces, number, chunks):
@@ -319,13 +305,7 @@
     smem = pl.BlockSpec(memory_space=pltpu.SMEM)
     return pl.pallas_call(
         functools.partial(
-            phonon_kernel,
-            [far for far, _ in pieces],
-            shifts.shape[0],
-            number * size,
-            size,
-            False,
-            1.0,
+            phonon_kernel, [far for far, _ in pieces], shifts.shape[0], number * size, size
         ),
         in_specs=[smem, smem] + [vmem] * (3 + len(pieces)),
         out_specs=vmem,
@@ -337,54 +317,56 @@
     )(shifts, at, contact, columns, lines, *[piece for _, piece in pieces])
 
 
-def skip_kernel(count, kernel, *refs):
-    kernel(*refs[:count], *refs[count + 1 :])
-
-
-def phonon_final(shifts, at, contact, columns, lines, pieces, number, chunks, so_far, ends):
-    rows = contact.shape[2]
-    size = rows // chunks
+def ending_kernel(fars, modes, rows, size, scale, *refs):
+    settings, refs = refs[:5], refs[5:]
+    piece_refs, refs = refs[: len(fars)], refs[len(fars) :]
+    row = rows - size
+    done_refs, refs = refs[: row // size], refs[row // size :]
+    _, over_ref, above_ref, sigma_ref, upper_ref, held, tail, sems = refs
+    copies = []
+
+    def send(source, target):
+        copies.append(pltpu.make_async_copy(source, target, sems.at[len(copies)]))
+        copies[-1].start()
+
+    for number, ref in enumerate(done_refs):
+        send(ref, sigma_ref.at[:, :, pl.ds(number * size, size)])
+    for j in range(2):
+        more = above_ref[0, :, j * B : (j + 1) * B].T * scale
+        tail[j, 0] = over_ref[j, 0] + more
+    send(tail, upper_ref.at[:, :, pl.ds(rows - B, B)])
+    for start, values in scattered(fars, modes, row, size, *settings, piece_refs):
+        for j in range(2):
+            held[j, 0, start : start + B] = values[j]
+        send(held.at[:, :, pl.ds(start, B)], sigma_ref.at[:, :, pl.ds(row + start, B)])
+    for copy in copies:
+        copy.wait()
+
+
+def ending(shifts, at, contact, columns, lines, pieces, done, upper, over, above):
+    parts, energies, rows = contact.shape[:3]
+    size = rows // (len(done) + 1)
     vmem = pl.BlockSpec(memory_space=pltpu.VMEM)
     smem = pl.BlockSpec(memory_space=pltpu.SMEM)
-    kernel = functools.partial(
-        phonon_kernel,
-        [far for far, _ in pieces],
-        shifts.shape[0],
-        number * size,
-        size,
-        True,
-        1.0 / math.sqrt(B),
-    )
-    operands = [shifts, at, contact, columns, lines, *[piece for _, piece in pieces]]
-    specs = [smem, smem] + [vmem] * (3 + len(pieces))
-    shapes = [jax.ShapeDtypeStruct(contact.shape, F32)]
-    out_specs = [pl.BlockSpec((2, 1, size, B), lambda i: (0, 0, number, 0))]
-    aliases = {}
-    if so_far is not None:
-        kernel = functools.partial(skip_kernel, len(operands), kernel)
-        aliases[len(operands)] = 0
-        operands.append(so_far)
-        specs.append(pl.BlockSpec(memory_space=pl.ANY))
-    if ends is not None:
-        upper, above = ends
-        tail = pl.BlockSpec((2, 1, B, B), lambda i: (0, 0, rows // B - 1, 0))
-        aliases[len(operands)] = 1
-        operands += [upper, above]
-        specs += [tail, vmem]
-        shapes.append(jax.ShapeDtypeStruct(upper.shape, F32))
-        out_specs.append(tail)
+    hbm = pl.BlockSpec(memory_space=pl.ANY)
+    operands = [shifts, at, contact, columns, lines, *[piece for _, piece in pieces], *done]
+    specs = [smem, smem] + [vmem] * (len(operands) - 2) + [hbm, vmem, vmem]
     return pl.pallas_call(
-        kernel,
-        grid=(1,),
+        functools.partial(ending_kernel, [far for far, _ in pieces], shifts.shape[0], rows, size, 1.0 / math.sqrt(B)),
         in_specs=specs,
-        out_specs=out_specs,
-        out_shape=shapes,
-        input_output_aliases=aliases,
+        out_specs=[hbm, hbm],
+        out_shape=[jax.ShapeDtypeStruct(contact.shape, F32), jax.ShapeDtypeStruct(upper.shape, F32)],
+        input_output_aliases={len(operands): 1},
+        scratch_shapes=[
+            pltpu.VMEM((parts, energies, size, B), F32),
+            pltpu.VMEM((parts, energies, B, B), F32),
+            pltpu.SemaphoreType.DMA((len(done) + 1 + size // B,)),
+        ],
         compiler_params=pltpu.CompilerParams(vmem_limit_bytes=VMEM_BYTES),
         cost_estimate=pl.CostEstimate(
             flops=size * B * 20, bytes_accessed=8 * size * B * 5, transcendentals=0
         ),
-    )(*operands)
+    )(*operands, upper, over, above)
 
 
 def cut_kernel(contact_ref, *refs):
@@ -472,10 +454,7 @@
     at = jnp.where(jnp.arange(2, dtype=jnp.int32) == 0, pan, energy)
     atoms = rows // ORB
     kinds = lax.dynamic_slice_in_dim(atom_kind, pan * atoms, atoms, 0)
-    per_atom = sum(
-        jnp.where(kinds[:, None] == kind, coupling[kind][None, :], 0.0)
-        for kind in range(coupling.shape[0])
-    )
+    per_atom = sum(jnp.where(kinds[:, None] == kind, coupling[kind][None, :], 0.0) for kind in range(coupling.shape[0]))
     per_row = jnp.repeat(per_atom, ORB, axis=0)
     per_line = jnp.repeat(per_atom.T, ORB, axis=1)
     edges, cuts = edge_rows(retarded, pan)
@@ -493,23 +472,19 @@
         if chunks > 1 and high > 1:
             far, _, blocks = groups.pop([far for far, _, _ in groups].index(high))
             groups.insert(1, (far, 0, blocks[:1]))
-            groups.append((far, 1, blocks[1:]))
+            groups.insert(2 if final else len(groups), (far, 1, blocks[1:]))
         sums = {}
         for far, number, blocks in groups:
             work = ("diag", "upper") if final else ("diag",)
             if final and 0 < far < high:
+                if "over" not in sums:
+                    sums = panel(at, retarded, 0, pieces[0][1], sums, edges, ("over", "back"), False)
                 work += ("over", "back")
             sums = panel(at, retarded, far, blocks, sums, edges, work, False)
-            if final and far == 0:
-                held = blocks
-        if final:
-            sums = panel(at, retarded, 0, held, sums, edges, ("over", "back"), False)
         far, blocks = pieces[-1]
         for number, block in enumerate(blocks):
             last = number == len(blocks) - 1
-            new = panel(
-                at, retarded, far, [block], sums, edges, ("diag",), last, chunks, final and last
-            )
+            new = panel(at, retarded, far, [block], sums, edges, ("diag",), last, chunks, final and last)
             sums = dict(sums, **new)
         found = spread(sums["diag"][:chunks], "en")
         settings = (shifts, at, copied, per_row, per_line)
@@ -522,14 +497,10 @@
         if far >= high:
             sums = panel(at, retarded, far, blocks, sums, edges, ("over",), False)
     far, blocks = pieces[-1]
-    upper = panel(at, retarded, far, blocks, sums, edges, ("upper", "over"), True)["upper"]
-    sigma = None
-    for number, own in enumerate(found):
-        ends = (upper, above) if number == 0 else None
-        sigma, *more = phonon_final(*settings, own[1:], number, chunks, sigma, ends)
-        if more:
-            (lesser_upper,) = more
-    return (sums["diag"][chunks], lesser_upper, sigma)
+    ends = panel(at, retarded, far, blocks, sums, edges, ("upper", "over"), True)
+    done = [phonon(*settings, own[1:], number, chunks) for number, own in enumerate(found[:-1])]
+    sigma, upper = ending(*settings, found[-1][1:], done, ends["upper"], ends["over"], above)
+    return (sums["diag"][chunks], upper, sigma)
 
 
 def solution(mesh):

time: 126 us -> 139 us (1.10)
  waiting for transfers between devices: 47.1 us -> 64.5 us
  starting transfers between devices: 28.5 us -> 23.2 us
    ppermute x23, waiting for transfers between devices: 47.1 us -> 64.5 us  [swapped(): lax.ppermute(x, axis, [(i, i ^ bit) for i in range(lax.axis_size(axis))])]
    ppermute x23, starting transfers between devices: 24.7 us -> 21 us  [swapped(): lax.ppermute(x, axis, [(i, i ^ bit) for i in range(lax.axis_size(axis))])]
    pallas_call x2 -> x1, Pallas kernels: 3.41 us -> 1.54 us  [ending(): pl.pallas_call(functools.partial(ending_kernel, [far for far, _ in pieces...]
    ppermute x2, starting transfers between devices: 2.51 us -> 0.91 us  [edge_rows(): found.append(lax.ppermute(part, 'pan', pairs))]
    unnamed x12 -> x10, local copies, waits for them, and re-layouts: 4.48 us -> 4.47 us
  transfers between devices with their start and end apart: 26 -> 26, of which waited for: 10 -> 11; matrix products, arithmetic and copies ran while one was open for 4% -> 4% of each run, Pallas kernels for 27% -> 26%
where the time goes in v6:
time: 139 us
  waiting for transfers between devices  64.5 us (46%)
  Pallas kernels  40.1 us (29%)
  starting transfers between devices  23.2 us (17%)
  local copies, waits for them, and re-layouts  8.66 us (6%)
    ppermute x23, waiting for transfers between devices, swapped(): lax.ppermute(x, axis, [(i, i ^ bit) for i in range(lax.axis_size(axis))])  64.5 us
    pallas_call x15, Pallas kernels, panel(): pl.pallas_call(functools.partial(panel_kernel, local, far, starts, kinds,...  35.4 us
    ppermute x23, starting transfers between devices, swapped(): lax.ppermute(x, axis, [(i, i ^ bit) for i in range(lax.axis_size(axis))])  21 us
    unnamed x10, local copies, waits for them, and re-layouts  4.47 us
    dynamic_slice x1, local copies, waits for them, and re-layouts, edge_rows(): lax.dynamic_slice(retarded, (0, 0, row, column), (2, 1, B, columns // 2))  3.14 us
  transfers between devices with their start and end apart: 26, of which 11 were waited for; matrix products, arithmetic and copies ran while one was open for 4% of the time, Pallas kernels for 26%

profile of v6, /device:TPU:0, one launch (start us, length us, event | category | flops | bytes accessed | tf_op | source)
XLA Modules:
  0.0 138.5 jit_solution(3656620293709760887)
XLA Ops:
  0.6 3.1 %collective-permute-start.4 = (f32[2,1,512,128]{3,2,1,0:T(8,128)}, f32[2,1,512,128]{3,2,1,0:T(8,128)S(1)}, u32[]{:S(2)}, u32[]{:S(2)}) collective-permute-start(f32[2,1,512,128]{3,2,1,0:T(8,128)} %contact_ref.1), channel_id=1, source_target_pairs={{0,4},{4,0},{8,12},{12,8},{1,5},{5,1},{9,13},{13,9},{2,6},{6,2},{1... | collective-permute-start | bytes 1572872 | tf_op jit(solution)/shard_map/ppermute | solution.py:22
  5.7 2.7 %collective-permute-start.2 = (f32[2,1,256,128]{3,2,1,0:T(8,128)}, f32[2,1,256,128]{3,2,1,0:T(8,128)}, u32[]{:S(2)}, u32[]{:S(2)}) collective-permute-start(f32[2,1,256,128]{3,2,1,0:T(8,128)} %get-tuple-element.35), channel_id=1, source_target_pairs={{0,8},{4,12},{8,0},{12,4},{1,9},{5,13},{9,1},{13,5},{2,10},{6,14},... | collective-permute-start | bytes 786440 | tf_op jit(solution)/shard_map/ppermute | solution.py:22
  8.7 3.1 %constant_dynamic-slice_fusion = (f32[2,1,128,1024]{3,2,1,0:T(8,128)}, f32[2,1,128,1024]{3,2,1,0:T(8,128)}) fusion(f32[2,1,512,2048]{3,2,1,0:T(8,128)} %refs_1_.29, s32[]{:T(128)S(6)} %select_n.76, s32[]{:T(128)S(6)} %select_n.78, s32[]{:T(128)S(6)} %select_n.73, s32[]{:T(128)S(6)} %select_n.75), kind=kLoop, calls=%fused_computation.8 | loop fusion | bytes 4194320 | tf_op jit(solution)/shard_map/dynamic_slice | solution.py:418
  14.8 3.4 %copy-done = f32[2,1,512,2048]{3,2,1,0:T(8,128)S(1)} copy-done((f32[2,1,512,2048]{3,2,1,0:T(8,128)S(1)}, f32[2,1,512,2048]{3,2,1,0:T(8,128)}, u32[]{:S(2)}) %copy-start) | copy-done | bytes 8388632
  18.2 2.4 %shard_map.76.refs_3_ = f32[4,128,256]{2,1,0:T(8,128)S(1)} custom-call(s32[2]{0:T(128)S(1)} %compare_select_fusion.refs_0_.refs_1_, f32[2,1,512,2048]{3,2,1,0:T(8,128)S(1)} %copy-done, f32[2,1,512,128]{3,2,1,0:T(8,128)S(1)} %get-tuple-element.31.refs_2_), custom_call_target="tpu_custom_call" | custom-call | flops 1610612736 | bytes 2097152 | tf_op jit(solution)/shard_map/pallas_call | solution.py:262
  22.0 3.6 %collective-permute-start.3 = (f32[2,1,256,128]{3,2,1,0:T(8,128)}, f32[2,1,256,128]{3,2,1,0:T(8,128)S(1)}, u32[]{:S(2)}, u32[]{:S(2)}) collective-permute-start(f32[2,1,256,128]{3,2,1,0:T(8,128)} %collective-permute-done.2.refs_2_), channel_id=1, source_target_pairs={{0,4},{4,0},{8,12},{12,8},{1,5},{5,1},{9,13},{13,9},{2,6},{6,2},{1... | collective-permute-start | bytes 786440 | tf_op jit(solution)/shard_map/ppermute | solution.py:22
  25.6 2.1 %shard_map.77.refs_3_ = f32[4,128,256]{2,1,0:T(8,128)S(1)} custom-call(s32[2]{0:T(128)S(1)} %compare_select_fusion.refs_0_.refs_1_, f32[2,1,512,2048]{3,2,1,0:T(8,128)S(1)} %copy-done, f32[2,1,256,128]{3,2,1,0:T(8,128)} %collective-permute-done.2.refs_2_, f32[4,128,256]{2,1,0:T(8,128)S(1)} %shard_map.76.refs_3_), custom_call_target="tpu_custom_call", output_to_operand_aliasing={{}: (3, {})} | custom-call | flops 805306368 | bytes 1048576 | tf_op jit(solution)/shard_map/pallas_call | solution.py:262
  27.7 5.3 %collective-permute-done.refs_2_ = f32[2,1,256,128]{3,2,1,0:T(8,128)} collective-permute-done((f32[2,1,256,128]{3,2,1,0:T(8,128)}, f32[2,1,256,128]{3,2,1,0:T(8,128)}, u32[]{:S(2)}, u32[]{:S(2)}) %collective-permute-start) | collective-permute-done | bytes 262176 | tf_op jit(solution)/shard_map/ppermute | solution.py:22
  33.0 2.5 %shard_map.78.refs_3_ = f32[4,128,256]{2,1,0:T(8,128)S(1)} custom-call(s32[2]{0:T(128)S(1)} %compare_select_fusion.refs_0_.refs_1_, f32[2,1,512,2048]{3,2,1,0:T(8,128)S(1)} %copy-done, f32[2,1,512,128]{3,2,1,0:T(8,128)S(1)} %collective-permute-done.4.refs_2_, f32[4,128,256]{2,1,0:T(8,128)S(1)} %shard_map.77.refs_3_), custom_call_target="tpu_custom_call", output_to_operand_aliasing={{}: (3, {})} | custom-call | flops 1610612736 | bytes 2097152 | tf_op jit(solution)/shard_map/pallas_call | solution.py:262
  37.7 18.4 %collective-permute-done.3.refs_2_ = f32[2,1,256,128]{3,2,1,0:T(8,128)S(1)} collective-permute-done((f32[2,1,256,128]{3,2,1,0:T(8,128)}, f32[2,1,256,128]{3,2,1,0:T(8,128)S(1)}, u32[]{:S(2)}, u32[]{:S(2)}) %collective-permute-start.3) | collective-permute-done | bytes 262176 | tf_op jit(solution)/shard_map/ppermute | solution.py:22
  57.8 3.1 %collective-permute-done.1.refs_2_ = f32[2,1,256,128]{3,2,1,0:T(8,128)S(1)} collective-permute-done((f32[2,1,256,128]{3,2,1,0:T(8,128)}, f32[2,1,256,128]{3,2,1,0:T(8,128)S(1)}, u32[]{:S(2)}, u32[]{:S(2)}) %collective-permute-start.1) | collective-permute-done | bytes 262176 | tf_op jit(solution)/shard_map/ppermute | solution.py:22
  64.7 7.2 %collective-permute-done.10.refs_5_ = f32[2,1,256,128]{3,2,1,0:T(8,128)S(1)} collective-permute-done((f32[2,1,256,128]{3,2,1,0:T(8,128)S(1)}, f32[2,1,256,128]{3,2,1,0:T(8,128)S(1)}, u32[]{:S(2)}, u32[]{:S(2)}) %collective-permute-start.10) | collective-permute-done | bytes 262176 | tf_op jit(solution)/shard_map/ppermute | solution.py:22
  72.3 3.4 %collective-permute-done.5.refs_5_ = f32[2,1,256,128]{3,2,1,0:T(8,128)S(1)} collective-permute-done((f32[2,1,256,128]{3,2,1,0:T(8,128)S(1)}, f32[2,1,256,128]{3,2,1,0:T(8,128)S(1)}, u32[]{:S(2)}, u32[]{:S(2)}) %collective-permute-start.5) | collective-permute-done | bytes 262176 | tf_op jit(solution)/shard_map/ppermute | solution.py:22
  76.5 2.6 %collective-permute-start.13 = (f32[2,1,256,128]{3,2,1,0:T(8,128)S(1)}, f32[2,1,256,128]{3,2,1,0:T(8,128)S(1)}, u32[]{:S(2)}, u32[]{:S(2)}) collective-permute-start(f32[2,1,256,128]{3,2,1,0:T(8,128)S(1)} %shard_map.83.refs_2_), channel_id=1, source_target_pairs={{0,8},{4,12},{8,0},{12,4},{1,9},{5,13},{9,1},{13,5},{2,10},{6,14},... | collective-permute-start | bytes 786440 | tf_op jit(solution)/shard_map/ppermute | solution.py:22
  81.9 3.2 %shard_map.84 = (f32[4,128,256]{2,1,0:T(8,128)S(1)}, f32[3,128,256]{2,1,0:T(8,128)S(1)}) custom-call(s32[2]{0:T(128)S(1)} %compare_select_fusion.refs_0_.refs_1_, f32[2,1,512,2048]{3,2,1,0:T(8,128)S(1)} %bitcast.11, f32[2,1,256,128]{3,2,1,0:T(8,128)S(1)} %shard_map.83.refs_2_, f32[2,1,256,128]{3,2,1,0:T(8,128)S(1)} %shard_map.82.refs_3_), custom_call_target="tpu_custom_call" | custom-call | flops 2415919104 | bytes 2097152 | tf_op jit(solution)/shard_map/pallas_call | solution.py:262
  87.3 5.0 %collective-permute-done.13.refs_2_ = f32[2,1,256,128]{3,2,1,0:T(8,128)S(1)} collective-permute-done((f32[2,1,256,128]{3,2,1,0:T(8,128)S(1)}, f32[2,1,256,128]{3,2,1,0:T(8,128)S(1)}, u32[]{:S(2)}, u32[]{:S(2)}) %collective-permute-start.13) | collective-permute-done | bytes 262176 | tf_op jit(solution)/shard_map/ppermute | solution.py:22
  92.8 10.4 %collective-permute-done.8.refs_2_.refs_3_ = f32[2,1,256,128]{3,2,1,0:T(8,128)S(1)} collective-permute-done((f32[2,1,256,128]{3,2,1,0:T(8,128)S(1)}, f32[2,1,256,128]{3,2,1,0:T(8,128)S(1)}, u32[]{:S(2)}, u32[]{:S(2)}) %collective-permute-start.8) | collective-permute-done | bytes 262176 | tf_op jit(solution)/shard_map/ppermute | solution.py:22
  103.8 2.2 %shard_map.85 = (f32[4,128,256]{2,1,0:T(8,128)S(1)}, f32[3,128,256]{2,1,0:T(8,128)S(1)}) custom-call(s32[2]{0:T(128)S(1)} %compare_select_fusion.refs_0_.refs_1_, f32[2,1,512,2048]{3,2,1,0:T(8,128)S(1)} %bitcast.11, f32[2,1,256,128]{3,2,1,0:T(8,128)S(1)} %collective-permute-done.13.refs_2_, ...), custom_call_target="tpu_custom_call", output_to_operand_aliasing={{0}: (3, {}), {1}: (4, {})} | custom-call | flops 1207959552 | bytes 1048576 | tf_op jit(solution)/shard_map/pallas_call | solution.py:262
  105.9 2.1 %shard_map.86 = (f32[4,128,256]{2,1,0:T(8,128)S(1)}, f32[3,128,256]{2,1,0:T(8,128)S(1)}) custom-call(s32[2]{0:T(128)S(1)} %compare_select_fusion.refs_0_.refs_1_, f32[2,1,512,2048]{3,2,1,0:T(8,128)S(1)} %bitcast.11, f32[2,1,256,128]{3,2,1,0:T(8,128)S(1)} %collective-permute-done.8.refs_2_.refs_3_, ...), custom_call_target="tpu_custom_call", output_to_operand_aliasing={{0}: (3, {}), {1}: (4, {})} | custom-call | flops 1207959552 | bytes 1048576 | tf_op jit(solution)/shard_map/pallas_call | solution.py:262
  108.1 4.0 %shard_map.88 = (f32[4,128,256]{2,1,0:T(8,128)S(1)}, f32[3,128,256]{2,1,0:T(8,128)S(1)}, f32[1,128,256]{2,1,0:T(8,128)S(1)}, f32[1,128,256]{2,1,0:T(8,128)S(1)}) custom-call(s32[2]{0:T(128)S(1)} %compare_select_fusion.refs_0_.refs_1_, f32[2,1,512,2048]{3,2,1,0:T(8,128)S(1)} %bitcast.11, ...), custom_call_target="tpu_custom_call", output_to_operand_aliasing={{0}: (6, {}), {1}: (7, {}), {2}: (8, {}), {3}: (9, {})} | custom-call | flops 4026531840 | bytes 2097152 | tf_op jit(solution)/shard_map/pallas_call | solution.py:262
  114.6 2.5 %shard_map.90 = (f32[2,1,256,128]{3,2,1,0:T(8,128)S(1)}, f32[2,1,256,128]{3,2,1,0:T(8,128)S(1)}, f32[2,1,512,128]{3,2,1,0:T(8,128)}) custom-call(s32[2]{0:T(128)S(1)} %compare_select_fusion.refs_0_.refs_1_, f32[2,1,512,2048]{3,2,1,0:T(8,128)S(1)} %bitcast.11, f32[2,1,256,128]{3,2,1,0:T(8,128)S(1)} %collective-permute-done.9.refs_2_.refs_3_, ...), custom_call_target="tpu_custom_call" | custom-call | flops 805306368 | bytes 1048576 | tf_op jit(solution)/shard_map/pallas_call | solution.py:262
  121.0 5.3 %collective-permute-done.22.refs_5_ = f32[2,1,256,128]{3,2,1,0:T(8,128)S(1)} collective-permute-done((f32[2,1,256,128]{3,2,1,0:T(8,128)S(1)}, f32[2,1,256,128]{3,2,1,0:T(8,128)S(1)}, u32[]{:S(2)}, u32[]{:S(2)}) %collective-permute-start.22) | collective-permute-done | bytes 262176 | tf_op jit(solution)/shard_map/ppermute | solution.py:22
  126.3 4.3 %collective-permute-done.19.refs_5_ = f32[2,1,256,128]{3,2,1,0:T(8,128)S(1)} collective-permute-done((f32[2,1,256,128]{3,2,1,0:T(8,128)S(1)}, f32[2,1,256,128]{3,2,1,0:T(8,128)S(1)}, u32[]{:S(2)}, u32[]{:S(2)}) %collective-permute-start.19) | collective-permute-done | bytes 262176 | tf_op jit(solution)/shard_map/ppermute | solution.py:22
  132.1 3.9 %shard_map.93 = (f32[2,1,512,128]{3,2,1,0:T(8,128)}, f32[2,1,128,128]{3,2,1,0:T(8,128)S(1)}) custom-call(s32[2]{0:T(128)S(1)} %compare_select_fusion.refs_0_.refs_1_, f32[2,1,512,2048]{3,2,1,0:T(8,128)S(1)} %bitcast.11, f32[2,1,256,128]{3,2,1,0:T(8,128)S(1)} %collective-permute-done.14.refs_2_, ...), custom_call_target="tpu_custom_call" | custom-call | flops 2415919104 | bytes 2097152 | tf_op jit(solution)/shard_map/pallas_call | solution.py:262
  (69 shorter events, 31.6 us)
Async XLA Ops:
  0.6 32.4 %collective-permute-start.4 = (f32[2,1,512,128]{3,2,1,0:T(8,128)}, f32[2,1,512,128]{3,2,1,0:T(8,128)S(1)}, u32[]{:S(2)}, u32[]{:S(2)}) collective-permute-start(f32[2,1,512,128]{3,2,1,0:T(8,128)} %contact_ref.1), channel_id=1, source_target_pairs={{0,4},{4,0},{8,12},{12,8},{1,5},{5,1},{9,13},{13,9},{2,6},{6,2},{1... | collective-permute-start | bytes 1572872 | tf_op jit(solution)/shard_map/ppermute | solution.py:22
  5.7 16.3 %collective-permute-start.2 = (f32[2,1,256,128]{3,2,1,0:T(8,128)}, f32[2,1,256,128]{3,2,1,0:T(8,128)}, u32[]{:S(2)}, u32[]{:S(2)}) collective-permute-start(f32[2,1,256,128]{3,2,1,0:T(8,128)} %get-tuple-element.35), channel_id=1, source_target_pairs={{0,8},{4,12},{8,0},{12,4},{1,9},{5,13},{9,1},{13,5},{2,10},{6,14},... | collective-permute-start | bytes 786440 | tf_op jit(solution)/shard_map/ppermute | solution.py:22
  8.4 24.7 %collective-permute-start = (f32[2,1,256,128]{3,2,1,0:T(8,128)}, f32[2,1,256,128]{3,2,1,0:T(8,128)}, u32[]{:S(2)}, u32[]{:S(2)}) collective-permute-start(f32[2,1,256,128]{3,2,1,0:T(8,128)} %get-tuple-element.34), channel_id=1, source_target_pairs={{0,8},{4,12},{8,0},{12,4},{1,9},{5,13},{9,1},{13,5},{2,10},{6,14},... | collective-permute-start | bytes 786440 | tf_op jit(solution)/shard_map/ppermute | solution.py:22
  11.9 73.2 %collective-permute-start.17 = (f32[2,1,128,1024]{3,2,1,0:T(8,128)}, f32[2,1,128,1024]{3,2,1,0:T(8,128)S(1)}, u32[]{:S(2)}, u32[]{:S(2)}) collective-permute-start(f32[2,1,128,1024]{3,2,1,0:T(8,128)} %get-tuple-element.60), channel_id=1, source_target_pairs={{0,4},{4,0},{8,12},{12,8},{1,5},{5,1},{9,13},{13,9},{2,6},{6,2},{1... | collective-permute-start | bytes 3145736 | tf_op jit(solution)/shard_map/ppermute | solution.py:423
  12.1 73.6 %collective-permute-start.18 = (f32[2,1,128,1024]{3,2,1,0:T(8,128)}, f32[2,1,128,1024]{3,2,1,0:T(8,128)S(1)}, u32[]{:S(2)}, u32[]{:S(2)}) collective-permute-start(f32[2,1,128,1024]{3,2,1,0:T(8,128)} %get-tuple-element.59), channel_id=1, source_target_pairs={{4,8},{8,4},{5,9},{9,5},{6,10},{10,6},{7,11},{11,7},{20,24},{24,20... | collective-permute-start | bytes 3145736 | tf_op jit(solution)/shard_map/ppermute | solution.py:423
  22.0 34.0 %collective-permute-start.3 = (f32[2,1,256,128]{3,2,1,0:T(8,128)}, f32[2,1,256,128]{3,2,1,0:T(8,128)S(1)}, u32[]{:S(2)}, u32[]{:S(2)}) collective-permute-start(f32[2,1,256,128]{3,2,1,0:T(8,128)} %collective-permute-done.2.refs_2_), channel_id=1, source_target_pairs={{0,4},{4,0},{8,12},{12,8},{1,5},{5,1},{9,13},{13,9},{2,6},{6,2},{1... | collective-permute-start | bytes 786440 | tf_op jit(solution)/shard_map/ppermute | solution.py:22
  33.0 27.8 %collective-permute-start.1 = (f32[2,1,256,128]{3,2,1,0:T(8,128)}, f32[2,1,256,128]{3,2,1,0:T(8,128)S(1)}, u32[]{:S(2)}, u32[]{:S(2)}) collective-permute-start(f32[2,1,256,128]{3,2,1,0:T(8,128)} %collective-permute-done.refs_2_), channel_id=1, source_target_pairs={{0,4},{4,0},{8,12},{12,8},{1,5},{5,1},{9,13},{13,9},{2,6},{6,2},{1... | collective-permute-start | bytes 786440 | tf_op jit(solution)/shard_map/ppermute | solution.py:22
  62.6 9.2 %collective-permute-start.10 = (f32[2,1,256,128]{3,2,1,0:T(8,128)S(1)}, f32[2,1,256,128]{3,2,1,0:T(8,128)S(1)}, u32[]{:S(2)}, u32[]{:S(2)}) collective-permute-start(f32[2,1,256,128]{3,2,1,0:T(8,128)S(1)} %get-tuple-element.37), channel_id=1, source_target_pairs={{0,2},{1,3},{2,0},{3,1},{4,6},{5,7},{6,4},{7,5},{8,10},{9,11},{10,... | collective-permute-start | bytes 786440 | tf_op jit(solution)/shard_map/ppermute | solution.py:22
  64.3 7.5 %collective-permute-start.11 = (f32[2,1,256,128]{3,2,1,0:T(8,128)S(1)}, f32[2,1,256,128]{3,2,1,0:T(8,128)S(1)}, u32[]{:S(2)}, u32[]{:S(2)}) collective-permute-start(f32[2,1,256,128]{3,2,1,0:T(8,128)S(1)} %get-tuple-element.37), channel_id=1, source_target_pairs={{0,1},{1,0},{2,3},{3,2},{4,5},{5,4},{6,7},{7,6},{8,9},{9,8},{10,11... | collective-permute-start | bytes 786440 | tf_op jit(solution)/shard_map/ppermute | solution.py:22
  64.3 11.4 %collective-permute-start.5 = (f32[2,1,256,128]{3,2,1,0:T(8,128)S(1)}, f32[2,1,256,128]{3,2,1,0:T(8,128)S(1)}, u32[]{:S(2)}, u32[]{:S(2)}) collective-permute-start(f32[2,1,256,128]{3,2,1,0:T(8,128)S(1)} %get-tuple-element.36), channel_id=1, source_target_pairs={{0,2},{1,3},{2,0},{3,1},{4,6},{5,7},{6,4},{7,5},{8,10},{9,11},{10,... | collective-permute-start | bytes 786440 | tf_op jit(solution)/shard_map/ppermute | solution.py:22
  71.8 7.3 %collective-permute-start.6 = (f32[2,1,256,128]{3,2,1,0:T(8,128)S(1)}, f32[2,1,256,128]{3,2,1,0:T(8,128)S(1)}, u32[]{:S(2)}, u32[]{:S(2)}) collective-permute-start(f32[2,1,256,128]{3,2,1,0:T(8,128)S(1)} %get-tuple-element.36), channel_id=1, source_target_pairs={{0,1},{1,0},{2,3},{3,2},{4,5},{5,4},{6,7},{7,6},{8,9},{9,8},{10,11... | collective-permute-start | bytes 786440 | tf_op jit(solution)/shard_map/ppermute | solution.py:22
  76.5 15.9 %collective-permute-start.13 = (f32[2,1,256,128]{3,2,1,0:T(8,128)S(1)}, f32[2,1,256,128]{3,2,1,0:T(8,128)S(1)}, u32[]{:S(2)}, u32[]{:S(2)}) collective-permute-start(f32[2,1,256,128]{3,2,1,0:T(8,128)S(1)} %shard_map.83.refs_2_), channel_id=1, source_target_pairs={{0,8},{4,12},{8,0},{12,4},{1,9},{5,13},{9,1},{13,5},{2,10},{6,14},... | collective-permute-start | bytes 786440 | tf_op jit(solution)/shard_map/ppermute | solution.py:22
  79.1 29.0 %collective-permute-start.15 = (f32[2,1,256,128]{3,2,1,0:T(8,128)S(1)}, f32[2,1,256,128]{3,2,1,0:T(8,128)S(1)}, u32[]{:S(2)}, u32[]{:S(2)}) collective-permute-start(f32[2,1,256,128]{3,2,1,0:T(8,128)S(1)} %shard_map.83.refs_2_), channel_id=1, source_target_pairs={{0,4},{4,0},{8,12},{12,8},{1,5},{5,1},{9,13},{13,9},{2,6},{6,2},{1... | collective-permute-start | bytes 786440 | tf_op jit(solution)/shard_map/ppermute | solution.py:22
  81.4 21.8 %collective-permute-start.8 = (f32[2,1,256,128]{3,2,1,0:T(8,128)S(1)}, f32[2,1,256,128]{3,2,1,0:T(8,128)S(1)}, u32[]{:S(2)}, u32[]{:S(2)}) collective-permute-start(f32[2,1,256,128]{3,2,1,0:T(8,128)S(1)} %shard_map.82.refs_3_), channel_id=1, source_target_pairs={{0,8},{4,12},{8,0},{12,4},{1,9},{5,13},{9,1},{13,5},{2,10},{6,14},... | collective-permute-start | bytes 786440 | tf_op jit(solution)/shard_map/ppermute | solution.py:22
  85.1 23.0 %collective-permute-start.16 = (f32[2,1,256,128]{3,2,1,0:T(8,128)S(1)}, f32[2,1,256,128]{3,2,1,0:T(8,128)S(1)}, u32[]{:S(2)}, u32[]{:S(2)}) collective-permute-start(f32[2,1,256,128]{3,2,1,0:T(8,128)S(1)} %shard_map.82.refs_3_), channel_id=1, source_target_pairs={{0,4},{4,0},{8,12},{12,8},{1,5},{5,1},{9,13},{13,9},{2,6},{6,2},{1... | collective-permute-start | bytes 786440 | tf_op jit(solution)/shard_map/ppermute | solution.py:22
  92.4 19.8 %collective-permute-start.14 = (f32[2,1,256,128]{3,2,1,0:T(8,128)S(1)}, f32[2,1,256,128]{3,2,1,0:T(8,128)S(1)}, u32[]{:S(2)}, u32[]{:S(2)}) collective-permute-start(f32[2,1,256,128]{3,2,1,0:T(8,128)S(1)} %collective-permute-done.13.refs_2_), channel_id=1, source_target_pairs={{0,4},{4,0},{8,12},{12,8},{1,5},{5,1},{9,13},{13,9},{2,6},{6,2},{1... | collective-permute-start | bytes 786440 | tf_op jit(solution)/shard_map/ppermute | solution.py:22
  103.2 11.4 %collective-permute-start.9 = (f32[2,1,256,128]{3,2,1,0:T(8,128)S(1)}, f32[2,1,256,128]{3,2,1,0:T(8,128)S(1)}, u32[]{:S(2)}, u32[]{:S(2)}) collective-permute-start(f32[2,1,256,128]{3,2,1,0:T(8,128)S(1)} %collective-permute-done.8.refs_2_.refs_3_), channel_id=1, source_target_pairs={{0,4},{4,0},{8,12},{12,8},{1,5},{5,1},{9,13},{13,9},{2,6},{6,2},{1... | collective-permute-start | bytes 786440 | tf_op jit(solution)/shard_map/ppermute | solution.py:22
  117.1 9.2 %collective-permute-start.22 = (f32[2,1,256,128]{3,2,1,0:T(8,128)S(1)}, f32[2,1,256,128]{3,2,1,0:T(8,128)S(1)}, u32[]{:S(2)}, u32[]{:S(2)}) collective-permute-start(f32[2,1,256,128]{3,2,1,0:T(8,128)S(1)} %get-tuple-element.49), channel_id=1, source_target_pairs={{0,2},{1,3},{2,0},{3,1},{4,6},{5,7},{6,4},{7,5},{8,10},{9,11},{10,... | collective-permute-start | bytes 786440 | tf_op jit(solution)/shard_map/ppermute | solution.py:22
  118.5 12.1 %collective-permute-start.19 = (f32[2,1,256,128]{3,2,1,0:T(8,128)S(1)}, f32[2,1,256,128]{3,2,1,0:T(8,128)S(1)}, u32[]{:S(2)}, u32[]{:S(2)}) collective-permute-start(f32[2,1,256,128]{3,2,1,0:T(8,128)S(1)} %get-tuple-element.48), channel_id=1, source_target_pairs={{0,2},{1,3},{2,0},{3,1},{4,6},{5,7},{6,4},{7,5},{8,10},{9,11},{10,... | collective-permute-start | bytes 786440 | tf_op jit(solution)/shard_map/ppermute | solution.py:22
  119.2 17.6 %collective-permute-start.25 = (f32[1,128,256]{2,1,0:T(8,128)S(1)}, f32[1,128,256]{2,1,0:T(8,128)S(1)}, u32[]{:S(2)}, u32[]{:S(2)}) collective-permute-start(f32[1,128,256]{2,1,0:T(8,128)S(1)} %get-tuple-element.54), channel_id=1, source_target_pairs={{4,0},{8,4},{12,8},{5,1},{9,5},{13,9},{6,2},{10,6},{14,10},{7,3},{... | collective-permute-start | bytes 393224 | tf_op jit(solution)/shard_map/ppermute | solution.py:495
  120.4 15.6 %collective-permute-start.23 = (f32[2,1,256,128]{3,2,1,0:T(8,128)S(1)}, f32[2,1,256,128]{3,2,1,0:T(8,128)S(1)}, u32[]{:S(2)}, u32[]{:S(2)}) collective-permute-start(f32[2,1,256,128]{3,2,1,0:T(8,128)S(1)} %get-tuple-element.49), channel_id=1, source_target_pairs={{0,1},{1,0},{2,3},{3,2},{4,5},{5,4},{6,7},{7,6},{8,9},{9,8},{10,11... | collective-permute-start | bytes 786440 | tf_op jit(solution)/shard_map/ppermute | solution.py:22
  120.5 16.3 %collective-permute-start.20 = (f32[2,1,256,128]{3,2,1,0:T(8,128)S(1)}, f32[2,1,256,128]{3,2,1,0:T(8,128)S(1)}, u32[]{:S(2)}, u32[]{:S(2)}) collective-permute-start(f32[2,1,256,128]{3,2,1,0:T(8,128)S(1)} %get-tuple-element.48), channel_id=1, source_target_pairs={{0,1},{1,0},{2,3},{3,2},{4,5},{5,4},{6,7},{7,6},{8,9},{9,8},{10,11... | collective-permute-start | bytes 786440 | tf_op jit(solution)/shard_map/ppermute | solution.py:22
  126.3 9.7 %collective-permute-start.24 = (f32[2,1,256,128]{3,2,1,0:T(8,128)S(1)}, f32[2,1,256,128]{3,2,1,0:T(8,128)S(1)}, u32[]{:S(2)}, u32[]{:S(2)}) collective-permute-start(f32[2,1,256,128]{3,2,1,0:T(8,128)S(1)} %collective-permute-done.22.refs_5_), channel_id=1, source_target_pairs={{0,1},{1,0},{2,3},{3,2},{4,5},{5,4},{6,7},{7,6},{8,9},{9,8},{10,11... | collective-permute-start | bytes 786440 | tf_op jit(solution)/shard_map/ppermute | solution.py:22
  130.6 6.2 %collective-permute-start.21 = (f32[2,1,256,128]{3,2,1,0:T(8,128)S(1)}, f32[2,1,256,128]{3,2,1,0:T(8,128)S(1)}, u32[]{:S(2)}, u32[]{:S(2)}) collective-permute-start(f32[2,1,256,128]{3,2,1,0:T(8,128)S(1)} %collective-permute-done.19.refs_5_), channel_id=1, source_target_pairs={{0,1},{1,0},{2,3},{3,2},{4,5},{5,4},{6,7},{7,6},{8,9},{9,8},{10,11... | collective-permute-start | bytes 786440 | tf_op jit(solution)/shard_map/ppermute | solution.py:22
  (7 other events, 101.3 us)

commit v7 on v6

--- a/solution.py
+++ b/solution.py
@@ -151,8 +151,6 @@
         if diag:
             value = old("diag", i) + terms[:B]
             if last:
-                for ref in outs[chunks:]:
-                    put(ref, i, value)
                 put(outs[i * chunks // local], i % (local // chunks), value)
             else:
                 outs["diag"][i] = value
@@ -225,7 +223,7 @@
                 outs["back"][0] += back_terms()
 
 
-def panel(at, green, far, pieces, carry, edges, kinds, last, chunks=1, whole=False):
+def panel(at, green, far, pieces, carry, edges, kinds, last, chunks=1):
     rows = green.shape[2]
     local = rows // B
     devices = lax.axis_size("pan")
@@ -255,8 +253,6 @@
         if "diag" in kinds:
             part = jax.ShapeDtypeStruct((2, 1, rows // chunks, B), F32)
             shapes = {number: part for number in range(chunks)}
-            if whole:
-                shapes["whole"] = tall
     full = "diag" in kinds or "upper" in kinds
     work = 3 * 2 * (2 * B) * (2 * B) * many * (rows if full else B) * (1 + len(kinds))
     out = pl.pallas_call(
@@ -322,15 +318,17 @@
     piece_refs, refs = refs[: len(fars)], refs[len(fars) :]
     row = rows - size
     done_refs, refs = refs[: row // size], refs[row // size :]
-    _, over_ref, above_ref, sigma_ref, upper_ref, held, tail, sems = refs
+    diag_refs, refs = refs[: rows // size], refs[rows // size :]
+    _, over_ref, above_ref, sigma_ref, upper_ref, diag_ref, held, tail, sems = refs
     copies = []
 
     def send(source, target):
         copies.append(pltpu.make_async_copy(source, target, sems.at[len(copies)]))
         copies[-1].start()
 
-    for number, ref in enumerate(done_refs):
-        send(ref, sigma_ref.at[:, :, pl.ds(number * size, size)])
+    for refs, target in ((done_refs, sigma_ref), (diag_refs, diag_ref)):
+        for number, ref in enumerate(refs):
+            send(ref, target.at[:, :, pl.ds(number * size, size)])
     for j in range(2):
         more = above_ref[0, :, j * B : (j + 1) * B].T * scale
         tail[j, 0] = over_ref[j, 0] + more
@@ -343,24 +341,24 @@
         copy.wait()
 
 
-def ending(shifts, at, contact, columns, lines, pieces, done, upper, over, above):
+def ending(shifts, at, contact, columns, lines, pieces, done, diag, upper, over, above):
     parts, energies, rows = contact.shape[:3]
     size = rows // (len(done) + 1)
     vmem = pl.BlockSpec(memory_space=pltpu.VMEM)
     smem = pl.BlockSpec(memory_space=pltpu.SMEM)
     hbm = pl.BlockSpec(memory_space=pl.ANY)
-    operands = [shifts, at, contact, columns, lines, *[piece for _, piece in pieces], *done]
+    operands = [shifts, at, contact, columns, lines, *[piece for _, piece in pieces], *done, *diag]
     specs = [smem, smem] + [vmem] * (len(operands) - 2) + [hbm, vmem, vmem]
     return pl.pallas_call(
         functools.partial(ending_kernel, [far for far, _ in pieces], shifts.shape[0], rows, size, 1.0 / math.sqrt(B)),
         in_specs=specs,
-        out_specs=[hbm, hbm],
-        out_shape=[jax.ShapeDtypeStruct(contact.shape, F32), jax.ShapeDtypeStruct(upper.shape, F32)],
+        out_specs=[hbm] * 3,
+        out_shape=[jax.ShapeDtypeStruct(contact.shape, F32)] * 3,
         input_output_aliases={len(operands): 1},
         scratch_shapes=[
             pltpu.VMEM((parts, energies, size, B), F32),
             pltpu.VMEM((parts, energies, B, B), F32),
-            pltpu.SemaphoreType.DMA((len(done) + 1 + size // B,)),
+            pltpu.SemaphoreType.DMA((len(done) + len(diag) + 1 + size // B,)),
         ],
         compiler_params=pltpu.CompilerParams(vmem_limit_bytes=VMEM_BYTES),
         cost_estimate=pl.CostEstimate(
@@ -484,9 +482,9 @@
         far, blocks = pieces[-1]
         for number, block in enumerate(blocks):
             last = number == len(blocks) - 1
-            new = panel(at, retarded, far, [block], sums, edges, ("diag",), last, chunks, final and last)
+            new = panel(at, retarded, far, [block], sums, edges, ("diag",), last, chunks)
             sums = dict(sums, **new)
-        found = spread(sums["diag"][:chunks], "en")
+        found = spread(sums["diag"], "en")
         settings = (shifts, at, copied, per_row, per_line)
         if not final:
             parts = [phonon(*settings, own[1:], number, chunks) for number, own in enumerate(found)]
@@ -499,8 +497,8 @@
     far, blocks = pieces[-1]
     ends = panel(at, retarded, far, blocks, sums, edges, ("upper", "over"), True)
     done = [phonon(*settings, own[1:], number, chunks) for number, own in enumerate(found[:-1])]
-    sigma, upper = ending(*settings, found[-1][1:], done, ends["upper"], ends["over"], above)
-    return (sums["diag"][chunks], upper, sigma)
+    sigma, upper, diag = ending(*settings, found[-1][1:], done, sums["diag"], ends["upper"], ends["over"], above)
+    return (diag, upper, sigma)
 
 
 def solution(mesh):

time: 139 us -> 138 us (level)
  no operation moved by 1% of the time
where the time goes in v7:
time: 138 us
  waiting for transfers between devices  64.5 us (47%)
  Pallas kernels  39.5 us (29%)
  starting transfers between devices  23.3 us (17%)
  local copies, waits for them, and re-layouts  8.66 us (6%)
    ppermute x23, waiting for transfers between devices, swapped(): lax.ppermute(x, axis, [(i, i ^ bit) for i in range(lax.axis_size(axis))])  64.5 us
    pallas_call x15, Pallas kernels, panel(): pl.pallas_call(functools.partial(panel_kernel, local, far, starts, kinds,...  34.6 us
    ppermute x23, starting transfers between devices, swapped(): lax.ppermute(x, axis, [(i, i ^ bit) for i in range(lax.axis_size(axis))])  21.1 us
    unnamed x10, local copies, waits for them, and re-layouts  4.47 us
    dynamic_slice x1, local copies, waits for them, and re-layouts, edge_rows(): lax.dynamic_slice(retarded, (0, 0, row, column), (2, 1, B, columns // 2))  3.14 us
  transfers between devices with their start and end apart: 26, of which 11 were waited for; matrix products, arithmetic and copies ran while one was open for 4% of the time, Pallas kernels for 26%

profile of v7, /device:TPU:0, one launch (start us, length us, event | category | flops | bytes accessed | tf_op | source)
XLA Modules:
  0.0 138.0 jit_solution(7087092603145176587)
XLA Ops:
  0.6 3.1 %collective-permute-start.4 = (f32[2,1,512,128]{3,2,1,0:T(8,128)}, f32[2,1,512,128]{3,2,1,0:T(8,128)S(1)}, u32[]{:S(2)}, u32[]{:S(2)}) collective-permute-start(f32[2,1,512,128]{3,2,1,0:T(8,128)} %contact_ref.1), channel_id=1, source_target_pairs={{0,4},{4,0},{8,12},{12,8},{1,5},{5,1},{9,13},{13,9},{2,6},{6,2},{1... | collective-permute-start | bytes 1572872 | tf_op jit(solution)/shard_map/ppermute | solution.py:22
  5.7 2.7 %collective-permute-start.2 = (f32[2,1,256,128]{3,2,1,0:T(8,128)}, f32[2,1,256,128]{3,2,1,0:T(8,128)}, u32[]{:S(2)}, u32[]{:S(2)}) collective-permute-start(f32[2,1,256,128]{3,2,1,0:T(8,128)} %get-tuple-element.35), channel_id=1, source_target_pairs={{0,8},{4,12},{8,0},{12,4},{1,9},{5,13},{9,1},{13,5},{2,10},{6,14},... | collective-permute-start | bytes 786440 | tf_op jit(solution)/shard_map/ppermute | solution.py:22
  8.7 3.1 %constant_dynamic-slice_fusion = (f32[2,1,128,1024]{3,2,1,0:T(8,128)}, f32[2,1,128,1024]{3,2,1,0:T(8,128)}) fusion(f32[2,1,512,2048]{3,2,1,0:T(8,128)} %refs_1_.29, s32[]{:T(128)S(6)} %select_n.76, s32[]{:T(128)S(6)} %select_n.78, s32[]{:T(128)S(6)} %select_n.73, s32[]{:T(128)S(6)} %select_n.75), kind=kLoop, calls=%fused_computation.8 | loop fusion | bytes 4194320 | tf_op jit(solution)/shard_map/dynamic_slice | solution.py:416
  14.8 3.4 %copy-done = f32[2,1,512,2048]{3,2,1,0:T(8,128)S(1)} copy-done((f32[2,1,512,2048]{3,2,1,0:T(8,128)S(1)}, f32[2,1,512,2048]{3,2,1,0:T(8,128)}, u32[]{:S(2)}) %copy-start) | copy-done | bytes 8388632
  18.2 2.4 %shard_map.76.refs_3_ = f32[4,128,256]{2,1,0:T(8,128)S(1)} custom-call(s32[2]{0:T(128)S(1)} %compare_select_fusion.refs_0_.refs_1_, f32[2,1,512,2048]{3,2,1,0:T(8,128)S(1)} %copy-done, f32[2,1,512,128]{3,2,1,0:T(8,128)S(1)} %get-tuple-element.31.refs_2_), custom_call_target="tpu_custom_call" | custom-call | flops 1610612736 | bytes 2097152 | tf_op jit(solution)/shard_map/pallas_call | solution.py:258
  22.0 3.6 %collective-permute-start.3 = (f32[2,1,256,128]{3,2,1,0:T(8,128)}, f32[2,1,256,128]{3,2,1,0:T(8,128)S(1)}, u32[]{:S(2)}, u32[]{:S(2)}) collective-permute-start(f32[2,1,256,128]{3,2,1,0:T(8,128)} %collective-permute-done.2.refs_2_), channel_id=1, source_target_pairs={{0,4},{4,0},{8,12},{12,8},{1,5},{5,1},{9,13},{13,9},{2,6},{6,2},{1... | collective-permute-start | bytes 786440 | tf_op jit(solution)/shard_map/ppermute | solution.py:22
  25.6 2.1 %shard_map.77.refs_3_ = f32[4,128,256]{2,1,0:T(8,128)S(1)} custom-call(s32[2]{0:T(128)S(1)} %compare_select_fusion.refs_0_.refs_1_, f32[2,1,512,2048]{3,2,1,0:T(8,128)S(1)} %copy-done, f32[2,1,256,128]{3,2,1,0:T(8,128)} %collective-permute-done.2.refs_2_, f32[4,128,256]{2,1,0:T(8,128)S(1)} %shard_map.76.refs_3_), custom_call_target="tpu_custom_call", output_to_operand_aliasing={{}: (3, {})} | custom-call | flops 805306368 | bytes 1048576 | tf_op jit(solution)/shard_map/pallas_call | solution.py:258
  27.7 5.3 %collective-permute-done.refs_2_ = f32[2,1,256,128]{3,2,1,0:T(8,128)} collective-permute-done((f32[2,1,256,128]{3,2,1,0:T(8,128)}, f32[2,1,256,128]{3,2,1,0:T(8,128)}, u32[]{:S(2)}, u32[]{:S(2)}) %collective-permute-start) | collective-permute-done | bytes 262176 | tf_op jit(solution)/shard_map/ppermute | solution.py:22
  33.0 2.5 %shard_map.78.refs_3_ = f32[4,128,256]{2,1,0:T(8,128)S(1)} custom-call(s32[2]{0:T(128)S(1)} %compare_select_fusion.refs_0_.refs_1_, f32[2,1,512,2048]{3,2,1,0:T(8,128)S(1)} %copy-done, f32[2,1,512,128]{3,2,1,0:T(8,128)S(1)} %collective-permute-done.4.refs_2_, f32[4,128,256]{2,1,0:T(8,128)S(1)} %shard_map.77.refs_3_), custom_call_target="tpu_custom_call", output_to_operand_aliasing={{}: (3, {})} | custom-call | flops 1610612736 | bytes 2097152 | tf_op jit(solution)/shard_map/pallas_call | solution.py:258
  35.5 2.1 %shard_map.79.refs_3_ = f32[4,128,256]{2,1,0:T(8,128)S(1)} custom-call(s32[2]{0:T(128)S(1)} %compare_select_fusion.refs_0_.refs_1_, f32[2,1,512,2048]{3,2,1,0:T(8,128)S(1)} %copy-done, f32[2,1,256,128]{3,2,1,0:T(8,128)} %collective-permute-done.refs_2_, f32[4,128,256]{2,1,0:T(8,128)S(1)} %shard_map.78.refs_3_), custom_call_target="tpu_custom_call", output_to_operand_aliasing={{}: (3, {})} | custom-call | flops 805306368 | bytes 1048576 | tf_op jit(solution)/shard_map/pallas_call | solution.py:258
  37.7 18.4 %collective-permute-done.3.refs_2_ = f32[2,1,256,128]{3,2,1,0:T(8,128)S(1)} collective-permute-done((f32[2,1,256,128]{3,2,1,0:T(8,128)}, f32[2,1,256,128]{3,2,1,0:T(8,128)S(1)}, u32[]{:S(2)}, u32[]{:S(2)}) %collective-permute-start.3) | collective-permute-done | bytes 262176 | tf_op jit(solution)/shard_map/ppermute | solution.py:22
  57.8 3.1 %collective-permute-done.1.refs_2_ = f32[2,1,256,128]{3,2,1,0:T(8,128)S(1)} collective-permute-done((f32[2,1,256,128]{3,2,1,0:T(8,128)}, f32[2,1,256,128]{3,2,1,0:T(8,128)S(1)}, u32[]{:S(2)}, u32[]{:S(2)}) %collective-permute-start.1) | collective-permute-done | bytes 262176 | tf_op jit(solution)/shard_map/ppermute | solution.py:22
  64.7 7.2 %collective-permute-done.10.refs_5_ = f32[2,1,256,128]{3,2,1,0:T(8,128)S(1)} collective-permute-done((f32[2,1,256,128]{3,2,1,0:T(8,128)S(1)}, f32[2,1,256,128]{3,2,1,0:T(8,128)S(1)}, u32[]{:S(2)}, u32[]{:S(2)}) %collective-permute-start.10) | collective-permute-done | bytes 262176 | tf_op jit(solution)/shard_map/ppermute | solution.py:22
  72.3 3.4 %collective-permute-done.5.refs_5_ = f32[2,1,256,128]{3,2,1,0:T(8,128)S(1)} collective-permute-done((f32[2,1,256,128]{3,2,1,0:T(8,128)S(1)}, f32[2,1,256,128]{3,2,1,0:T(8,128)S(1)}, u32[]{:S(2)}, u32[]{:S(2)}) %collective-permute-start.5) | collective-permute-done | bytes 262176 | tf_op jit(solution)/shard_map/ppermute | solution.py:22
  76.5 2.6 %collective-permute-start.13 = (f32[2,1,256,128]{3,2,1,0:T(8,128)S(1)}, f32[2,1,256,128]{3,2,1,0:T(8,128)S(1)}, u32[]{:S(2)}, u32[]{:S(2)}) collective-permute-start(f32[2,1,256,128]{3,2,1,0:T(8,128)S(1)} %shard_map.83.refs_2_), channel_id=1, source_target_pairs={{0,8},{4,12},{8,0},{12,4},{1,9},{5,13},{9,1},{13,5},{2,10},{6,14},... | collective-permute-start | bytes 786440 | tf_op jit(solution)/shard_map/ppermute | solution.py:22
  81.9 3.2 %shard_map.84 = (f32[4,128,256]{2,1,0:T(8,128)S(1)}, f32[3,128,256]{2,1,0:T(8,128)S(1)}) custom-call(s32[2]{0:T(128)S(1)} %compare_select_fusion.refs_0_.refs_1_, f32[2,1,512,2048]{3,2,1,0:T(8,128)S(1)} %bitcast.11, f32[2,1,256,128]{3,2,1,0:T(8,128)S(1)} %shard_map.83.refs_2_, f32[2,1,256,128]{3,2,1,0:T(8,128)S(1)} %shard_map.82.refs_3_), custom_call_target="tpu_custom_call" | custom-call | flops 2415919104 | bytes 2097152 | tf_op jit(solution)/shard_map/pallas_call | solution.py:258
  87.3 5.0 %collective-permute-done.13.refs_2_ = f32[2,1,256,128]{3,2,1,0:T(8,128)S(1)} collective-permute-done((f32[2,1,256,128]{3,2,1,0:T(8,128)S(1)}, f32[2,1,256,128]{3,2,1,0:T(8,128)S(1)}, u32[]{:S(2)}, u32[]{:S(2)}) %collective-permute-start.13) | collective-permute-done | bytes 262176 | tf_op jit(solution)/shard_map/ppermute | solution.py:22
  92.8 10.4 %collective-permute-done.8.refs_2_.refs_3_ = f32[2,1,256,128]{3,2,1,0:T(8,128)S(1)} collective-permute-done((f32[2,1,256,128]{3,2,1,0:T(8,128)S(1)}, f32[2,1,256,128]{3,2,1,0:T(8,128)S(1)}, u32[]{:S(2)}, u32[]{:S(2)}) %collective-permute-start.8) | collective-permute-done | bytes 262176 | tf_op jit(solution)/shard_map/ppermute | solution.py:22
  103.8 2.2 %shard_map.85 = (f32[4,128,256]{2,1,0:T(8,128)S(1)}, f32[3,128,256]{2,1,0:T(8,128)S(1)}) custom-call(s32[2]{0:T(128)S(1)} %compare_select_fusion.refs_0_.refs_1_, f32[2,1,512,2048]{3,2,1,0:T(8,128)S(1)} %bitcast.11, f32[2,1,256,128]{3,2,1,0:T(8,128)S(1)} %collective-permute-done.13.refs_2_, ...), custom_call_target="tpu_custom_call", output_to_operand_aliasing={{0}: (3, {}), {1}: (4, {})} | custom-call | flops 1207959552 | bytes 1048576 | tf_op jit(solution)/shard_map/pallas_call | solution.py:258
  105.9 2.1 %shard_map.86 = (f32[4,128,256]{2,1,0:T(8,128)S(1)}, f32[3,128,256]{2,1,0:T(8,128)S(1)}) custom-call(s32[2]{0:T(128)S(1)} %compare_select_fusion.refs_0_.refs_1_, f32[2,1,512,2048]{3,2,1,0:T(8,128)S(1)} %bitcast.11, f32[2,1,256,128]{3,2,1,0:T(8,128)S(1)} %collective-permute-done.8.refs_2_.refs_3_, ...), custom_call_target="tpu_custom_call", output_to_operand_aliasing={{0}: (3, {}), {1}: (4, {})} | custom-call | flops 1207959552 | bytes 1048576 | tf_op jit(solution)/shard_map/pallas_call | solution.py:258
  108.1 4.0 %shard_map.88 = (f32[4,128,256]{2,1,0:T(8,128)S(1)}, f32[3,128,256]{2,1,0:T(8,128)S(1)}, f32[1,128,256]{2,1,0:T(8,128)S(1)}, f32[1,128,256]{2,1,0:T(8,128)S(1)}) custom-call(s32[2]{0:T(128)S(1)} %compare_select_fusion.refs_0_.refs_1_, f32[2,1,512,2048]{3,2,1,0:T(8,128)S(1)} %bitcast.11, ...), custom_call_target="tpu_custom_call", output_to_operand_aliasing={{0}: (6, {}), {1}: (7, {}), {2}: (8, {}), {3}: (9, {})} | custom-call | flops 4026531840 | bytes 2097152 | tf_op jit(solution)/shard_map/pallas_call | solution.py:258
  120.3 5.3 %collective-permute-done.22.refs_5_ = f32[2,1,256,128]{3,2,1,0:T(8,128)S(1)} collective-permute-done((f32[2,1,256,128]{3,2,1,0:T(8,128)S(1)}, f32[2,1,256,128]{3,2,1,0:T(8,128)S(1)}, u32[]{:S(2)}, u32[]{:S(2)}) %collective-permute-start.22) | collective-permute-done | bytes 262176 | tf_op jit(solution)/shard_map/ppermute | solution.py:22
  125.6 4.3 %collective-permute-done.19.refs_5_ = f32[2,1,256,128]{3,2,1,0:T(8,128)S(1)} collective-permute-done((f32[2,1,256,128]{3,2,1,0:T(8,128)S(1)}, f32[2,1,256,128]{3,2,1,0:T(8,128)S(1)}, u32[]{:S(2)}, u32[]{:S(2)}) %collective-permute-start.19) | collective-permute-done | bytes 262176 | tf_op jit(solution)/shard_map/ppermute | solution.py:22
  131.3 3.9 %shard_map.93 = (f32[2,1,512,128]{3,2,1,0:T(8,128)}, f32[2,1,128,128]{3,2,1,0:T(8,128)S(1)}) custom-call(s32[2]{0:T(128)S(1)} %compare_select_fusion.refs_0_.refs_1_, f32[2,1,512,2048]{3,2,1,0:T(8,128)S(1)} %bitcast.11, f32[2,1,256,128]{3,2,1,0:T(8,128)S(1)} %collective-permute-done.14.refs_2_, ...), custom_call_target="tpu_custom_call" | custom-call | flops 2415919104 | bytes 2097152 | tf_op jit(solution)/shard_map/pallas_call | solution.py:258
  (69 shorter events, 31.5 us)
Async XLA Ops:
  0.6 32.4 %collective-permute-start.4 = (f32[2,1,512,128]{3,2,1,0:T(8,128)}, f32[2,1,512,128]{3,2,1,0:T(8,128)S(1)}, u32[]{:S(2)}, u32[]{:S(2)}) collective-permute-start(f32[2,1,512,128]{3,2,1,0:T(8,128)} %contact_ref.1), channel_id=1, source_target_pairs={{0,4},{4,0},{8,12},{12,8},{1,5},{5,1},{9,13},{13,9},{2,6},{6,2},{1... | collective-permute-start | bytes 1572872 | tf_op jit(solution)/shard_map/ppermute | solution.py:22
  5.7 16.3 %collective-permute-start.2 = (f32[2,1,256,128]{3,2,1,0:T(8,128)}, f32[2,1,256,128]{3,2,1,0:T(8,128)}, u32[]{:S(2)}, u32[]{:S(2)}) collective-permute-start(f32[2,1,256,128]{3,2,1,0:T(8,128)} %get-tuple-element.35), channel_id=1, source_target_pairs={{0,8},{4,12},{8,0},{12,4},{1,9},{5,13},{9,1},{13,5},{2,10},{6,14},... | collective-permute-start | bytes 786440 | tf_op jit(solution)/shard_map/ppermute | solution.py:22
  8.4 24.7 %collective-permute-start = (f32[2,1,256,128]{3,2,1,0:T(8,128)}, f32[2,1,256,128]{3,2,1,0:T(8,128)}, u32[]{:S(2)}, u32[]{:S(2)}) collective-permute-start(f32[2,1,256,128]{3,2,1,0:T(8,128)} %get-tuple-element.34), channel_id=1, source_target_pairs={{0,8},{4,12},{8,0},{12,4},{1,9},{5,13},{9,1},{13,5},{2,10},{6,14},... | collective-permute-start | bytes 786440 | tf_op jit(solution)/shard_map/ppermute | solution.py:22
  11.9 73.2 %collective-permute-start.17 = (f32[2,1,128,1024]{3,2,1,0:T(8,128)}, f32[2,1,128,1024]{3,2,1,0:T(8,128)S(1)}, u32[]{:S(2)}, u32[]{:S(2)}) collective-permute-start(f32[2,1,128,1024]{3,2,1,0:T(8,128)} %get-tuple-element.60), channel_id=1, source_target_pairs={{0,4},{4,0},{8,12},{12,8},{1,5},{5,1},{9,13},{13,9},{2,6},{6,2},{1... | collective-permute-start | bytes 3145736 | tf_op jit(solution)/shard_map/ppermute | solution.py:421
  12.1 73.6 %collective-permute-start.18 = (f32[2,1,128,1024]{3,2,1,0:T(8,128)}, f32[2,1,128,1024]{3,2,1,0:T(8,128)S(1)}, u32[]{:S(2)}, u32[]{:S(2)}) collective-permute-start(f32[2,1,128,1024]{3,2,1,0:T(8,128)} %get-tuple-element.59), channel_id=1, source_target_pairs={{4,8},{8,4},{5,9},{9,5},{6,10},{10,6},{7,11},{11,7},{20,24},{24,20... | collective-permute-start | bytes 3145736 | tf_op jit(solution)/shard_map/ppermute | solution.py:421
  22.0 34.0 %collective-permute-start.3 = (f32[2,1,256,128]{3,2,1,0:T(8,128)}, f32[2,1,256,128]{3,2,1,0:T(8,128)S(1)}, u32[]{:S(2)}, u32[]{:S(2)}) collective-permute-start(f32[2,1,256,128]{3,2,1,0:T(8,128)} %collective-permute-done.2.refs_2_), channel_id=1, source_target_pairs={{0,4},{4,0},{8,12},{12,8},{1,5},{5,1},{9,13},{13,9},{2,6},{6,2},{1... | collective-permute-start | bytes 786440 | tf_op jit(solution)/shard_map/ppermute | solution.py:22
  33.0 27.8 %collective-permute-start.1 = (f32[2,1,256,128]{3,2,1,0:T(8,128)}, f32[2,1,256,128]{3,2,1,0:T(8,128)S(1)}, u32[]{:S(2)}, u32[]{:S(2)}) collective-permute-start(f32[2,1,256,128]{3,2,1,0:T(8,128)} %collective-permute-done.refs_2_), channel_id=1, source_target_pairs={{0,4},{4,0},{8,12},{12,8},{1,5},{5,1},{9,13},{13,9},{2,6},{6,2},{1... | collective-permute-start | bytes 786440 | tf_op jit(solution)/shard_map/ppermute | solution.py:22
  62.6 9.2 %collective-permute-start.10 = (f32[2,1,256,128]{3,2,1,0:T(8,128)S(1)}, f32[2,1,256,128]{3,2,1,0:T(8,128)S(1)}, u32[]{:S(2)}, u32[]{:S(2)}) collective-permute-start(f32[2,1,256,128]{3,2,1,0:T(8,128)S(1)} %get-tuple-element.37), channel_id=1, source_target_pairs={{0,2},{1,3},{2,0},{3,1},{4,6},{5,7},{6,4},{7,5},{8,10},{9,11},{10,... | collective-permute-start | bytes 786440 | tf_op jit(solution)/shard_map/ppermute | solution.py:22
  64.3 7.5 %collective-permute-start.11 = (f32[2,1,256,128]{3,2,1,0:T(8,128)S(1)}, f32[2,1,256,128]{3,2,1,0:T(8,128)S(1)}, u32[]{:S(2)}, u32[]{:S(2)}) collective-permute-start(f32[2,1,256,128]{3,2,1,0:T(8,128)S(1)} %get-tuple-element.37), channel_id=1, source_target_pairs={{0,1},{1,0},{2,3},{3,2},{4,5},{5,4},{6,7},{7,6},{8,9},{9,8},{10,11... | collective-permute-start | bytes 786440 | tf_op jit(solution)/shard_map/ppermute | solution.py:22
  64.3 11.4 %collective-permute-start.5 = (f32[2,1,256,128]{3,2,1,0:T(8,128)S(1)}, f32[2,1,256,128]{3,2,1,0:T(8,128)S(1)}, u32[]{:S(2)}, u32[]{:S(2)}) collective-permute-start(f32[2,1,256,128]{3,2,1,0:T(8,128)S(1)} %get-tuple-element.36), channel_id=1, source_target_pairs={{0,2},{1,3},{2,0},{3,1},{4,6},{5,7},{6,4},{7,5},{8,10},{9,11},{10,... | collective-permute-start | bytes 786440 | tf_op jit(solution)/shard_map/ppermute | solution.py:22
  71.8 7.3 %collective-permute-start.6 = (f32[2,1,256,128]{3,2,1,0:T(8,128)S(1)}, f32[2,1,256,128]{3,2,1,0:T(8,128)S(1)}, u32[]{:S(2)}, u32[]{:S(2)}) collective-permute-start(f32[2,1,256,128]{3,2,1,0:T(8,128)S(1)} %get-tuple-element.36), channel_id=1, source_target_pairs={{0,1},{1,0},{2,3},{3,2},{4,5},{5,4},{6,7},{7,6},{8,9},{9,8},{10,11... | collective-permute-start | bytes 786440 | tf_op jit(solution)/shard_map/ppermute | solution.py:22
  76.5 15.9 %collective-permute-start.13 = (f32[2,1,256,128]{3,2,1,0:T(8,128)S(1)}, f32[2,1,256,128]{3,2,1,0:T(8,128)S(1)}, u32[]{:S(2)}, u32[]{:S(2)}) collective-permute-start(f32[2,1,256,128]{3,2,1,0:T(8,128)S(1)} %shard_map.83.refs_2_), channel_id=1, source_target_pairs={{0,8},{4,12},{8,0},{12,4},{1,9},{5,13},{9,1},{13,5},{2,10},{6,14},... | collective-permute-start | bytes 786440 | tf_op jit(solution)/shard_map/ppermute | solution.py:22
  79.1 29.0 %collective-permute-start.15 = (f32[2,1,256,128]{3,2,1,0:T(8,128)S(1)}, f32[2,1,256,128]{3,2,1,0:T(8,128)S(1)}, u32[]{:S(2)}, u32[]{:S(2)}) collective-permute-start(f32[2,1,256,128]{3,2,1,0:T(8,128)S(1)} %shard_map.83.refs_2_), channel_id=1, source_target_pairs={{0,4},{4,0},{8,12},{12,8},{1,5},{5,1},{9,13},{13,9},{2,6},{6,2},{1... | collective-permute-start | bytes 786440 | tf_op jit(solution)/shard_map/ppermute | solution.py:22
  81.4 21.8 %collective-permute-start.8 = (f32[2,1,256,128]{3,2,1,0:T(8,128)S(1)}, f32[2,1,256,128]{3,2,1,0:T(8,128)S(1)}, u32[]{:S(2)}, u32[]{:S(2)}) collective-permute-start(f32[2,1,256,128]{3,2,1,0:T(8,128)S(1)} %shard_map.82.refs_3_), channel_id=1, source_target_pairs={{0,8},{4,12},{8,0},{12,4},{1,9},{5,13},{9,1},{13,5},{2,10},{6,14},... | collective-permute-start | bytes 786440 | tf_op jit(solution)/shard_map/ppermute | solution.py:22
  85.1 23.0 %collective-permute-start.16 = (f32[2,1,256,128]{3,2,1,0:T(8,128)S(1)}, f32[2,1,256,128]{3,2,1,0:T(8,128)S(1)}, u32[]{:S(2)}, u32[]{:S(2)}) collective-permute-start(f32[2,1,256,128]{3,2,1,0:T(8,128)S(1)} %shard_map.82.refs_3_), channel_id=1, source_target_pairs={{0,4},{4,0},{8,12},{12,8},{1,5},{5,1},{9,13},{13,9},{2,6},{6,2},{1... | collective-permute-start | bytes 786440 | tf_op jit(solution)/shard_map/ppermute | solution.py:22
  92.4 19.8 %collective-permute-start.14 = (f32[2,1,256,128]{3,2,1,0:T(8,128)S(1)}, f32[2,1,256,128]{3,2,1,0:T(8,128)S(1)}, u32[]{:S(2)}, u32[]{:S(2)}) collective-permute-start(f32[2,1,256,128]{3,2,1,0:T(8,128)S(1)} %collective-permute-done.13.refs_2_), channel_id=1, source_target_pairs={{0,4},{4,0},{8,12},{12,8},{1,5},{5,1},{9,13},{13,9},{2,6},{6,2},{1... | collective-permute-start | bytes 786440 | tf_op jit(solution)/shard_map/ppermute | solution.py:22
  103.2 11.4 %collective-permute-start.9 = (f32[2,1,256,128]{3,2,1,0:T(8,128)S(1)}, f32[2,1,256,128]{3,2,1,0:T(8,128)S(1)}, u32[]{:S(2)}, u32[]{:S(2)}) collective-permute-start(f32[2,1,256,128]{3,2,1,0:T(8,128)S(1)} %collective-permute-done.8.refs_2_.refs_3_), channel_id=1, source_target_pairs={{0,4},{4,0},{8,12},{12,8},{1,5},{5,1},{9,13},{13,9},{2,6},{6,2},{1... | collective-permute-start | bytes 786440 | tf_op jit(solution)/shard_map/ppermute | solution.py:22
  116.3 9.2 %collective-permute-start.22 = (f32[2,1,256,128]{3,2,1,0:T(8,128)S(1)}, f32[2,1,256,128]{3,2,1,0:T(8,128)S(1)}, u32[]{:S(2)}, u32[]{:S(2)}) collective-permute-start(f32[2,1,256,128]{3,2,1,0:T(8,128)S(1)} %get-tuple-element.48.refs_9_), channel_id=1, source_target_pairs={{0,2},{1,3},{2,0},{3,1},{4,6},{5,7},{6,4},{7,5},{8,10},{9,11},{10,... | collective-permute-start | bytes 786440 | tf_op jit(solution)/shard_map/ppermute | solution.py:22
  117.8 12.1 %collective-permute-start.19 = (f32[2,1,256,128]{3,2,1,0:T(8,128)S(1)}, f32[2,1,256,128]{3,2,1,0:T(8,128)S(1)}, u32[]{:S(2)}, u32[]{:S(2)}) collective-permute-start(f32[2,1,256,128]{3,2,1,0:T(8,128)S(1)} %get-tuple-element.47.refs_10_), channel_id=1, source_target_pairs={{0,2},{1,3},{2,0},{3,1},{4,6},{5,7},{6,4},{7,5},{8,10},{9,11},{10,... | collective-permute-start | bytes 786440 | tf_op jit(solution)/shard_map/ppermute | solution.py:22
  118.4 17.6 %collective-permute-start.25 = (f32[1,128,256]{2,1,0:T(8,128)S(1)}, f32[1,128,256]{2,1,0:T(8,128)S(1)}, u32[]{:S(2)}, u32[]{:S(2)}) collective-permute-start(f32[1,128,256]{2,1,0:T(8,128)S(1)} %get-tuple-element.53), channel_id=1, source_target_pairs={{4,0},{8,4},{12,8},{5,1},{9,5},{13,9},{6,2},{10,6},{14,10},{7,3},{... | collective-permute-start | bytes 393224 | tf_op jit(solution)/shard_map/ppermute | solution.py:493
  119.7 15.5 %collective-permute-start.23 = (f32[2,1,256,128]{3,2,1,0:T(8,128)S(1)}, f32[2,1,256,128]{3,2,1,0:T(8,128)S(1)}, u32[]{:S(2)}, u32[]{:S(2)}) collective-permute-start(f32[2,1,256,128]{3,2,1,0:T(8,128)S(1)} %get-tuple-element.48.refs_9_), channel_id=1, source_target_pairs={{0,1},{1,0},{2,3},{3,2},{4,5},{5,4},{6,7},{7,6},{8,9},{9,8},{10,11... | collective-permute-start | bytes 786440 | tf_op jit(solution)/shard_map/ppermute | solution.py:22
  119.8 16.3 %collective-permute-start.20 = (f32[2,1,256,128]{3,2,1,0:T(8,128)S(1)}, f32[2,1,256,128]{3,2,1,0:T(8,128)S(1)}, u32[]{:S(2)}, u32[]{:S(2)}) collective-permute-start(f32[2,1,256,128]{3,2,1,0:T(8,128)S(1)} %get-tuple-element.47.refs_10_), channel_id=1, source_target_pairs={{0,1},{1,0},{2,3},{3,2},{4,5},{5,4},{6,7},{7,6},{8,9},{9,8},{10,11... | collective-permute-start | bytes 786440 | tf_op jit(solution)/shard_map/ppermute | solution.py:22
  125.6 9.7 %collective-permute-start.24 = (f32[2,1,256,128]{3,2,1,0:T(8,128)S(1)}, f32[2,1,256,128]{3,2,1,0:T(8,128)S(1)}, u32[]{:S(2)}, u32[]{:S(2)}) collective-permute-start(f32[2,1,256,128]{3,2,1,0:T(8,128)S(1)} %collective-permute-done.22.refs_5_), channel_id=1, source_target_pairs={{0,1},{1,0},{2,3},{3,2},{4,5},{5,4},{6,7},{7,6},{8,9},{9,8},{10,11... | collective-permute-start | bytes 786440 | tf_op jit(solution)/shard_map/ppermute | solution.py:22
  129.9 6.2 %collective-permute-start.21 = (f32[2,1,256,128]{3,2,1,0:T(8,128)S(1)}, f32[2,1,256,128]{3,2,1,0:T(8,128)S(1)}, u32[]{:S(2)}, u32[]{:S(2)}) collective-permute-start(f32[2,1,256,128]{3,2,1,0:T(8,128)S(1)} %collective-permute-done.19.refs_5_), channel_id=1, source_target_pairs={{0,1},{1,0},{2,3},{3,2},{4,5},{5,4},{6,7},{7,6},{8,9},{9,8},{10,11... | collective-permute-start | bytes 786440 | tf_op jit(solution)/shard_map/ppermute | solution.py:22
  (7 other events, 101.3 us)

commit v8 on v7

--- a/solution.py
+++ b/solution.py
@@ -85,19 +85,48 @@
     return jnp.concatenate([re[:, :B] + im[:, B:], re[:, B:] - im[:, :B]], axis=1)
 
 
-def panel_kernel(local, far, starts, kinds, first, last, chunks, devices, scale, *refs):
+def edge_plan(kinds, far, blocks, local, devices):
+    part = local // 2
+    plan = {}
+    for kind in kinds:
+        for odd in range(2):
+            found = []
+            for place, block in enumerate(blocks):
+                if (kind == "over") == (odd == 0):
+                    if kind == "over":
+                        column = {
+                            0: ("even", block) if block < part else None,
+                            devices // 2: ("late", block),
+                            devices - 1: ("even", part + block),
+                        }.get(far)
+                    else:
+                        column = {
+                            0: ("even", part + block),
+                            1: ("even", block - part) if block >= part else None,
+                        }.get(far)
+                    if column:
+                        found.append((place, column[0], column[1] * B))
+                elif far < devices // 2:
+                    found.append((place, "odd", None))
+            plan[kind, odd] = found
+    return plan
+
+
+def in_thirds(local, devices):
+    return devices == 4 and local % 2 == 0
+
+
+def panel_kernel(local, far, starts, kinds, names, first, last, chunks, devices, scale, *refs):
     refs = list(refs)
     at_ref, g_ref = refs[:2]
     piece_refs, refs = refs[2 : 2 + len(starts)], refs[2 + len(starts) :]
     edges = "over" in kinds or "back" in kinds
-    if edges:
-        even_ref, odd_ref = refs[:2]
-        refs = refs[2:]
+    edge_refs, refs = dict(zip(names, refs)), refs[len(names) :]
     ins = {}
     for kind in kinds:
         if kind not in first:
             ins[kind] = refs.pop(0)
-    outs = refs if last else dict(zip(kinds, refs))
+    outs = refs if last and "diag" in kinds else dict(zip(kinds, refs))
     pan = at_ref[0]
     source = pan ^ far
     middle = devices // 2
@@ -157,70 +186,85 @@
         if upper and i < local - 1:
             value = old("upper", i) + terms[-B:]
             if last:
-                put(outs[0], i, value)
+                put(outs["upper"], i, value)
             else:
                 outs["upper"][i] = value
-    if edges:
-        source_high = source >= middle
-        even = pan % 2 == 0
-
-        def edge(near, column):
-            return split(
-                jnp.concatenate(
-                    [
-                        jnp.where(near, even_ref[j, 0, :, column], odd_ref[j, 0, :, column])
-                        for j in range(2)
-                    ],
-                    axis=1,
+    if not edges:
+        return
+    even = pan % 2 == 0
+
+    def rows_at(ref, column):
+        return split(
+            jnp.concatenate([ref[0, 0, :, column], ref[1, 0, :, column]], axis=1)
+        )
+
+    def last_rows(number):
+        if whole:
+            return rows_of(products[number], (local - 1) * B, B)
+        return split(times(greens[number](low, local * B), sigmas[number]))
+
+    def add(kind, when, terms):
+        @pl.when(when)
+        def _():
+            outs[kind][0] += terms()
+
+    for kind in ("over", "back"):
+        if kind in kinds:
+            outs[kind][0] = ins[kind][0] if kind in ins else jnp.zeros((B, 2 * B), F32)
+
+    if in_thirds(local, devices):
+        blocks = [
+            start + u for start, ref in zip(starts, piece_refs) for u in range(ref.shape[2] // B)
+        ]
+        plan = edge_plan([k for k in kinds if k in ("over", "back")], far, blocks, local, devices)
+        for (kind, odd), found in plan.items():
+            if not found:
+                continue
+
+            def terms(kind=kind, found=found):
+                taken = [
+                    (n, rows_at(edge_refs[name], columns[n] if at is None else slice(at, at + B)))
+                    for n, name, at in found
+                ]
+                if kind == "over":
+                    return against([edge for _, edge in taken], [last_rows(n) for n, _ in taken])
+                return against(
+                    [greens[n](0, B) for n, _ in taken],
+                    [split(times(edge, sigmas[n])) for n, edge in taken],
                 )
-            )
-
-        def over_terms():
-            rights = []
-            for number in range(len(columns)):
-                if whole:
-                    rights.append(rows_of(products[number], (local - 1) * B, B))
-                else:
-                    rights.append(split(times(greens[number](low, local * B), sigmas[number])))
-            return against([edge(even, column) for column in columns], rights)
-
-        def back_terms():
-            return against(
+
+            add(kind, even if odd == 0 else jnp.logical_not(even), terms)
+        return
+
+    source_high = source >= middle
+
+    def edge(near, column):
+        return tuple(
+            jnp.where(near, a, b)
+            for a, b in zip(rows_at(edge_refs["even"], column), rows_at(edge_refs["odd"], column))
+        )
+
+    if "over" in kinds:
+        add(
+            "over",
+            source_high != (pan + 1 >= middle),
+            lambda: against(
+                [edge(even, column) for column in columns],
+                [last_rows(number) for number in range(len(columns))],
+            ),
+        )
+    if "back" in kinds:
+        add(
+            "back",
+            source_high == (pan >= middle),
+            lambda: against(
                 [green(0, B) for green in greens],
                 [
                     split(times(edge(jnp.logical_not(even), column), sigma))
                     for sigma, column in zip(sigmas, columns)
                 ],
-            )
-
-        if "over" in kinds:
-            theirs = source_high != (pan + 1 >= middle)
-            if last:
-                end = outs[1]
-
-                @pl.when(theirs)
-                def _():
-                    put(end, 0, old("over", 0) + over_terms())
-
-                @pl.when(jnp.logical_not(theirs))
-                def _():
-                    put(end, 0, jnp.zeros((B, 2 * B), F32) + old("over", 0))
-
-            else:
-                if "over" not in ins:
-                    outs["over"][0] = jnp.zeros((B, 2 * B), F32)
-
-                @pl.when(theirs)
-                def _():
-                    outs["over"][0] += over_terms()
-
-        if "back" in kinds:
-            if "back" not in ins:
-                outs["back"][0] = jnp.zeros((B, 2 * B), F32)
-
-            @pl.when(source_high == (pan >= middle))
-            def _():
-                outs["back"][0] += back_terms()
+            ),
+        )
 
 
 def panel(at, green, far, pieces, carry, edges, kinds, last, chunks=1):
@@ -235,8 +279,14 @@
         starts.append(start)
         many += piece.shape[2] // B
     operands = [at, green] + [piece for _, piece in pieces]
+    names = []
     if "over" in kinds or "back" in kinds:
-        operands += edges
+        names = ["even", "odd"]
+        if in_thirds(local, devices):
+            blocks = [start + u for start, piece in pieces for u in range(piece.shape[2] // B)]
+            plan = edge_plan([k for k in kinds if k in ("over", "back")], far, blocks, local, devices)
+            names = sorted({name for found in plan.values() for _, name, _ in found})
+        operands += [edges[name] for name in names]
     shapes = {kind: jax.ShapeDtypeStruct((counts[kind], B, 2 * B), F32) for kind in kinds}
     aliases = {}
     first = []
@@ -244,19 +294,31 @@
         if kind not in carry:
             first.append(kind)
             continue
-        if not last:
+        if not last or kind == "over":
             aliases[len(operands)] = number
         operands.append(carry[kind])
     if last:
         tall = jax.ShapeDtypeStruct((2, 1, rows, B), F32)
-        shapes = {"upper": tall, "over": jax.ShapeDtypeStruct((2, 1, B, B), F32)}
+        shapes["upper"] = tall
         if "diag" in kinds:
             part = jax.ShapeDtypeStruct((2, 1, rows // chunks, B), F32)
             shapes = {number: part for number in range(chunks)}
     full = "diag" in kinds or "upper" in kinds
     work = 3 * 2 * (2 * B) * (2 * B) * many * (rows if full else B) * (1 + len(kinds))
     out = pl.pallas_call(
-        functools.partial(panel_kernel, local, far, starts, kinds, first, last, chunks, devices, 1.0 / math.sqrt(B)),
+        functools.partial(
+            panel_kernel,
+            local,
+            far,
+            starts,
+            kinds,
+            names,
+            first,
+            last,
+            chunks,
+            devices,
+            1.0 / math.sqrt(B),
+        ),
         in_specs=[pl.BlockSpec(memory_space=pltpu.SMEM)] + [vmem] * (len(operands) - 1),
         out_specs=[vmem] * len(shapes),
         out_shape=list(shapes.values()),
@@ -266,9 +328,9 @@
             flops=work, bytes_accessed=8 * rows * B * many, transcendentals=0
         ),
     )(*operands)
-    if last:
-        return {"diag": out} if "diag" in kinds else {"upper": out[0], "over": out[1]}
-    return dict(carry, **dict(zip(kinds, out)))
+    if last and "diag" in kinds:
+        return {"diag": out}
+    return dict(carry, **dict(zip(shapes, out)))
 
 
 def scattered(fars, modes, row, size, shift_ref, at_ref, contact_ref, col_ref, row_ref, piece_refs):
@@ -330,8 +392,8 @@
         for number, ref in enumerate(refs):
             send(ref, target.at[:, :, pl.ds(number * size, size)])
     for j in range(2):
-        more = above_ref[0, :, j * B : (j + 1) * B].T * scale
-        tail[j, 0] = over_ref[j, 0] + more
+        part = slice(j * B, (j + 1) * B)
+        tail[j, 0] = (over_ref[0, :, part] + above_ref[0, :, part]).T * scale
     send(tail, upper_ref.at[:, :, pl.ds(rows - B, B)])
     for start, values in scattered(fars, modes, row, size, *settings, piece_refs):
         for j in range(2):
@@ -405,20 +467,36 @@
 def edge_rows(retarded, pan):
     rows, columns = retarded.shape[2:]
     devices = lax.axis_size("pan")
+    local = rows // B
     middle = devices // 2
-    up_start = (pan + 1 >= middle).astype(jnp.int32)
-    down_start = (pan < middle).astype(jnp.int32)
-    found, cuts = [], []
-    for odd in (0, 1):
+    thirds = in_thirds(local, devices)
+    even = pan % 2 == 0
+
+    def take(row, column, size):
+        return lax.dynamic_slice(retarded, (0, 0, row, column), (2, 1, B, size))
+
+    found, cuts = {}, []
+    for odd, name in ((0, "even"), (1, "odd")):
         up = pan % 2 == odd
         row = jnp.where(up, rows - B, 0)
-        column = jnp.where(up, up_start, down_start) * (columns // 2)
-        part = lax.dynamic_slice(retarded, (0, 0, row, column), (2, 1, B, columns // 2))
+        if odd or not thirds:
+            up_start = (pan + 1 >= middle).astype(jnp.int32)
+            down_start = (pan < middle).astype(jnp.int32)
+            column = jnp.where(up, up_start, down_start) * (columns // 2)
+            part = take(row, column, columns // 2)
+        else:
+            short = jnp.where(even, pan * rows + rows // 2, (pan - 1) * rows)
+            long = jnp.where(even, pan + 1, pan ^ middle) * rows
+            part = jnp.concatenate([take(row, short, rows // 2), take(row, long, rows)], axis=3)
         pairs = []
         for i in range(odd, devices - 1, 2):
             pairs += [(i, i + 1), (i + 1, i)]
         cuts.append(part)
-        found.append(lax.ppermute(part, "pan", pairs))
+        found[name] = lax.ppermute(part, "pan", pairs)
+    if thirds:
+        part = take(0, (pan ^ (devices - 1)) * rows, rows)
+        cuts.append(part)
+        found["late"] = swapped(part, "pan", 1)
     return found, cuts
 
 
@@ -470,7 +548,7 @@
         if chunks > 1 and high > 1:
             far, _, blocks = groups.pop([far for far, _, _ in groups].index(high))
             groups.insert(1, (far, 0, blocks[:1]))
-            groups.insert(2 if final else len(groups), (far, 1, blocks[1:]))
+            groups.append((far, 1, blocks[1:]))
         sums = {}
         for far, number, blocks in groups:
             work = ("diag", "upper") if final else ("diag",)
@@ -491,13 +569,13 @@
             near = [(i * (local // chunks), part) for i, part in enumerate(parts)]
     devices = lax.axis_size("pan")
     above = lax.ppermute(sums["back"], "pan", [(i + 1, i) for i in range(devices - 1)])
+    far, blocks = pieces[-1]
+    sums = panel(at, retarded, far, blocks, sums, edges, ("upper", "over"), True)
     for far, blocks in pieces[1:-1]:
         if far >= high:
             sums = panel(at, retarded, far, blocks, sums, edges, ("over",), False)
-    far, blocks = pieces[-1]
-    ends = panel(at, retarded, far, blocks, sums, edges, ("upper", "over"), True)
     done = [phonon(*settings, own[1:], number, chunks) for number, own in enumerate(found[:-1])]
-    sigma, upper, diag = ending(*settings, found[-1][1:], done, sums["diag"], ends["upper"], ends["over"], above)
+    sigma, upper, diag = ending(*settings, found[-1][1:], done, sums["diag"], sums["upper"], sums["over"], above)
     return (diag, upper, sigma)
 
 

time: 138 us -> 143 us (1.036)
  starting transfers between devices: 23.3 us -> 32.1 us
  waiting for transfers between devices: 64.5 us -> 56.9 us
  local copies, waits for them, and re-layouts: 8.66 us -> 10.9 us
    ppermute x23 -> x24, starting transfers between devices: 21.1 us -> 29.7 us  [swapped(): lax.ppermute(x, axis, [(i, i ^ bit) for i in range(lax.axis_size(axis))])]
    ppermute x23 -> x24, waiting for transfers between devices: 64.5 us -> 56.9 us  [swapped(): lax.ppermute(x, axis, [(i, i ^ bit) for i in range(lax.axis_size(axis))])]
    dynamic_slice x1 -> x3, local copies, waits for them, and re-layouts: 3.14 us -> 5.43 us  [take(): return lax.dynamic_slice(retarded, (0, 0, row, column), (2, 1, B, size))]
    unnamed x10 -> x12, local copies, waits for them, and re-layouts: 4.47 us -> 4.48 us
  transfers between devices with their start and end apart: 26 -> 27, of which waited for: 11 -> 9; matrix products, arithmetic and copies ran while one was open for 4% -> 6% of each run, Pallas kernels for 26% -> 26%
where the time goes in v8:
time: 143 us; the launch traced here: 142 us
  waiting for transfers between devices  56.9 us (40%)
  Pallas kernels  39.4 us (28%)
  starting transfers between devices  32.1 us (22%)
  local copies, waits for them, and re-layouts  10.9 us (8%)
  other arithmetic  1.89 us (1%)
    ppermute x24, waiting for transfers between devices, swapped(): lax.ppermute(x, axis, [(i, i ^ bit) for i in range(lax.axis_size(axis))])  56.9 us
    pallas_call x15, Pallas kernels, panel(): pl.pallas_call(functools.partial(panel_kernel, local, far, starts, kinds,...  34.6 us
    ppermute x24, starting transfers between devices, swapped(): lax.ppermute(x, axis, [(i, i ^ bit) for i in range(lax.axis_size(axis))])  29.7 us
    dynamic_slice x3, local copies, waits for them, and re-layouts, take(): return lax.dynamic_slice(retarded, (0, 0, row, column), (2, 1, B, size))  5.43 us
    unnamed x12, local copies, waits for them, and re-layouts  4.48 us
  transfers between devices with their start and end apart: 27, of which 9 were waited for; matrix products, arithmetic and copies ran while one was open for 6% of the time, Pallas kernels for 26%

profile of v8, /device:TPU:0, one launch (start us, length us, event | category | flops | bytes accessed | tf_op | source)
XLA Modules:
  0.0 142.5 jit_solution(3249001783827014706)
XLA Ops:
  0.6 3.1 %collective-permute-start.4 = (f32[2,1,512,128]{3,2,1,0:T(8,128)}, f32[2,1,512,128]{3,2,1,0:T(8,128)S(1)}, u32[]{:S(2)}, u32[]{:S(2)}) collective-permute-start(f32[2,1,512,128]{3,2,1,0:T(8,128)} %contact_ref.1), channel_id=1, source_target_pairs={{0,4},{4,0},{8,12},{12,8},{1,5},{5,1},{9,13},{13,9},{2,6},{6,2},{1... | collective-permute-start | bytes 1572872 | tf_op jit(solution)/shard_map/ppermute | solution.py:22
  5.7 2.7 %collective-permute-start.2 = (f32[2,1,256,128]{3,2,1,0:T(8,128)}, f32[2,1,256,128]{3,2,1,0:T(8,128)}, u32[]{:S(2)}, u32[]{:S(2)}) collective-permute-start(f32[2,1,256,128]{3,2,1,0:T(8,128)} %get-tuple-element.35), channel_id=1, source_target_pairs={{0,8},{4,12},{8,0},{12,4},{1,9},{5,13},{9,1},{13,5},{2,10},{6,14},... | collective-permute-start | bytes 786440 | tf_op jit(solution)/shard_map/ppermute | solution.py:22
  12.9 2.3 %constant_dynamic-slice_fusion.1 = f32[2,1,128,1024]{3,2,1,0:T(8,128)} fusion(f32[2,1,512,2048]{3,2,1,0:T(8,128)} %refs_1_.29, s32[]{:T(128)S(6)} %select_n.90, s32[]{:T(128)S(6)} %select_n.92), kind=kLoop, calls=%fused_computation.6 | loop fusion | bytes 2097160 | tf_op jit(solution)/shard_map/dynamic_slice | solution.py:476
  18.0 3.4 %copy-done = f32[2,1,512,2048]{3,2,1,0:T(8,128)S(1)} copy-done((f32[2,1,512,2048]{3,2,1,0:T(8,128)S(1)}, f32[2,1,512,2048]{3,2,1,0:T(8,128)}, u32[]{:S(2)}) %copy-start) | copy-done | bytes 8388632
  21.4 2.4 %shard_map.76.refs_3_ = f32[4,128,256]{2,1,0:T(8,128)S(1)} custom-call(s32[2]{0:T(128)S(1)} %compare_select_fusion.refs_0_.refs_1_, f32[2,1,512,2048]{3,2,1,0:T(8,128)S(1)} %copy-done, f32[2,1,512,128]{3,2,1,0:T(8,128)S(1)} %get-tuple-element.31.refs_2_), custom_call_target="tpu_custom_call" | custom-call | flops 1610612736 | bytes 2097152 | tf_op jit(solution)/shard_map/pallas_call | solution.py:308
  23.9 4.7 %collective-permute-start.3 = (f32[2,1,256,128]{3,2,1,0:T(8,128)}, f32[2,1,256,128]{3,2,1,0:T(8,128)S(1)}, u32[]{:S(2)}, u32[]{:S(2)}) collective-permute-start(f32[2,1,256,128]{3,2,1,0:T(8,128)} %collective-permute-done.2.refs_2_), channel_id=1, source_target_pairs={{0,4},{4,0},{8,12},{12,8},{1,5},{5,1},{9,13},{13,9},{2,6},{6,2},{1... | collective-permute-start | bytes 786440 | tf_op jit(solution)/shard_map/ppermute | solution.py:22
  30.7 2.2 %collective-permute-done.refs_2_ = f32[2,1,256,128]{3,2,1,0:T(8,128)S(1)} collective-permute-done((f32[2,1,256,128]{3,2,1,0:T(8,128)}, f32[2,1,256,128]{3,2,1,0:T(8,128)S(1)}, u32[]{:S(2)}, u32[]{:S(2)}) %collective-permute-start) | collective-permute-done | bytes 262176 | tf_op jit(solution)/shard_map/ppermute | solution.py:22
  32.9 2.5 %shard_map.78.refs_3_ = f32[4,128,256]{2,1,0:T(8,128)S(1)} custom-call(s32[2]{0:T(128)S(1)} %compare_select_fusion.refs_0_.refs_1_, f32[2,1,512,2048]{3,2,1,0:T(8,128)S(1)} %copy-done, f32[2,1,512,128]{3,2,1,0:T(8,128)S(1)} %collective-permute-done.4.refs_2_, f32[4,128,256]{2,1,0:T(8,128)S(1)} %shard_map.77.refs_3_), custom_call_target="tpu_custom_call", output_to_operand_aliasing={{}: (3, {})} | custom-call | flops 1610612736 | bytes 2097152 | tf_op jit(solution)/shard_map/pallas_call | solution.py:308
  37.2 13.3 %collective-permute-done.3.refs_2_ = f32[2,1,256,128]{3,2,1,0:T(8,128)S(1)} collective-permute-done((f32[2,1,256,128]{3,2,1,0:T(8,128)}, f32[2,1,256,128]{3,2,1,0:T(8,128)S(1)}, u32[]{:S(2)}, u32[]{:S(2)}) %collective-permute-start.3) | collective-permute-done | bytes 262176 | tf_op jit(solution)/shard_map/ppermute | solution.py:22
  52.2 3.1 %collective-permute-done.1.refs_2_ = f32[2,1,256,128]{3,2,1,0:T(8,128)S(1)} collective-permute-done((f32[2,1,256,128]{3,2,1,0:T(8,128)S(1)}, f32[2,1,256,128]{3,2,1,0:T(8,128)S(1)}, u32[]{:S(2)}, u32[]{:S(2)}) %collective-permute-start.1) | collective-permute-done | bytes 262176 | tf_op jit(solution)/shard_map/ppermute | solution.py:22
  59.1 7.1 %collective-permute-done.10.refs_5_ = f32[2,1,256,128]{3,2,1,0:T(8,128)S(1)} collective-permute-done((f32[2,1,256,128]{3,2,1,0:T(8,128)S(1)}, f32[2,1,256,128]{3,2,1,0:T(8,128)S(1)}, u32[]{:S(2)}, u32[]{:S(2)}) %collective-permute-start.10) | collective-permute-done | bytes 262176 | tf_op jit(solution)/shard_map/ppermute | solution.py:22
  66.7 3.4 %collective-permute-done.5.refs_5_ = f32[2,1,256,128]{3,2,1,0:T(8,128)S(1)} collective-permute-done((f32[2,1,256,128]{3,2,1,0:T(8,128)S(1)}, f32[2,1,256,128]{3,2,1,0:T(8,128)S(1)}, u32[]{:S(2)}, u32[]{:S(2)}) %collective-permute-start.5) | collective-permute-done | bytes 262176 | tf_op jit(solution)/shard_map/ppermute | solution.py:22
  72.5 2.6 %collective-permute-start.13 = (f32[2,1,256,128]{3,2,1,0:T(8,128)S(1)}, f32[2,1,256,128]{3,2,1,0:T(8,128)S(1)}, u32[]{:S(2)}, u32[]{:S(2)}) collective-permute-start(f32[2,1,256,128]{3,2,1,0:T(8,128)S(1)} %shard_map.83.refs_2_), channel_id=1, source_target_pairs={{0,8},{4,12},{8,0},{12,4},{1,9},{5,13},{9,1},{13,5},{2,10},{6,14},... | collective-permute-start | bytes 786440 | tf_op jit(solution)/shard_map/ppermute | solution.py:22
  78.4 2.2 %shard_map.86 = (f32[1,128,256]{2,1,0:T(8,128)S(1)}, f32[1,128,256]{2,1,0:T(8,128)S(1)}) custom-call(s32[2]{0:T(128)S(1)} %compare_select_fusion.refs_0_.refs_1_, f32[2,1,512,2048]{3,2,1,0:T(8,128)S(1)} %bitcast.11, f32[2,1,256,128]{3,2,1,0:T(8,128)S(1)} %shard_map.83.refs_2_, f32[2,1,256,128]{3,2,1,0:T(8,128)S(1)} %shard_map.82.refs_3_, ...), custom_call_target="tpu_custom_call" | custom-call | flops 603979776 | bytes 2097152 | tf_op jit(solution)/shard_map/pallas_call | solution.py:308
  80.6 3.2 %shard_map.84 = (f32[4,128,256]{2,1,0:T(8,128)S(1)}, f32[3,128,256]{2,1,0:T(8,128)S(1)}) custom-call(s32[2]{0:T(128)S(1)} %compare_select_fusion.refs_0_.refs_1_, f32[2,1,512,2048]{3,2,1,0:T(8,128)S(1)} %bitcast.11, f32[2,1,256,128]{3,2,1,0:T(8,128)S(1)} %shard_map.83.refs_2_, f32[2,1,256,128]{3,2,1,0:T(8,128)S(1)} %shard_map.82.refs_3_), custom_call_target="tpu_custom_call" | custom-call | flops 2415919104 | bytes 2097152 | tf_op jit(solution)/shard_map/pallas_call | solution.py:308
  83.8 5.9 %collective-permute-done.13.refs_2_ = f32[2,1,256,128]{3,2,1,0:T(8,128)S(1)} collective-permute-done((f32[2,1,256,128]{3,2,1,0:T(8,128)S(1)}, f32[2,1,256,128]{3,2,1,0:T(8,128)S(1)}, u32[]{:S(2)}, u32[]{:S(2)}) %collective-permute-start.13) | collective-permute-done | bytes 262176 | tf_op jit(solution)/shard_map/ppermute | solution.py:22
  89.7 3.5 %collective-permute-start.14 = (f32[2,1,256,128]{3,2,1,0:T(8,128)S(1)}, f32[2,1,256,128]{3,2,1,0:T(8,128)S(1)}, u32[]{:S(2)}, u32[]{:S(2)}) collective-permute-start(f32[2,1,256,128]{3,2,1,0:T(8,128)S(1)} %collective-permute-done.13.refs_2_), channel_id=1, source_target_pairs={{0,4},{4,0},{8,12},{12,8},{1,5},{5,1},{9,13},{13,9},{2,6},{6,2},{1... | collective-permute-start | bytes 786440 | tf_op jit(solution)/shard_map/ppermute | solution.py:22
  93.2 13.4 %collective-permute-done.8.refs_2_.refs_3_ = f32[2,1,256,128]{3,2,1,0:T(8,128)S(1)} collective-permute-done((f32[2,1,256,128]{3,2,1,0:T(8,128)S(1)}, f32[2,1,256,128]{3,2,1,0:T(8,128)S(1)}, u32[]{:S(2)}, u32[]{:S(2)}) %collective-permute-start.8) | collective-permute-done | bytes 262176 | tf_op jit(solution)/shard_map/ppermute | solution.py:22
  106.5 3.5 %collective-permute-start.9 = (f32[2,1,256,128]{3,2,1,0:T(8,128)S(1)}, f32[2,1,256,128]{3,2,1,0:T(8,128)S(1)}, u32[]{:S(2)}, u32[]{:S(2)}) collective-permute-start(f32[2,1,256,128]{3,2,1,0:T(8,128)S(1)} %collective-permute-done.8.refs_2_.refs_3_), channel_id=1, source_target_pairs={{0,4},{4,0},{8,12},{12,8},{1,5},{5,1},{9,13},{13,9},{2,6},{6,2},{1... | collective-permute-start | bytes 786440 | tf_op jit(solution)/shard_map/ppermute | solution.py:22
  110.0 2.1 %shard_map.85 = (f32[4,128,256]{2,1,0:T(8,128)S(1)}, f32[3,128,256]{2,1,0:T(8,128)S(1)}) custom-call(s32[2]{0:T(128)S(1)} %compare_select_fusion.refs_0_.refs_1_, f32[2,1,512,2048]{3,2,1,0:T(8,128)S(1)} %bitcast.11, f32[2,1,256,128]{3,2,1,0:T(8,128)S(1)} %collective-permute-done.13.refs_2_, ...), custom_call_target="tpu_custom_call", output_to_operand_aliasing={{0}: (3, {}), {1}: (4, {})} | custom-call | flops 1207959552 | bytes 1048576 | tf_op jit(solution)/shard_map/pallas_call | solution.py:308
  112.2 4.0 %shard_map.87 = (f32[4,128,256]{2,1,0:T(8,128)S(1)}, f32[3,128,256]{2,1,0:T(8,128)S(1)}, f32[1,128,256]{2,1,0:T(8,128)S(1)}, f32[1,128,256]{2,1,0:T(8,128)S(1)}) custom-call(s32[2]{0:T(128)S(1)} %compare_select_fusion.refs_0_.refs_1_, f32[2,1,512,2048]{3,2,1,0:T(8,128)S(1)} %bitcast.11, ...), custom_call_target="tpu_custom_call", output_to_operand_aliasing={{0}: (6, {}), {1}: (7, {}), {2}: (8, {}), {3}: (9, {})} | custom-call | flops 4026531840 | bytes 2097152 | tf_op jit(solution)/shard_map/pallas_call | solution.py:308
  126.0 5.1 %collective-permute-done.22.refs_5_ = f32[2,1,256,128]{3,2,1,0:T(8,128)S(1)} collective-permute-done((f32[2,1,256,128]{3,2,1,0:T(8,128)S(1)}, f32[2,1,256,128]{3,2,1,0:T(8,128)S(1)}, u32[]{:S(2)}, u32[]{:S(2)}) %collective-permute-start.22) | collective-permute-done | bytes 262176 | tf_op jit(solution)/shard_map/ppermute | solution.py:22
  131.1 3.4 %collective-permute-done.19.refs_5_ = f32[2,1,256,128]{3,2,1,0:T(8,128)S(1)} collective-permute-done((f32[2,1,256,128]{3,2,1,0:T(8,128)S(1)}, f32[2,1,256,128]{3,2,1,0:T(8,128)S(1)}, u32[]{:S(2)}, u32[]{:S(2)}) %collective-permute-start.19) | collective-permute-done | bytes 262176 | tf_op jit(solution)/shard_map/ppermute | solution.py:22
  134.5 3.8 %shard_map.92 = (f32[2,1,512,128]{3,2,1,0:T(8,128)}, f32[1,128,256]{2,1,0:T(8,128)S(1)}) custom-call(s32[2]{0:T(128)S(1)} %compare_select_fusion.refs_0_.refs_1_, f32[2,1,512,2048]{3,2,1,0:T(8,128)S(1)} %bitcast.11, f32[2,1,256,128]{3,2,1,0:T(8,128)S(1)} %collective-permute-done.14.refs_2_, ...), custom_call_target="tpu_custom_call", output_to_operand_aliasing={{1}: (6, {})} | custom-call | flops 2415919104 | bytes 2097152 | tf_op jit(solution)/shard_map/pallas_call | solution.py:308
  (76 shorter events, 38.4 us)
Async XLA Ops:
  0.6 32.3 %collective-permute-start.4 = (f32[2,1,512,128]{3,2,1,0:T(8,128)}, f32[2,1,512,128]{3,2,1,0:T(8,128)S(1)}, u32[]{:S(2)}, u32[]{:S(2)}) collective-permute-start(f32[2,1,512,128]{3,2,1,0:T(8,128)} %contact_ref.1), channel_id=1, source_target_pairs={{0,4},{4,0},{8,12},{12,8},{1,5},{5,1},{9,13},{13,9},{2,6},{6,2},{1... | collective-permute-start | bytes 1572872 | tf_op jit(solution)/shard_map/ppermute | solution.py:22
  5.7 18.1 %collective-permute-start.2 = (f32[2,1,256,128]{3,2,1,0:T(8,128)}, f32[2,1,256,128]{3,2,1,0:T(8,128)}, u32[]{:S(2)}, u32[]{:S(2)}) collective-permute-start(f32[2,1,256,128]{3,2,1,0:T(8,128)} %get-tuple-element.35), channel_id=1, source_target_pairs={{0,8},{4,12},{8,0},{12,4},{1,9},{5,13},{9,1},{13,5},{2,10},{6,14},... | collective-permute-start | bytes 786440 | tf_op jit(solution)/shard_map/ppermute | solution.py:22
  8.4 24.6 %collective-permute-start = (f32[2,1,256,128]{3,2,1,0:T(8,128)}, f32[2,1,256,128]{3,2,1,0:T(8,128)S(1)}, u32[]{:S(2)}, u32[]{:S(2)}) collective-permute-start(f32[2,1,256,128]{3,2,1,0:T(8,128)} %get-tuple-element.34), channel_id=1, source_target_pairs={{0,8},{4,12},{8,0},{12,4},{1,9},{5,13},{9,1},{13,5},{2,10},{6,14},... | collective-permute-start | bytes 786440 | tf_op jit(solution)/shard_map/ppermute | solution.py:22
  12.7 63.6 %collective-permute-start.17 = (f32[2,1,128,768]{3,2,1,0:T(8,128)}, f32[2,1,128,768]{3,2,1,0:T(8,128)S(1)}, u32[]{:S(2)}, u32[]{:S(2)}) collective-permute-start(f32[2,1,128,768]{3,2,1,0:T(8,128)} %pad_maximum_fusion), channel_id=1, source_target_pairs={{0,4},{4,0},{8,12},{12,8},{1,5},{5,1},{9,13},{13,9},{2,6},{6,2},{1... | collective-permute-start | bytes 2359304 | tf_op jit(solution)/shard_map/ppermute | solution.py:495
  15.3 62.7 %collective-permute-start.18 = (f32[2,1,128,1024]{3,2,1,0:T(8,128)}, f32[2,1,128,1024]{3,2,1,0:T(8,128)S(1)}, u32[]{:S(2)}, u32[]{:S(2)}) collective-permute-start(f32[2,1,128,1024]{3,2,1,0:T(8,128)} %constant_dynamic-slice_fusion.1), channel_id=1, source_target_pairs={{4,8},{8,4},{5,9},{9,5},{6,10},{10,6},{7,11},{11,7},{20,24},{24,20... | collective-permute-start | bytes 3145736 | tf_op jit(solution)/shard_map/ppermute | solution.py:495
  23.9 26.6 %collective-permute-start.3 = (f32[2,1,256,128]{3,2,1,0:T(8,128)}, f32[2,1,256,128]{3,2,1,0:T(8,128)S(1)}, u32[]{:S(2)}, u32[]{:S(2)}) collective-permute-start(f32[2,1,256,128]{3,2,1,0:T(8,128)} %collective-permute-done.2.refs_2_), channel_id=1, source_target_pairs={{0,4},{4,0},{8,12},{12,8},{1,5},{5,1},{9,13},{13,9},{2,6},{6,2},{1... | collective-permute-start | bytes 786440 | tf_op jit(solution)/shard_map/ppermute | solution.py:22
  32.9 22.3 %collective-permute-start.1 = (f32[2,1,256,128]{3,2,1,0:T(8,128)S(1)}, f32[2,1,256,128]{3,2,1,0:T(8,128)S(1)}, u32[]{:S(2)}, u32[]{:S(2)}) collective-permute-start(f32[2,1,256,128]{3,2,1,0:T(8,128)S(1)} %collective-permute-done.refs_2_), channel_id=1, source_target_pairs={{0,4},{4,0},{8,12},{12,8},{1,5},{5,1},{9,13},{13,9},{2,6},{6,2},{1... | collective-permute-start | bytes 786440 | tf_op jit(solution)/shard_map/ppermute | solution.py:22
  57.0 9.2 %collective-permute-start.10 = (f32[2,1,256,128]{3,2,1,0:T(8,128)S(1)}, f32[2,1,256,128]{3,2,1,0:T(8,128)S(1)}, u32[]{:S(2)}, u32[]{:S(2)}) collective-permute-start(f32[2,1,256,128]{3,2,1,0:T(8,128)S(1)} %get-tuple-element.37), channel_id=1, source_target_pairs={{0,2},{1,3},{2,0},{3,1},{4,6},{5,7},{6,4},{7,5},{8,10},{9,11},{10,... | collective-permute-start | bytes 786440 | tf_op jit(solution)/shard_map/ppermute | solution.py:22
  58.7 7.5 %collective-permute-start.11 = (f32[2,1,256,128]{3,2,1,0:T(8,128)S(1)}, f32[2,1,256,128]{3,2,1,0:T(8,128)S(1)}, u32[]{:S(2)}, u32[]{:S(2)}) collective-permute-start(f32[2,1,256,128]{3,2,1,0:T(8,128)S(1)} %get-tuple-element.37), channel_id=1, source_target_pairs={{0,1},{1,0},{2,3},{3,2},{4,5},{5,4},{6,7},{7,6},{8,9},{9,8},{10,11... | collective-permute-start | bytes 786440 | tf_op jit(solution)/shard_map/ppermute | solution.py:22
  58.7 11.4 %collective-permute-start.5 = (f32[2,1,256,128]{3,2,1,0:T(8,128)S(1)}, f32[2,1,256,128]{3,2,1,0:T(8,128)S(1)}, u32[]{:S(2)}, u32[]{:S(2)}) collective-permute-start(f32[2,1,256,128]{3,2,1,0:T(8,128)S(1)} %get-tuple-element.36), channel_id=1, source_target_pairs={{0,2},{1,3},{2,0},{3,1},{4,6},{5,7},{6,4},{7,5},{8,10},{9,11},{10,... | collective-permute-start | bytes 786440 | tf_op jit(solution)/shard_map/ppermute | solution.py:22
  66.2 6.3 %collective-permute-start.6 = (f32[2,1,256,128]{3,2,1,0:T(8,128)S(1)}, f32[2,1,256,128]{3,2,1,0:T(8,128)S(1)}, u32[]{:S(2)}, u32[]{:S(2)}) collective-permute-start(f32[2,1,256,128]{3,2,1,0:T(8,128)S(1)} %get-tuple-element.36), channel_id=1, source_target_pairs={{0,1},{1,0},{2,3},{3,2},{4,5},{5,4},{6,7},{7,6},{8,9},{9,8},{10,11... | collective-permute-start | bytes 786440 | tf_op jit(solution)/shard_map/ppermute | solution.py:22
  70.1 55.4 %collective-permute-start.25 = (f32[2,1,128,512]{3,2,1,0:T(8,128)S(1)}, f32[2,1,128,512]{3,2,1,0:T(8,128)S(1)}, u32[]{:S(2)}, u32[]{:S(2)}) collective-permute-start(f32[2,1,128,512]{3,2,1,0:T(8,128)S(1)} %copy-done.3), channel_id=1, source_target_pairs={{0,4},{4,0},{8,12},{12,8},{1,5},{5,1},{9,13},{13,9},{2,6},{6,2},{1... | collective-permute-start | bytes 1572872 | tf_op jit(solution)/shard_map/ppermute | solution.py:22
  72.5 17.2 %collective-permute-start.13 = (f32[2,1,256,128]{3,2,1,0:T(8,128)S(1)}, f32[2,1,256,128]{3,2,1,0:T(8,128)S(1)}, u32[]{:S(2)}, u32[]{:S(2)}) collective-permute-start(f32[2,1,256,128]{3,2,1,0:T(8,128)S(1)} %shard_map.83.refs_2_), channel_id=1, source_target_pairs={{0,8},{4,12},{8,0},{12,4},{1,9},{5,13},{9,1},{13,5},{2,10},{6,14},... | collective-permute-start | bytes 786440 | tf_op jit(solution)/shard_map/ppermute | solution.py:22
  75.1 37.1 %collective-permute-start.15 = (f32[2,1,256,128]{3,2,1,0:T(8,128)S(1)}, f32[2,1,256,128]{3,2,1,0:T(8,128)S(1)}, u32[]{:S(2)}, u32[]{:S(2)}) collective-permute-start(f32[2,1,256,128]{3,2,1,0:T(8,128)S(1)} %shard_map.83.refs_2_), channel_id=1, source_target_pairs={{0,4},{4,0},{8,12},{12,8},{1,5},{5,1},{9,13},{13,9},{2,6},{6,2},{1... | collective-permute-start | bytes 786440 | tf_op jit(solution)/shard_map/ppermute | solution.py:22
  76.4 35.8 %collective-permute-start.16 = (f32[2,1,256,128]{3,2,1,0:T(8,128)S(1)}, f32[2,1,256,128]{3,2,1,0:T(8,128)S(1)}, u32[]{:S(2)}, u32[]{:S(2)}) collective-permute-start(f32[2,1,256,128]{3,2,1,0:T(8,128)S(1)} %shard_map.82.refs_3_), channel_id=1, source_target_pairs={{0,4},{4,0},{8,12},{12,8},{1,5},{5,1},{9,13},{13,9},{2,6},{6,2},{1... | collective-permute-start | bytes 786440 | tf_op jit(solution)/shard_map/ppermute | solution.py:22
  78.0 28.6 %collective-permute-start.8 = (f32[2,1,256,128]{3,2,1,0:T(8,128)S(1)}, f32[2,1,256,128]{3,2,1,0:T(8,128)S(1)}, u32[]{:S(2)}, u32[]{:S(2)}) collective-permute-start(f32[2,1,256,128]{3,2,1,0:T(8,128)S(1)} %shard_map.82.refs_3_), channel_id=1, source_target_pairs={{0,8},{4,12},{8,0},{12,4},{1,9},{5,13},{9,1},{13,5},{2,10},{6,14},... | collective-permute-start | bytes 786440 | tf_op jit(solution)/shard_map/ppermute | solution.py:22
  89.7 28.7 %collective-permute-start.14 = (f32[2,1,256,128]{3,2,1,0:T(8,128)S(1)}, f32[2,1,256,128]{3,2,1,0:T(8,128)S(1)}, u32[]{:S(2)}, u32[]{:S(2)}) collective-permute-start(f32[2,1,256,128]{3,2,1,0:T(8,128)S(1)} %collective-permute-done.13.refs_2_), channel_id=1, source_target_pairs={{0,4},{4,0},{8,12},{12,8},{1,5},{5,1},{9,13},{13,9},{2,6},{6,2},{1... | collective-permute-start | bytes 786440 | tf_op jit(solution)/shard_map/ppermute | solution.py:22
  106.5 13.5 %collective-permute-start.9 = (f32[2,1,256,128]{3,2,1,0:T(8,128)S(1)}, f32[2,1,256,128]{3,2,1,0:T(8,128)S(1)}, u32[]{:S(2)}, u32[]{:S(2)}) collective-permute-start(f32[2,1,256,128]{3,2,1,0:T(8,128)S(1)} %collective-permute-done.8.refs_2_.refs_3_), channel_id=1, source_target_pairs={{0,4},{4,0},{8,12},{12,8},{1,5},{5,1},{9,13},{13,9},{2,6},{6,2},{1... | collective-permute-start | bytes 786440 | tf_op jit(solution)/shard_map/ppermute | solution.py:22
  121.8 9.2 %collective-permute-start.22 = (f32[2,1,256,128]{3,2,1,0:T(8,128)S(1)}, f32[2,1,256,128]{3,2,1,0:T(8,128)S(1)}, u32[]{:S(2)}, u32[]{:S(2)}) collective-permute-start(f32[2,1,256,128]{3,2,1,0:T(8,128)S(1)} %get-tuple-element.48.refs_9_), channel_id=1, source_target_pairs={{0,2},{1,3},{2,0},{3,1},{4,6},{5,7},{6,4},{7,5},{8,10},{9,11},{10,... | collective-permute-start | bytes 786440 | tf_op jit(solution)/shard_map/ppermute | solution.py:22
  123.4 11.1 %collective-permute-start.19 = (f32[2,1,256,128]{3,2,1,0:T(8,128)S(1)}, f32[2,1,256,128]{3,2,1,0:T(8,128)S(1)}, u32[]{:S(2)}, u32[]{:S(2)}) collective-permute-start(f32[2,1,256,128]{3,2,1,0:T(8,128)S(1)} %get-tuple-element.47.refs_10_), channel_id=1, source_target_pairs={{0,2},{1,3},{2,0},{3,1},{4,6},{5,7},{6,4},{7,5},{8,10},{9,11},{10,... | collective-permute-start | bytes 786440 | tf_op jit(solution)/shard_map/ppermute | solution.py:22
  123.9 16.6 %collective-permute-start.26 = (f32[1,128,256]{2,1,0:T(8,128)S(1)}, f32[1,128,256]{2,1,0:T(8,128)S(1)}, u32[]{:S(2)}, u32[]{:S(2)}) collective-permute-start(f32[1,128,256]{2,1,0:T(8,128)S(1)} %get-tuple-element.53), channel_id=1, source_target_pairs={{4,0},{8,4},{12,8},{5,1},{9,5},{13,9},{6,2},{10,6},{14,10},{7,3},{... | collective-permute-start | bytes 393224 | tf_op jit(solution)/shard_map/ppermute | solution.py:571
  125.4 14.3 %collective-permute-start.23 = (f32[2,1,256,128]{3,2,1,0:T(8,128)S(1)}, f32[2,1,256,128]{3,2,1,0:T(8,128)S(1)}, u32[]{:S(2)}, u32[]{:S(2)}) collective-permute-start(f32[2,1,256,128]{3,2,1,0:T(8,128)S(1)} %get-tuple-element.48.refs_9_), channel_id=1, source_target_pairs={{0,1},{1,0},{2,3},{3,2},{4,5},{5,4},{6,7},{7,6},{8,9},{9,8},{10,11... | collective-permute-start | bytes 786440 | tf_op jit(solution)/shard_map/ppermute | solution.py:22
  125.5 15.0 %collective-permute-start.20 = (f32[2,1,256,128]{3,2,1,0:T(8,128)S(1)}, f32[2,1,256,128]{3,2,1,0:T(8,128)S(1)}, u32[]{:S(2)}, u32[]{:S(2)}) collective-permute-start(f32[2,1,256,128]{3,2,1,0:T(8,128)S(1)} %get-tuple-element.47.refs_10_), channel_id=1, source_target_pairs={{0,1},{1,0},{2,3},{3,2},{4,5},{5,4},{6,7},{7,6},{8,9},{9,8},{10,11... | collective-permute-start | bytes 786440 | tf_op jit(solution)/shard_map/ppermute | solution.py:22
  131.1 8.7 %collective-permute-start.24 = (f32[2,1,256,128]{3,2,1,0:T(8,128)S(1)}, f32[2,1,256,128]{3,2,1,0:T(8,128)S(1)}, u32[]{:S(2)}, u32[]{:S(2)}) collective-permute-start(f32[2,1,256,128]{3,2,1,0:T(8,128)S(1)} %collective-permute-done.22.refs_5_), channel_id=1, source_target_pairs={{0,1},{1,0},{2,3},{3,2},{4,5},{5,4},{6,7},{7,6},{8,9},{9,8},{10,11... | collective-permute-start | bytes 786440 | tf_op jit(solution)/shard_map/ppermute | solution.py:22
  (9 other events, 141.1 us)

commit v9 on v8

--- a/solution.py
+++ b/solution.py
@@ -549,6 +549,11 @@
             far, _, blocks = groups.pop([far for far, _, _ in groups].index(high))
             groups.insert(1, (far, 0, blocks[:1]))
             groups.append((far, 1, blocks[1:]))
+            for place, (near_far, _, blocks) in enumerate(groups):
+                if near_far == 1 and len(blocks) > 1:
+                    groups[place] = (1, 0, blocks[:1])
+                    groups.append((1, 1, blocks[1:]))
+                    break
         sums = {}
         for far, number, blocks in groups:
             work = ("diag", "upper") if final else ("diag",)

time: 143 us -> 142 us (level)
  waiting for transfers between devices: 56.9 us -> 54.2 us
  Pallas kernels: 39.4 us -> 41 us
    ppermute x24, waiting for transfers between devices: 56.9 us -> 54.2 us  [swapped(): lax.ppermute(x, axis, [(i, i ^ bit) for i in range(lax.axis_size(axis))])]
    pallas_call x15 -> x16, Pallas kernels: 34.6 us -> 36.1 us  [panel(): pl.pallas_call(functools.partial(panel_kernel, local, far, starts, kinds,...]
  transfers between devices with their start and end apart: 27 -> 27, of which waited for: 9 -> 10; matrix products, arithmetic and copies ran while one was open for 6% -> 6% of each run, Pallas kernels for 26% -> 28%
where the time goes in v9:
time: 142 us; the launch traced here: 141 us
  waiting for transfers between devices  54.2 us (38%)
  Pallas kernels  41 us (29%)
  starting transfers between devices  32.1 us (23%)
  local copies, waits for them, and re-layouts  10.9 us (8%)
  other arithmetic  1.88 us (1%)
    ppermute x24, waiting for transfers between devices, swapped(): lax.ppermute(x, axis, [(i, i ^ bit) for i in range(lax.axis_size(axis))])  54.2 us
    pallas_call x16, Pallas kernels, panel(): pl.pallas_call(functools.partial(panel_kernel, local, far, starts, kinds,...  36.1 us
    ppermute x24, starting transfers between devices, swapped(): lax.ppermute(x, axis, [(i, i ^ bit) for i in range(lax.axis_size(axis))])  29.7 us
    dynamic_slice x3, local copies, waits for them, and re-layouts, take(): return lax.dynamic_slice(retarded, (0, 0, row, column), (2, 1, B, size))  5.42 us
    unnamed x12, local copies, waits for them, and re-layouts  4.48 us
  transfers between devices with their start and end apart: 27, of which 10 were waited for; matrix products, arithmetic and copies ran while one was open for 6% of the time, Pallas kernels for 28%

profile of v9, /device:TPU:0, one launch (start us, length us, event | category | flops | bytes accessed | tf_op | source)
XLA Modules:
  0.0 141.3 jit_solution(5393704512792363543)
XLA Ops:
  0.6 3.1 %collective-permute-start.4 = (f32[2,1,512,128]{3,2,1,0:T(8,128)}, f32[2,1,512,128]{3,2,1,0:T(8,128)S(1)}, u32[]{:S(2)}, u32[]{:S(2)}) collective-permute-start(f32[2,1,512,128]{3,2,1,0:T(8,128)} %contact_ref.1), channel_id=1, source_target_pairs={{0,4},{4,0},{8,12},{12,8},{1,5},{5,1},{9,13},{13,9},{2,6},{6,2},{1... | collective-permute-start | bytes 1572872 | tf_op jit(solution)/shard_map/ppermute | solution.py:22
  5.7 2.7 %collective-permute-start.2 = (f32[2,1,256,128]{3,2,1,0:T(8,128)}, f32[2,1,256,128]{3,2,1,0:T(8,128)}, u32[]{:S(2)}, u32[]{:S(2)}) collective-permute-start(f32[2,1,256,128]{3,2,1,0:T(8,128)} %get-tuple-element.39), channel_id=1, source_target_pairs={{0,8},{4,12},{8,0},{12,4},{1,9},{5,13},{9,1},{13,5},{2,10},{6,14},... | collective-permute-start | bytes 786440 | tf_op jit(solution)/shard_map/ppermute | solution.py:22
  12.9 2.3 %constant_dynamic-slice_fusion.1 = f32[2,1,128,1024]{3,2,1,0:T(8,128)} fusion(f32[2,1,512,2048]{3,2,1,0:T(8,128)} %refs_1_.31, s32[]{:T(128)S(6)} %select_n.90, s32[]{:T(128)S(6)} %select_n.92), kind=kLoop, calls=%fused_computation.6 | loop fusion | bytes 2097160 | tf_op jit(solution)/shard_map/dynamic_slice | solution.py:476
  18.0 3.4 %copy-done = f32[2,1,512,2048]{3,2,1,0:T(8,128)S(1)} copy-done((f32[2,1,512,2048]{3,2,1,0:T(8,128)S(1)}, f32[2,1,512,2048]{3,2,1,0:T(8,128)}, u32[]{:S(2)}) %copy-start) | copy-done | bytes 8388632
  21.4 2.4 %shard_map.76.refs_3_ = f32[4,128,256]{2,1,0:T(8,128)S(1)} custom-call(s32[2]{0:T(128)S(1)} %compare_select_fusion.refs_0_.refs_1_, f32[2,1,512,2048]{3,2,1,0:T(8,128)S(1)} %copy-done, f32[2,1,512,128]{3,2,1,0:T(8,128)S(1)} %get-tuple-element.35.refs_2_), custom_call_target="tpu_custom_call" | custom-call | flops 1610612736 | bytes 2097152 | tf_op jit(solution)/shard_map/pallas_call | solution.py:308
  23.9 4.7 %collective-permute-start.3 = (f32[2,1,256,128]{3,2,1,0:T(8,128)}, f32[2,1,256,128]{3,2,1,0:T(8,128)S(1)}, u32[]{:S(2)}, u32[]{:S(2)}) collective-permute-start(f32[2,1,256,128]{3,2,1,0:T(8,128)} %collective-permute-done.2.refs_2_), channel_id=1, source_target_pairs={{0,4},{4,0},{8,12},{12,8},{1,5},{5,1},{9,13},{13,9},{2,6},{6,2},{1... | collective-permute-start | bytes 786440 | tf_op jit(solution)/shard_map/ppermute | solution.py:22
  30.7 2.3 %collective-permute-done.refs_2_ = f32[2,1,256,128]{3,2,1,0:T(8,128)S(1)} collective-permute-done((f32[2,1,256,128]{3,2,1,0:T(8,128)}, f32[2,1,256,128]{3,2,1,0:T(8,128)S(1)}, u32[]{:S(2)}, u32[]{:S(2)}) %collective-permute-start) | collective-permute-done | bytes 262176 | tf_op jit(solution)/shard_map/ppermute | solution.py:22
  32.9 2.5 %shard_map.78.refs_3_ = f32[4,128,256]{2,1,0:T(8,128)S(1)} custom-call(s32[2]{0:T(128)S(1)} %compare_select_fusion.refs_0_.refs_1_, f32[2,1,512,2048]{3,2,1,0:T(8,128)S(1)} %copy-done, f32[2,1,512,128]{3,2,1,0:T(8,128)S(1)} %collective-permute-done.4.refs_2_, f32[4,128,256]{2,1,0:T(8,128)S(1)} %shard_map.77.refs_3_), custom_call_target="tpu_custom_call", output_to_operand_aliasing={{}: (3, {})} | custom-call | flops 1610612736 | bytes 2097152 | tf_op jit(solution)/shard_map/pallas_call | solution.py:308
  37.2 13.3 %collective-permute-done.3.refs_2_ = f32[2,1,256,128]{3,2,1,0:T(8,128)S(1)} collective-permute-done((f32[2,1,256,128]{3,2,1,0:T(8,128)}, f32[2,1,256,128]{3,2,1,0:T(8,128)S(1)}, u32[]{:S(2)}, u32[]{:S(2)}) %collective-permute-start.3) | collective-permute-done | bytes 262176 | tf_op jit(solution)/shard_map/ppermute | solution.py:22
  52.2 3.1 %collective-permute-done.1.refs_2_ = f32[2,1,256,128]{3,2,1,0:T(8,128)S(1)} collective-permute-done((f32[2,1,256,128]{3,2,1,0:T(8,128)S(1)}, f32[2,1,256,128]{3,2,1,0:T(8,128)S(1)}, u32[]{:S(2)}, u32[]{:S(2)}) %collective-permute-start.1) | collective-permute-done | bytes 262176 | tf_op jit(solution)/shard_map/ppermute | solution.py:22
  59.1 7.1 %collective-permute-done.10.refs_5_ = f32[2,1,256,128]{3,2,1,0:T(8,128)S(1)} collective-permute-done((f32[2,1,256,128]{3,2,1,0:T(8,128)S(1)}, f32[2,1,256,128]{3,2,1,0:T(8,128)S(1)}, u32[]{:S(2)}, u32[]{:S(2)}) %collective-permute-start.10) | collective-permute-done | bytes 262176 | tf_op jit(solution)/shard_map/ppermute | solution.py:22
  66.7 3.4 %collective-permute-done.5.refs_5_ = f32[2,1,256,128]{3,2,1,0:T(8,128)S(1)} collective-permute-done((f32[2,1,256,128]{3,2,1,0:T(8,128)S(1)}, f32[2,1,256,128]{3,2,1,0:T(8,128)S(1)}, u32[]{:S(2)}, u32[]{:S(2)}) %collective-permute-start.5) | collective-permute-done | bytes 262176 | tf_op jit(solution)/shard_map/ppermute | solution.py:22
  72.5 2.6 %collective-permute-start.13 = (f32[2,1,256,128]{3,2,1,0:T(8,128)S(1)}, f32[2,1,256,128]{3,2,1,0:T(8,128)S(1)}, u32[]{:S(2)}, u32[]{:S(2)}) collective-permute-start(f32[2,1,256,128]{3,2,1,0:T(8,128)S(1)} %shard_map.83.refs_2_), channel_id=1, source_target_pairs={{0,8},{4,12},{8,0},{12,4},{1,9},{5,13},{9,1},{13,5},{2,10},{6,14},... | collective-permute-start | bytes 786440 | tf_op jit(solution)/shard_map/ppermute | solution.py:22
  78.4 2.2 %shard_map.86 = (f32[1,128,256]{2,1,0:T(8,128)S(1)}, f32[1,128,256]{2,1,0:T(8,128)S(1)}) custom-call(s32[2]{0:T(128)S(1)} %compare_select_fusion.refs_0_.refs_1_, f32[2,1,512,2048]{3,2,1,0:T(8,128)S(1)} %bitcast.11, f32[2,1,256,128]{3,2,1,0:T(8,128)S(1)} %shard_map.83.refs_2_, f32[2,1,256,128]{3,2,1,0:T(8,128)S(1)} %shard_map.82.refs_3_, ...), custom_call_target="tpu_custom_call" | custom-call | flops 603979776 | bytes 2097152 | tf_op jit(solution)/shard_map/pallas_call | solution.py:308
  80.6 3.2 %shard_map.84 = (f32[4,128,256]{2,1,0:T(8,128)S(1)}, f32[3,128,256]{2,1,0:T(8,128)S(1)}) custom-call(s32[2]{0:T(128)S(1)} %compare_select_fusion.refs_0_.refs_1_, f32[2,1,512,2048]{3,2,1,0:T(8,128)S(1)} %bitcast.11, f32[2,1,256,128]{3,2,1,0:T(8,128)S(1)} %shard_map.83.refs_2_, f32[2,1,256,128]{3,2,1,0:T(8,128)S(1)} %shard_map.82.refs_3_), custom_call_target="tpu_custom_call" | custom-call | flops 2415919104 | bytes 2097152 | tf_op jit(solution)/shard_map/pallas_call | solution.py:308
  83.8 5.9 %collective-permute-done.13.refs_2_ = f32[2,1,256,128]{3,2,1,0:T(8,128)S(1)} collective-permute-done((f32[2,1,256,128]{3,2,1,0:T(8,128)S(1)}, f32[2,1,256,128]{3,2,1,0:T(8,128)S(1)}, u32[]{:S(2)}, u32[]{:S(2)}) %collective-permute-start.13) | collective-permute-done | bytes 262176 | tf_op jit(solution)/shard_map/ppermute | solution.py:22
  89.7 3.5 %collective-permute-start.14 = (f32[2,1,256,128]{3,2,1,0:T(8,128)S(1)}, f32[2,1,256,128]{3,2,1,0:T(8,128)S(1)}, u32[]{:S(2)}, u32[]{:S(2)}) collective-permute-start(f32[2,1,256,128]{3,2,1,0:T(8,128)S(1)} %collective-permute-done.13.refs_2_), channel_id=1, source_target_pairs={{0,4},{4,0},{8,12},{12,8},{1,5},{5,1},{9,13},{13,9},{2,6},{6,2},{1... | collective-permute-start | bytes 786440 | tf_op jit(solution)/shard_map/ppermute | solution.py:22
  93.2 7.7 %collective-permute-done.8.refs_2_.refs_3_ = f32[2,1,256,128]{3,2,1,0:T(8,128)S(1)} collective-permute-done((f32[2,1,256,128]{3,2,1,0:T(8,128)S(1)}, f32[2,1,256,128]{3,2,1,0:T(8,128)S(1)}, u32[]{:S(2)}, u32[]{:S(2)}) %collective-permute-start.8) | collective-permute-done | bytes 262176 | tf_op jit(solution)/shard_map/ppermute | solution.py:22
  100.9 3.5 %collective-permute-start.9 = (f32[2,1,256,128]{3,2,1,0:T(8,128)S(1)}, f32[2,1,256,128]{3,2,1,0:T(8,128)S(1)}, u32[]{:S(2)}, u32[]{:S(2)}) collective-permute-start(f32[2,1,256,128]{3,2,1,0:T(8,128)S(1)} %collective-permute-done.8.refs_2_.refs_3_), channel_id=1, source_target_pairs={{0,4},{4,0},{8,12},{12,8},{1,5},{5,1},{9,13},{13,9},{2,6},{6,2},{1... | collective-permute-start | bytes 786440 | tf_op jit(solution)/shard_map/ppermute | solution.py:22
  106.6 2.8 %shard_map.87 = (f32[4,128,256]{2,1,0:T(8,128)S(1)}, f32[3,128,256]{2,1,0:T(8,128)S(1)}, f32[1,128,256]{2,1,0:T(8,128)S(1)}, f32[1,128,256]{2,1,0:T(8,128)S(1)}) custom-call(s32[2]{0:T(128)S(1)} %compare_select_fusion.refs_0_.refs_1_, f32[2,1,512,2048]{3,2,1,0:T(8,128)S(1)} %bitcast.11, ...), custom_call_target="tpu_custom_call", output_to_operand_aliasing={{0}: (4, {}), {1}: (5, {}), {2}: (6, {}), {3}: (7, {})} | custom-call | flops 2013265920 | bytes 1048576 | tf_op jit(solution)/shard_map/pallas_call | solution.py:308
  111.5 2.8 %shard_map.89 = (f32[4,128,256]{2,1,0:T(8,128)S(1)}, f32[3,128,256]{2,1,0:T(8,128)S(1)}, f32[1,128,256]{2,1,0:T(8,128)S(1)}, f32[1,128,256]{2,1,0:T(8,128)S(1)}) custom-call(s32[2]{0:T(128)S(1)} %compare_select_fusion.refs_0_.refs_1_, f32[2,1,512,2048]{3,2,1,0:T(8,128)S(1)} %bitcast.11, ...), custom_call_target="tpu_custom_call", output_to_operand_aliasing={{0}: (5, {}), {1}: (6, {}), {2}: (7, {}), {3}: (8, {})} | custom-call | flops 2013265920 | bytes 1048576 | tf_op jit(solution)/shard_map/pallas_call | solution.py:308
  124.1 5.1 %collective-permute-done.22.refs_5_ = f32[2,1,256,128]{3,2,1,0:T(8,128)S(1)} collective-permute-done((f32[2,1,256,128]{3,2,1,0:T(8,128)S(1)}, f32[2,1,256,128]{3,2,1,0:T(8,128)S(1)}, u32[]{:S(2)}, u32[]{:S(2)}) %collective-permute-start.22) | collective-permute-done | bytes 262176 | tf_op jit(solution)/shard_map/ppermute | solution.py:22
  129.2 4.2 %collective-permute-done.19.refs_5_ = f32[2,1,256,128]{3,2,1,0:T(8,128)S(1)} collective-permute-done((f32[2,1,256,128]{3,2,1,0:T(8,128)S(1)}, f32[2,1,256,128]{3,2,1,0:T(8,128)S(1)}, u32[]{:S(2)}, u32[]{:S(2)}) %collective-permute-start.19) | collective-permute-done | bytes 262176 | tf_op jit(solution)/shard_map/ppermute | solution.py:22
  133.4 3.8 %shard_map.93 = (f32[2,1,512,128]{3,2,1,0:T(8,128)}, f32[1,128,256]{2,1,0:T(8,128)S(1)}) custom-call(s32[2]{0:T(128)S(1)} %compare_select_fusion.refs_0_.refs_1_, f32[2,1,512,2048]{3,2,1,0:T(8,128)S(1)} %bitcast.11, f32[2,1,256,128]{3,2,1,0:T(8,128)S(1)} %collective-permute-done.14.refs_2_, ...), custom_call_target="tpu_custom_call", output_to_operand_aliasing={{1}: (6, {})} | custom-call | flops 2415919104 | bytes 2097152 | tf_op jit(solution)/shard_map/pallas_call | solution.py:308
  (77 shorter events, 42.7 us)
Async XLA Ops:
  0.6 32.3 %collective-permute-start.4 = (f32[2,1,512,128]{3,2,1,0:T(8,128)}, f32[2,1,512,128]{3,2,1,0:T(8,128)S(1)}, u32[]{:S(2)}, u32[]{:S(2)}) collective-permute-start(f32[2,1,512,128]{3,2,1,0:T(8,128)} %contact_ref.1), channel_id=1, source_target_pairs={{0,4},{4,0},{8,12},{12,8},{1,5},{5,1},{9,13},{13,9},{2,6},{6,2},{1... | collective-permute-start | bytes 1572872 | tf_op jit(solution)/shard_map/ppermute | solution.py:22
  5.7 18.1 %collective-permute-start.2 = (f32[2,1,256,128]{3,2,1,0:T(8,128)}, f32[2,1,256,128]{3,2,1,0:T(8,128)}, u32[]{:S(2)}, u32[]{:S(2)}) collective-permute-start(f32[2,1,256,128]{3,2,1,0:T(8,128)} %get-tuple-element.39), channel_id=1, source_target_pairs={{0,8},{4,12},{8,0},{12,4},{1,9},{5,13},{9,1},{13,5},{2,10},{6,14},... | collective-permute-start | bytes 786440 | tf_op jit(solution)/shard_map/ppermute | solution.py:22
  8.4 24.6 %collective-permute-start = (f32[2,1,256,128]{3,2,1,0:T(8,128)}, f32[2,1,256,128]{3,2,1,0:T(8,128)S(1)}, u32[]{:S(2)}, u32[]{:S(2)}) collective-permute-start(f32[2,1,256,128]{3,2,1,0:T(8,128)} %get-tuple-element.38), channel_id=1, source_target_pairs={{0,8},{4,12},{8,0},{12,4},{1,9},{5,13},{9,1},{13,5},{2,10},{6,14},... | collective-permute-start | bytes 786440 | tf_op jit(solution)/shard_map/ppermute | solution.py:22
  12.7 63.6 %collective-permute-start.16 = (f32[2,1,128,768]{3,2,1,0:T(8,128)}, f32[2,1,128,768]{3,2,1,0:T(8,128)S(1)}, u32[]{:S(2)}, u32[]{:S(2)}) collective-permute-start(f32[2,1,128,768]{3,2,1,0:T(8,128)} %pad_maximum_fusion), channel_id=1, source_target_pairs={{0,4},{4,0},{8,12},{12,8},{1,5},{5,1},{9,13},{13,9},{2,6},{6,2},{1... | collective-permute-start | bytes 2359304 | tf_op jit(solution)/shard_map/ppermute | solution.py:495
  15.3 61.6 %collective-permute-start.17 = (f32[2,1,128,1024]{3,2,1,0:T(8,128)}, f32[2,1,128,1024]{3,2,1,0:T(8,128)S(1)}, u32[]{:S(2)}, u32[]{:S(2)}) collective-permute-start(f32[2,1,128,1024]{3,2,1,0:T(8,128)} %constant_dynamic-slice_fusion.1), channel_id=1, source_target_pairs={{4,8},{8,4},{5,9},{9,5},{6,10},{10,6},{7,11},{11,7},{20,24},{24,20... | collective-permute-start | bytes 3145736 | tf_op jit(solution)/shard_map/ppermute | solution.py:495
  23.9 26.6 %collective-permute-start.3 = (f32[2,1,256,128]{3,2,1,0:T(8,128)}, f32[2,1,256,128]{3,2,1,0:T(8,128)S(1)}, u32[]{:S(2)}, u32[]{:S(2)}) collective-permute-start(f32[2,1,256,128]{3,2,1,0:T(8,128)} %collective-permute-done.2.refs_2_), channel_id=1, source_target_pairs={{0,4},{4,0},{8,12},{12,8},{1,5},{5,1},{9,13},{13,9},{2,6},{6,2},{1... | collective-permute-start | bytes 786440 | tf_op jit(solution)/shard_map/ppermute | solution.py:22
  32.9 22.3 %collective-permute-start.1 = (f32[2,1,256,128]{3,2,1,0:T(8,128)S(1)}, f32[2,1,256,128]{3,2,1,0:T(8,128)S(1)}, u32[]{:S(2)}, u32[]{:S(2)}) collective-permute-start(f32[2,1,256,128]{3,2,1,0:T(8,128)S(1)} %collective-permute-done.refs_2_), channel_id=1, source_target_pairs={{0,4},{4,0},{8,12},{12,8},{1,5},{5,1},{9,13},{13,9},{2,6},{6,2},{1... | collective-permute-start | bytes 786440 | tf_op jit(solution)/shard_map/ppermute | solution.py:22
  57.0 9.2 %collective-permute-start.10 = (f32[2,1,256,128]{3,2,1,0:T(8,128)S(1)}, f32[2,1,256,128]{3,2,1,0:T(8,128)S(1)}, u32[]{:S(2)}, u32[]{:S(2)}) collective-permute-start(f32[2,1,256,128]{3,2,1,0:T(8,128)S(1)} %get-tuple-element.41), channel_id=1, source_target_pairs={{0,2},{1,3},{2,0},{3,1},{4,6},{5,7},{6,4},{7,5},{8,10},{9,11},{10,... | collective-permute-start | bytes 786440 | tf_op jit(solution)/shard_map/ppermute | solution.py:22
  58.7 7.5 %collective-permute-start.11 = (f32[2,1,256,128]{3,2,1,0:T(8,128)S(1)}, f32[2,1,256,128]{3,2,1,0:T(8,128)S(1)}, u32[]{:S(2)}, u32[]{:S(2)}) collective-permute-start(f32[2,1,256,128]{3,2,1,0:T(8,128)S(1)} %get-tuple-element.41), channel_id=1, source_target_pairs={{0,1},{1,0},{2,3},{3,2},{4,5},{5,4},{6,7},{7,6},{8,9},{9,8},{10,11... | collective-permute-start | bytes 786440 | tf_op jit(solution)/shard_map/ppermute | solution.py:22
  58.7 11.4 %collective-permute-start.5 = (f32[2,1,256,128]{3,2,1,0:T(8,128)S(1)}, f32[2,1,256,128]{3,2,1,0:T(8,128)S(1)}, u32[]{:S(2)}, u32[]{:S(2)}) collective-permute-start(f32[2,1,256,128]{3,2,1,0:T(8,128)S(1)} %get-tuple-element.40), channel_id=1, source_target_pairs={{0,2},{1,3},{2,0},{3,1},{4,6},{5,7},{6,4},{7,5},{8,10},{9,11},{10,... | collective-permute-start | bytes 786440 | tf_op jit(solution)/shard_map/ppermute | solution.py:22
  66.2 6.3 %collective-permute-start.6 = (f32[2,1,256,128]{3,2,1,0:T(8,128)S(1)}, f32[2,1,256,128]{3,2,1,0:T(8,128)S(1)}, u32[]{:S(2)}, u32[]{:S(2)}) collective-permute-start(f32[2,1,256,128]{3,2,1,0:T(8,128)S(1)} %get-tuple-element.40), channel_id=1, source_target_pairs={{0,1},{1,0},{2,3},{3,2},{4,5},{5,4},{6,7},{7,6},{8,9},{9,8},{10,11... | collective-permute-start | bytes 786440 | tf_op jit(solution)/shard_map/ppermute | solution.py:22
  70.1 53.5 %collective-permute-start.25 = (f32[2,1,128,512]{3,2,1,0:T(8,128)S(1)}, f32[2,1,128,512]{3,2,1,0:T(8,128)S(1)}, u32[]{:S(2)}, u32[]{:S(2)}) collective-permute-start(f32[2,1,128,512]{3,2,1,0:T(8,128)S(1)} %copy-done.3), channel_id=1, source_target_pairs={{0,4},{4,0},{8,12},{12,8},{1,5},{5,1},{9,13},{13,9},{2,6},{6,2},{1... | collective-permute-start | bytes 1572872 | tf_op jit(solution)/shard_map/ppermute | solution.py:22
  72.5 17.2 %collective-permute-start.13 = (f32[2,1,256,128]{3,2,1,0:T(8,128)S(1)}, f32[2,1,256,128]{3,2,1,0:T(8,128)S(1)}, u32[]{:S(2)}, u32[]{:S(2)}) collective-permute-start(f32[2,1,256,128]{3,2,1,0:T(8,128)S(1)} %shard_map.83.refs_2_), channel_id=1, source_target_pairs={{0,8},{4,12},{8,0},{12,4},{1,9},{5,13},{9,1},{13,5},{2,10},{6,14},... | collective-permute-start | bytes 786440 | tf_op jit(solution)/shard_map/ppermute | solution.py:22
  75.1 31.5 %collective-permute-start.18 = (f32[2,1,256,128]{3,2,1,0:T(8,128)S(1)}, f32[2,1,256,128]{3,2,1,0:T(8,128)S(1)}, u32[]{:S(2)}, u32[]{:S(2)}) collective-permute-start(f32[2,1,256,128]{3,2,1,0:T(8,128)S(1)} %shard_map.83.refs_2_), channel_id=1, source_target_pairs={{0,4},{4,0},{8,12},{12,8},{1,5},{5,1},{9,13},{13,9},{2,6},{6,2},{1... | collective-permute-start | bytes 786440 | tf_op jit(solution)/shard_map/ppermute | solution.py:22
  76.4 24.5 %collective-permute-start.8 = (f32[2,1,256,128]{3,2,1,0:T(8,128)S(1)}, f32[2,1,256,128]{3,2,1,0:T(8,128)S(1)}, u32[]{:S(2)}, u32[]{:S(2)}) collective-permute-start(f32[2,1,256,128]{3,2,1,0:T(8,128)S(1)} %shard_map.82.refs_3_), channel_id=1, source_target_pairs={{0,8},{4,12},{8,0},{12,4},{1,9},{5,13},{9,1},{13,5},{2,10},{6,14},... | collective-permute-start | bytes 786440 | tf_op jit(solution)/shard_map/ppermute | solution.py:22
  76.9 34.7 %collective-permute-start.15 = (f32[2,1,256,128]{3,2,1,0:T(8,128)S(1)}, f32[2,1,256,128]{3,2,1,0:T(8,128)S(1)}, u32[]{:S(2)}, u32[]{:S(2)}) collective-permute-start(f32[2,1,256,128]{3,2,1,0:T(8,128)S(1)} %shard_map.82.refs_3_), channel_id=1, source_target_pairs={{0,4},{4,0},{8,12},{12,8},{1,5},{5,1},{9,13},{13,9},{2,6},{6,2},{1... | collective-permute-start | bytes 786440 | tf_op jit(solution)/shard_map/ppermute | solution.py:22
  89.7 24.6 %collective-permute-start.14 = (f32[2,1,256,128]{3,2,1,0:T(8,128)S(1)}, f32[2,1,256,128]{3,2,1,0:T(8,128)S(1)}, u32[]{:S(2)}, u32[]{:S(2)}) collective-permute-start(f32[2,1,256,128]{3,2,1,0:T(8,128)S(1)} %collective-permute-done.13.refs_2_), channel_id=1, source_target_pairs={{0,4},{4,0},{8,12},{12,8},{1,5},{5,1},{9,13},{13,9},{2,6},{6,2},{1... | collective-permute-start | bytes 786440 | tf_op jit(solution)/shard_map/ppermute | solution.py:22
  100.9 17.3 %collective-permute-start.9 = (f32[2,1,256,128]{3,2,1,0:T(8,128)S(1)}, f32[2,1,256,128]{3,2,1,0:T(8,128)S(1)}, u32[]{:S(2)}, u32[]{:S(2)}) collective-permute-start(f32[2,1,256,128]{3,2,1,0:T(8,128)S(1)} %collective-permute-done.8.refs_2_.refs_3_), channel_id=1, source_target_pairs={{0,4},{4,0},{8,12},{12,8},{1,5},{5,1},{9,13},{13,9},{2,6},{6,2},{1... | collective-permute-start | bytes 786440 | tf_op jit(solution)/shard_map/ppermute | solution.py:22
  119.9 9.2 %collective-permute-start.22 = (f32[2,1,256,128]{3,2,1,0:T(8,128)S(1)}, f32[2,1,256,128]{3,2,1,0:T(8,128)S(1)}, u32[]{:S(2)}, u32[]{:S(2)}) collective-permute-start(f32[2,1,256,128]{3,2,1,0:T(8,128)S(1)} %get-tuple-element.56.refs_9_), channel_id=1, source_target_pairs={{0,2},{1,3},{2,0},{3,1},{4,6},{5,7},{6,4},{7,5},{8,10},{9,11},{10,... | collective-permute-start | bytes 786440 | tf_op jit(solution)/shard_map/ppermute | solution.py:22
  121.4 12.0 %collective-permute-start.19 = (f32[2,1,256,128]{3,2,1,0:T(8,128)S(1)}, f32[2,1,256,128]{3,2,1,0:T(8,128)S(1)}, u32[]{:S(2)}, u32[]{:S(2)}) collective-permute-start(f32[2,1,256,128]{3,2,1,0:T(8,128)S(1)} %get-tuple-element.55.refs_10_), channel_id=1, source_target_pairs={{0,2},{1,3},{2,0},{3,1},{4,6},{5,7},{6,4},{7,5},{8,10},{9,11},{10,... | collective-permute-start | bytes 786440 | tf_op jit(solution)/shard_map/ppermute | solution.py:22
  122.0 17.4 %collective-permute-start.26 = (f32[1,128,256]{2,1,0:T(8,128)S(1)}, f32[1,128,256]{2,1,0:T(8,128)S(1)}, u32[]{:S(2)}, u32[]{:S(2)}) collective-permute-start(f32[1,128,256]{2,1,0:T(8,128)S(1)} %get-tuple-element.61), channel_id=1, source_target_pairs={{4,0},{8,4},{12,8},{5,1},{9,5},{13,9},{6,2},{10,6},{14,10},{7,3},{... | collective-permute-start | bytes 393224 | tf_op jit(solution)/shard_map/ppermute | solution.py:576
  123.5 15.1 %collective-permute-start.23 = (f32[2,1,256,128]{3,2,1,0:T(8,128)S(1)}, f32[2,1,256,128]{3,2,1,0:T(8,128)S(1)}, u32[]{:S(2)}, u32[]{:S(2)}) collective-permute-start(f32[2,1,256,128]{3,2,1,0:T(8,128)S(1)} %get-tuple-element.56.refs_9_), channel_id=1, source_target_pairs={{0,1},{1,0},{2,3},{3,2},{4,5},{5,4},{6,7},{7,6},{8,9},{9,8},{10,11... | collective-permute-start | bytes 786440 | tf_op jit(solution)/shard_map/ppermute | solution.py:22
  123.6 15.8 %collective-permute-start.20 = (f32[2,1,256,128]{3,2,1,0:T(8,128)S(1)}, f32[2,1,256,128]{3,2,1,0:T(8,128)S(1)}, u32[]{:S(2)}, u32[]{:S(2)}) collective-permute-start(f32[2,1,256,128]{3,2,1,0:T(8,128)S(1)} %get-tuple-element.55.refs_10_), channel_id=1, source_target_pairs={{0,1},{1,0},{2,3},{3,2},{4,5},{5,4},{6,7},{7,6},{8,9},{9,8},{10,11... | collective-permute-start | bytes 786440 | tf_op jit(solution)/shard_map/ppermute | solution.py:22
  129.2 9.5 %collective-permute-start.24 = (f32[2,1,256,128]{3,2,1,0:T(8,128)S(1)}, f32[2,1,256,128]{3,2,1,0:T(8,128)S(1)}, u32[]{:S(2)}, u32[]{:S(2)}) collective-permute-start(f32[2,1,256,128]{3,2,1,0:T(8,128)S(1)} %collective-permute-done.22.refs_5_), channel_id=1, source_target_pairs={{0,1},{1,0},{2,3},{3,2},{4,5},{5,4},{6,7},{7,6},{8,9},{9,8},{10,11... | collective-permute-start | bytes 786440 | tf_op jit(solution)/shard_map/ppermute | solution.py:22
  (9 other events, 141.1 us)

commit v10 on v8

--- a/solution.py
+++ b/solution.py
@@ -549,6 +549,11 @@
             far, _, blocks = groups.pop([far for far, _, _ in groups].index(high))
             groups.insert(1, (far, 0, blocks[:1]))
             groups.append((far, 1, blocks[1:]))
+            if final:
+                place = [far for far, _, _ in groups].index(1)
+                blocks = groups.pop(place)[2]
+                for number, block in enumerate(blocks):
+                    groups.insert(1 + number, (1, number, [block]))
         sums = {}
         for far, number, blocks in groups:
             work = ("diag", "upper") if final else ("diag",)

time: 143 us -> 143 us (level)
  starting transfers between devices: 32.1 us -> 26.3 us
  waiting for transfers between devices: 56.9 us -> 61 us
  Pallas kernels: 39.4 us -> 41 us
    ppermute x24, starting transfers between devices: 29.7 us -> 23.8 us  [swapped(): lax.ppermute(x, axis, [(i, i ^ bit) for i in range(lax.axis_size(axis))])]
    ppermute x24, waiting for transfers between devices: 56.9 us -> 61 us  [swapped(): lax.ppermute(x, axis, [(i, i ^ bit) for i in range(lax.axis_size(axis))])]
    pallas_call x15 -> x16, Pallas kernels: 34.6 us -> 36.1 us  [panel(): pl.pallas_call(functools.partial(panel_kernel, local, far, starts, kinds,...]
  transfers between devices with their start and end apart: 27 -> 27, of which waited for: 9 -> 11; matrix products, arithmetic and copies ran while one was open for 6% -> 6% of each run, Pallas kernels for 26% -> 28%
where the time goes in v10:
time: 143 us; the launch traced here: 142 us
  waiting for transfers between devices  61 us (43%)
  Pallas kernels  41 us (29%)
  starting transfers between devices  26.3 us (18%)
  local copies, waits for them, and re-layouts  10.9 us (8%)
  other arithmetic  1.88 us (1%)
    ppermute x24, waiting for transfers between devices, swapped(): lax.ppermute(x, axis, [(i, i ^ bit) for i in range(lax.axis_size(axis))])  61 us
    pallas_call x16, Pallas kernels, panel(): pl.pallas_call(functools.partial(panel_kernel, local, far, starts, kinds,...  36.1 us
    ppermute x24, starting transfers between devices, swapped(): lax.ppermute(x, axis, [(i, i ^ bit) for i in range(lax.axis_size(axis))])  23.8 us
    dynamic_slice x3, local copies, waits for them, and re-layouts, take(): return lax.dynamic_slice(retarded, (0, 0, row, column), (2, 1, B, size))  5.42 us
    unnamed x12, local copies, waits for them, and re-layouts  4.48 us
  transfers between devices with their start and end apart: 27, of which 11 were waited for; matrix products, arithmetic and copies ran while one was open for 6% of the time, Pallas kernels for 28%

profile of v10, /device:TPU:0, one launch (start us, length us, event | category | flops | bytes accessed | tf_op | source)
XLA Modules:
  0.0 142.2 jit_solution(812756321014050399)
XLA Ops:
  0.6 3.1 %collective-permute-start.4 = (f32[2,1,512,128]{3,2,1,0:T(8,128)}, f32[2,1,512,128]{3,2,1,0:T(8,128)S(1)}, u32[]{:S(2)}, u32[]{:S(2)}) collective-permute-start(f32[2,1,512,128]{3,2,1,0:T(8,128)} %contact_ref.1), channel_id=1, source_target_pairs={{0,4},{4,0},{8,12},{12,8},{1,5},{5,1},{9,13},{13,9},{2,6},{6,2},{1... | collective-permute-start | bytes 1572872 | tf_op jit(solution)/shard_map/ppermute | solution.py:22
  5.7 2.7 %collective-permute-start.2 = (f32[2,1,256,128]{3,2,1,0:T(8,128)}, f32[2,1,256,128]{3,2,1,0:T(8,128)}, u32[]{:S(2)}, u32[]{:S(2)}) collective-permute-start(f32[2,1,256,128]{3,2,1,0:T(8,128)} %get-tuple-element.39), channel_id=1, source_target_pairs={{0,8},{4,12},{8,0},{12,4},{1,9},{5,13},{9,1},{13,5},{2,10},{6,14},... | collective-permute-start | bytes 786440 | tf_op jit(solution)/shard_map/ppermute | solution.py:22
  12.9 2.3 %constant_dynamic-slice_fusion.1 = f32[2,1,128,1024]{3,2,1,0:T(8,128)} fusion(f32[2,1,512,2048]{3,2,1,0:T(8,128)} %refs_1_.31, s32[]{:T(128)S(6)} %select_n.90, s32[]{:T(128)S(6)} %select_n.92), kind=kLoop, calls=%fused_computation.6 | loop fusion | bytes 2097160 | tf_op jit(solution)/shard_map/dynamic_slice | solution.py:476
  18.0 3.4 %copy-done = f32[2,1,512,2048]{3,2,1,0:T(8,128)S(1)} copy-done((f32[2,1,512,2048]{3,2,1,0:T(8,128)S(1)}, f32[2,1,512,2048]{3,2,1,0:T(8,128)}, u32[]{:S(2)}) %copy-start) | copy-done | bytes 8388632
  21.4 2.4 %shard_map.76.refs_3_ = f32[4,128,256]{2,1,0:T(8,128)S(1)} custom-call(s32[2]{0:T(128)S(1)} %compare_select_fusion.refs_0_.refs_1_, f32[2,1,512,2048]{3,2,1,0:T(8,128)S(1)} %copy-done, f32[2,1,512,128]{3,2,1,0:T(8,128)S(1)} %get-tuple-element.35.refs_2_), custom_call_target="tpu_custom_call" | custom-call | flops 1610612736 | bytes 2097152 | tf_op jit(solution)/shard_map/pallas_call | solution.py:308
  23.9 4.7 %collective-permute-start.3 = (f32[2,1,256,128]{3,2,1,0:T(8,128)}, f32[2,1,256,128]{3,2,1,0:T(8,128)S(1)}, u32[]{:S(2)}, u32[]{:S(2)}) collective-permute-start(f32[2,1,256,128]{3,2,1,0:T(8,128)} %collective-permute-done.2.refs_2_), channel_id=1, source_target_pairs={{0,4},{4,0},{8,12},{12,8},{1,5},{5,1},{9,13},{13,9},{2,6},{6,2},{1... | collective-permute-start | bytes 786440 | tf_op jit(solution)/shard_map/ppermute | solution.py:22
  30.7 2.3 %collective-permute-done.refs_2_ = f32[2,1,256,128]{3,2,1,0:T(8,128)S(1)} collective-permute-done((f32[2,1,256,128]{3,2,1,0:T(8,128)}, f32[2,1,256,128]{3,2,1,0:T(8,128)S(1)}, u32[]{:S(2)}, u32[]{:S(2)}) %collective-permute-start) | collective-permute-done | bytes 262176 | tf_op jit(solution)/shard_map/ppermute | solution.py:22
  32.9 2.5 %shard_map.78.refs_3_ = f32[4,128,256]{2,1,0:T(8,128)S(1)} custom-call(s32[2]{0:T(128)S(1)} %compare_select_fusion.refs_0_.refs_1_, f32[2,1,512,2048]{3,2,1,0:T(8,128)S(1)} %copy-done, f32[2,1,512,128]{3,2,1,0:T(8,128)S(1)} %collective-permute-done.4.refs_2_, f32[4,128,256]{2,1,0:T(8,128)S(1)} %shard_map.77.refs_3_), custom_call_target="tpu_custom_call", output_to_operand_aliasing={{}: (3, {})} | custom-call | flops 1610612736 | bytes 2097152 | tf_op jit(solution)/shard_map/pallas_call | solution.py:308
  37.1 13.3 %collective-permute-done.3.refs_2_ = f32[2,1,256,128]{3,2,1,0:T(8,128)S(1)} collective-permute-done((f32[2,1,256,128]{3,2,1,0:T(8,128)}, f32[2,1,256,128]{3,2,1,0:T(8,128)S(1)}, u32[]{:S(2)}, u32[]{:S(2)}) %collective-permute-start.3) | collective-permute-done | bytes 262176 | tf_op jit(solution)/shard_map/ppermute | solution.py:22
  52.2 3.1 %collective-permute-done.1.refs_2_ = f32[2,1,256,128]{3,2,1,0:T(8,128)S(1)} collective-permute-done((f32[2,1,256,128]{3,2,1,0:T(8,128)S(1)}, f32[2,1,256,128]{3,2,1,0:T(8,128)S(1)}, u32[]{:S(2)}, u32[]{:S(2)}) %collective-permute-start.1) | collective-permute-done | bytes 262176 | tf_op jit(solution)/shard_map/ppermute | solution.py:22
  59.1 7.1 %collective-permute-done.10.refs_5_ = f32[2,1,256,128]{3,2,1,0:T(8,128)S(1)} collective-permute-done((f32[2,1,256,128]{3,2,1,0:T(8,128)S(1)}, f32[2,1,256,128]{3,2,1,0:T(8,128)S(1)}, u32[]{:S(2)}, u32[]{:S(2)}) %collective-permute-start.10) | collective-permute-done | bytes 262176 | tf_op jit(solution)/shard_map/ppermute | solution.py:22
  66.7 3.4 %collective-permute-done.5.refs_5_ = f32[2,1,256,128]{3,2,1,0:T(8,128)S(1)} collective-permute-done((f32[2,1,256,128]{3,2,1,0:T(8,128)S(1)}, f32[2,1,256,128]{3,2,1,0:T(8,128)S(1)}, u32[]{:S(2)}, u32[]{:S(2)}) %collective-permute-start.5) | collective-permute-done | bytes 262176 | tf_op jit(solution)/shard_map/ppermute | solution.py:22
  72.5 2.5 %collective-permute-start.13 = (f32[2,1,256,128]{3,2,1,0:T(8,128)S(1)}, f32[2,1,256,128]{3,2,1,0:T(8,128)S(1)}, u32[]{:S(2)}, u32[]{:S(2)}) collective-permute-start(f32[2,1,256,128]{3,2,1,0:T(8,128)S(1)} %shard_map.83.refs_2_), channel_id=1, source_target_pairs={{0,8},{4,12},{8,0},{12,4},{1,9},{5,13},{9,1},{13,5},{2,10},{6,14},... | collective-permute-start | bytes 786440 | tf_op jit(solution)/shard_map/ppermute | solution.py:22
  76.8 3.2 %shard_map.84 = (f32[4,128,256]{2,1,0:T(8,128)S(1)}, f32[3,128,256]{2,1,0:T(8,128)S(1)}) custom-call(s32[2]{0:T(128)S(1)} %compare_select_fusion.refs_0_.refs_1_, f32[2,1,512,2048]{3,2,1,0:T(8,128)S(1)} %bitcast.11, f32[2,1,256,128]{3,2,1,0:T(8,128)S(1)} %shard_map.83.refs_2_, f32[2,1,256,128]{3,2,1,0:T(8,128)S(1)} %shard_map.82.refs_3_), custom_call_target="tpu_custom_call" | custom-call | flops 2415919104 | bytes 2097152 | tf_op jit(solution)/shard_map/pallas_call | solution.py:308
  81.6 2.2 %shard_map.85 = (f32[1,128,256]{2,1,0:T(8,128)S(1)}, f32[1,128,256]{2,1,0:T(8,128)S(1)}) custom-call(s32[2]{0:T(128)S(1)} %compare_select_fusion.refs_0_.refs_1_, f32[2,1,512,2048]{3,2,1,0:T(8,128)S(1)} %bitcast.11, f32[2,1,256,128]{3,2,1,0:T(8,128)S(1)} %shard_map.83.refs_2_, f32[2,1,256,128]{3,2,1,0:T(8,128)S(1)} %shard_map.82.refs_3_, ...), custom_call_target="tpu_custom_call" | custom-call | flops 603979776 | bytes 2097152 | tf_op jit(solution)/shard_map/pallas_call | solution.py:308
  83.8 4.5 %collective-permute-done.13.refs_2_ = f32[2,1,256,128]{3,2,1,0:T(8,128)S(1)} collective-permute-done((f32[2,1,256,128]{3,2,1,0:T(8,128)S(1)}, f32[2,1,256,128]{3,2,1,0:T(8,128)S(1)}, u32[]{:S(2)}, u32[]{:S(2)}) %collective-permute-start.13) | collective-permute-done | bytes 262176 | tf_op jit(solution)/shard_map/ppermute | solution.py:22
  88.3 10.1 %collective-permute-done.8.refs_2_.refs_3_ = f32[2,1,256,128]{3,2,1,0:T(8,128)S(1)} collective-permute-done((f32[2,1,256,128]{3,2,1,0:T(8,128)S(1)}, f32[2,1,256,128]{3,2,1,0:T(8,128)S(1)}, u32[]{:S(2)}, u32[]{:S(2)}) %collective-permute-start.8) | collective-permute-done | bytes 262176 | tf_op jit(solution)/shard_map/ppermute | solution.py:22
  99.6 2.8 %shard_map.86 = (f32[4,128,256]{2,1,0:T(8,128)S(1)}, f32[3,128,256]{2,1,0:T(8,128)S(1)}, f32[1,128,256]{2,1,0:T(8,128)S(1)}, f32[1,128,256]{2,1,0:T(8,128)S(1)}) custom-call(s32[2]{0:T(128)S(1)} %compare_select_fusion.refs_0_.refs_1_, f32[2,1,512,2048]{3,2,1,0:T(8,128)S(1)} %bitcast.11, ...), custom_call_target="tpu_custom_call", output_to_operand_aliasing={{0}: (4, {}), {1}: (5, {}), {2}: (6, {}), {3}: (7, {})} | custom-call | flops 2013265920 | bytes 1048576 | tf_op jit(solution)/shard_map/pallas_call | solution.py:308
  102.4 2.8 %shard_map.87 = (f32[4,128,256]{2,1,0:T(8,128)S(1)}, f32[3,128,256]{2,1,0:T(8,128)S(1)}, f32[1,128,256]{2,1,0:T(8,128)S(1)}, f32[1,128,256]{2,1,0:T(8,128)S(1)}) custom-call(s32[2]{0:T(128)S(1)} %compare_select_fusion.refs_0_.refs_1_, f32[2,1,512,2048]{3,2,1,0:T(8,128)S(1)} %bitcast.11, ...), custom_call_target="tpu_custom_call", output_to_operand_aliasing={{0}: (5, {}), {1}: (6, {}), {2}: (7, {}), {3}: (8, {})} | custom-call | flops 2013265920 | bytes 1048576 | tf_op jit(solution)/shard_map/pallas_call | solution.py:308
  109.5 4.4 %collective-permute-done.14.refs_2_ = f32[2,1,256,128]{3,2,1,0:T(8,128)S(1)} collective-permute-done((f32[2,1,256,128]{3,2,1,0:T(8,128)S(1)}, f32[2,1,256,128]{3,2,1,0:T(8,128)S(1)}, u32[]{:S(2)}, u32[]{:S(2)}) %collective-permute-start.14) | collective-permute-done | bytes 262176 | tf_op jit(solution)/shard_map/ppermute | solution.py:22
  115.6 3.4 %collective-permute-done.9.refs_2_.refs_3_ = f32[2,1,256,128]{3,2,1,0:T(8,128)S(1)} collective-permute-done((f32[2,1,256,128]{3,2,1,0:T(8,128)S(1)}, f32[2,1,256,128]{3,2,1,0:T(8,128)S(1)}, u32[]{:S(2)}, u32[]{:S(2)}) %collective-permute-start.9) | collective-permute-done | bytes 262176 | tf_op jit(solution)/shard_map/ppermute | solution.py:22
  124.9 5.1 %collective-permute-done.22.refs_5_ = f32[2,1,256,128]{3,2,1,0:T(8,128)S(1)} collective-permute-done((f32[2,1,256,128]{3,2,1,0:T(8,128)S(1)}, f32[2,1,256,128]{3,2,1,0:T(8,128)S(1)}, u32[]{:S(2)}, u32[]{:S(2)}) %collective-permute-start.22) | collective-permute-done | bytes 262176 | tf_op jit(solution)/shard_map/ppermute | solution.py:22
  130.0 4.3 %collective-permute-done.19.refs_5_ = f32[2,1,256,128]{3,2,1,0:T(8,128)S(1)} collective-permute-done((f32[2,1,256,128]{3,2,1,0:T(8,128)S(1)}, f32[2,1,256,128]{3,2,1,0:T(8,128)S(1)}, u32[]{:S(2)}, u32[]{:S(2)}) %collective-permute-start.19) | collective-permute-done | bytes 262176 | tf_op jit(solution)/shard_map/ppermute | solution.py:22
  134.3 3.8 %shard_map.93 = (f32[2,1,512,128]{3,2,1,0:T(8,128)}, f32[1,128,256]{2,1,0:T(8,128)S(1)}) custom-call(s32[2]{0:T(128)S(1)} %compare_select_fusion.refs_0_.refs_1_, f32[2,1,512,2048]{3,2,1,0:T(8,128)S(1)} %bitcast.11, f32[2,1,256,128]{3,2,1,0:T(8,128)S(1)} %collective-permute-done.14.refs_2_, ...), custom_call_target="tpu_custom_call", output_to_operand_aliasing={{1}: (6, {})} | custom-call | flops 2415919104 | bytes 2097152 | tf_op jit(solution)/shard_map/pallas_call | solution.py:308
  (77 shorter events, 41.8 us)
Async XLA Ops:
  0.6 32.3 %collective-permute-start.4 = (f32[2,1,512,128]{3,2,1,0:T(8,128)}, f32[2,1,512,128]{3,2,1,0:T(8,128)S(1)}, u32[]{:S(2)}, u32[]{:S(2)}) collective-permute-start(f32[2,1,512,128]{3,2,1,0:T(8,128)} %contact_ref.1), channel_id=1, source_target_pairs={{0,4},{4,0},{8,12},{12,8},{1,5},{5,1},{9,13},{13,9},{2,6},{6,2},{1... | collective-permute-start | bytes 1572872 | tf_op jit(solution)/shard_map/ppermute | solution.py:22
  5.7 18.1 %collective-permute-start.2 = (f32[2,1,256,128]{3,2,1,0:T(8,128)}, f32[2,1,256,128]{3,2,1,0:T(8,128)}, u32[]{:S(2)}, u32[]{:S(2)}) collective-permute-start(f32[2,1,256,128]{3,2,1,0:T(8,128)} %get-tuple-element.39), channel_id=1, source_target_pairs={{0,8},{4,12},{8,0},{12,4},{1,9},{5,13},{9,1},{13,5},{2,10},{6,14},... | collective-permute-start | bytes 786440 | tf_op jit(solution)/shard_map/ppermute | solution.py:22
  8.4 24.6 %collective-permute-start = (f32[2,1,256,128]{3,2,1,0:T(8,128)}, f32[2,1,256,128]{3,2,1,0:T(8,128)S(1)}, u32[]{:S(2)}, u32[]{:S(2)}) collective-permute-start(f32[2,1,256,128]{3,2,1,0:T(8,128)} %get-tuple-element.38), channel_id=1, source_target_pairs={{0,8},{4,12},{8,0},{12,4},{1,9},{5,13},{9,1},{13,5},{2,10},{6,14},... | collective-permute-start | bytes 786440 | tf_op jit(solution)/shard_map/ppermute | solution.py:22
  12.7 63.6 %collective-permute-start.16 = (f32[2,1,128,768]{3,2,1,0:T(8,128)}, f32[2,1,128,768]{3,2,1,0:T(8,128)S(1)}, u32[]{:S(2)}, u32[]{:S(2)}) collective-permute-start(f32[2,1,128,768]{3,2,1,0:T(8,128)} %pad_maximum_fusion), channel_id=1, source_target_pairs={{0,4},{4,0},{8,12},{12,8},{1,5},{5,1},{9,13},{13,9},{2,6},{6,2},{1... | collective-permute-start | bytes 2359304 | tf_op jit(solution)/shard_map/ppermute | solution.py:495
  15.3 64.7 %collective-permute-start.17 = (f32[2,1,128,1024]{3,2,1,0:T(8,128)}, f32[2,1,128,1024]{3,2,1,0:T(8,128)S(1)}, u32[]{:S(2)}, u32[]{:S(2)}) collective-permute-start(f32[2,1,128,1024]{3,2,1,0:T(8,128)} %constant_dynamic-slice_fusion.1), channel_id=1, source_target_pairs={{4,8},{8,4},{5,9},{9,5},{6,10},{10,6},{7,11},{11,7},{20,24},{24,20... | collective-permute-start | bytes 3145736 | tf_op jit(solution)/shard_map/ppermute | solution.py:495
  23.9 26.6 %collective-permute-start.3 = (f32[2,1,256,128]{3,2,1,0:T(8,128)}, f32[2,1,256,128]{3,2,1,0:T(8,128)S(1)}, u32[]{:S(2)}, u32[]{:S(2)}) collective-permute-start(f32[2,1,256,128]{3,2,1,0:T(8,128)} %collective-permute-done.2.refs_2_), channel_id=1, source_target_pairs={{0,4},{4,0},{8,12},{12,8},{1,5},{5,1},{9,13},{13,9},{2,6},{6,2},{1... | collective-permute-start | bytes 786440 | tf_op jit(solution)/shard_map/ppermute | solution.py:22
  32.9 22.3 %collective-permute-start.1 = (f32[2,1,256,128]{3,2,1,0:T(8,128)S(1)}, f32[2,1,256,128]{3,2,1,0:T(8,128)S(1)}, u32[]{:S(2)}, u32[]{:S(2)}) collective-permute-start(f32[2,1,256,128]{3,2,1,0:T(8,128)S(1)} %collective-permute-done.refs_2_), channel_id=1, source_target_pairs={{0,4},{4,0},{8,12},{12,8},{1,5},{5,1},{9,13},{13,9},{2,6},{6,2},{1... | collective-permute-start | bytes 786440 | tf_op jit(solution)/shard_map/ppermute | solution.py:22
  57.0 9.2 %collective-permute-start.10 = (f32[2,1,256,128]{3,2,1,0:T(8,128)S(1)}, f32[2,1,256,128]{3,2,1,0:T(8,128)S(1)}, u32[]{:S(2)}, u32[]{:S(2)}) collective-permute-start(f32[2,1,256,128]{3,2,1,0:T(8,128)S(1)} %get-tuple-element.41), channel_id=1, source_target_pairs={{0,2},{1,3},{2,0},{3,1},{4,6},{5,7},{6,4},{7,5},{8,10},{9,11},{10,... | collective-permute-start | bytes 786440 | tf_op jit(solution)/shard_map/ppermute | solution.py:22
  58.7 7.5 %collective-permute-start.11 = (f32[2,1,256,128]{3,2,1,0:T(8,128)S(1)}, f32[2,1,256,128]{3,2,1,0:T(8,128)S(1)}, u32[]{:S(2)}, u32[]{:S(2)}) collective-permute-start(f32[2,1,256,128]{3,2,1,0:T(8,128)S(1)} %get-tuple-element.41), channel_id=1, source_target_pairs={{0,1},{1,0},{2,3},{3,2},{4,5},{5,4},{6,7},{7,6},{8,9},{9,8},{10,11... | collective-permute-start | bytes 786440 | tf_op jit(solution)/shard_map/ppermute | solution.py:22
  58.7 11.4 %collective-permute-start.5 = (f32[2,1,256,128]{3,2,1,0:T(8,128)S(1)}, f32[2,1,256,128]{3,2,1,0:T(8,128)S(1)}, u32[]{:S(2)}, u32[]{:S(2)}) collective-permute-start(f32[2,1,256,128]{3,2,1,0:T(8,128)S(1)} %get-tuple-element.40), channel_id=1, source_target_pairs={{0,2},{1,3},{2,0},{3,1},{4,6},{5,7},{6,4},{7,5},{8,10},{9,11},{10,... | collective-permute-start | bytes 786440 | tf_op jit(solution)/shard_map/ppermute | solution.py:22
  66.2 6.3 %collective-permute-start.6 = (f32[2,1,256,128]{3,2,1,0:T(8,128)S(1)}, f32[2,1,256,128]{3,2,1,0:T(8,128)S(1)}, u32[]{:S(2)}, u32[]{:S(2)}) collective-permute-start(f32[2,1,256,128]{3,2,1,0:T(8,128)S(1)} %get-tuple-element.40), channel_id=1, source_target_pairs={{0,1},{1,0},{2,3},{3,2},{4,5},{5,4},{6,7},{7,6},{8,9},{9,8},{10,11... | collective-permute-start | bytes 786440 | tf_op jit(solution)/shard_map/ppermute | solution.py:22
  70.9 28.7 %collective-permute-start.18 = (f32[2,1,256,128]{3,2,1,0:T(8,128)S(1)}, f32[2,1,256,128]{3,2,1,0:T(8,128)S(1)}, u32[]{:S(2)}, u32[]{:S(2)}) collective-permute-start(f32[2,1,256,128]{3,2,1,0:T(8,128)S(1)} %shard_map.83.refs_2_), channel_id=1, source_target_pairs={{0,4},{4,0},{8,12},{12,8},{1,5},{5,1},{9,13},{13,9},{2,6},{6,2},{1... | collective-permute-start | bytes 786440 | tf_op jit(solution)/shard_map/ppermute | solution.py:22
  72.5 15.8 %collective-permute-start.13 = (f32[2,1,256,128]{3,2,1,0:T(8,128)S(1)}, f32[2,1,256,128]{3,2,1,0:T(8,128)S(1)}, u32[]{:S(2)}, u32[]{:S(2)}) collective-permute-start(f32[2,1,256,128]{3,2,1,0:T(8,128)S(1)} %shard_map.83.refs_2_), channel_id=1, source_target_pairs={{0,8},{4,12},{8,0},{12,4},{1,9},{5,13},{9,1},{13,5},{2,10},{6,14},... | collective-permute-start | bytes 786440 | tf_op jit(solution)/shard_map/ppermute | solution.py:22
  75.8 26.6 %collective-permute-start.15 = (f32[2,1,256,128]{3,2,1,0:T(8,128)S(1)}, f32[2,1,256,128]{3,2,1,0:T(8,128)S(1)}, u32[]{:S(2)}, u32[]{:S(2)}) collective-permute-start(f32[2,1,256,128]{3,2,1,0:T(8,128)S(1)} %shard_map.82.refs_3_), channel_id=1, source_target_pairs={{0,4},{4,0},{8,12},{12,8},{1,5},{5,1},{9,13},{13,9},{2,6},{6,2},{1... | collective-permute-start | bytes 786440 | tf_op jit(solution)/shard_map/ppermute | solution.py:22
  76.4 22.1 %collective-permute-start.8 = (f32[2,1,256,128]{3,2,1,0:T(8,128)S(1)}, f32[2,1,256,128]{3,2,1,0:T(8,128)S(1)}, u32[]{:S(2)}, u32[]{:S(2)}) collective-permute-start(f32[2,1,256,128]{3,2,1,0:T(8,128)S(1)} %shard_map.82.refs_3_), channel_id=1, source_target_pairs={{0,8},{4,12},{8,0},{12,4},{1,9},{5,13},{9,1},{13,5},{2,10},{6,14},... | collective-permute-start | bytes 786440 | tf_op jit(solution)/shard_map/ppermute | solution.py:22
  80.0 44.4 %collective-permute-start.25 = (f32[2,1,128,512]{3,2,1,0:T(8,128)S(1)}, f32[2,1,128,512]{3,2,1,0:T(8,128)S(1)}, u32[]{:S(2)}, u32[]{:S(2)}) collective-permute-start(f32[2,1,128,512]{3,2,1,0:T(8,128)S(1)} %copy-done.3), channel_id=1, source_target_pairs={{0,4},{4,0},{8,12},{12,8},{1,5},{5,1},{9,13},{13,9},{2,6},{6,2},{1... | collective-permute-start | bytes 1572872 | tf_op jit(solution)/shard_map/ppermute | solution.py:22
  88.3 25.5 %collective-permute-start.14 = (f32[2,1,256,128]{3,2,1,0:T(8,128)S(1)}, f32[2,1,256,128]{3,2,1,0:T(8,128)S(1)}, u32[]{:S(2)}, u32[]{:S(2)}) collective-permute-start(f32[2,1,256,128]{3,2,1,0:T(8,128)S(1)} %collective-permute-done.13.refs_2_), channel_id=1, source_target_pairs={{0,4},{4,0},{8,12},{12,8},{1,5},{5,1},{9,13},{13,9},{2,6},{6,2},{1... | collective-permute-start | bytes 786440 | tf_op jit(solution)/shard_map/ppermute | solution.py:22
  98.5 20.5 %collective-permute-start.9 = (f32[2,1,256,128]{3,2,1,0:T(8,128)S(1)}, f32[2,1,256,128]{3,2,1,0:T(8,128)S(1)}, u32[]{:S(2)}, u32[]{:S(2)}) collective-permute-start(f32[2,1,256,128]{3,2,1,0:T(8,128)S(1)} %collective-permute-done.8.refs_2_.refs_3_), channel_id=1, source_target_pairs={{0,4},{4,0},{8,12},{12,8},{1,5},{5,1},{9,13},{13,9},{2,6},{6,2},{1... | collective-permute-start | bytes 786440 | tf_op jit(solution)/shard_map/ppermute | solution.py:22
  120.8 9.2 %collective-permute-start.22 = (f32[2,1,256,128]{3,2,1,0:T(8,128)S(1)}, f32[2,1,256,128]{3,2,1,0:T(8,128)S(1)}, u32[]{:S(2)}, u32[]{:S(2)}) collective-permute-start(f32[2,1,256,128]{3,2,1,0:T(8,128)S(1)} %get-tuple-element.56.refs_9_), channel_id=1, source_target_pairs={{0,2},{1,3},{2,0},{3,1},{4,6},{5,7},{6,4},{7,5},{8,10},{9,11},{10,... | collective-permute-start | bytes 786440 | tf_op jit(solution)/shard_map/ppermute | solution.py:22
  122.2 12.1 %collective-permute-start.19 = (f32[2,1,256,128]{3,2,1,0:T(8,128)S(1)}, f32[2,1,256,128]{3,2,1,0:T(8,128)S(1)}, u32[]{:S(2)}, u32[]{:S(2)}) collective-permute-start(f32[2,1,256,128]{3,2,1,0:T(8,128)S(1)} %get-tuple-element.55.refs_10_), channel_id=1, source_target_pairs={{0,2},{1,3},{2,0},{3,1},{4,6},{5,7},{6,4},{7,5},{8,10},{9,11},{10,... | collective-permute-start | bytes 786440 | tf_op jit(solution)/shard_map/ppermute | solution.py:22
  122.8 17.5 %collective-permute-start.26 = (f32[1,128,256]{2,1,0:T(8,128)S(1)}, f32[1,128,256]{2,1,0:T(8,128)S(1)}, u32[]{:S(2)}, u32[]{:S(2)}) collective-permute-start(f32[1,128,256]{2,1,0:T(8,128)S(1)} %get-tuple-element.61), channel_id=1, source_target_pairs={{4,0},{8,4},{12,8},{5,1},{9,5},{13,9},{6,2},{10,6},{14,10},{7,3},{... | collective-permute-start | bytes 393224 | tf_op jit(solution)/shard_map/ppermute | solution.py:576
  124.4 15.2 %collective-permute-start.23 = (f32[2,1,256,128]{3,2,1,0:T(8,128)S(1)}, f32[2,1,256,128]{3,2,1,0:T(8,128)S(1)}, u32[]{:S(2)}, u32[]{:S(2)}) collective-permute-start(f32[2,1,256,128]{3,2,1,0:T(8,128)S(1)} %get-tuple-element.56.refs_9_), channel_id=1, source_target_pairs={{0,1},{1,0},{2,3},{3,2},{4,5},{5,4},{6,7},{7,6},{8,9},{9,8},{10,11... | collective-permute-start | bytes 786440 | tf_op jit(solution)/shard_map/ppermute | solution.py:22
  124.4 15.9 %collective-permute-start.20 = (f32[2,1,256,128]{3,2,1,0:T(8,128)S(1)}, f32[2,1,256,128]{3,2,1,0:T(8,128)S(1)}, u32[]{:S(2)}, u32[]{:S(2)}) collective-permute-start(f32[2,1,256,128]{3,2,1,0:T(8,128)S(1)} %get-tuple-element.55.refs_10_), channel_id=1, source_target_pairs={{0,1},{1,0},{2,3},{3,2},{4,5},{5,4},{6,7},{7,6},{8,9},{9,8},{10,11... | collective-permute-start | bytes 786440 | tf_op jit(solution)/shard_map/ppermute | solution.py:22
  130.0 9.5 %collective-permute-start.24 = (f32[2,1,256,128]{3,2,1,0:T(8,128)S(1)}, f32[2,1,256,128]{3,2,1,0:T(8,128)S(1)}, u32[]{:S(2)}, u32[]{:S(2)}) collective-permute-start(f32[2,1,256,128]{3,2,1,0:T(8,128)S(1)} %collective-permute-done.22.refs_5_), channel_id=1, source_target_pairs={{0,1},{1,0},{2,3},{3,2},{4,5},{5,4},{6,7},{7,6},{8,9},{9,8},{10,11... | collective-permute-start | bytes 786440 | tf_op jit(solution)/shard_map/ppermute | solution.py:22
  (9 other events, 126.3 us)

commit v11 on v9

--- a/solution.py
+++ b/solution.py
@@ -116,7 +116,7 @@
     return devices == 4 and local % 2 == 0
 
 
-def panel_kernel(local, far, starts, kinds, names, first, last, chunks, devices, scale, *refs):
+def panel_kernel(local, far, starts, kinds, names, first, last, span, devices, scale, *refs):
     refs = list(refs)
     at_ref, g_ref = refs[:2]
     piece_refs, refs = refs[2 : 2 + len(starts)], refs[2 + len(starts) :]
@@ -133,6 +133,7 @@
     half = devices * local // 2
     whole = "diag" in kinds or "upper" in kinds
     low = 0 if whole else (local - 1) * B
+    top, end = (0, local) if span is None else span
 
     greens, sigmas, products, columns = [], [], [], []
     for start, s_ref in zip(starts, piece_refs):
@@ -155,10 +156,10 @@
             ))
             if whole:
                 greens[-1] = functools.partial(
-                    lambda whole, low, high: rows_of(whole, low, high - low),
-                    greens[-1](0, local * B),
+                    lambda whole, low, high: rows_of(whole, low - top * B, high - low),
+                    greens[-1](top * B, end * B),
                 )
-                products.append(split(times(greens[-1](0, local * B), sigmas[-1])))
+                products.append(split(times(greens[-1](top * B, end * B), sigmas[-1])))
 
     def old(kind, i):
         return ins[kind][i] if kind in ins else 0.0
@@ -168,19 +169,19 @@
         ref[1, 0, row * B : (row + 1) * B] = value[:, B:].T * scale
 
     diag, upper = "diag" in kinds, "upper" in kinds
-    for i in range(local):
+    for i in range(top, end):
         start = 0 if diag else 1
         size = int(diag) + int(upper and i < local - 1)
         if not size:
             continue
         terms = against(
             [green((i + start) * B, (i + start + size) * B) for green in greens],
-            [rows_of(product, i * B, B) for product in products],
+            [rows_of(product, (i - top) * B, B) for product in products],
         )
         if diag:
             value = old("diag", i) + terms[:B]
             if last:
-                put(outs[i * chunks // local], i % (local // chunks), value)
+                put(outs[0], i - top, value)
             else:
                 outs["diag"][i] = value
         if upper and i < local - 1:
@@ -267,7 +268,7 @@
         )
 
 
-def panel(at, green, far, pieces, carry, edges, kinds, last, chunks=1):
+def panel(at, green, far, pieces, carry, edges, kinds, last, span=None):
     rows = green.shape[2]
     local = rows // B
     devices = lax.axis_size("pan")
@@ -301,8 +302,7 @@
         tall = jax.ShapeDtypeStruct((2, 1, rows, B), F32)
         shapes["upper"] = tall
         if "diag" in kinds:
-            part = jax.ShapeDtypeStruct((2, 1, rows // chunks, B), F32)
-            shapes = {number: part for number in range(chunks)}
+            shapes = {"diag": jax.ShapeDtypeStruct((2, 1, (span[1] - span[0]) * B, B), F32)}
     full = "diag" in kinds or "upper" in kinds
     work = 3 * 2 * (2 * B) * (2 * B) * many * (rows if full else B) * (1 + len(kinds))
     out = pl.pallas_call(
@@ -315,7 +315,7 @@
             names,
             first,
             last,
-            chunks,
+            span,
             devices,
             1.0 / math.sqrt(B),
         ),
@@ -328,8 +328,6 @@
             flops=work, bytes_accessed=8 * rows * B * many, transcendentals=0
         ),
     )(*operands)
-    if last and "diag" in kinds:
-        return {"diag": out}
     return dict(carry, **dict(zip(shapes, out)))
 
 
@@ -563,11 +561,14 @@
                 work += ("over", "back")
             sums = panel(at, retarded, far, blocks, sums, edges, work, False)
         far, blocks = pieces[-1]
-        for number, block in enumerate(blocks):
-            last = number == len(blocks) - 1
-            new = panel(at, retarded, far, [block], sums, edges, ("diag",), last, chunks)
-            sums = dict(sums, **new)
-        found = spread(sums["diag"], "en")
+        for block in blocks[:-1]:
+            sums = panel(at, retarded, far, [block], sums, edges, ("diag",), False)
+        diags = []
+        for number in range(chunks):
+            span = (number * local // chunks, (number + 1) * local // chunks)
+            made = panel(at, retarded, far, blocks[-1:], sums, edges, ("diag",), True, span)
+            diags.append(made["diag"])
+        found = spread(diags, "en")
         settings = (shifts, at, copied, per_row, per_line)
         if not final:
             parts = [phonon(*settings, own[1:], number, chunks) for number, own in enumerate(found)]
@@ -580,7 +581,7 @@
         if far >= high:
             sums = panel(at, retarded, far, blocks, sums, edges, ("over",), False)
     done = [phonon(*settings, own[1:], number, chunks) for number, own in enumerate(found[:-1])]
-    sigma, upper, diag = ending(*settings, found[-1][1:], done, sums["diag"], sums["upper"], sums["over"], above)
+    sigma, upper, diag = ending(*settings, found[-1][1:], done, diags, sums["upper"], sums["over"], above)
     return (diag, upper, sigma)
 
 

time: 142 us -> 141 us (level)
  waiting for transfers between devices: 54.2 us -> 51.4 us
  Pallas kernels: 41 us -> 42.9 us
    ppermute x24, waiting for transfers between devices: 54.2 us -> 51.4 us  [swapped(): lax.ppermute(x, axis, [(i, i ^ bit) for i in range(lax.axis_size(axis))])]
    pallas_call x16 -> x18, Pallas kernels: 36.1 us -> 38 us  [panel(): pl.pallas_call(functools.partial(panel_kernel, local, far, starts, kinds,...]
  transfers between devices with their start and end apart: 27 -> 27, of which waited for: 10 -> 10; matrix products, arithmetic and copies ran while one was open for 6% -> 6% of each run, Pallas kernels for 28% -> 29%
where the time goes in v11:
time: 141 us
  waiting for transfers between devices  51.4 us (36%)
  Pallas kernels  42.9 us (30%)
  starting transfers between devices  32.2 us (23%)
  local copies, waits for them, and re-layouts  11 us (8%)
  other arithmetic  1.88 us (1%)
    ppermute x24, waiting for transfers between devices, swapped(): lax.ppermute(x, axis, [(i, i ^ bit) for i in range(lax.axis_size(axis))])  51.4 us
    pallas_call x18, Pallas kernels, panel(): pl.pallas_call(functools.partial(panel_kernel, local, far, starts, kinds,...  38 us
    ppermute x24, starting transfers between devices, swapped(): lax.ppermute(x, axis, [(i, i ^ bit) for i in range(lax.axis_size(axis))])  29.8 us
    dynamic_slice x3, local copies, waits for them, and re-layouts, take(): return lax.dynamic_slice(retarded, (0, 0, row, column), (2, 1, B, size))  5.43 us
    unnamed x12, local copies, waits for them, and re-layouts  4.48 us
  transfers between devices with their start and end apart: 27, of which 10 were waited for; matrix products, arithmetic and copies ran while one was open for 6% of the time, Pallas kernels for 29%

profile of v11, /device:TPU:0, one launch (start us, length us, event | category | flops | bytes accessed | tf_op | source)
XLA Modules:
  0.0 140.6 jit_solution(11217570169504299837)
XLA Ops:
  0.6 3.1 %collective-permute-start.4 = (f32[2,1,512,128]{3,2,1,0:T(8,128)}, f32[2,1,512,128]{3,2,1,0:T(8,128)S(1)}, u32[]{:S(2)}, u32[]{:S(2)}) collective-permute-start(f32[2,1,512,128]{3,2,1,0:T(8,128)} %contact_ref.1), channel_id=1, source_target_pairs={{0,4},{4,0},{8,12},{12,8},{1,5},{5,1},{9,13},{13,9},{2,6},{6,2},{1... | collective-permute-start | bytes 1572872 | tf_op jit(solution)/shard_map/ppermute | solution.py:22
  5.7 2.7 %collective-permute-start.2 = (f32[2,1,256,128]{3,2,1,0:T(8,128)}, f32[2,1,256,128]{3,2,1,0:T(8,128)}, u32[]{:S(2)}, u32[]{:S(2)}) collective-permute-start(f32[2,1,256,128]{3,2,1,0:T(8,128)} %get-tuple-element.35), channel_id=1, source_target_pairs={{0,8},{4,12},{8,0},{12,4},{1,9},{5,13},{9,1},{13,5},{2,10},{6,14},... | collective-permute-start | bytes 786440 | tf_op jit(solution)/shard_map/ppermute | solution.py:22
  12.9 2.3 %constant_dynamic-slice_fusion.1 = f32[2,1,128,1024]{3,2,1,0:T(8,128)} fusion(f32[2,1,512,2048]{3,2,1,0:T(8,128)} %refs_1_.35, s32[]{:T(128)S(6)} %select_n.90, s32[]{:T(128)S(6)} %select_n.92), kind=kLoop, calls=%fused_computation.6 | loop fusion | bytes 2097160 | tf_op jit(solution)/shard_map/dynamic_slice | solution.py:474
  18.0 3.4 %copy-done = f32[2,1,512,2048]{3,2,1,0:T(8,128)S(1)} copy-done((f32[2,1,512,2048]{3,2,1,0:T(8,128)S(1)}, f32[2,1,512,2048]{3,2,1,0:T(8,128)}, u32[]{:S(2)}) %copy-start) | copy-done | bytes 8388632
  21.4 2.4 %shard_map.76.refs_3_ = f32[4,128,256]{2,1,0:T(8,128)S(1)} custom-call(s32[2]{0:T(128)S(1)} %compare_select_fusion.refs_0_.refs_1_, f32[2,1,512,2048]{3,2,1,0:T(8,128)S(1)} %copy-done, f32[2,1,512,128]{3,2,1,0:T(8,128)S(1)} %get-tuple-element.31.refs_2_), custom_call_target="tpu_custom_call" | custom-call | flops 1610612736 | bytes 2097152 | tf_op jit(solution)/shard_map/pallas_call | solution.py:308
  23.9 4.7 %collective-permute-start.3 = (f32[2,1,256,128]{3,2,1,0:T(8,128)}, f32[2,1,256,128]{3,2,1,0:T(8,128)S(1)}, u32[]{:S(2)}, u32[]{:S(2)}) collective-permute-start(f32[2,1,256,128]{3,2,1,0:T(8,128)} %collective-permute-done.2.refs_2_), channel_id=1, source_target_pairs={{0,4},{4,0},{8,12},{12,8},{1,5},{5,1},{9,13},{13,9},{2,6},{6,2},{1... | collective-permute-start | bytes 786440 | tf_op jit(solution)/shard_map/ppermute | solution.py:22
  30.7 2.3 %collective-permute-done.refs_2_ = f32[2,1,256,128]{3,2,1,0:T(8,128)S(1)} collective-permute-done((f32[2,1,256,128]{3,2,1,0:T(8,128)}, f32[2,1,256,128]{3,2,1,0:T(8,128)S(1)}, u32[]{:S(2)}, u32[]{:S(2)}) %collective-permute-start) | collective-permute-done | bytes 262176 | tf_op jit(solution)/shard_map/ppermute | solution.py:22
  32.9 2.5 %shard_map.78.refs_3_ = f32[4,128,256]{2,1,0:T(8,128)S(1)} custom-call(s32[2]{0:T(128)S(1)} %compare_select_fusion.refs_0_.refs_1_, f32[2,1,512,2048]{3,2,1,0:T(8,128)S(1)} %copy-done, f32[2,1,512,128]{3,2,1,0:T(8,128)S(1)} %collective-permute-done.4.refs_2_, f32[4,128,256]{2,1,0:T(8,128)S(1)} %shard_map.77.refs_3_), custom_call_target="tpu_custom_call", output_to_operand_aliasing={{}: (3, {})} | custom-call | flops 1610612736 | bytes 2097152 | tf_op jit(solution)/shard_map/pallas_call | solution.py:308
  37.1 13.3 %collective-permute-done.3.refs_2_ = f32[2,1,256,128]{3,2,1,0:T(8,128)S(1)} collective-permute-done((f32[2,1,256,128]{3,2,1,0:T(8,128)}, f32[2,1,256,128]{3,2,1,0:T(8,128)S(1)}, u32[]{:S(2)}, u32[]{:S(2)}) %collective-permute-start.3) | collective-permute-done | bytes 262176 | tf_op jit(solution)/shard_map/ppermute | solution.py:22
  52.2 3.1 %collective-permute-done.1.refs_2_ = f32[2,1,256,128]{3,2,1,0:T(8,128)S(1)} collective-permute-done((f32[2,1,256,128]{3,2,1,0:T(8,128)S(1)}, f32[2,1,256,128]{3,2,1,0:T(8,128)S(1)}, u32[]{:S(2)}, u32[]{:S(2)}) %collective-permute-start.1) | collective-permute-done | bytes 262176 | tf_op jit(solution)/shard_map/ppermute | solution.py:22
  60.1 5.3 %collective-permute-done.10.refs_5_ = f32[2,1,256,128]{3,2,1,0:T(8,128)S(1)} collective-permute-done((f32[2,1,256,128]{3,2,1,0:T(8,128)S(1)}, f32[2,1,256,128]{3,2,1,0:T(8,128)S(1)}, u32[]{:S(2)}, u32[]{:S(2)}) %collective-permute-start.10) | collective-permute-done | bytes 262176 | tf_op jit(solution)/shard_map/ppermute | solution.py:22
  65.9 3.8 %collective-permute-done.5.refs_5_ = f32[2,1,256,128]{3,2,1,0:T(8,128)S(1)} collective-permute-done((f32[2,1,256,128]{3,2,1,0:T(8,128)S(1)}, f32[2,1,256,128]{3,2,1,0:T(8,128)S(1)}, u32[]{:S(2)}, u32[]{:S(2)}) %collective-permute-start.5) | collective-permute-done | bytes 262176 | tf_op jit(solution)/shard_map/ppermute | solution.py:22
  72.1 2.6 %collective-permute-start.13 = (f32[2,1,256,128]{3,2,1,0:T(8,128)S(1)}, f32[2,1,256,128]{3,2,1,0:T(8,128)S(1)}, u32[]{:S(2)}, u32[]{:S(2)}) collective-permute-start(f32[2,1,256,128]{3,2,1,0:T(8,128)S(1)} %shard_map.84.refs_2_), channel_id=1, source_target_pairs={{0,8},{4,12},{8,0},{12,4},{1,9},{5,13},{9,1},{13,5},{2,10},{6,14},... | collective-permute-start | bytes 786440 | tf_op jit(solution)/shard_map/ppermute | solution.py:22
  78.0 2.2 %shard_map.87 = (f32[1,128,256]{2,1,0:T(8,128)S(1)}, f32[1,128,256]{2,1,0:T(8,128)S(1)}) custom-call(s32[2]{0:T(128)S(1)} %compare_select_fusion.refs_0_.refs_1_, f32[2,1,512,2048]{3,2,1,0:T(8,128)S(1)} %bitcast.11, f32[2,1,256,128]{3,2,1,0:T(8,128)S(1)} %shard_map.84.refs_2_, f32[2,1,256,128]{3,2,1,0:T(8,128)S(1)} %shard_map.82.refs_3_, ...), custom_call_target="tpu_custom_call" | custom-call | flops 603979776 | bytes 2097152 | tf_op jit(solution)/shard_map/pallas_call | solution.py:308
  80.2 3.2 %shard_map.85 = (f32[4,128,256]{2,1,0:T(8,128)S(1)}, f32[3,128,256]{2,1,0:T(8,128)S(1)}) custom-call(s32[2]{0:T(128)S(1)} %compare_select_fusion.refs_0_.refs_1_, f32[2,1,512,2048]{3,2,1,0:T(8,128)S(1)} %bitcast.11, f32[2,1,256,128]{3,2,1,0:T(8,128)S(1)} %shard_map.84.refs_2_, f32[2,1,256,128]{3,2,1,0:T(8,128)S(1)} %shard_map.82.refs_3_), custom_call_target="tpu_custom_call" | custom-call | flops 2415919104 | bytes 2097152 | tf_op jit(solution)/shard_map/pallas_call | solution.py:308
  83.4 5.9 %collective-permute-done.13.refs_2_ = f32[2,1,256,128]{3,2,1,0:T(8,128)S(1)} collective-permute-done((f32[2,1,256,128]{3,2,1,0:T(8,128)S(1)}, f32[2,1,256,128]{3,2,1,0:T(8,128)S(1)}, u32[]{:S(2)}, u32[]{:S(2)}) %collective-permute-start.13) | collective-permute-done | bytes 262176 | tf_op jit(solution)/shard_map/ppermute | solution.py:22
  89.3 3.5 %collective-permute-start.14 = (f32[2,1,256,128]{3,2,1,0:T(8,128)S(1)}, f32[2,1,256,128]{3,2,1,0:T(8,128)S(1)}, u32[]{:S(2)}, u32[]{:S(2)}) collective-permute-start(f32[2,1,256,128]{3,2,1,0:T(8,128)S(1)} %collective-permute-done.13.refs_2_), channel_id=1, source_target_pairs={{0,4},{4,0},{8,12},{12,8},{1,5},{5,1},{9,13},{13,9},{2,6},{6,2},{1... | collective-permute-start | bytes 786440 | tf_op jit(solution)/shard_map/ppermute | solution.py:22
  92.8 7.7 %collective-permute-done.8.refs_2_.refs_3_ = f32[2,1,256,128]{3,2,1,0:T(8,128)S(1)} collective-permute-done((f32[2,1,256,128]{3,2,1,0:T(8,128)S(1)}, f32[2,1,256,128]{3,2,1,0:T(8,128)S(1)}, u32[]{:S(2)}, u32[]{:S(2)}) %collective-permute-start.8) | collective-permute-done | bytes 262176 | tf_op jit(solution)/shard_map/ppermute | solution.py:22
  100.5 3.5 %collective-permute-start.9 = (f32[2,1,256,128]{3,2,1,0:T(8,128)S(1)}, f32[2,1,256,128]{3,2,1,0:T(8,128)S(1)}, u32[]{:S(2)}, u32[]{:S(2)}) collective-permute-start(f32[2,1,256,128]{3,2,1,0:T(8,128)S(1)} %collective-permute-done.8.refs_2_.refs_3_), channel_id=1, source_target_pairs={{0,4},{4,0},{8,12},{12,8},{1,5},{5,1},{9,13},{13,9},{2,6},{6,2},{1... | collective-permute-start | bytes 786440 | tf_op jit(solution)/shard_map/ppermute | solution.py:22
  106.2 2.8 %shard_map.88 = (f32[4,128,256]{2,1,0:T(8,128)S(1)}, f32[3,128,256]{2,1,0:T(8,128)S(1)}, f32[1,128,256]{2,1,0:T(8,128)S(1)}, f32[1,128,256]{2,1,0:T(8,128)S(1)}) custom-call(s32[2]{0:T(128)S(1)} %compare_select_fusion.refs_0_.refs_1_, f32[2,1,512,2048]{3,2,1,0:T(8,128)S(1)} %bitcast.11, ...), custom_call_target="tpu_custom_call", output_to_operand_aliasing={{0}: (4, {}), {1}: (5, {}), {2}: (6, {}), {3}: (7, {})} | custom-call | flops 2013265920 | bytes 1048576 | tf_op jit(solution)/shard_map/pallas_call | solution.py:308
  111.1 2.8 %shard_map.90 = (f32[4,128,256]{2,1,0:T(8,128)S(1)}, f32[3,128,256]{2,1,0:T(8,128)S(1)}, f32[1,128,256]{2,1,0:T(8,128)S(1)}, f32[1,128,256]{2,1,0:T(8,128)S(1)}) custom-call(s32[2]{0:T(128)S(1)} %compare_select_fusion.refs_0_.refs_1_, f32[2,1,512,2048]{3,2,1,0:T(8,128)S(1)} %bitcast.11, ...), custom_call_target="tpu_custom_call", output_to_operand_aliasing={{0}: (5, {}), {1}: (6, {}), {2}: (7, {}), {3}: (8, {})} | custom-call | flops 2013265920 | bytes 1048576 | tf_op jit(solution)/shard_map/pallas_call | solution.py:308
  124.8 3.6 %collective-permute-done.22.refs_5_ = f32[2,1,256,128]{3,2,1,0:T(8,128)S(1)} collective-permute-done((f32[2,1,256,128]{3,2,1,0:T(8,128)S(1)}, f32[2,1,256,128]{3,2,1,0:T(8,128)S(1)}, u32[]{:S(2)}, u32[]{:S(2)}) %collective-permute-start.22) | collective-permute-done | bytes 262176 | tf_op jit(solution)/shard_map/ppermute | solution.py:22
  128.4 4.2 %collective-permute-done.19.refs_5_ = f32[2,1,256,128]{3,2,1,0:T(8,128)S(1)} collective-permute-done((f32[2,1,256,128]{3,2,1,0:T(8,128)S(1)}, f32[2,1,256,128]{3,2,1,0:T(8,128)S(1)}, u32[]{:S(2)}, u32[]{:S(2)}) %collective-permute-start.19) | collective-permute-done | bytes 262176 | tf_op jit(solution)/shard_map/ppermute | solution.py:22
  132.6 3.8 %shard_map.95 = (f32[2,1,512,128]{3,2,1,0:T(8,128)}, f32[1,128,256]{2,1,0:T(8,128)S(1)}) custom-call(s32[2]{0:T(128)S(1)} %compare_select_fusion.refs_0_.refs_1_, f32[2,1,512,2048]{3,2,1,0:T(8,128)S(1)} %bitcast.11, f32[2,1,256,128]{3,2,1,0:T(8,128)S(1)} %collective-permute-done.14.refs_2_, ...), custom_call_target="tpu_custom_call", output_to_operand_aliasing={{1}: (6, {})} | custom-call | flops 2415919104 | bytes 2097152 | tf_op jit(solution)/shard_map/pallas_call | solution.py:308
  (79 shorter events, 44.8 us)
Async XLA Ops:
  0.6 32.3 %collective-permute-start.4 = (f32[2,1,512,128]{3,2,1,0:T(8,128)}, f32[2,1,512,128]{3,2,1,0:T(8,128)S(1)}, u32[]{:S(2)}, u32[]{:S(2)}) collective-permute-start(f32[2,1,512,128]{3,2,1,0:T(8,128)} %contact_ref.1), channel_id=1, source_target_pairs={{0,4},{4,0},{8,12},{12,8},{1,5},{5,1},{9,13},{13,9},{2,6},{6,2},{1... | collective-permute-start | bytes 1572872 | tf_op jit(solution)/shard_map/ppermute | solution.py:22
  5.7 18.1 %collective-permute-start.2 = (f32[2,1,256,128]{3,2,1,0:T(8,128)}, f32[2,1,256,128]{3,2,1,0:T(8,128)}, u32[]{:S(2)}, u32[]{:S(2)}) collective-permute-start(f32[2,1,256,128]{3,2,1,0:T(8,128)} %get-tuple-element.35), channel_id=1, source_target_pairs={{0,8},{4,12},{8,0},{12,4},{1,9},{5,13},{9,1},{13,5},{2,10},{6,14},... | collective-permute-start | bytes 786440 | tf_op jit(solution)/shard_map/ppermute | solution.py:22
  8.4 24.6 %collective-permute-start = (f32[2,1,256,128]{3,2,1,0:T(8,128)}, f32[2,1,256,128]{3,2,1,0:T(8,128)S(1)}, u32[]{:S(2)}, u32[]{:S(2)}) collective-permute-start(f32[2,1,256,128]{3,2,1,0:T(8,128)} %get-tuple-element.34), channel_id=1, source_target_pairs={{0,8},{4,12},{8,0},{12,4},{1,9},{5,13},{9,1},{13,5},{2,10},{6,14},... | collective-permute-start | bytes 786440 | tf_op jit(solution)/shard_map/ppermute | solution.py:22
  12.7 63.3 %collective-permute-start.16 = (f32[2,1,128,768]{3,2,1,0:T(8,128)}, f32[2,1,128,768]{3,2,1,0:T(8,128)S(1)}, u32[]{:S(2)}, u32[]{:S(2)}) collective-permute-start(f32[2,1,128,768]{3,2,1,0:T(8,128)} %pad_maximum_fusion), channel_id=1, source_target_pairs={{0,4},{4,0},{8,12},{12,8},{1,5},{5,1},{9,13},{13,9},{2,6},{6,2},{1... | collective-permute-start | bytes 2359304 | tf_op jit(solution)/shard_map/ppermute | solution.py:493
  15.3 61.2 %collective-permute-start.17 = (f32[2,1,128,1024]{3,2,1,0:T(8,128)}, f32[2,1,128,1024]{3,2,1,0:T(8,128)S(1)}, u32[]{:S(2)}, u32[]{:S(2)}) collective-permute-start(f32[2,1,128,1024]{3,2,1,0:T(8,128)} %constant_dynamic-slice_fusion.1), channel_id=1, source_target_pairs={{4,8},{8,4},{5,9},{9,5},{6,10},{10,6},{7,11},{11,7},{20,24},{24,20... | collective-permute-start | bytes 3145736 | tf_op jit(solution)/shard_map/ppermute | solution.py:493
  23.9 26.6 %collective-permute-start.3 = (f32[2,1,256,128]{3,2,1,0:T(8,128)}, f32[2,1,256,128]{3,2,1,0:T(8,128)S(1)}, u32[]{:S(2)}, u32[]{:S(2)}) collective-permute-start(f32[2,1,256,128]{3,2,1,0:T(8,128)} %collective-permute-done.2.refs_2_), channel_id=1, source_target_pairs={{0,4},{4,0},{8,12},{12,8},{1,5},{5,1},{9,13},{13,9},{2,6},{6,2},{1... | collective-permute-start | bytes 786440 | tf_op jit(solution)/shard_map/ppermute | solution.py:22
  32.9 22.3 %collective-permute-start.1 = (f32[2,1,256,128]{3,2,1,0:T(8,128)S(1)}, f32[2,1,256,128]{3,2,1,0:T(8,128)S(1)}, u32[]{:S(2)}, u32[]{:S(2)}) collective-permute-start(f32[2,1,256,128]{3,2,1,0:T(8,128)S(1)} %collective-permute-done.refs_2_), channel_id=1, source_target_pairs={{0,4},{4,0},{8,12},{12,8},{1,5},{5,1},{9,13},{13,9},{2,6},{6,2},{1... | collective-permute-start | bytes 786440 | tf_op jit(solution)/shard_map/ppermute | solution.py:22
  56.6 8.8 %collective-permute-start.10 = (f32[2,1,256,128]{3,2,1,0:T(8,128)S(1)}, f32[2,1,256,128]{3,2,1,0:T(8,128)S(1)}, u32[]{:S(2)}, u32[]{:S(2)}) collective-permute-start(f32[2,1,256,128]{3,2,1,0:T(8,128)S(1)} %shard_map.83), channel_id=1, source_target_pairs={{0,2},{1,3},{2,0},{3,1},{4,6},{5,7},{6,4},{7,5},{8,10},{9,11},{10,... | collective-permute-start | bytes 786440 | tf_op jit(solution)/shard_map/ppermute | solution.py:22
  58.3 7.1 %collective-permute-start.11 = (f32[2,1,256,128]{3,2,1,0:T(8,128)S(1)}, f32[2,1,256,128]{3,2,1,0:T(8,128)S(1)}, u32[]{:S(2)}, u32[]{:S(2)}) collective-permute-start(f32[2,1,256,128]{3,2,1,0:T(8,128)S(1)} %shard_map.83), channel_id=1, source_target_pairs={{0,1},{1,0},{2,3},{3,2},{4,5},{5,4},{6,7},{7,6},{8,9},{9,8},{10,11... | collective-permute-start | bytes 786440 | tf_op jit(solution)/shard_map/ppermute | solution.py:22
  59.7 10.1 %collective-permute-start.5 = (f32[2,1,256,128]{3,2,1,0:T(8,128)S(1)}, f32[2,1,256,128]{3,2,1,0:T(8,128)S(1)}, u32[]{:S(2)}, u32[]{:S(2)}) collective-permute-start(f32[2,1,256,128]{3,2,1,0:T(8,128)S(1)} %shard_map.81), channel_id=1, source_target_pairs={{0,2},{1,3},{2,0},{3,1},{4,6},{5,7},{6,4},{7,5},{8,10},{9,11},{10,... | collective-permute-start | bytes 786440 | tf_op jit(solution)/shard_map/ppermute | solution.py:22
  65.4 6.7 %collective-permute-start.6 = (f32[2,1,256,128]{3,2,1,0:T(8,128)S(1)}, f32[2,1,256,128]{3,2,1,0:T(8,128)S(1)}, u32[]{:S(2)}, u32[]{:S(2)}) collective-permute-start(f32[2,1,256,128]{3,2,1,0:T(8,128)S(1)} %shard_map.81), channel_id=1, source_target_pairs={{0,1},{1,0},{2,3},{3,2},{4,5},{5,4},{6,7},{7,6},{8,9},{9,8},{10,11... | collective-permute-start | bytes 786440 | tf_op jit(solution)/shard_map/ppermute | solution.py:22
  69.7 54.5 %collective-permute-start.25 = (f32[2,1,128,512]{3,2,1,0:T(8,128)S(1)}, f32[2,1,128,512]{3,2,1,0:T(8,128)S(1)}, u32[]{:S(2)}, u32[]{:S(2)}) collective-permute-start(f32[2,1,128,512]{3,2,1,0:T(8,128)S(1)} %copy-done.3), channel_id=1, source_target_pairs={{0,4},{4,0},{8,12},{12,8},{1,5},{5,1},{9,13},{13,9},{2,6},{6,2},{1... | collective-permute-start | bytes 1572872 | tf_op jit(solution)/shard_map/ppermute | solution.py:22
  72.1 17.2 %collective-permute-start.13 = (f32[2,1,256,128]{3,2,1,0:T(8,128)S(1)}, f32[2,1,256,128]{3,2,1,0:T(8,128)S(1)}, u32[]{:S(2)}, u32[]{:S(2)}) collective-permute-start(f32[2,1,256,128]{3,2,1,0:T(8,128)S(1)} %shard_map.84.refs_2_), channel_id=1, source_target_pairs={{0,8},{4,12},{8,0},{12,4},{1,9},{5,13},{9,1},{13,5},{2,10},{6,14},... | collective-permute-start | bytes 786440 | tf_op jit(solution)/shard_map/ppermute | solution.py:22
  74.7 31.5 %collective-permute-start.18 = (f32[2,1,256,128]{3,2,1,0:T(8,128)S(1)}, f32[2,1,256,128]{3,2,1,0:T(8,128)S(1)}, u32[]{:S(2)}, u32[]{:S(2)}) collective-permute-start(f32[2,1,256,128]{3,2,1,0:T(8,128)S(1)} %shard_map.84.refs_2_), channel_id=1, source_target_pairs={{0,4},{4,0},{8,12},{12,8},{1,5},{5,1},{9,13},{13,9},{2,6},{6,2},{1... | collective-permute-start | bytes 786440 | tf_op jit(solution)/shard_map/ppermute | solution.py:22
  76.0 24.5 %collective-permute-start.8 = (f32[2,1,256,128]{3,2,1,0:T(8,128)S(1)}, f32[2,1,256,128]{3,2,1,0:T(8,128)S(1)}, u32[]{:S(2)}, u32[]{:S(2)}) collective-permute-start(f32[2,1,256,128]{3,2,1,0:T(8,128)S(1)} %shard_map.82.refs_3_), channel_id=1, source_target_pairs={{0,8},{4,12},{8,0},{12,4},{1,9},{5,13},{9,1},{13,5},{2,10},{6,14},... | collective-permute-start | bytes 786440 | tf_op jit(solution)/shard_map/ppermute | solution.py:22
  76.5 34.7 %collective-permute-start.15 = (f32[2,1,256,128]{3,2,1,0:T(8,128)S(1)}, f32[2,1,256,128]{3,2,1,0:T(8,128)S(1)}, u32[]{:S(2)}, u32[]{:S(2)}) collective-permute-start(f32[2,1,256,128]{3,2,1,0:T(8,128)S(1)} %shard_map.82.refs_3_), channel_id=1, source_target_pairs={{0,4},{4,0},{8,12},{12,8},{1,5},{5,1},{9,13},{13,9},{2,6},{6,2},{1... | collective-permute-start | bytes 786440 | tf_op jit(solution)/shard_map/ppermute | solution.py:22
  89.3 24.6 %collective-permute-start.14 = (f32[2,1,256,128]{3,2,1,0:T(8,128)S(1)}, f32[2,1,256,128]{3,2,1,0:T(8,128)S(1)}, u32[]{:S(2)}, u32[]{:S(2)}) collective-permute-start(f32[2,1,256,128]{3,2,1,0:T(8,128)S(1)} %collective-permute-done.13.refs_2_), channel_id=1, source_target_pairs={{0,4},{4,0},{8,12},{12,8},{1,5},{5,1},{9,13},{13,9},{2,6},{6,2},{1... | collective-permute-start | bytes 786440 | tf_op jit(solution)/shard_map/ppermute | solution.py:22
  100.5 17.2 %collective-permute-start.9 = (f32[2,1,256,128]{3,2,1,0:T(8,128)S(1)}, f32[2,1,256,128]{3,2,1,0:T(8,128)S(1)}, u32[]{:S(2)}, u32[]{:S(2)}) collective-permute-start(f32[2,1,256,128]{3,2,1,0:T(8,128)S(1)} %collective-permute-done.8.refs_2_.refs_3_), channel_id=1, source_target_pairs={{0,4},{4,0},{8,12},{12,8},{1,5},{5,1},{9,13},{13,9},{2,6},{6,2},{1... | collective-permute-start | bytes 786440 | tf_op jit(solution)/shard_map/ppermute | solution.py:22
  119.1 9.2 %collective-permute-start.22 = (f32[2,1,256,128]{3,2,1,0:T(8,128)S(1)}, f32[2,1,256,128]{3,2,1,0:T(8,128)S(1)}, u32[]{:S(2)}, u32[]{:S(2)}) collective-permute-start(f32[2,1,256,128]{3,2,1,0:T(8,128)S(1)} %shard_map.93.refs_9_), channel_id=1, source_target_pairs={{0,2},{1,3},{2,0},{3,1},{4,6},{5,7},{6,4},{7,5},{8,10},{9,11},{10,... | collective-permute-start | bytes 786440 | tf_op jit(solution)/shard_map/ppermute | solution.py:22
  122.0 10.7 %collective-permute-start.19 = (f32[2,1,256,128]{3,2,1,0:T(8,128)S(1)}, f32[2,1,256,128]{3,2,1,0:T(8,128)S(1)}, u32[]{:S(2)}, u32[]{:S(2)}) collective-permute-start(f32[2,1,256,128]{3,2,1,0:T(8,128)S(1)} %shard_map.92.refs_10_), channel_id=1, source_target_pairs={{0,2},{1,3},{2,0},{3,1},{4,6},{5,7},{6,4},{7,5},{8,10},{9,11},{10,... | collective-permute-start | bytes 786440 | tf_op jit(solution)/shard_map/ppermute | solution.py:22
  122.7 16.0 %collective-permute-start.26 = (f32[1,128,256]{2,1,0:T(8,128)S(1)}, f32[1,128,256]{2,1,0:T(8,128)S(1)}, u32[]{:S(2)}, u32[]{:S(2)}) collective-permute-start(f32[1,128,256]{2,1,0:T(8,128)S(1)} %get-tuple-element.53), channel_id=1, source_target_pairs={{4,0},{8,4},{12,8},{5,1},{9,5},{13,9},{6,2},{10,6},{14,10},{7,3},{... | collective-permute-start | bytes 393224 | tf_op jit(solution)/shard_map/ppermute | solution.py:577
  124.2 13.7 %collective-permute-start.23 = (f32[2,1,256,128]{3,2,1,0:T(8,128)S(1)}, f32[2,1,256,128]{3,2,1,0:T(8,128)S(1)}, u32[]{:S(2)}, u32[]{:S(2)}) collective-permute-start(f32[2,1,256,128]{3,2,1,0:T(8,128)S(1)} %shard_map.93.refs_9_), channel_id=1, source_target_pairs={{0,1},{1,0},{2,3},{3,2},{4,5},{5,4},{6,7},{7,6},{8,9},{9,8},{10,11... | collective-permute-start | bytes 786440 | tf_op jit(solution)/shard_map/ppermute | solution.py:22
  124.3 14.4 %collective-permute-start.20 = (f32[2,1,256,128]{3,2,1,0:T(8,128)S(1)}, f32[2,1,256,128]{3,2,1,0:T(8,128)S(1)}, u32[]{:S(2)}, u32[]{:S(2)}) collective-permute-start(f32[2,1,256,128]{3,2,1,0:T(8,128)S(1)} %shard_map.92.refs_10_), channel_id=1, source_target_pairs={{0,1},{1,0},{2,3},{3,2},{4,5},{5,4},{6,7},{7,6},{8,9},{9,8},{10,11... | collective-permute-start | bytes 786440 | tf_op jit(solution)/shard_map/ppermute | solution.py:22
  128.4 9.5 %collective-permute-start.24 = (f32[2,1,256,128]{3,2,1,0:T(8,128)S(1)}, f32[2,1,256,128]{3,2,1,0:T(8,128)S(1)}, u32[]{:S(2)}, u32[]{:S(2)}) collective-permute-start(f32[2,1,256,128]{3,2,1,0:T(8,128)S(1)} %collective-permute-done.22.refs_5_), channel_id=1, source_target_pairs={{0,1},{1,0},{2,3},{3,2},{4,5},{5,4},{6,7},{7,6},{8,9},{9,8},{10,11... | collective-permute-start | bytes 786440 | tf_op jit(solution)/shard_map/ppermute | solution.py:22
  (9 other events, 100.8 us)

commit v12 on v11

--- a/solution.py
+++ b/solution.py
@@ -562,7 +562,8 @@
             sums = panel(at, retarded, far, blocks, sums, edges, work, False)
         far, blocks = pieces[-1]
         for block in blocks[:-1]:
-            sums = panel(at, retarded, far, [block], sums, edges, ("diag",), False)
+            work = ("diag", "upper", "over") if final else ("diag",)
+            sums = panel(at, retarded, far, [block], sums, edges, work, False)
         diags = []
         for number in range(chunks):
             span = (number * local // chunks, (number + 1) * local // chunks)
@@ -576,7 +577,7 @@
     devices = lax.axis_size("pan")
     above = lax.ppermute(sums["back"], "pan", [(i + 1, i) for i in range(devices - 1)])
     far, blocks = pieces[-1]
-    sums = panel(at, retarded, far, blocks, sums, edges, ("upper", "over"), True)
+    sums = panel(at, retarded, far, blocks[-1:], sums, edges, ("upper", "over"), True)
     for far, blocks in pieces[1:-1]:
         if far >= high:
             sums = panel(at, retarded, far, blocks, sums, edges, ("over",), False)

time: 141 us -> 143 us (1.014)
  waiting for transfers between devices: 51.4 us -> 53.4 us
  transfers between devices with their start and end apart: 27 -> 27, of which waited for: 10 -> 11; matrix products, arithmetic and copies ran while one was open for 6% -> 6% of each run, Pallas kernels for 29% -> 29%
where the time goes in v12:
time: 143 us; the launch traced here: 142 us
  waiting for transfers between devices  53.4 us (37%)
  Pallas kernels  43 us (30%)
  starting transfers between devices  32 us (22%)
  local copies, waits for them, and re-layouts  10.9 us (8%)
  other arithmetic  1.89 us (1%)
    ppermute x24, waiting for transfers between devices, swapped(): lax.ppermute(x, axis, [(i, i ^ bit) for i in range(lax.axis_size(axis))])  52 us
    pallas_call x18, Pallas kernels, panel(): pl.pallas_call(functools.partial(panel_kernel, local, far, starts, kinds,...  38.1 us
    ppermute x24, starting transfers between devices, swapped(): lax.ppermute(x, axis, [(i, i ^ bit) for i in range(lax.axis_size(axis))])  29.8 us
    dynamic_slice x3, local copies, waits for them, and re-layouts, take(): return lax.dynamic_slice(retarded, (0, 0, row, column), (2, 1, B, size))  5.43 us
    unnamed x12, local copies, waits for them, and re-layouts  4.48 us
  transfers between devices with their start and end apart: 27, of which 11 were waited for; matrix products, arithmetic and copies ran while one was open for 6% of the time, Pallas kernels for 29%

profile of v12, /device:TPU:0, one launch (start us, length us, event | category | flops | bytes accessed | tf_op | source)
XLA Modules:
  0.0 142.3 jit_solution(9152803453091860350)
XLA Ops:
  0.6 3.1 %collective-permute-start.4 = (f32[2,1,512,128]{3,2,1,0:T(8,128)}, f32[2,1,512,128]{3,2,1,0:T(8,128)S(1)}, u32[]{:S(2)}, u32[]{:S(2)}) collective-permute-start(f32[2,1,512,128]{3,2,1,0:T(8,128)} %contact_ref.1), channel_id=1, source_target_pairs={{0,4},{4,0},{8,12},{12,8},{1,5},{5,1},{9,13},{13,9},{2,6},{6,2},{1... | collective-permute-start | bytes 1572872 | tf_op jit(solution)/shard_map/ppermute | solution.py:22
  5.7 2.7 %collective-permute-start.2 = (f32[2,1,256,128]{3,2,1,0:T(8,128)}, f32[2,1,256,128]{3,2,1,0:T(8,128)}, u32[]{:S(2)}, u32[]{:S(2)}) collective-permute-start(f32[2,1,256,128]{3,2,1,0:T(8,128)} %get-tuple-element.38), channel_id=1, source_target_pairs={{0,8},{4,12},{8,0},{12,4},{1,9},{5,13},{9,1},{13,5},{2,10},{6,14},... | collective-permute-start | bytes 786440 | tf_op jit(solution)/shard_map/ppermute | solution.py:22
  12.9 2.3 %constant_dynamic-slice_fusion.1 = f32[2,1,128,1024]{3,2,1,0:T(8,128)} fusion(f32[2,1,512,2048]{3,2,1,0:T(8,128)} %refs_1_.35, s32[]{:T(128)S(6)} %select_n.90, s32[]{:T(128)S(6)} %select_n.92), kind=kLoop, calls=%fused_computation.6 | loop fusion | bytes 2097160 | tf_op jit(solution)/shard_map/dynamic_slice | solution.py:474
  18.0 3.4 %copy-done = f32[2,1,512,2048]{3,2,1,0:T(8,128)S(1)} copy-done((f32[2,1,512,2048]{3,2,1,0:T(8,128)S(1)}, f32[2,1,512,2048]{3,2,1,0:T(8,128)}, u32[]{:S(2)}) %copy-start) | copy-done | bytes 8388632
  21.4 2.4 %shard_map.76.refs_3_ = f32[4,128,256]{2,1,0:T(8,128)S(1)} custom-call(s32[2]{0:T(128)S(1)} %compare_select_fusion.refs_0_.refs_1_, f32[2,1,512,2048]{3,2,1,0:T(8,128)S(1)} %copy-done, f32[2,1,512,128]{3,2,1,0:T(8,128)S(1)} %get-tuple-element.34.refs_2_), custom_call_target="tpu_custom_call" | custom-call | flops 1610612736 | bytes 2097152 | tf_op jit(solution)/shard_map/pallas_call | solution.py:308
  23.9 4.7 %collective-permute-start.3 = (f32[2,1,256,128]{3,2,1,0:T(8,128)}, f32[2,1,256,128]{3,2,1,0:T(8,128)S(1)}, u32[]{:S(2)}, u32[]{:S(2)}) collective-permute-start(f32[2,1,256,128]{3,2,1,0:T(8,128)} %collective-permute-done.2.refs_2_), channel_id=1, source_target_pairs={{0,4},{4,0},{8,12},{12,8},{1,5},{5,1},{9,13},{13,9},{2,6},{6,2},{1... | collective-permute-start | bytes 786440 | tf_op jit(solution)/shard_map/ppermute | solution.py:22
  30.7 2.2 %collective-permute-done.refs_2_ = f32[2,1,256,128]{3,2,1,0:T(8,128)S(1)} collective-permute-done((f32[2,1,256,128]{3,2,1,0:T(8,128)}, f32[2,1,256,128]{3,2,1,0:T(8,128)S(1)}, u32[]{:S(2)}, u32[]{:S(2)}) %collective-permute-start) | collective-permute-done | bytes 262176 | tf_op jit(solution)/shard_map/ppermute | solution.py:22
  32.9 2.5 %shard_map.78.refs_3_ = f32[4,128,256]{2,1,0:T(8,128)S(1)} custom-call(s32[2]{0:T(128)S(1)} %compare_select_fusion.refs_0_.refs_1_, f32[2,1,512,2048]{3,2,1,0:T(8,128)S(1)} %copy-done, f32[2,1,512,128]{3,2,1,0:T(8,128)S(1)} %collective-permute-done.4.refs_2_, f32[4,128,256]{2,1,0:T(8,128)S(1)} %shard_map.77.refs_3_), custom_call_target="tpu_custom_call", output_to_operand_aliasing={{}: (3, {})} | custom-call | flops 1610612736 | bytes 2097152 | tf_op jit(solution)/shard_map/pallas_call | solution.py:308
  37.1 13.3 %collective-permute-done.3.refs_2_ = f32[2,1,256,128]{3,2,1,0:T(8,128)S(1)} collective-permute-done((f32[2,1,256,128]{3,2,1,0:T(8,128)}, f32[2,1,256,128]{3,2,1,0:T(8,128)S(1)}, u32[]{:S(2)}, u32[]{:S(2)}) %collective-permute-start.3) | collective-permute-done | bytes 262176 | tf_op jit(solution)/shard_map/ppermute | solution.py:22
  52.2 3.1 %collective-permute-done.1.refs_2_ = f32[2,1,256,128]{3,2,1,0:T(8,128)S(1)} collective-permute-done((f32[2,1,256,128]{3,2,1,0:T(8,128)S(1)}, f32[2,1,256,128]{3,2,1,0:T(8,128)S(1)}, u32[]{:S(2)}, u32[]{:S(2)}) %collective-permute-start.1) | collective-permute-done | bytes 262176 | tf_op jit(solution)/shard_map/ppermute | solution.py:22
  60.1 5.3 %collective-permute-done.10.refs_5_ = f32[2,1,256,128]{3,2,1,0:T(8,128)S(1)} collective-permute-done((f32[2,1,256,128]{3,2,1,0:T(8,128)S(1)}, f32[2,1,256,128]{3,2,1,0:T(8,128)S(1)}, u32[]{:S(2)}, u32[]{:S(2)}) %collective-permute-start.10) | collective-permute-done | bytes 262176 | tf_op jit(solution)/shard_map/ppermute | solution.py:22
  65.9 3.8 %collective-permute-done.5.refs_5_ = f32[2,1,256,128]{3,2,1,0:T(8,128)S(1)} collective-permute-done((f32[2,1,256,128]{3,2,1,0:T(8,128)S(1)}, f32[2,1,256,128]{3,2,1,0:T(8,128)S(1)}, u32[]{:S(2)}, u32[]{:S(2)}) %collective-permute-start.5) | collective-permute-done | bytes 262176 | tf_op jit(solution)/shard_map/ppermute | solution.py:22
  72.1 2.6 %collective-permute-start.13 = (f32[2,1,256,128]{3,2,1,0:T(8,128)S(1)}, f32[2,1,256,128]{3,2,1,0:T(8,128)S(1)}, u32[]{:S(2)}, u32[]{:S(2)}) collective-permute-start(f32[2,1,256,128]{3,2,1,0:T(8,128)S(1)} %shard_map.84.refs_2_), channel_id=1, source_target_pairs={{0,8},{4,12},{8,0},{12,4},{1,9},{5,13},{9,1},{13,5},{2,10},{6,14},... | collective-permute-start | bytes 786440 | tf_op jit(solution)/shard_map/ppermute | solution.py:22
  80.2 3.2 %shard_map.85 = (f32[4,128,256]{2,1,0:T(8,128)S(1)}, f32[3,128,256]{2,1,0:T(8,128)S(1)}) custom-call(s32[2]{0:T(128)S(1)} %compare_select_fusion.refs_0_.refs_1_, f32[2,1,512,2048]{3,2,1,0:T(8,128)S(1)} %bitcast.11, f32[2,1,256,128]{3,2,1,0:T(8,128)S(1)} %shard_map.84.refs_2_, f32[2,1,256,128]{3,2,1,0:T(8,128)S(1)} %shard_map.82.refs_3_), custom_call_target="tpu_custom_call" | custom-call | flops 2415919104 | bytes 2097152 | tf_op jit(solution)/shard_map/pallas_call | solution.py:308
  83.4 5.9 %collective-permute-done.13.refs_2_ = f32[2,1,256,128]{3,2,1,0:T(8,128)S(1)} collective-permute-done((f32[2,1,256,128]{3,2,1,0:T(8,128)S(1)}, f32[2,1,256,128]{3,2,1,0:T(8,128)S(1)}, u32[]{:S(2)}, u32[]{:S(2)}) %collective-permute-start.13) | collective-permute-done | bytes 262176 | tf_op jit(solution)/shard_map/ppermute | solution.py:22
  89.3 3.5 %collective-permute-start.14 = (f32[2,1,256,128]{3,2,1,0:T(8,128)S(1)}, f32[2,1,256,128]{3,2,1,0:T(8,128)S(1)}, u32[]{:S(2)}, u32[]{:S(2)}) collective-permute-start(f32[2,1,256,128]{3,2,1,0:T(8,128)S(1)} %collective-permute-done.13.refs_2_), channel_id=1, source_target_pairs={{0,4},{4,0},{8,12},{12,8},{1,5},{5,1},{9,13},{13,9},{2,6},{6,2},{1... | collective-permute-start | bytes 786440 | tf_op jit(solution)/shard_map/ppermute | solution.py:22
  92.8 7.7 %collective-permute-done.8.refs_2_.refs_3_ = f32[2,1,256,128]{3,2,1,0:T(8,128)S(1)} collective-permute-done((f32[2,1,256,128]{3,2,1,0:T(8,128)S(1)}, f32[2,1,256,128]{3,2,1,0:T(8,128)S(1)}, u32[]{:S(2)}, u32[]{:S(2)}) %collective-permute-start.8) | collective-permute-done | bytes 262176 | tf_op jit(solution)/shard_map/ppermute | solution.py:22
  100.5 3.5 %collective-permute-start.9 = (f32[2,1,256,128]{3,2,1,0:T(8,128)S(1)}, f32[2,1,256,128]{3,2,1,0:T(8,128)S(1)}, u32[]{:S(2)}, u32[]{:S(2)}) collective-permute-start(f32[2,1,256,128]{3,2,1,0:T(8,128)S(1)} %collective-permute-done.8.refs_2_.refs_3_), channel_id=1, source_target_pairs={{0,4},{4,0},{8,12},{12,8},{1,5},{5,1},{9,13},{13,9},{2,6},{6,2},{1... | collective-permute-start | bytes 786440 | tf_op jit(solution)/shard_map/ppermute | solution.py:22
  106.2 2.8 %shard_map.88 = (f32[4,128,256]{2,1,0:T(8,128)S(1)}, f32[3,128,256]{2,1,0:T(8,128)S(1)}, f32[1,128,256]{2,1,0:T(8,128)S(1)}, f32[1,128,256]{2,1,0:T(8,128)S(1)}) custom-call(s32[2]{0:T(128)S(1)} %compare_select_fusion.refs_0_.refs_1_, f32[2,1,512,2048]{3,2,1,0:T(8,128)S(1)} %bitcast.11, ...), custom_call_target="tpu_custom_call", output_to_operand_aliasing={{0}: (4, {}), {1}: (5, {}), {2}: (6, {}), {3}: (7, {})} | custom-call | flops 2013265920 | bytes 1048576 | tf_op jit(solution)/shard_map/pallas_call | solution.py:308
  111.1 2.8 %shard_map.90 = (f32[4,128,256]{2,1,0:T(8,128)S(1)}, f32[3,128,256]{2,1,0:T(8,128)S(1)}, f32[1,128,256]{2,1,0:T(8,128)S(1)}, f32[1,128,256]{2,1,0:T(8,128)S(1)}) custom-call(s32[2]{0:T(128)S(1)} %compare_select_fusion.refs_0_.refs_1_, f32[2,1,512,2048]{3,2,1,0:T(8,128)S(1)} %bitcast.11, ...), custom_call_target="tpu_custom_call", output_to_operand_aliasing={{0}: (5, {}), {1}: (6, {}), {2}: (7, {}), {3}: (8, {})} | custom-call | flops 2013265920 | bytes 1048576 | tf_op jit(solution)/shard_map/pallas_call | solution.py:308
  113.9 2.7 %shard_map.91 = (f32[4,128,256]{2,1,0:T(8,128)S(1)}, f32[3,128,256]{2,1,0:T(8,128)S(1)}, f32[1,128,256]{2,1,0:T(8,128)S(1)}) custom-call(s32[2]{0:T(128)S(1)} %compare_select_fusion.refs_0_.refs_1_, f32[2,1,512,2048]{3,2,1,0:T(8,128)S(1)} %bitcast.11, ...), custom_call_target="tpu_custom_call", output_to_operand_aliasing={{0}: (4, {}), {1}: (5, {}), {2}: (6, {})} | custom-call | flops 1610612736 | bytes 1048576 | tf_op jit(solution)/shard_map/pallas_call | solution.py:308
  122.7 5.7 %collective-permute-done.22.refs_5_ = f32[2,1,256,128]{3,2,1,0:T(8,128)S(1)} collective-permute-done((f32[2,1,256,128]{3,2,1,0:T(8,128)S(1)}, f32[2,1,256,128]{3,2,1,0:T(8,128)S(1)}, u32[]{:S(2)}, u32[]{:S(2)}) %collective-permute-start.22) | collective-permute-done | bytes 262176 | tf_op jit(solution)/shard_map/ppermute | solution.py:22
  128.9 3.7 %collective-permute-done.19.refs_5_ = f32[2,1,256,128]{3,2,1,0:T(8,128)S(1)} collective-permute-done((f32[2,1,256,128]{3,2,1,0:T(8,128)S(1)}, f32[2,1,256,128]{3,2,1,0:T(8,128)S(1)}, u32[]{:S(2)}, u32[]{:S(2)}) %collective-permute-start.19) | collective-permute-done | bytes 262176 | tf_op jit(solution)/shard_map/ppermute | solution.py:22
  133.9 2.9 %shard_map.95 = (f32[2,1,512,128]{3,2,1,0:T(8,128)}, f32[1,128,256]{2,1,0:T(8,128)S(1)}) custom-call(s32[2]{0:T(128)S(1)} %compare_select_fusion.refs_0_.refs_1_, f32[2,1,512,2048]{3,2,1,0:T(8,128)S(1)} %bitcast.11, f32[2,1,256,128]{3,2,1,0:T(8,128)S(1)} %collective-permute-done.9.refs_2_, ...), custom_call_target="tpu_custom_call", output_to_operand_aliasing={{1}: (5, {})} | custom-call | flops 1207959552 | bytes 1048576 | tf_op jit(solution)/shard_map/pallas_call | solution.py:308
  (79 shorter events, 45.4 us)
Async XLA Ops:
  0.6 32.3 %collective-permute-start.4 = (f32[2,1,512,128]{3,2,1,0:T(8,128)}, f32[2,1,512,128]{3,2,1,0:T(8,128)S(1)}, u32[]{:S(2)}, u32[]{:S(2)}) collective-permute-start(f32[2,1,512,128]{3,2,1,0:T(8,128)} %contact_ref.1), channel_id=1, source_target_pairs={{0,4},{4,0},{8,12},{12,8},{1,5},{5,1},{9,13},{13,9},{2,6},{6,2},{1... | collective-permute-start | bytes 1572872 | tf_op jit(solution)/shard_map/ppermute | solution.py:22
  5.7 18.1 %collective-permute-start.2 = (f32[2,1,256,128]{3,2,1,0:T(8,128)}, f32[2,1,256,128]{3,2,1,0:T(8,128)}, u32[]{:S(2)}, u32[]{:S(2)}) collective-permute-start(f32[2,1,256,128]{3,2,1,0:T(8,128)} %get-tuple-element.38), channel_id=1, source_target_pairs={{0,8},{4,12},{8,0},{12,4},{1,9},{5,13},{9,1},{13,5},{2,10},{6,14},... | collective-permute-start | bytes 786440 | tf_op jit(solution)/shard_map/ppermute | solution.py:22
  8.4 24.6 %collective-permute-start = (f32[2,1,256,128]{3,2,1,0:T(8,128)}, f32[2,1,256,128]{3,2,1,0:T(8,128)S(1)}, u32[]{:S(2)}, u32[]{:S(2)}) collective-permute-start(f32[2,1,256,128]{3,2,1,0:T(8,128)} %get-tuple-element.37), channel_id=1, source_target_pairs={{0,8},{4,12},{8,0},{12,4},{1,9},{5,13},{9,1},{13,5},{2,10},{6,14},... | collective-permute-start | bytes 786440 | tf_op jit(solution)/shard_map/ppermute | solution.py:22
  12.7 63.2 %collective-permute-start.15 = (f32[2,1,128,768]{3,2,1,0:T(8,128)}, f32[2,1,128,768]{3,2,1,0:T(8,128)S(1)}, u32[]{:S(2)}, u32[]{:S(2)}) collective-permute-start(f32[2,1,128,768]{3,2,1,0:T(8,128)} %pad_maximum_fusion), channel_id=1, source_target_pairs={{0,4},{4,0},{8,12},{12,8},{1,5},{5,1},{9,13},{13,9},{2,6},{6,2},{1... | collective-permute-start | bytes 2359304 | tf_op jit(solution)/shard_map/ppermute | solution.py:493
  15.3 61.2 %collective-permute-start.17 = (f32[2,1,128,1024]{3,2,1,0:T(8,128)}, f32[2,1,128,1024]{3,2,1,0:T(8,128)S(1)}, u32[]{:S(2)}, u32[]{:S(2)}) collective-permute-start(f32[2,1,128,1024]{3,2,1,0:T(8,128)} %constant_dynamic-slice_fusion.1), channel_id=1, source_target_pairs={{4,8},{8,4},{5,9},{9,5},{6,10},{10,6},{7,11},{11,7},{20,24},{24,20... | collective-permute-start | bytes 3145736 | tf_op jit(solution)/shard_map/ppermute | solution.py:493
  23.9 26.6 %collective-permute-start.3 = (f32[2,1,256,128]{3,2,1,0:T(8,128)}, f32[2,1,256,128]{3,2,1,0:T(8,128)S(1)}, u32[]{:S(2)}, u32[]{:S(2)}) collective-permute-start(f32[2,1,256,128]{3,2,1,0:T(8,128)} %collective-permute-done.2.refs_2_), channel_id=1, source_target_pairs={{0,4},{4,0},{8,12},{12,8},{1,5},{5,1},{9,13},{13,9},{2,6},{6,2},{1... | collective-permute-start | bytes 786440 | tf_op jit(solution)/shard_map/ppermute | solution.py:22
  32.9 22.3 %collective-permute-start.1 = (f32[2,1,256,128]{3,2,1,0:T(8,128)S(1)}, f32[2,1,256,128]{3,2,1,0:T(8,128)S(1)}, u32[]{:S(2)}, u32[]{:S(2)}) collective-permute-start(f32[2,1,256,128]{3,2,1,0:T(8,128)S(1)} %collective-permute-done.refs_2_), channel_id=1, source_target_pairs={{0,4},{4,0},{8,12},{12,8},{1,5},{5,1},{9,13},{13,9},{2,6},{6,2},{1... | collective-permute-start | bytes 786440 | tf_op jit(solution)/shard_map/ppermute | solution.py:22
  56.6 8.8 %collective-permute-start.10 = (f32[2,1,256,128]{3,2,1,0:T(8,128)S(1)}, f32[2,1,256,128]{3,2,1,0:T(8,128)S(1)}, u32[]{:S(2)}, u32[]{:S(2)}) collective-permute-start(f32[2,1,256,128]{3,2,1,0:T(8,128)S(1)} %shard_map.83), channel_id=1, source_target_pairs={{0,2},{1,3},{2,0},{3,1},{4,6},{5,7},{6,4},{7,5},{8,10},{9,11},{10,... | collective-permute-start | bytes 786440 | tf_op jit(solution)/shard_map/ppermute | solution.py:22
  58.3 7.1 %collective-permute-start.11 = (f32[2,1,256,128]{3,2,1,0:T(8,128)S(1)}, f32[2,1,256,128]{3,2,1,0:T(8,128)S(1)}, u32[]{:S(2)}, u32[]{:S(2)}) collective-permute-start(f32[2,1,256,128]{3,2,1,0:T(8,128)S(1)} %shard_map.83), channel_id=1, source_target_pairs={{0,1},{1,0},{2,3},{3,2},{4,5},{5,4},{6,7},{7,6},{8,9},{9,8},{10,11... | collective-permute-start | bytes 786440 | tf_op jit(solution)/shard_map/ppermute | solution.py:22
  59.7 10.1 %collective-permute-start.5 = (f32[2,1,256,128]{3,2,1,0:T(8,128)S(1)}, f32[2,1,256,128]{3,2,1,0:T(8,128)S(1)}, u32[]{:S(2)}, u32[]{:S(2)}) collective-permute-start(f32[2,1,256,128]{3,2,1,0:T(8,128)S(1)} %shard_map.81), channel_id=1, source_target_pairs={{0,2},{1,3},{2,0},{3,1},{4,6},{5,7},{6,4},{7,5},{8,10},{9,11},{10,... | collective-permute-start | bytes 786440 | tf_op jit(solution)/shard_map/ppermute | solution.py:22
  69.7 62.9 %collective-permute-start.25 = (f32[2,1,128,512]{3,2,1,0:T(8,128)S(1)}, f32[2,1,128,512]{3,2,1,0:T(8,128)S(1)}, u32[]{:S(2)}, u32[]{:S(2)}) collective-permute-start(f32[2,1,128,512]{3,2,1,0:T(8,128)S(1)} %copy-done.3), channel_id=1, source_target_pairs={{0,4},{4,0},{8,12},{12,8},{1,5},{5,1},{9,13},{13,9},{2,6},{6,2},{1... | collective-permute-start | bytes 1572872 | tf_op jit(solution)/shard_map/ppermute | solution.py:22
  72.1 17.2 %collective-permute-start.13 = (f32[2,1,256,128]{3,2,1,0:T(8,128)S(1)}, f32[2,1,256,128]{3,2,1,0:T(8,128)S(1)}, u32[]{:S(2)}, u32[]{:S(2)}) collective-permute-start(f32[2,1,256,128]{3,2,1,0:T(8,128)S(1)} %shard_map.84.refs_2_), channel_id=1, source_target_pairs={{0,8},{4,12},{8,0},{12,4},{1,9},{5,13},{9,1},{13,5},{2,10},{6,14},... | collective-permute-start | bytes 786440 | tf_op jit(solution)/shard_map/ppermute | solution.py:22
  74.7 31.5 %collective-permute-start.18 = (f32[2,1,256,128]{3,2,1,0:T(8,128)S(1)}, f32[2,1,256,128]{3,2,1,0:T(8,128)S(1)}, u32[]{:S(2)}, u32[]{:S(2)}) collective-permute-start(f32[2,1,256,128]{3,2,1,0:T(8,128)S(1)} %shard_map.84.refs_2_), channel_id=1, source_target_pairs={{0,4},{4,0},{8,12},{12,8},{1,5},{5,1},{9,13},{13,9},{2,6},{6,2},{1... | collective-permute-start | bytes 786440 | tf_op jit(solution)/shard_map/ppermute | solution.py:22
  76.0 24.5 %collective-permute-start.8 = (f32[2,1,256,128]{3,2,1,0:T(8,128)S(1)}, f32[2,1,256,128]{3,2,1,0:T(8,128)S(1)}, u32[]{:S(2)}, u32[]{:S(2)}) collective-permute-start(f32[2,1,256,128]{3,2,1,0:T(8,128)S(1)} %shard_map.82.refs_3_), channel_id=1, source_target_pairs={{0,8},{4,12},{8,0},{12,4},{1,9},{5,13},{9,1},{13,5},{2,10},{6,14},... | collective-permute-start | bytes 786440 | tf_op jit(solution)/shard_map/ppermute | solution.py:22
  76.5 34.7 %collective-permute-start.16 = (f32[2,1,256,128]{3,2,1,0:T(8,128)S(1)}, f32[2,1,256,128]{3,2,1,0:T(8,128)S(1)}, u32[]{:S(2)}, u32[]{:S(2)}) collective-permute-start(f32[2,1,256,128]{3,2,1,0:T(8,128)S(1)} %shard_map.82.refs_3_), channel_id=1, source_target_pairs={{0,4},{4,0},{8,12},{12,8},{1,5},{5,1},{9,13},{13,9},{2,6},{6,2},{1... | collective-permute-start | bytes 786440 | tf_op jit(solution)/shard_map/ppermute | solution.py:22
  89.3 24.6 %collective-permute-start.14 = (f32[2,1,256,128]{3,2,1,0:T(8,128)S(1)}, f32[2,1,256,128]{3,2,1,0:T(8,128)S(1)}, u32[]{:S(2)}, u32[]{:S(2)}) collective-permute-start(f32[2,1,256,128]{3,2,1,0:T(8,128)S(1)} %collective-permute-done.13.refs_2_), channel_id=1, source_target_pairs={{0,4},{4,0},{8,12},{12,8},{1,5},{5,1},{9,13},{13,9},{2,6},{6,2},{1... | collective-permute-start | bytes 786440 | tf_op jit(solution)/shard_map/ppermute | solution.py:22
  100.5 17.2 %collective-permute-start.9 = (f32[2,1,256,128]{3,2,1,0:T(8,128)S(1)}, f32[2,1,256,128]{3,2,1,0:T(8,128)S(1)}, u32[]{:S(2)}, u32[]{:S(2)}) collective-permute-start(f32[2,1,256,128]{3,2,1,0:T(8,128)S(1)} %collective-permute-done.8.refs_2_.refs_3_), channel_id=1, source_target_pairs={{0,4},{4,0},{8,12},{12,8},{1,5},{5,1},{9,13},{13,9},{2,6},{6,2},{1... | collective-permute-start | bytes 786440 | tf_op jit(solution)/shard_map/ppermute | solution.py:22
  119.1 9.2 %collective-permute-start.22 = (f32[2,1,256,128]{3,2,1,0:T(8,128)S(1)}, f32[2,1,256,128]{3,2,1,0:T(8,128)S(1)}, u32[]{:S(2)}, u32[]{:S(2)}) collective-permute-start(f32[2,1,256,128]{3,2,1,0:T(8,128)S(1)} %shard_map.93.refs_9_), channel_id=1, source_target_pairs={{0,2},{1,3},{2,0},{3,1},{4,6},{5,7},{6,4},{7,5},{8,10},{9,11},{10,... | collective-permute-start | bytes 786440 | tf_op jit(solution)/shard_map/ppermute | solution.py:22
  122.0 10.7 %collective-permute-start.19 = (f32[2,1,256,128]{3,2,1,0:T(8,128)S(1)}, f32[2,1,256,128]{3,2,1,0:T(8,128)S(1)}, u32[]{:S(2)}, u32[]{:S(2)}) collective-permute-start(f32[2,1,256,128]{3,2,1,0:T(8,128)S(1)} %shard_map.92.refs_10_), channel_id=1, source_target_pairs={{0,2},{1,3},{2,0},{3,1},{4,6},{5,7},{6,4},{7,5},{8,10},{9,11},{10,... | collective-permute-start | bytes 786440 | tf_op jit(solution)/shard_map/ppermute | solution.py:22
  122.7 15.6 %collective-permute-start.23 = (f32[2,1,256,128]{3,2,1,0:T(8,128)S(1)}, f32[2,1,256,128]{3,2,1,0:T(8,128)S(1)}, u32[]{:S(2)}, u32[]{:S(2)}) collective-permute-start(f32[2,1,256,128]{3,2,1,0:T(8,128)S(1)} %shard_map.93.refs_9_), channel_id=1, source_target_pairs={{0,1},{1,0},{2,3},{3,2},{4,5},{5,4},{6,7},{7,6},{8,9},{9,8},{10,11... | collective-permute-start | bytes 786440 | tf_op jit(solution)/shard_map/ppermute | solution.py:22
  128.4 9.9 %collective-permute-start.24 = (f32[2,1,256,128]{3,2,1,0:T(8,128)S(1)}, f32[2,1,256,128]{3,2,1,0:T(8,128)S(1)}, u32[]{:S(2)}, u32[]{:S(2)}) collective-permute-start(f32[2,1,256,128]{3,2,1,0:T(8,128)S(1)} %collective-permute-done.22.refs_5_), channel_id=1, source_target_pairs={{0,1},{1,0},{2,3},{3,2},{4,5},{5,4},{6,7},{7,6},{8,9},{9,8},{10,11... | collective-permute-start | bytes 786440 | tf_op jit(solution)/shard_map/ppermute | solution.py:22
  128.4 12.0 %collective-permute-start.20 = (f32[2,1,256,128]{3,2,1,0:T(8,128)S(1)}, f32[2,1,256,128]{3,2,1,0:T(8,128)S(1)}, u32[]{:S(2)}, u32[]{:S(2)}) collective-permute-start(f32[2,1,256,128]{3,2,1,0:T(8,128)S(1)} %shard_map.92.refs_10_), channel_id=1, source_target_pairs={{0,1},{1,0},{2,3},{3,2},{4,5},{5,4},{6,7},{7,6},{8,9},{9,8},{10,11... | collective-permute-start | bytes 786440 | tf_op jit(solution)/shard_map/ppermute | solution.py:22
  132.6 7.8 %collective-permute-start.21 = (f32[2,1,256,128]{3,2,1,0:T(8,128)S(1)}, f32[2,1,256,128]{3,2,1,0:T(8,128)S(1)}, u32[]{:S(2)}, u32[]{:S(2)}) collective-permute-start(f32[2,1,256,128]{3,2,1,0:T(8,128)S(1)} %collective-permute-done.19.refs_5_), channel_id=1, source_target_pairs={{0,1},{1,0},{2,3},{3,2},{4,5},{5,4},{6,7},{7,6},{8,9},{9,8},{10,11... | collective-permute-start | bytes 786440 | tf_op jit(solution)/shard_map/ppermute | solution.py:22
  132.6 7.8 %collective-permute-start.26 = (f32[1,128,256]{2,1,0:T(8,128)S(1)}, f32[1,128,256]{2,1,0:T(8,128)S(1)}, u32[]{:S(2)}, u32[]{:S(2)}) collective-permute-start(f32[1,128,256]{2,1,0:T(8,128)S(1)} %get-tuple-element.59), channel_id=1, source_target_pairs={{4,0},{8,4},{12,8},{5,1},{9,5},{13,9},{6,2},{10,6},{14,10},{7,3},{... | collective-permute-start | bytes 393224 | tf_op jit(solution)/shard_map/ppermute | solution.py:578
  (9 other events, 101.5 us)

commit v13 on v12

--- a/solution.py
+++ b/solution.py
@@ -136,9 +136,9 @@
     top, end = (0, local) if span is None else span
 
     greens, sigmas, products, columns = [], [], [], []
-    for start, s_ref in zip(starts, piece_refs):
+    for (start, piece_far), s_ref in zip(starts, piece_refs):
         for u in range(s_ref.shape[2] // B):
-            k = source * local + start + u
+            k = (pan ^ piece_far) * local + start + u
             columns.append(pl.ds(pl.multiple_of((k % half) * B, B), B))
             cut = pl.ds(pl.multiple_of(k * B, B), B)
             rows = slice(u * B, (u + 1) * B)
@@ -215,7 +215,7 @@
 
     if in_thirds(local, devices):
         blocks = [
-            start + u for start, ref in zip(starts, piece_refs) for u in range(ref.shape[2] // B)
+            start + u for (start, _), ref in zip(starts, piece_refs) for u in range(ref.shape[2] // B)
         ]
         plan = edge_plan([k for k in kinds if k in ("over", "back")], far, blocks, local, devices)
         for (kind, odd), found in plan.items():
@@ -276,10 +276,10 @@
     kinds = tuple(kind for kind in kinds if counts[kind])
     vmem = pl.BlockSpec(memory_space=pltpu.VMEM)
     starts, many = [], 0
-    for start, piece in pieces:
-        starts.append(start)
+    for start, piece, *other in pieces:
+        starts.append((start, other[0] if other else far))
         many += piece.shape[2] // B
-    operands = [at, green] + [piece for _, piece in pieces]
+    operands = [at, green] + [piece for _, piece, *_ in pieces]
     names = []
     if "over" in kinds or "back" in kinds:
         names = ["even", "odd"]
@@ -552,6 +552,10 @@
                     groups[place] = (1, 0, blocks[:1])
                     groups.append((1, 1, blocks[1:]))
                     break
+        joined = []
+        if not final and chunks > 1 and high > 1:
+            far, _, blocks = groups.pop()
+            joined = [(start, block, far) for start, block in blocks]
         sums = {}
         for far, number, blocks in groups:
             work = ("diag", "upper") if final else ("diag",)
@@ -563,7 +567,8 @@
         far, blocks = pieces[-1]
         for block in blocks[:-1]:
             work = ("diag", "upper", "over") if final else ("diag",)
-            sums = panel(at, retarded, far, [block], sums, edges, work, False)
+            sums = panel(at, retarded, far, [block, *joined], sums, edges, work, False)
+            joined = []
         diags = []
         for number in range(chunks):
             span = (number * local // chunks, (number + 1) * local // chunks)

time: 143 us -> 143 us (level)
  waiting for transfers between devices: 53.4 us -> 55.4 us
    ppermute x24, waiting for transfers between devices: 52 us -> 54.2 us  [swapped(): lax.ppermute(x, axis, [(i, i ^ bit) for i in range(lax.axis_size(axis))])]
    pallas_call x18 -> x17, Pallas kernels: 38.1 us -> 37 us  [panel(): pl.pallas_call(functools.partial(panel_kernel, local, far, starts, kinds,...]
  transfers between devices with their start and end apart: 27 -> 27, of which waited for: 11 -> 12; matrix products, arithmetic and copies ran while one was open for 6% -> 6% of each run, Pallas kernels for 29% -> 28%
where the time goes in v13:
time: 143 us; the launch traced here: 142 us
  waiting for transfers between devices  55.4 us (39%)
  Pallas kernels  41.9 us (29%)
  starting transfers between devices  31.1 us (22%)
  local copies, waits for them, and re-layouts  11 us (8%)
  other arithmetic  1.9 us (1%)
    ppermute x24, waiting for transfers between devices, swapped(): lax.ppermute(x, axis, [(i, i ^ bit) for i in range(lax.axis_size(axis))])  54.2 us
    pallas_call x17, Pallas kernels, panel(): pl.pallas_call(functools.partial(panel_kernel, local, far, starts, kinds,...  37 us
    ppermute x24, starting transfers between devices, swapped(): lax.ppermute(x, axis, [(i, i ^ bit) for i in range(lax.axis_size(axis))])  28.7 us
    dynamic_slice x3, local copies, waits for them, and re-layouts, take(): return lax.dynamic_slice(retarded, (0, 0, row, column), (2, 1, B, size))  5.43 us
    unnamed x12, local copies, waits for them, and re-layouts  4.48 us
  transfers between devices with their start and end apart: 27, of which 12 were waited for; matrix products, arithmetic and copies ran while one was open for 6% of the time, Pallas kernels for 28%

profile of v13, /device:TPU:0, one launch (start us, length us, event | category | flops | bytes accessed | tf_op | source)
XLA Modules:
  0.0 142.3 jit_solution(3426177446111451805)
XLA Ops:
  0.6 3.1 %collective-permute-start.4 = (f32[2,1,512,128]{3,2,1,0:T(8,128)}, f32[2,1,512,128]{3,2,1,0:T(8,128)S(1)}, u32[]{:S(2)}, u32[]{:S(2)}) collective-permute-start(f32[2,1,512,128]{3,2,1,0:T(8,128)} %contact_ref.1), channel_id=1, source_target_pairs={{0,4},{4,0},{8,12},{12,8},{1,5},{5,1},{9,13},{13,9},{2,6},{6,2},{1... | collective-permute-start | bytes 1572872 | tf_op jit(solution)/shard_map/ppermute | solution.py:22
  5.7 2.7 %collective-permute-start.2 = (f32[2,1,256,128]{3,2,1,0:T(8,128)}, f32[2,1,256,128]{3,2,1,0:T(8,128)}, u32[]{:S(2)}, u32[]{:S(2)}) collective-permute-start(f32[2,1,256,128]{3,2,1,0:T(8,128)} %get-tuple-element.38), channel_id=1, source_target_pairs={{0,8},{4,12},{8,0},{12,4},{1,9},{5,13},{9,1},{13,5},{2,10},{6,14},... | collective-permute-start | bytes 786440 | tf_op jit(solution)/shard_map/ppermute | solution.py:22
  12.9 2.3 %constant_dynamic-slice_fusion.1 = f32[2,1,128,1024]{3,2,1,0:T(8,128)} fusion(f32[2,1,512,2048]{3,2,1,0:T(8,128)} %refs_1_.33, s32[]{:T(128)S(6)} %select_n.90, s32[]{:T(128)S(6)} %select_n.92), kind=kLoop, calls=%fused_computation.6 | loop fusion | bytes 2097160 | tf_op jit(solution)/shard_map/dynamic_slice | solution.py:474
  18.0 4.0 %collective-permute-done.2.refs_2_ = f32[2,1,256,128]{3,2,1,0:T(8,128)} collective-permute-done((f32[2,1,256,128]{3,2,1,0:T(8,128)}, f32[2,1,256,128]{3,2,1,0:T(8,128)}, u32[]{:S(2)}, u32[]{:S(2)}) %collective-permute-start.2) | collective-permute-done | bytes 262176 | tf_op jit(solution)/shard_map/ppermute | solution.py:22
  22.0 3.6 %collective-permute-start.3 = (f32[2,1,256,128]{3,2,1,0:T(8,128)}, f32[2,1,256,128]{3,2,1,0:T(8,128)S(1)}, u32[]{:S(2)}, u32[]{:S(2)}) collective-permute-start(f32[2,1,256,128]{3,2,1,0:T(8,128)} %collective-permute-done.2.refs_2_), channel_id=1, source_target_pairs={{0,4},{4,0},{8,12},{12,8},{1,5},{5,1},{9,13},{13,9},{2,6},{6,2},{1... | collective-permute-start | bytes 786440 | tf_op jit(solution)/shard_map/ppermute | solution.py:22
  25.6 3.4 %copy-done = f32[2,1,512,2048]{3,2,1,0:T(8,128)S(1)} copy-done((f32[2,1,512,2048]{3,2,1,0:T(8,128)S(1)}, f32[2,1,512,2048]{3,2,1,0:T(8,128)}, u32[]{:S(2)}) %copy-start) | copy-done | bytes 8388632
  29.0 2.4 %shard_map.76.refs_3_ = f32[4,128,256]{2,1,0:T(8,128)S(1)} custom-call(s32[2]{0:T(128)S(1)} %compare_select_fusion.refs_0_.refs_1_, f32[2,1,512,2048]{3,2,1,0:T(8,128)S(1)} %copy-done, f32[2,1,512,128]{3,2,1,0:T(8,128)S(1)} %get-tuple-element.34.refs_2_), custom_call_target="tpu_custom_call" | custom-call | flops 1610612736 | bytes 2097152 | tf_op jit(solution)/shard_map/pallas_call | solution.py:308
  35.1 2.5 %shard_map.78.refs_4_ = f32[4,128,256]{2,1,0:T(8,128)S(1)} custom-call(s32[2]{0:T(128)S(1)} %compare_select_fusion.refs_0_.refs_1_, f32[2,1,512,2048]{3,2,1,0:T(8,128)S(1)} %copy-done, f32[2,1,512,128]{3,2,1,0:T(8,128)S(1)} %collective-permute-done.4.refs_2_, f32[4,128,256]{2,1,0:T(8,128)S(1)} %shard_map.77.refs_3_), custom_call_target="tpu_custom_call", output_to_operand_aliasing={{}: (3, {})} | custom-call | flops 1610612736 | bytes 2097152 | tf_op jit(solution)/shard_map/pallas_call | solution.py:308
  37.5 12.9 %collective-permute-done.3.refs_2_ = f32[2,1,256,128]{3,2,1,0:T(8,128)S(1)} collective-permute-done((f32[2,1,256,128]{3,2,1,0:T(8,128)}, f32[2,1,256,128]{3,2,1,0:T(8,128)S(1)}, u32[]{:S(2)}, u32[]{:S(2)}) %collective-permute-start.3) | collective-permute-done | bytes 262176 | tf_op jit(solution)/shard_map/ppermute | solution.py:22
  50.4 2.5 %shard_map.79.refs_3_ = f32[4,128,256]{2,1,0:T(8,128)S(1)} custom-call(s32[2]{0:T(128)S(1)} %compare_select_fusion.refs_0_.refs_1_, f32[2,1,512,2048]{3,2,1,0:T(8,128)S(1)} %copy-done, f32[2,1,256,128]{3,2,1,0:T(8,128)S(1)} %collective-permute-done.3.refs_2_, f32[2,1,256,128]{3,2,1,0:T(8,128)S(1)} %collective-permute-done.refs_3_, ...), custom_call_target="tpu_custom_call", output_to_operand_aliasing={{}: (4, {})} | custom-call | flops 1610612736 | bytes 2097152 | tf_op jit(solution)/shard_map/pallas_call | solution.py:308
  60.1 5.3 %collective-permute-done.10.refs_5_ = f32[2,1,256,128]{3,2,1,0:T(8,128)S(1)} collective-permute-done((f32[2,1,256,128]{3,2,1,0:T(8,128)S(1)}, f32[2,1,256,128]{3,2,1,0:T(8,128)S(1)}, u32[]{:S(2)}, u32[]{:S(2)}) %collective-permute-start.10) | collective-permute-done | bytes 262176 | tf_op jit(solution)/shard_map/ppermute | solution.py:22
  65.9 3.8 %collective-permute-done.5.refs_5_ = f32[2,1,256,128]{3,2,1,0:T(8,128)S(1)} collective-permute-done((f32[2,1,256,128]{3,2,1,0:T(8,128)S(1)}, f32[2,1,256,128]{3,2,1,0:T(8,128)S(1)}, u32[]{:S(2)}, u32[]{:S(2)}) %collective-permute-start.5) | collective-permute-done | bytes 262176 | tf_op jit(solution)/shard_map/ppermute | solution.py:22
  72.1 2.6 %collective-permute-start.13 = (f32[2,1,256,128]{3,2,1,0:T(8,128)S(1)}, f32[2,1,256,128]{3,2,1,0:T(8,128)S(1)}, u32[]{:S(2)}, u32[]{:S(2)}) collective-permute-start(f32[2,1,256,128]{3,2,1,0:T(8,128)S(1)} %shard_map.83.refs_2_), channel_id=1, source_target_pairs={{0,8},{4,12},{8,0},{12,4},{1,9},{5,13},{9,1},{13,5},{2,10},{6,14},... | collective-permute-start | bytes 786440 | tf_op jit(solution)/shard_map/ppermute | solution.py:22
  80.2 3.2 %shard_map.84 = (f32[4,128,256]{2,1,0:T(8,128)S(1)}, f32[3,128,256]{2,1,0:T(8,128)S(1)}) custom-call(s32[2]{0:T(128)S(1)} %compare_select_fusion.refs_0_.refs_1_, f32[2,1,512,2048]{3,2,1,0:T(8,128)S(1)} %bitcast.11, f32[2,1,256,128]{3,2,1,0:T(8,128)S(1)} %shard_map.83.refs_2_, f32[2,1,256,128]{3,2,1,0:T(8,128)S(1)} %shard_map.81.refs_3_), custom_call_target="tpu_custom_call" | custom-call | flops 2415919104 | bytes 2097152 | tf_op jit(solution)/shard_map/pallas_call | solution.py:308
  83.4 5.9 %collective-permute-done.13.refs_2_ = f32[2,1,256,128]{3,2,1,0:T(8,128)S(1)} collective-permute-done((f32[2,1,256,128]{3,2,1,0:T(8,128)S(1)}, f32[2,1,256,128]{3,2,1,0:T(8,128)S(1)}, u32[]{:S(2)}, u32[]{:S(2)}) %collective-permute-start.13) | collective-permute-done | bytes 262176 | tf_op jit(solution)/shard_map/ppermute | solution.py:22
  89.3 3.5 %collective-permute-start.14 = (f32[2,1,256,128]{3,2,1,0:T(8,128)S(1)}, f32[2,1,256,128]{3,2,1,0:T(8,128)S(1)}, u32[]{:S(2)}, u32[]{:S(2)}) collective-permute-start(f32[2,1,256,128]{3,2,1,0:T(8,128)S(1)} %collective-permute-done.13.refs_2_), channel_id=1, source_target_pairs={{0,4},{4,0},{8,12},{12,8},{1,5},{5,1},{9,13},{13,9},{2,6},{6,2},{1... | collective-permute-start | bytes 786440 | tf_op jit(solution)/shard_map/ppermute | solution.py:22
  92.8 7.7 %collective-permute-done.8.refs_2_.refs_3_ = f32[2,1,256,128]{3,2,1,0:T(8,128)S(1)} collective-permute-done((f32[2,1,256,128]{3,2,1,0:T(8,128)S(1)}, f32[2,1,256,128]{3,2,1,0:T(8,128)S(1)}, u32[]{:S(2)}, u32[]{:S(2)}) %collective-permute-start.8) | collective-permute-done | bytes 262176 | tf_op jit(solution)/shard_map/ppermute | solution.py:22
  100.5 3.5 %collective-permute-start.9 = (f32[2,1,256,128]{3,2,1,0:T(8,128)S(1)}, f32[2,1,256,128]{3,2,1,0:T(8,128)S(1)}, u32[]{:S(2)}, u32[]{:S(2)}) collective-permute-start(f32[2,1,256,128]{3,2,1,0:T(8,128)S(1)} %collective-permute-done.8.refs_2_.refs_3_), channel_id=1, source_target_pairs={{0,4},{4,0},{8,12},{12,8},{1,5},{5,1},{9,13},{13,9},{2,6},{6,2},{1... | collective-permute-start | bytes 786440 | tf_op jit(solution)/shard_map/ppermute | solution.py:22
  106.2 2.8 %shard_map.87 = (f32[4,128,256]{2,1,0:T(8,128)S(1)}, f32[3,128,256]{2,1,0:T(8,128)S(1)}, f32[1,128,256]{2,1,0:T(8,128)S(1)}, f32[1,128,256]{2,1,0:T(8,128)S(1)}) custom-call(s32[2]{0:T(128)S(1)} %compare_select_fusion.refs_0_.refs_1_, f32[2,1,512,2048]{3,2,1,0:T(8,128)S(1)} %bitcast.11, ...), custom_call_target="tpu_custom_call", output_to_operand_aliasing={{0}: (4, {}), {1}: (5, {}), {2}: (6, {}), {3}: (7, {})} | custom-call | flops 2013265920 | bytes 1048576 | tf_op jit(solution)/shard_map/pallas_call | solution.py:308
  111.1 2.8 %shard_map.89 = (f32[4,128,256]{2,1,0:T(8,128)S(1)}, f32[3,128,256]{2,1,0:T(8,128)S(1)}, f32[1,128,256]{2,1,0:T(8,128)S(1)}, f32[1,128,256]{2,1,0:T(8,128)S(1)}) custom-call(s32[2]{0:T(128)S(1)} %compare_select_fusion.refs_0_.refs_1_, f32[2,1,512,2048]{3,2,1,0:T(8,128)S(1)} %bitcast.11, ...), custom_call_target="tpu_custom_call", output_to_operand_aliasing={{0}: (5, {}), {1}: (6, {}), {2}: (7, {}), {3}: (8, {})} | custom-call | flops 2013265920 | bytes 1048576 | tf_op jit(solution)/shard_map/pallas_call | solution.py:308
  113.9 2.5 %shard_map.90 = (f32[4,128,256]{2,1,0:T(8,128)S(1)}, f32[3,128,256]{2,1,0:T(8,128)S(1)}, f32[1,128,256]{2,1,0:T(8,128)S(1)}) custom-call(s32[2]{0:T(128)S(1)} %compare_select_fusion.refs_0_.refs_1_, f32[2,1,512,2048]{3,2,1,0:T(8,128)S(1)} %bitcast.11, ...), custom_call_target="tpu_custom_call", output_to_operand_aliasing={{0}: (4, {}), {1}: (5, {}), {2}: (6, {})} | custom-call | flops 1610612736 | bytes 1048576 | tf_op jit(solution)/shard_map/pallas_call | solution.py:308
  122.7 5.7 %collective-permute-done.22.refs_5_ = f32[2,1,256,128]{3,2,1,0:T(8,128)S(1)} collective-permute-done((f32[2,1,256,128]{3,2,1,0:T(8,128)S(1)}, f32[2,1,256,128]{3,2,1,0:T(8,128)S(1)}, u32[]{:S(2)}, u32[]{:S(2)}) %collective-permute-start.22) | collective-permute-done | bytes 262176 | tf_op jit(solution)/shard_map/ppermute | solution.py:22
  128.9 3.7 %collective-permute-done.19.refs_5_ = f32[2,1,256,128]{3,2,1,0:T(8,128)S(1)} collective-permute-done((f32[2,1,256,128]{3,2,1,0:T(8,128)S(1)}, f32[2,1,256,128]{3,2,1,0:T(8,128)S(1)}, u32[]{:S(2)}, u32[]{:S(2)}) %collective-permute-start.19) | collective-permute-done | bytes 262176 | tf_op jit(solution)/shard_map/ppermute | solution.py:22
  134.1 2.9 %shard_map.94 = (f32[2,1,512,128]{3,2,1,0:T(8,128)}, f32[1,128,256]{2,1,0:T(8,128)S(1)}) custom-call(s32[2]{0:T(128)S(1)} %compare_select_fusion.refs_0_.refs_1_, f32[2,1,512,2048]{3,2,1,0:T(8,128)S(1)} %bitcast.11, f32[2,1,256,128]{3,2,1,0:T(8,128)S(1)} %collective-permute-done.9.refs_2_, ...), custom_call_target="tpu_custom_call", output_to_operand_aliasing={{1}: (5, {})} | custom-call | flops 1207959552 | bytes 1048576 | tf_op jit(solution)/shard_map/pallas_call | solution.py:308
  (78 shorter events, 46.0 us)
Async XLA Ops:
  0.6 34.4 %collective-permute-start.4 = (f32[2,1,512,128]{3,2,1,0:T(8,128)}, f32[2,1,512,128]{3,2,1,0:T(8,128)S(1)}, u32[]{:S(2)}, u32[]{:S(2)}) collective-permute-start(f32[2,1,512,128]{3,2,1,0:T(8,128)} %contact_ref.1), channel_id=1, source_target_pairs={{0,4},{4,0},{8,12},{12,8},{1,5},{5,1},{9,13},{13,9},{2,6},{6,2},{1... | collective-permute-start | bytes 1572872 | tf_op jit(solution)/shard_map/ppermute | solution.py:22
  5.7 16.3 %collective-permute-start.2 = (f32[2,1,256,128]{3,2,1,0:T(8,128)}, f32[2,1,256,128]{3,2,1,0:T(8,128)}, u32[]{:S(2)}, u32[]{:S(2)}) collective-permute-start(f32[2,1,256,128]{3,2,1,0:T(8,128)} %get-tuple-element.38), channel_id=1, source_target_pairs={{0,8},{4,12},{8,0},{12,4},{1,9},{5,13},{9,1},{13,5},{2,10},{6,14},... | collective-permute-start | bytes 786440 | tf_op jit(solution)/shard_map/ppermute | solution.py:22
  8.4 24.6 %collective-permute-start = (f32[2,1,256,128]{3,2,1,0:T(8,128)}, f32[2,1,256,128]{3,2,1,0:T(8,128)S(1)}, u32[]{:S(2)}, u32[]{:S(2)}) collective-permute-start(f32[2,1,256,128]{3,2,1,0:T(8,128)} %get-tuple-element.37), channel_id=1, source_target_pairs={{0,8},{4,12},{8,0},{12,4},{1,9},{5,13},{9,1},{13,5},{2,10},{6,14},... | collective-permute-start | bytes 786440 | tf_op jit(solution)/shard_map/ppermute | solution.py:22
  12.7 63.2 %collective-permute-start.15 = (f32[2,1,128,768]{3,2,1,0:T(8,128)}, f32[2,1,128,768]{3,2,1,0:T(8,128)S(1)}, u32[]{:S(2)}, u32[]{:S(2)}) collective-permute-start(f32[2,1,128,768]{3,2,1,0:T(8,128)} %pad_maximum_fusion), channel_id=1, source_target_pairs={{0,4},{4,0},{8,12},{12,8},{1,5},{5,1},{9,13},{13,9},{2,6},{6,2},{1... | collective-permute-start | bytes 2359304 | tf_op jit(solution)/shard_map/ppermute | solution.py:493
  15.3 61.2 %collective-permute-start.17 = (f32[2,1,128,1024]{3,2,1,0:T(8,128)}, f32[2,1,128,1024]{3,2,1,0:T(8,128)S(1)}, u32[]{:S(2)}, u32[]{:S(2)}) collective-permute-start(f32[2,1,128,1024]{3,2,1,0:T(8,128)} %constant_dynamic-slice_fusion.1), channel_id=1, source_target_pairs={{4,8},{8,4},{5,9},{9,5},{6,10},{10,6},{7,11},{11,7},{20,24},{24,20... | collective-permute-start | bytes 3145736 | tf_op jit(solution)/shard_map/ppermute | solution.py:493
  22.0 28.4 %collective-permute-start.3 = (f32[2,1,256,128]{3,2,1,0:T(8,128)}, f32[2,1,256,128]{3,2,1,0:T(8,128)S(1)}, u32[]{:S(2)}, u32[]{:S(2)}) collective-permute-start(f32[2,1,256,128]{3,2,1,0:T(8,128)} %collective-permute-done.2.refs_2_), channel_id=1, source_target_pairs={{0,4},{4,0},{8,12},{12,8},{1,5},{5,1},{9,13},{13,9},{2,6},{6,2},{1... | collective-permute-start | bytes 786440 | tf_op jit(solution)/shard_map/ppermute | solution.py:22
  32.9 22.3 %collective-permute-start.1 = (f32[2,1,256,128]{3,2,1,0:T(8,128)S(1)}, f32[2,1,256,128]{3,2,1,0:T(8,128)S(1)}, u32[]{:S(2)}, u32[]{:S(2)}) collective-permute-start(f32[2,1,256,128]{3,2,1,0:T(8,128)S(1)} %collective-permute-done.refs_3_), channel_id=1, source_target_pairs={{0,4},{4,0},{8,12},{12,8},{1,5},{5,1},{9,13},{13,9},{2,6},{6,2},{1... | collective-permute-start | bytes 786440 | tf_op jit(solution)/shard_map/ppermute | solution.py:22
  56.6 8.8 %collective-permute-start.10 = (f32[2,1,256,128]{3,2,1,0:T(8,128)S(1)}, f32[2,1,256,128]{3,2,1,0:T(8,128)S(1)}, u32[]{:S(2)}, u32[]{:S(2)}) collective-permute-start(f32[2,1,256,128]{3,2,1,0:T(8,128)S(1)} %shard_map.82), channel_id=1, source_target_pairs={{0,2},{1,3},{2,0},{3,1},{4,6},{5,7},{6,4},{7,5},{8,10},{9,11},{10,... | collective-permute-start | bytes 786440 | tf_op jit(solution)/shard_map/ppermute | solution.py:22
  58.3 7.1 %collective-permute-start.11 = (f32[2,1,256,128]{3,2,1,0:T(8,128)S(1)}, f32[2,1,256,128]{3,2,1,0:T(8,128)S(1)}, u32[]{:S(2)}, u32[]{:S(2)}) collective-permute-start(f32[2,1,256,128]{3,2,1,0:T(8,128)S(1)} %shard_map.82), channel_id=1, source_target_pairs={{0,1},{1,0},{2,3},{3,2},{4,5},{5,4},{6,7},{7,6},{8,9},{9,8},{10,11... | collective-permute-start | bytes 786440 | tf_op jit(solution)/shard_map/ppermute | solution.py:22
  59.7 10.1 %collective-permute-start.5 = (f32[2,1,256,128]{3,2,1,0:T(8,128)S(1)}, f32[2,1,256,128]{3,2,1,0:T(8,128)S(1)}, u32[]{:S(2)}, u32[]{:S(2)}) collective-permute-start(f32[2,1,256,128]{3,2,1,0:T(8,128)S(1)} %shard_map.80), channel_id=1, source_target_pairs={{0,2},{1,3},{2,0},{3,1},{4,6},{5,7},{6,4},{7,5},{8,10},{9,11},{10,... | collective-permute-start | bytes 786440 | tf_op jit(solution)/shard_map/ppermute | solution.py:22
  69.7 62.9 %collective-permute-start.25 = (f32[2,1,128,512]{3,2,1,0:T(8,128)S(1)}, f32[2,1,128,512]{3,2,1,0:T(8,128)S(1)}, u32[]{:S(2)}, u32[]{:S(2)}) collective-permute-start(f32[2,1,128,512]{3,2,1,0:T(8,128)S(1)} %copy-done.3), channel_id=1, source_target_pairs={{0,4},{4,0},{8,12},{12,8},{1,5},{5,1},{9,13},{13,9},{2,6},{6,2},{1... | collective-permute-start | bytes 1572872 | tf_op jit(solution)/shard_map/ppermute | solution.py:22
  72.1 17.2 %collective-permute-start.13 = (f32[2,1,256,128]{3,2,1,0:T(8,128)S(1)}, f32[2,1,256,128]{3,2,1,0:T(8,128)S(1)}, u32[]{:S(2)}, u32[]{:S(2)}) collective-permute-start(f32[2,1,256,128]{3,2,1,0:T(8,128)S(1)} %shard_map.83.refs_2_), channel_id=1, source_target_pairs={{0,8},{4,12},{8,0},{12,4},{1,9},{5,13},{9,1},{13,5},{2,10},{6,14},... | collective-permute-start | bytes 786440 | tf_op jit(solution)/shard_map/ppermute | solution.py:22
  74.7 31.5 %collective-permute-start.18 = (f32[2,1,256,128]{3,2,1,0:T(8,128)S(1)}, f32[2,1,256,128]{3,2,1,0:T(8,128)S(1)}, u32[]{:S(2)}, u32[]{:S(2)}) collective-permute-start(f32[2,1,256,128]{3,2,1,0:T(8,128)S(1)} %shard_map.83.refs_2_), channel_id=1, source_target_pairs={{0,4},{4,0},{8,12},{12,8},{1,5},{5,1},{9,13},{13,9},{2,6},{6,2},{1... | collective-permute-start | bytes 786440 | tf_op jit(solution)/shard_map/ppermute | solution.py:22
  76.0 24.5 %collective-permute-start.8 = (f32[2,1,256,128]{3,2,1,0:T(8,128)S(1)}, f32[2,1,256,128]{3,2,1,0:T(8,128)S(1)}, u32[]{:S(2)}, u32[]{:S(2)}) collective-permute-start(f32[2,1,256,128]{3,2,1,0:T(8,128)S(1)} %shard_map.81.refs_3_), channel_id=1, source_target_pairs={{0,8},{4,12},{8,0},{12,4},{1,9},{5,13},{9,1},{13,5},{2,10},{6,14},... | collective-permute-start | bytes 786440 | tf_op jit(solution)/shard_map/ppermute | solution.py:22
  76.5 34.7 %collective-permute-start.16 = (f32[2,1,256,128]{3,2,1,0:T(8,128)S(1)}, f32[2,1,256,128]{3,2,1,0:T(8,128)S(1)}, u32[]{:S(2)}, u32[]{:S(2)}) collective-permute-start(f32[2,1,256,128]{3,2,1,0:T(8,128)S(1)} %shard_map.81.refs_3_), channel_id=1, source_target_pairs={{0,4},{4,0},{8,12},{12,8},{1,5},{5,1},{9,13},{13,9},{2,6},{6,2},{1... | collective-permute-start | bytes 786440 | tf_op jit(solution)/shard_map/ppermute | solution.py:22
  89.3 24.6 %collective-permute-start.14 = (f32[2,1,256,128]{3,2,1,0:T(8,128)S(1)}, f32[2,1,256,128]{3,2,1,0:T(8,128)S(1)}, u32[]{:S(2)}, u32[]{:S(2)}) collective-permute-start(f32[2,1,256,128]{3,2,1,0:T(8,128)S(1)} %collective-permute-done.13.refs_2_), channel_id=1, source_target_pairs={{0,4},{4,0},{8,12},{12,8},{1,5},{5,1},{9,13},{13,9},{2,6},{6,2},{1... | collective-permute-start | bytes 786440 | tf_op jit(solution)/shard_map/ppermute | solution.py:22
  100.5 17.2 %collective-permute-start.9 = (f32[2,1,256,128]{3,2,1,0:T(8,128)S(1)}, f32[2,1,256,128]{3,2,1,0:T(8,128)S(1)}, u32[]{:S(2)}, u32[]{:S(2)}) collective-permute-start(f32[2,1,256,128]{3,2,1,0:T(8,128)S(1)} %collective-permute-done.8.refs_2_.refs_3_), channel_id=1, source_target_pairs={{0,4},{4,0},{8,12},{12,8},{1,5},{5,1},{9,13},{13,9},{2,6},{6,2},{1... | collective-permute-start | bytes 786440 | tf_op jit(solution)/shard_map/ppermute | solution.py:22
  119.1 9.2 %collective-permute-start.22 = (f32[2,1,256,128]{3,2,1,0:T(8,128)S(1)}, f32[2,1,256,128]{3,2,1,0:T(8,128)S(1)}, u32[]{:S(2)}, u32[]{:S(2)}) collective-permute-start(f32[2,1,256,128]{3,2,1,0:T(8,128)S(1)} %shard_map.92.refs_9_), channel_id=1, source_target_pairs={{0,2},{1,3},{2,0},{3,1},{4,6},{5,7},{6,4},{7,5},{8,10},{9,11},{10,... | collective-permute-start | bytes 786440 | tf_op jit(solution)/shard_map/ppermute | solution.py:22
  122.0 10.7 %collective-permute-start.19 = (f32[2,1,256,128]{3,2,1,0:T(8,128)S(1)}, f32[2,1,256,128]{3,2,1,0:T(8,128)S(1)}, u32[]{:S(2)}, u32[]{:S(2)}) collective-permute-start(f32[2,1,256,128]{3,2,1,0:T(8,128)S(1)} %shard_map.91.refs_10_), channel_id=1, source_target_pairs={{0,2},{1,3},{2,0},{3,1},{4,6},{5,7},{6,4},{7,5},{8,10},{9,11},{10,... | collective-permute-start | bytes 786440 | tf_op jit(solution)/shard_map/ppermute | solution.py:22
  122.7 15.8 %collective-permute-start.23 = (f32[2,1,256,128]{3,2,1,0:T(8,128)S(1)}, f32[2,1,256,128]{3,2,1,0:T(8,128)S(1)}, u32[]{:S(2)}, u32[]{:S(2)}) collective-permute-start(f32[2,1,256,128]{3,2,1,0:T(8,128)S(1)} %shard_map.92.refs_9_), channel_id=1, source_target_pairs={{0,1},{1,0},{2,3},{3,2},{4,5},{5,4},{6,7},{7,6},{8,9},{9,8},{10,11... | collective-permute-start | bytes 786440 | tf_op jit(solution)/shard_map/ppermute | solution.py:22
  128.4 10.1 %collective-permute-start.24 = (f32[2,1,256,128]{3,2,1,0:T(8,128)S(1)}, f32[2,1,256,128]{3,2,1,0:T(8,128)S(1)}, u32[]{:S(2)}, u32[]{:S(2)}) collective-permute-start(f32[2,1,256,128]{3,2,1,0:T(8,128)S(1)} %collective-permute-done.22.refs_5_), channel_id=1, source_target_pairs={{0,1},{1,0},{2,3},{3,2},{4,5},{5,4},{6,7},{7,6},{8,9},{9,8},{10,11... | collective-permute-start | bytes 786440 | tf_op jit(solution)/shard_map/ppermute | solution.py:22
  128.4 12.0 %collective-permute-start.20 = (f32[2,1,256,128]{3,2,1,0:T(8,128)S(1)}, f32[2,1,256,128]{3,2,1,0:T(8,128)S(1)}, u32[]{:S(2)}, u32[]{:S(2)}) collective-permute-start(f32[2,1,256,128]{3,2,1,0:T(8,128)S(1)} %shard_map.91.refs_10_), channel_id=1, source_target_pairs={{0,1},{1,0},{2,3},{3,2},{4,5},{5,4},{6,7},{7,6},{8,9},{9,8},{10,11... | collective-permute-start | bytes 786440 | tf_op jit(solution)/shard_map/ppermute | solution.py:22
  132.6 7.8 %collective-permute-start.21 = (f32[2,1,256,128]{3,2,1,0:T(8,128)S(1)}, f32[2,1,256,128]{3,2,1,0:T(8,128)S(1)}, u32[]{:S(2)}, u32[]{:S(2)}) collective-permute-start(f32[2,1,256,128]{3,2,1,0:T(8,128)S(1)} %collective-permute-done.19.refs_5_), channel_id=1, source_target_pairs={{0,1},{1,0},{2,3},{3,2},{4,5},{5,4},{6,7},{7,6},{8,9},{9,8},{10,11... | collective-permute-start | bytes 786440 | tf_op jit(solution)/shard_map/ppermute | solution.py:22
  132.6 7.8 %collective-permute-start.26 = (f32[1,128,256]{2,1,0:T(8,128)S(1)}, f32[1,128,256]{2,1,0:T(8,128)S(1)}, u32[]{:S(2)}, u32[]{:S(2)}) collective-permute-start(f32[1,128,256]{2,1,0:T(8,128)S(1)} %get-tuple-element.59), channel_id=1, source_target_pairs={{4,0},{8,4},{12,8},{5,1},{9,5},{13,9},{6,2},{10,6},{14,10},{7,3},{... | collective-permute-start | bytes 393224 | tf_op jit(solution)/shard_map/ppermute | solution.py:583
  (9 other events, 99.9 us)
